TPU v7x, 256 devices: a whole 4x4x8 slice. The times are simulated.
256 devices in a mesh: seq: 32 (over x, z_hi, y), tp: 8 (over z_lo, core).
Axes of the slice: x: 4, y: 4, z: 8 (z_hi: 2, z_lo: 4; z = z_hi * 4 + z_lo), core: 2. Of those that a mesh axis runs over, the one named last changes fastest.
Arguments:
- residual: bfloat16 [4096, 1024], P(('seq', 'tp')), may hold values from -6 to 6
- queries: bfloat16 [2, 4096, 1024], P(None, 'seq', 'tp'), may hold values from -41 to 41
- keys: bfloat16 [2, 4096, 1024], P(None, 'seq', 'tp'), may hold values from -5.1 to 5.1
- values: bfloat16 [2, 4096, 1024], P(None, 'seq', 'tp'), may hold values from -6 to 6
- slopes: float32 [16], P('tp'), may hold values from 0.002 to 0.1
- out_weight: bfloat16 [1024, 1024], P('tp'), may hold values from -0.1875 to 0.1875
- cotangent: bfloat16 [4096, 1024], P(('seq', 'tp')), may hold values from -6 to 6
- far_blocks: int32 [32, 24], replicated, may hold values from -1 to 63, as said below
- far_count: int32 [32], replicated, may hold values from 8 to 24, as said below
Outputs:
- mixed: bfloat16 [4096, 1024], P(('seq', 'tp'))
- grad_queries: bfloat16 [2, 4096, 1024], P(None, 'seq', 'tp')
- grad_keys: bfloat16 [2, 4096, 1024], P(None, 'seq', 'tp')
- grad_values: bfloat16 [2, 4096, 1024], P(None, 'seq', 'tp')
Inputs may be any that keep to these rules, and one draw needn't show every extreme that they name: `far_blocks`: row s holds, in its first far_count[s] entries, global key blocks of 64 positions on distinct shards, none of them on shard s - 1, s or s + 1; the remaining entries are -1. `far_count`: some shard lists exactly 24 blocks.
All inputs are finite; a program needn't handle non-finite values.
Results may differ from a plain program's by a relative error of at most 0.01.
Values may be sent and summed in bfloat16 or wider, within the bound.
No kernel may reach another device: no remote copies, remote signals or barrier semaphores. Data moves between devices by JAX's collectives and lax.ppermute only.
A program may use at most 128 MiB of HBM per device.

v0:
```python
import functools

import jax
import jax.numpy as jnp
from jax import lax
from jax.experimental import pallas as pl
from jax.experimental.pallas import tpu as pltpu
from jax.sharding import PartitionSpec as P

HD = 64
BLK = 64
BAND = 2

masked_value = -1e30
f32 = jnp.float32
bf16 = jnp.bfloat16

NT = (((1,), (1,)), ((), ()))
NN = (((1,), (0,)), ((), ()))


def dot(a, b, dims):
    return lax.dot_general(a, b, dims, preferred_element_type=f32)


def two_heads(x):
    first = lax.broadcasted_iota(jnp.int32, x.shape, 1) < HD
    zero = jnp.zeros_like(x)
    return jnp.concatenate([jnp.where(first, x, zero), jnp.where(first, zero, x)], axis=0)


def pick_heads(xt):
    rows = xt.shape[1] // 2
    own = jnp.concatenate([xt[:HD, :rows], xt[HD:, rows:]], axis=0)
    return own.T


def flipped(x):
    n = x.shape[0]
    there = lax.broadcasted_iota(jnp.int32, (n, n), 0) + lax.broadcasted_iota(jnp.int32, (n, n), 1)
    return dot((there == n - 1).astype(bf16), x, NN).astype(bf16)


def stage(meta, slot_ref, own_ref, prev_ref, next_ref, far_ref, kbuf, vbuf):
    for which, buf in ((0, kbuf), (1, vbuf)):
        buf[0:128] = prev_ref[which]
        buf[128:256] = own_ref[which]
        buf[256:384] = next_ref[which]
        for f in range(slot_ref.shape[0]):
            buf[384 + f * BLK : 384 + (f + 1) * BLK] = far_ref[slot_ref[f], which]


def biased(meta, slopes_ref, q2, kbuf, put):
    shard, shards, count = meta[0], meta[1], meta[2]
    cols = q2.shape[0]
    half = cols // 2
    head_col = lax.broadcasted_iota(jnp.int32, (1, cols), 1)
    slope = jnp.where(head_col < half, slopes_ref[0], slopes_ref[1])
    r = lax.broadcasted_iota(jnp.int32, (384, cols), 0)
    c = lax.broadcasted_iota(jnp.int32, (384, cols), 1)
    c = jnp.where(c < half, c, c - half)
    delta = r - 128 - c
    low = jnp.where(shard > 0, 0, 128)
    high = jnp.where(shard < shards - 1, 384, 256)
    edge = jnp.where(c < BLK, 0, BLK)
    ok = (r >= jnp.maximum(edge, low)) & (r < jnp.minimum(edge + 320, high))
    scores = dot(kbuf[0:384], q2, NT) - slope * jnp.abs(delta).astype(f32)
    scores = jnp.where(ok, scores, masked_value)
    put(0, 384, scores)
    top = jnp.max(scores, axis=0, keepdims=True)
    far_bias = slope * (-float((BAND + 1) * BLK))
    total = kbuf.shape[0]
    step = 384
    for lo in range(384, total, step):
        scores = dot(kbuf[lo : lo + step], q2, NT)
        parts = []
        for i in range(step // BLK):
            f = (lo - 384) // BLK + i
            row = jnp.where(f < count, far_bias, masked_value)
            parts.append(scores[i * BLK : (i + 1) * BLK] + row)
        scores = jnp.concatenate(parts, axis=0)
        put(lo, lo + step, scores)
        top = jnp.maximum(top, jnp.max(scores, axis=0, keepdims=True))
    return top


def forward_kernel(flip, meta, slot_ref, slopes_ref, q_ref, own_ref, prev_ref, next_ref, far_ref, ctx_ref, stat_ref, kbuf, vbuf, sbuf):
    stage(meta, slot_ref, own_ref, prev_ref, next_ref, far_ref, kbuf, vbuf)
    q2 = two_heads(q_ref[...] * HD ** (-0.5))

    def put(lo, hi, scores):
        sbuf[lo:hi] = scores

    top = biased(meta, slopes_ref, q2, kbuf, put)
    total = kbuf.shape[0]
    norm = jnp.zeros_like(top)
    for lo in range(0, total, 384):
        w = jnp.exp(sbuf[lo : lo + 384] - top)
        sbuf[lo : lo + 384] = w
        norm = norm + jnp.sum(w, axis=0, keepdims=True)
    inv = 1.0 / norm
    stat_ref[0:1] = top
    stat_ref[1:2] = inv
    n = 2 * HD
    eye = (lax.broadcasted_iota(jnp.int32, (n, n), 0) == lax.broadcasted_iota(jnp.int32, (n, n), 1)).astype(bf16)
    acc = jnp.zeros((n, q2.shape[0]), f32)
    for lo in range(0, total, 384):
        low = (sbuf[lo : lo + 384] * inv).astype(bf16)
        vt = dot(eye, vbuf[lo : lo + 384], NT).astype(bf16)
        acc = acc + dot(vt, low, NN)
    ctx = pick_heads(acc).astype(bf16)
    ctx_ref[...] = flipped(ctx) if flip else ctx


def backward_kernel(
    flip, meta, slot_ref, slopes_ref, q_ref, own_ref, prev_ref, next_ref, far_ref, stat_ref, grad_ref,
    gq_ref, own_out, prev_out, next_out, far_out, kbuf, vbuf, pbuf, gbuf,
):
    stage(meta, slot_ref, own_ref, prev_ref, next_ref, far_ref, kbuf, vbuf)
    q2 = two_heads(q_ref[...] * HD ** (-0.5))
    grad = grad_ref[...]
    g2 = two_heads(flipped(grad) if flip else grad)
    total = kbuf.shape[0]
    cols = q2.shape[0]
    top = stat_ref[0:1]
    inv = stat_ref[1:2]

    def put(lo, hi, scores):
        pbuf[lo:hi] = jnp.exp(scores - top) * inv

    biased(meta, slopes_ref, q2, kbuf, put)
    row_dot = jnp.zeros((1, cols), f32)
    for lo in range(0, total, 384):
        gp = dot(vbuf[lo : lo + 384], g2, NT)
        gbuf[lo : lo + 384] = gp
        row_dot = row_dot + jnp.sum(pbuf[lo : lo + 384] * gp, axis=0, keepdims=True)
    n = 2 * HD
    eye = (lax.broadcasted_iota(jnp.int32, (n, n), 0) == lax.broadcasted_iota(jnp.int32, (n, n), 1)).astype(bf16)
    acc = jnp.zeros((n, cols), f32)
    for lo in range(0, total, 384):
        p = pbuf[lo : lo + 384]
        ds = (p * (gbuf[lo : lo + 384] - row_dot)).astype(bf16)
        kt = dot(eye, kbuf[lo : lo + 384], NT).astype(bf16)
        acc = acc + dot(kt, ds, NN)
        for which, x in ((0, dot(ds, q2, NN)), (1, dot(p.astype(bf16), g2, NN))):
            if lo == 0:
                prev_out[which] = x[0:128].astype(bf16)
                own_out[which] = x[128:256]
                next_out[which] = x[256:384].astype(bf16)
            else:
                low = x.astype(bf16)
                for i in range(384 // BLK):
                    f = (lo - 384) // BLK + i

                    @pl.when(f < meta[2])
                    def _():
                        far_out[slot_ref[f], which] = low[i * BLK : (i + 1) * BLK]

    gq_ref[...] = (pick_heads(acc) * HD ** (-0.5)).astype(bf16)


def combine_kernel(blk_ref, own_ref, prev_ref, next_ref, far_ref, out_ref):
    for t in range(2):
        for which in range(2):
            for lo in range(0, BLK, 32):
                first = jnp.zeros((32, 2 * HD), f32)
                second = jnp.zeros((32, 2 * HD), f32)
                for d in range(far_ref[0].shape[0]):
                    x = far_ref[t][d, which, lo : lo + 32].astype(f32)
                    first = first + jnp.where(blk_ref[t, d] == 0, x, 0.0)
                    second = second + jnp.where(blk_ref[t, d] == 1, x, 0.0)
                for at, far in ((lo, first), (BLK + lo, second)):
                    rows = slice(at, at + 32)
                    total = own_ref[t][which, rows] + prev_ref[t, which, rows].astype(f32)
                    total = total + next_ref[t, which, rows].astype(f32)
                    out_ref[which, t, rows] = (total + far).astype(bf16)


def smem():
    return pl.BlockSpec(memory_space=pltpu.SMEM)


def vmem():
    return pl.BlockSpec(memory_space=pltpu.VMEM)


def per_device(
    residual, queries, keys, values, slopes, out_weight, cotangent, far_blocks, far_count
):
    seq_count = lax.axis_size("seq")
    tp_count = lax.axis_size("tp")
    seq_index = lax.axis_index("seq")
    tok_rows = queries.shape[1]
    width_here = queries.shape[2]
    per_shard = tok_rows // BLK
    total_blocks = per_shard * seq_count
    nfar = far_blocks.shape[1]
    total_keys = 3 * tok_rows + nfar * BLK
    model = out_weight.shape[1]

    block_lists = jnp.stack([far_blocks, total_blocks - 1 - far_blocks[::-1]])
    list_counts = jnp.stack([far_count, far_count[::-1]])
    listed_ok = jnp.arange(nfar)[None, None, :] < list_counts[:, :, None]
    owners = jnp.where(listed_ok, block_lists // per_shard, -1)
    asked_me = owners == seq_index
    asked_block = jnp.sum(jnp.where(asked_me, block_lists % per_shard + 1, 0), axis=2) - 1
    mine = jnp.maximum(jnp.take(owners, seq_index, axis=1), 0).astype(jnp.int32)
    counts = jnp.take(list_counts, seq_index, axis=1).astype(jnp.int32)

    key_value = jnp.stack([keys, values], axis=1)
    blocks = key_value.reshape(2, 2, per_shard, BLK, width_here)

    def far_of(t):
        second = (asked_block[t] == 1)[:, None, None, None]
        outgoing = jnp.where(second, blocks[t, :, 1][None], blocks[t, :, 0][None])
        return lax.all_to_all(outgoing, "seq", split_axis=0, concat_axis=0, tiled=True)

    far = [far_of(0), far_of(1)]
    up = [(i, i + 1) for i in range(seq_count - 1)]
    down = [(j, i) for i, j in up]
    from_prev = lax.ppermute(key_value, "seq", up)
    from_next = lax.ppermute(key_value, "seq", down)

    mirror = [(i, seq_count - 1 - i) for i in range(seq_count)]
    copies = jnp.broadcast_to(cotangent[None], (tp_count,) + cotangent.shape)
    cot_rows = lax.all_to_all(copies, "tp", split_axis=0, concat_axis=0, tiled=True)
    grad_context = lax.dot_general(
        cot_rows.reshape(tok_rows, model), out_weight, NT, preferred_element_type=f32
    ).astype(bf16)
    grads = [grad_context, lax.ppermute(grad_context, "seq", mirror)]

    metas = [
        jnp.stack([seq_index, seq_count, counts[t]]).astype(jnp.int32) for t in range(2)
    ]
    square = jax.ShapeDtypeStruct((tok_rows, width_here), bf16)
    pair = (2, tok_rows, width_here)
    cols = 2 * tok_rows

    def forward(t):
        return pl.pallas_call(
            functools.partial(forward_kernel, t == 1),
            out_shape=(square, jax.ShapeDtypeStruct((2, cols), f32)),
            in_specs=[smem()] * 3 + [vmem()] * 5,
            out_specs=(vmem(), vmem()),
            scratch_shapes=[
                pltpu.VMEM((total_keys, width_here), bf16),
                pltpu.VMEM((total_keys, width_here), bf16),
                pltpu.VMEM((total_keys, cols), f32),
            ],
            cost_estimate=pl.CostEstimate(flops=800_000_000, bytes_accessed=2_000_000, transcendentals=500_000),
            name="attend_forward",
        )(metas[t], mine[t], slopes, queries[t], key_value[t], from_prev[t], from_next[t], far[t])

    def backward(t, stats):
        return pl.pallas_call(
            functools.partial(backward_kernel, t == 1),
            out_shape=(
                square,
                jax.ShapeDtypeStruct(pair, f32),
                jax.ShapeDtypeStruct(pair, bf16),
                jax.ShapeDtypeStruct(pair, bf16),
                jax.ShapeDtypeStruct((seq_count, 2, BLK, width_here), bf16),
            ),
            in_specs=[smem()] * 3 + [vmem()] * 7,
            out_specs=(vmem(),) * 5,
            scratch_shapes=[
                pltpu.VMEM((total_keys, width_here), bf16),
                pltpu.VMEM((total_keys, width_here), bf16),
                pltpu.VMEM((total_keys, cols), f32),
                pltpu.VMEM((total_keys, cols), f32),
            ],
            cost_estimate=pl.CostEstimate(flops=1_600_000_000, bytes_accessed=4_000_000, transcendentals=500_000),
            name="attend_backward",
        )(metas[t], mine[t], slopes, queries[t], key_value[t], from_prev[t], from_next[t], far[t], stats, grads[t])

    context_fwd, stats_fwd = forward(0)
    context_rev, stats_rev = forward(1)
    context_back = lax.ppermute(context_rev, "seq", mirror)

    gq0, own0, prev0, next0, far0 = backward(0, stats_fwd)
    back0 = lax.all_to_all(far0, "seq", split_axis=0, concat_axis=0, tiled=True)
    gq1, own1, prev1, next1, far1 = backward(1, stats_rev)
    back1 = lax.all_to_all(far1, "seq", split_axis=0, concat_axis=0, tiled=True)

    context_sum = (context_fwd.astype(f32) + context_back.astype(f32)).astype(bf16)
    partial = jnp.dot(context_sum, out_weight, preferred_element_type=f32).astype(bf16)
    pieces = lax.all_to_all(
        partial.reshape(tp_count, tok_rows // tp_count, model), "tp", split_axis=0, concat_axis=0, tiled=True
    )
    mixed = (residual.astype(f32) + jnp.sum(pieces.astype(f32), axis=0)).astype(bf16)

    to_owner_next = lax.ppermute(jnp.stack([next0, next1]), "seq", up)
    to_owner_prev = lax.ppermute(jnp.stack([prev0, prev1]), "seq", down)
    totals = pl.pallas_call(
        lambda b, o0, o1, p, n, f0, f1, out: combine_kernel(b, (o0, o1), p, n, (f0, f1), out),
        out_shape=jax.ShapeDtypeStruct((2,) + pair, bf16),
        in_specs=[smem()] + [vmem()] * 6,
        out_specs=vmem(),
        cost_estimate=pl.CostEstimate(flops=4_000_000, bytes_accessed=3_000_000, transcendentals=0),
        name="combine",
    )(asked_block, own0, own1, to_owner_next, to_owner_prev, back0, back1)
    return (mixed, jnp.stack([gq0, gq1]), totals[0], totals[1])


def solution(mesh):
    return jax.shard_map(
        per_device,
        mesh=mesh,
        in_specs=(
            P(("seq", "tp"), None),
            P(None, "seq", "tp"),
            P(None, "seq", "tp"),
            P(None, "seq", "tp"),
            P("tp"),
            P("tp", None),
            P(("seq", "tp"), None),
            P(),
            P(),
        ),
        out_specs=(
            P(("seq", "tp"), None),
            P(None, "seq", "tp"),
            P(None, "seq", "tp"),
            P(None, "seq", "tp"),
        ),
        check_vma=False,
    )
```

profile of v0, /device:TPU:38, one launch (start us, length us, event | category | flops | bytes accessed | tf_op | source)
XLA Modules:
  0.0 207.7 jit_solution(7851155724478672406)
XLA Ops:
  4.4 1.1 broadcast_select_fusion
  5.5 13.3 %all-to-all-start.1 = ((bf16[32,2,64,128]{3,2,1,0:T(8,128)(2,1)}), bf16[32,2,64,128]{3,2,1,0:T(8,128)(2,1)S(1)}, u32[]{:S(2)}, u32[]{:S(2)}) async-start(bf16[32,2,64,128]{3,2,1,0:T(8,128)(2,1)} %broadcast_select_fusion), calls=%async_computation.1 | async-start | bytes 2097152 | tf_op jit(solution)/shard_map/all_to_all | solution.py:216
  18.9 1.1 broadcast_select_fusion.1
  20.0 28.9 %all-to-all-done.1.far_ref = bf16[32,2,64,128]{3,2,1,0:T(8,128)(2,1)S(1)} async-done(((bf16[32,2,64,128]{3,2,1,0:T(8,128)(2,1)}), bf16[32,2,64,128]{3,2,1,0:T(8,128)(2,1)S(1)}, u32[]{:S(2)}, u32[]{:S(2)}) %all-to-all-start.1) | async-done | bytes 1048608 | tf_op jit(solution)/shard_map/all_to_all | solution.py:216
  48.8 1.0 copy-done.3
  49.8 6.4 %all-to-all-start = ((bf16[32,2,64,128]{3,2,1,0:T(8,128)(2,1)}), bf16[32,2,64,128]{3,2,1,0:T(8,128)(2,1)S(1)}, u32[]{:S(2)}, u32[]{:S(2)}) async-start(bf16[32,2,64,128]{3,2,1,0:T(8,128)(2,1)} %broadcast_select_fusion.1), calls=%async_computation | async-start | bytes 2097152 | tf_op jit(solution)/shard_map/all_to_all | solution.py:216
  56.3 3.4 %collective-permute-start = (bf16[2,2,128,128]{3,2,1,0:T(8,128)(2,1)S(1)}, bf16[2,2,128,128]{3,2,1,0:T(8,128)(2,1)S(1)}, u32[]{:S(2)}, u32[]{:S(2)}) collective-permute-start(bf16[2,2,128,128]{3,2,1,0:T(8,128)(2,1)S(1)} %pad_maximum_fusion), channel_id=1, source_target_pairs={{0,8},{8,16},{16,24},{24,32},{32,40},{40,48},{48,56},{56,64},{64,7... | collective-permute-start | bytes 393224 | tf_op jit(solution)/shard_map/ppermute | solution.py:221
  59.7 9.4 %collective-permute-start.1 = (bf16[2,2,128,128]{3,2,1,0:T(8,128)(2,1)S(1)}, bf16[2,2,128,128]{3,2,1,0:T(8,128)(2,1)S(1)}, u32[]{:S(2)}, u32[]{:S(2)}) collective-permute-start(bf16[2,2,128,128]{3,2,1,0:T(8,128)(2,1)S(1)} %pad_maximum_fusion), channel_id=1, source_target_pairs={{8,0},{16,8},{24,16},{32,24},{40,32},{48,40},{56,48},{64,56},{72,6... | collective-permute-start | bytes 393224 | tf_op jit(solution)/shard_map/ppermute | solution.py:222
  70.1 1.2 pad_add_fusion.4.meta
  72.5 1.2 pad_add_fusion.2.meta
  74.4 9.6 %collective-permute-done = bf16[2,2,128,128]{3,2,1,0:T(8,128)(2,1)S(1)} collective-permute-done((bf16[2,2,128,128]{3,2,1,0:T(8,128)(2,1)S(1)}, bf16[2,2,128,128]{3,2,1,0:T(8,128)(2,1)S(1)}, u32[]{:S(2)}, u32[]{:S(2)}) %collective-permute-start) | collective-permute-done | bytes 131104 | tf_op jit(solution)/shard_map/ppermute | solution.py:221
  84.6 0.8 broadcast_in_dim.92
  85.4 3.8 %all-to-all-start.3 = ((bf16[8,16,1024]{2,1,0:T(8,128)(2,1)}), bf16[8,16,1024]{2,1,0:T(8,128)(2,1)S(1)}, u32[]{:S(2)}, u32[]{:S(2)}) async-start(bf16[8,16,1024]{2,1,0:T(8,128)(2,1)} %broadcast_in_dim.92), calls=%async_computation.3 | async-start | bytes 524288 | tf_op jit(solution)/shard_map/all_to_all | solution.py:226
  89.9 3.7 %attend_forward.3 = (bf16[128,128]{1,0:T(8,128)(2,1)}, f32[2,256]{1,0:T(2,128)}) custom-call(s32[3]{0:T(128)} %pad_add_fusion.4.meta, s32[24]{0:T(128)} %get-tuple-element.73.slot_ref, f32[2]{0:T(128)} %slopes_ref.7, bf16[128,128]{1,0:T(8,128)(2,1)} %get-tuple-element.69.q_ref, bf16[2,128,128]{2,1,0:T(8,128)(2,1)} %get-tuple-element.67.own_ref, ...), custom_call_target="tpu_custom_call" | custom-call | flops 800000000 | bytes 2000000 | tf_op jit(solution)/shard_map/attend_forward/pallas_call | solution.py:240
  93.5 3.5 %attend_forward.2 = (bf16[128,128]{1,0:T(8,128)(2,1)}, f32[2,256]{1,0:T(2,128)}) custom-call(s32[3]{0:T(128)} %pad_add_fusion.2.meta, s32[24]{0:T(128)} %get-tuple-element.72.slot_ref, f32[2]{0:T(128)} %slopes_ref.7, bf16[128,128]{1,0:T(8,128)(2,1)} %get-tuple-element.68.q_ref, bf16[2,128,128]{2,1,0:T(8,128)(2,1)} %get-tuple-element.66.own_ref, ...), custom_call_target="tpu_custom_call" | custom-call | flops 800000000 | bytes 2000000 | tf_op jit(solution)/shard_map/attend_forward/pallas_call | solution.py:240
  97.1 8.7 %collective-permute-done.2 = bf16[128,128]{1,0:T(8,128)(2,1)S(1)} collective-permute-done((bf16[128,128]{1,0:T(8,128)(2,1)}, bf16[128,128]{1,0:T(8,128)(2,1)S(1)}, u32[]{:S(2)}, u32[]{:S(2)}) %collective-permute-start.2) | collective-permute-done | bytes 32800 | tf_op jit(solution)/shard_map/ppermute | solution.py:278
  105.8 1.7 convolution_convert_fusion
  107.5 5.1 %all-to-all-start.2 = ((bf16[8,16,1024]{2,1,0:T(8,128)(2,1)}), bf16[8,16,1024]{2,1,0:T(8,128)(2,1)S(1)}, u32[]{:S(2)}, u32[]{:S(2)}) async-start(bf16[8,16,1024]{2,1,0:T(8,128)(2,1)} %bitcast.29), calls=%async_computation.2 | async-start | bytes 524288 | tf_op jit(solution)/shard_map/all_to_all | solution.py:287
  112.6 0.9 convolution_convert_fusion.1.grad_ref
  113.4 5.5 %attend_backward.2 = (bf16[128,128]{1,0:T(8,128)(2,1)}, f32[2,128,128]{2,1,0:T(8,128)}, bf16[2,128,128]{2,1,0:T(8,128)(2,1)}, bf16[2,128,128]{2,1,0:T(8,128)(2,1)}, bf16[32,2,64,128]{3,2,1,0:T(8,128)(2,1)}) custom-call(s32[3]{0:T(128)} %pad_add_fusion.2.meta, s32[24]{0:T(128)} %get-tuple-element.72.slot_ref, f32[2]{0:T(128)} %slopes_ref.7, ...), custom_call_target="tpu_custom_call" | custom-call | flops 1600000000 | bytes 4000000 | tf_op jit(solution)/shard_map/attend_backward/pallas_call | solution.py:255
  118.9 1.6 all-to-all-done.2
  120.5 4.9 %all-to-all-start.4 = ((bf16[32,2,64,128]{3,2,1,0:T(8,128)(2,1)}), bf16[32,2,64,128]{3,2,1,0:T(8,128)(2,1)S(1)}, u32[]{:S(2)}, u32[]{:S(2)}) async-start(bf16[32,2,64,128]{3,2,1,0:T(8,128)(2,1)} %get-tuple-element.30), calls=%async_computation.4 | async-start | bytes 2097152 | tf_op jit(solution)/shard_map/all_to_all | solution.py:281
  125.4 7.5 %collective-permute-start.3 = (bf16[128,128]{1,0:T(8,128)(2,1)S(1)}, bf16[128,128]{1,0:T(8,128)(2,1)S(1)}, u32[]{:S(2)}, u32[]{:S(2)}) collective-permute-start(bf16[128,128]{1,0:T(8,128)(2,1)S(1)} %copy-done.15), channel_id=1, source_target_pairs={{0,248},{8,240},{16,232},{24,224},{32,216},{40,208},{48,200},{56,1... | collective-permute-start | bytes 98312 | tf_op jit(solution)/shard_map/ppermute | solution.py:230
  132.9 23.6 %collective-permute-done.3.grad_ref = bf16[128,128]{1,0:T(8,128)(2,1)S(1)} collective-permute-done((bf16[128,128]{1,0:T(8,128)(2,1)S(1)}, bf16[128,128]{1,0:T(8,128)(2,1)S(1)}, u32[]{:S(2)}, u32[]{:S(2)}) %collective-permute-start.3) | collective-permute-done | bytes 32800 | tf_op jit(solution)/shard_map/ppermute | solution.py:230
  157.1 5.6 %attend_backward.3 = (bf16[128,128]{1,0:T(8,128)(2,1)}, f32[2,128,128]{2,1,0:T(8,128)}, bf16[2,128,128]{2,1,0:T(8,128)(2,1)}, bf16[2,128,128]{2,1,0:T(8,128)(2,1)}, bf16[32,2,64,128]{3,2,1,0:T(8,128)(2,1)}) custom-call(s32[3]{0:T(128)} %pad_add_fusion.4.meta, s32[24]{0:T(128)} %get-tuple-element.73.slot_ref, f32[2]{0:T(128)} %slopes_ref.7, ...), custom_call_target="tpu_custom_call" | custom-call | flops 1600000000 | bytes 4000000 | tf_op jit(solution)/shard_map/attend_backward/pallas_call | solution.py:255
  162.7 1.0 copy-done.1
  163.7 6.5 %all-to-all-start.5 = ((bf16[32,2,64,128]{3,2,1,0:T(8,128)(2,1)}), bf16[32,2,64,128]{3,2,1,0:T(8,128)(2,1)S(1)}, u32[]{:S(2)}, u32[]{:S(2)}) async-start(bf16[32,2,64,128]{3,2,1,0:T(8,128)(2,1)} %get-tuple-element.31), calls=%async_computation.5 | async-start | bytes 2097152 | tf_op jit(solution)/shard_map/all_to_all | solution.py:283
  170.3 3.5 %collective-permute-start.4 = (bf16[2,2,128,128]{3,2,1,0:T(8,128)(2,1)S(1)}, bf16[2,2,128,128]{3,2,1,0:T(8,128)(2,1)S(1)}, u32[]{:S(2)}, u32[]{:S(2)}) collective-permute-start(bf16[2,2,128,128]{3,2,1,0:T(8,128)(2,1)S(1)} %pad_maximum_fusion.1), channel_id=1, source_target_pairs={{0,8},{8,16},{16,24},{24,32},{32,40},{40,48},{48,56},{56,64},{64,7... | collective-permute-start | bytes 393224 | tf_op jit(solution)/shard_map/ppermute | solution.py:292
  173.8 9.4 %collective-permute-start.5 = (bf16[2,2,128,128]{3,2,1,0:T(8,128)(2,1)S(1)}, bf16[2,2,128,128]{3,2,1,0:T(8,128)(2,1)S(1)}, u32[]{:S(2)}, u32[]{:S(2)}) collective-permute-start(bf16[2,2,128,128]{3,2,1,0:T(8,128)(2,1)S(1)} %pad_maximum_fusion.2), channel_id=1, source_target_pairs={{8,0},{16,8},{24,16},{32,24},{40,32},{48,40},{56,48},{64,56},{72,6... | collective-permute-start | bytes 393224 | tf_op jit(solution)/shard_map/ppermute | solution.py:293
  185.3 16.3 %collective-permute-done.4.p = bf16[2,2,128,128]{3,2,1,0:T(8,128)(2,1)S(1)} collective-permute-done((bf16[2,2,128,128]{3,2,1,0:T(8,128)(2,1)S(1)}, bf16[2,2,128,128]{3,2,1,0:T(8,128)(2,1)S(1)}, u32[]{:S(2)}, u32[]{:S(2)}) %collective-permute-start.4) | collective-permute-done | bytes 131104 | tf_op jit(solution)/shard_map/ppermute | solution.py:292
  202.6 3.6 %combine.1 = bf16[2,2,128,128]{3,2,1,0:T(8,128)(2,1)} custom-call(s32[2,32]{1,0:T(2,128)} %copy-done.19, f32[2,128,128]{2,1,0:T(8,128)} %get-tuple-element.24.o0, f32[2,128,128]{2,1,0:T(8,128)} %get-tuple-element.25.o1, bf16[2,2,128,128]{3,2,1,0:T(8,128)(2,1)} %copy-done.7, bf16[2,2,128,128]{3,2,1,0:T(8,128)(2,1)} %copy-done.8, ...), custom_call_target="tpu_custom_call" | custom-call | flops 4000000 | bytes 3000000 | tf_op jit(solution)/shard_map/combine/pallas_call | solution.py:294
  206.2 1.5 slice_bitcast_fusion
  (71 shorter events, 11.6 us)
Async XLA Ops:
  0.6 105.1 %copy-start = (bf16[128,1024]{1,0:T(8,128)(2,1)S(1)}, bf16[128,1024]{1,0:T(8,128)(2,1)}, u32[]{:S(2)}) copy-start(bf16[128,1024]{1,0:T(8,128)(2,1)} %param.14) | copy-start | bytes 786436
  0.6 0.7 copy-start.20
  0.7 2.9 %copy-start.5 = (bf16[2,128,128]{2,1,0:T(8,128)(2,1)S(1)}, bf16[2,128,128]{2,1,0:T(8,128)(2,1)}, u32[]{:S(2)}) copy-start(bf16[2,128,128]{2,1,0:T(8,128)(2,1)} %param.11) | copy-start | bytes 196612
  5.5 43.3 %all-to-all-start.1 = ((bf16[32,2,64,128]{3,2,1,0:T(8,128)(2,1)}), bf16[32,2,64,128]{3,2,1,0:T(8,128)(2,1)S(1)}, u32[]{:S(2)}, u32[]{:S(2)}) async-start(bf16[32,2,64,128]{3,2,1,0:T(8,128)(2,1)} %broadcast_select_fusion), calls=%async_computation.1 | async-start | bytes 2097152 | tf_op jit(solution)/shard_map/all_to_all | solution.py:216
  20.0 36.3 %copy-start.6 = (bf16[2,128,128]{2,1,0:T(8,128)(2,1)S(1)}, bf16[2,128,128]{2,1,0:T(8,128)(2,1)}, u32[]{:S(2)}) copy-start(bf16[2,128,128]{2,1,0:T(8,128)(2,1)} %param.12) | copy-start | bytes 196612
  48.8 1.0 copy-start.3
  49.8 34.8 %all-to-all-start = ((bf16[32,2,64,128]{3,2,1,0:T(8,128)(2,1)}), bf16[32,2,64,128]{3,2,1,0:T(8,128)(2,1)S(1)}, u32[]{:S(2)}, u32[]{:S(2)}) async-start(bf16[32,2,64,128]{3,2,1,0:T(8,128)(2,1)} %broadcast_select_fusion.1), calls=%async_computation | async-start | bytes 2097152 | tf_op jit(solution)/shard_map/all_to_all | solution.py:216
  56.3 15.6 %copy-start.9 = (bf16[2,128,128]{2,1,0:T(8,128)(2,1)S(1)}, bf16[2,128,128]{2,1,0:T(8,128)(2,1)}, u32[]{:S(2)}) copy-start(bf16[2,128,128]{2,1,0:T(8,128)(2,1)} %param.10) | copy-start | bytes 196612
  56.3 27.7 %collective-permute-start = (bf16[2,2,128,128]{3,2,1,0:T(8,128)(2,1)S(1)}, bf16[2,2,128,128]{3,2,1,0:T(8,128)(2,1)S(1)}, u32[]{:S(2)}, u32[]{:S(2)}) collective-permute-start(bf16[2,2,128,128]{3,2,1,0:T(8,128)(2,1)S(1)} %pad_maximum_fusion), channel_id=1, source_target_pairs={{0,8},{8,16},{16,24},{24,32},{32,40},{40,48},{48,56},{56,64},{64,7... | collective-permute-start | bytes 393224 | tf_op jit(solution)/shard_map/ppermute | solution.py:221
  59.7 29.5 %collective-permute-start.1 = (bf16[2,2,128,128]{3,2,1,0:T(8,128)(2,1)S(1)}, bf16[2,2,128,128]{3,2,1,0:T(8,128)(2,1)S(1)}, u32[]{:S(2)}, u32[]{:S(2)}) collective-permute-start(bf16[2,2,128,128]{3,2,1,0:T(8,128)(2,1)S(1)} %pad_maximum_fusion), channel_id=1, source_target_pairs={{8,0},{16,8},{24,16},{32,24},{40,32},{48,40},{56,48},{64,56},{72,6... | collective-permute-start | bytes 393224 | tf_op jit(solution)/shard_map/ppermute | solution.py:222
  74.4 10.3 %copy-start.14 = (bf16[16,1024]{1,0:T(8,128)(2,1)S(1)}, bf16[16,1024]{1,0:T(8,128)(2,1)}, u32[]{:S(2)}) copy-start(bf16[16,1024]{1,0:T(8,128)(2,1)} %param.15) | copy-start | bytes 98308
  84.6 8.9 %copy-start.4 = (bf16[32,2,64,128]{3,2,1,0:T(8,128)(2,1)}, bf16[32,2,64,128]{3,2,1,0:T(8,128)(2,1)S(1)}, u32[]{:S(2)}) copy-start(bf16[32,2,64,128]{3,2,1,0:T(8,128)(2,1)S(1)} %all-to-all-done.far_ref) | copy-start | bytes 3145732
  85.4 22.0 %all-to-all-start.3 = ((bf16[8,16,1024]{2,1,0:T(8,128)(2,1)}), bf16[8,16,1024]{2,1,0:T(8,128)(2,1)S(1)}, u32[]{:S(2)}, u32[]{:S(2)}) async-start(bf16[8,16,1024]{2,1,0:T(8,128)(2,1)} %broadcast_in_dim.92), calls=%async_computation.3 | async-start | bytes 524288 | tf_op jit(solution)/shard_map/all_to_all | solution.py:226
  93.5 12.3 %collective-permute-start.2 = (bf16[128,128]{1,0:T(8,128)(2,1)}, bf16[128,128]{1,0:T(8,128)(2,1)S(1)}, u32[]{:S(2)}, u32[]{:S(2)}) collective-permute-start(bf16[128,128]{1,0:T(8,128)(2,1)} %get-tuple-element.19), channel_id=1, source_target_pairs={{0,248},{8,240},{16,232},{24,224},{32,216},{40,208},{48,200},{56,1... | collective-permute-start | bytes 98312 | tf_op jit(solution)/shard_map/ppermute | solution.py:278
  107.5 13.0 %all-to-all-start.2 = ((bf16[8,16,1024]{2,1,0:T(8,128)(2,1)}), bf16[8,16,1024]{2,1,0:T(8,128)(2,1)S(1)}, u32[]{:S(2)}, u32[]{:S(2)}) async-start(bf16[8,16,1024]{2,1,0:T(8,128)(2,1)} %bitcast.29), calls=%async_computation.2 | async-start | bytes 524288 | tf_op jit(solution)/shard_map/all_to_all | solution.py:287
  120.5 4.9 %copy-start.15 = (bf16[128,128]{1,0:T(8,128)(2,1)S(1)}, bf16[128,128]{1,0:T(8,128)(2,1)}, u32[]{:S(2)}) copy-start(bf16[128,128]{1,0:T(8,128)(2,1)} %convolution_convert_fusion.1.grad_ref) | copy-start | bytes 98308
  120.5 42.3 %all-to-all-start.4 = ((bf16[32,2,64,128]{3,2,1,0:T(8,128)(2,1)}), bf16[32,2,64,128]{3,2,1,0:T(8,128)(2,1)S(1)}, u32[]{:S(2)}, u32[]{:S(2)}) async-start(bf16[32,2,64,128]{3,2,1,0:T(8,128)(2,1)} %get-tuple-element.30), calls=%async_computation.4 | async-start | bytes 2097152 | tf_op jit(solution)/shard_map/all_to_all | solution.py:281
  125.4 31.2 %collective-permute-start.3 = (bf16[128,128]{1,0:T(8,128)(2,1)S(1)}, bf16[128,128]{1,0:T(8,128)(2,1)S(1)}, u32[]{:S(2)}, u32[]{:S(2)}) collective-permute-start(bf16[128,128]{1,0:T(8,128)(2,1)S(1)} %copy-done.15), channel_id=1, source_target_pairs={{0,248},{8,240},{16,232},{24,224},{32,216},{40,208},{48,200},{56,1... | collective-permute-start | bytes 98312 | tf_op jit(solution)/shard_map/ppermute | solution.py:230
  162.7 1.0 copy-start.1
  162.7 7.5 %copy-start.11 = (bf16[2,128,128]{2,1,0:T(8,128)(2,1)S(1)}, bf16[2,128,128]{2,1,0:T(8,128)(2,1)}, u32[]{:S(2)}) copy-start(bf16[2,128,128]{2,1,0:T(8,128)(2,1)} %get-tuple-element.26) | copy-start | bytes 196612
  162.7 7.5 %copy-start.13 = (bf16[2,128,128]{2,1,0:T(8,128)(2,1)S(1)}, bf16[2,128,128]{2,1,0:T(8,128)(2,1)}, u32[]{:S(2)}) copy-start(bf16[2,128,128]{2,1,0:T(8,128)(2,1)} %get-tuple-element.27) | copy-start | bytes 196612
  163.7 37.8 %all-to-all-start.5 = ((bf16[32,2,64,128]{3,2,1,0:T(8,128)(2,1)}), bf16[32,2,64,128]{3,2,1,0:T(8,128)(2,1)S(1)}, u32[]{:S(2)}, u32[]{:S(2)}) async-start(bf16[32,2,64,128]{3,2,1,0:T(8,128)(2,1)} %get-tuple-element.31), calls=%async_computation.5 | async-start | bytes 2097152 | tf_op jit(solution)/shard_map/all_to_all | solution.py:283
  170.2 3.6 %copy-start.10 = (bf16[2,128,128]{2,1,0:T(8,128)(2,1)S(1)}, bf16[2,128,128]{2,1,0:T(8,128)(2,1)}, u32[]{:S(2)}) copy-start(bf16[2,128,128]{2,1,0:T(8,128)(2,1)} %get-tuple-element.28) | copy-start | bytes 196612
  170.2 3.6 %copy-start.12 = (bf16[2,128,128]{2,1,0:T(8,128)(2,1)S(1)}, bf16[2,128,128]{2,1,0:T(8,128)(2,1)}, u32[]{:S(2)}) copy-start(bf16[2,128,128]{2,1,0:T(8,128)(2,1)} %get-tuple-element.29) | copy-start | bytes 196612
  170.3 31.3 %collective-permute-start.4 = (bf16[2,2,128,128]{3,2,1,0:T(8,128)(2,1)S(1)}, bf16[2,2,128,128]{3,2,1,0:T(8,128)(2,1)S(1)}, u32[]{:S(2)}, u32[]{:S(2)}) collective-permute-start(bf16[2,2,128,128]{3,2,1,0:T(8,128)(2,1)S(1)} %pad_maximum_fusion.1), channel_id=1, source_target_pairs={{0,8},{8,16},{16,24},{24,32},{32,40},{40,48},{48,56},{56,64},{64,7... | collective-permute-start | bytes 393224 | tf_op jit(solution)/shard_map/ppermute | solution.py:292
  173.8 9.4 %copy-start.17 = (bf16[128,128]{1,0:T(8,128)(2,1)S(1)}, bf16[128,128]{1,0:T(8,128)(2,1)}, u32[]{:S(2)}) copy-start(bf16[128,128]{1,0:T(8,128)(2,1)} %get-tuple-element.21) | copy-start | bytes 98308
  173.8 9.4 %copy-start.18 = (bf16[128,128]{1,0:T(8,128)(2,1)S(1)}, bf16[128,128]{1,0:T(8,128)(2,1)}, u32[]{:S(2)}) copy-start(bf16[128,128]{1,0:T(8,128)(2,1)} %get-tuple-element.23) | copy-start | bytes 98308
  173.8 27.7 %collective-permute-start.5 = (bf16[2,2,128,128]{3,2,1,0:T(8,128)(2,1)S(1)}, bf16[2,2,128,128]{3,2,1,0:T(8,128)(2,1)S(1)}, u32[]{:S(2)}, u32[]{:S(2)}) collective-permute-start(bf16[2,2,128,128]{3,2,1,0:T(8,128)(2,1)S(1)} %pad_maximum_fusion.2), channel_id=1, source_target_pairs={{8,0},{16,8},{24,16},{32,24},{40,32},{48,40},{56,48},{64,56},{72,6... | collective-permute-start | bytes 393224 | tf_op jit(solution)/shard_map/ppermute | solution.py:293
  183.9 0.8 copy-start.16
  201.5 0.7 copy-start.7
  201.6 0.7 copy-start.8
  201.6 1.1 copy-start.2
  (2 other events, 1.2 us)
where the time goes:
time: 209 us; the launch traced here: 208 us
  waiting for transfers between devices  88.7 us (42%)
  starting transfers between devices  73.2 us (35%)
  Pallas kernels  21.8 us (10%)
  local copies, waits for them, and re-layouts  12 us (6%)
  other arithmetic  8.63 us (4%)
  matrix products  2.54 us (1%)
    all_to_all x2, waiting for transfers between devices, far_of(): lax.all_to_all(outgoing, 'seq', split_axis=0, concat_axis=0, tiled=True)  28.9 us
    ppermute x1, waiting for transfers between devices, per_device(): grads = [grad_context, lax.ppermute(grad_context, 'seq', mirror)]  23.6 us
    all_to_all x2, starting transfers between devices, far_of(): lax.all_to_all(outgoing, 'seq', split_axis=0, concat_axis=0, tiled=True)  19.8 us
    ppermute x1, waiting for transfers between devices, per_device(): to_owner_next = lax.ppermute(jnp.stack([next0, next1]), 'seq', up)  16.3 us
    pallas_call x2, Pallas kernels, backward(): pl.pallas_call(functools.partial(backward_kernel, t == 1), out_shape=(squ...  11 us
    ppermute x1, waiting for transfers between devices, per_device(): from_prev = lax.ppermute(key_value, 'seq', up)  9.62 us
    ppermute x1, starting transfers between devices, per_device(): from_next = lax.ppermute(key_value, 'seq', down)  9.38 us
    ppermute x1, starting transfers between devices, per_device(): to_owner_prev = lax.ppermute(jnp.stack([prev0, prev1]), 'seq', down)  9.38 us
  transfers between devices with their start and end apart: 12, of which 6 were waited for; matrix products, arithmetic and copies ran while one was open for 6% of the time, Pallas kernels for 9%

commit v1 on v0

v1 whole, which is shorter than its diff:
```python
import jax
import jax.numpy as jnp
from jax import lax
from jax.experimental import pallas as pl
from jax.experimental.pallas import tpu as pltpu
from jax.sharding import PartitionSpec as P

HD = 64
BLK = 64
BAND = 2
STEP = 384
LIMIT = 24 << 20

masked_value = -1e30
f32 = jnp.float32
bf16 = jnp.bfloat16

NT = (((1,), (1,)), ((), ()))
NN = (((1,), (0,)), ((), ()))


def dot(a, b, dims):
    return lax.dot_general(a, b, dims, preferred_element_type=f32)


def two_heads(x):
    first = lax.broadcasted_iota(jnp.int32, x.shape, 1) < HD
    zero = jnp.zeros_like(x)
    return jnp.concatenate([jnp.where(first, x, zero), jnp.where(first, zero, x)], axis=0)


def pick_heads(xt):
    rows = xt.shape[1] // 2
    own = jnp.concatenate([xt[:HD, :rows], xt[HD:, rows:]], axis=0)
    return own.T


def one_hot(n, at):
    r = lax.broadcasted_iota(jnp.int32, (n, n), 0)
    c = lax.broadcasted_iota(jnp.int32, (n, n), 1)
    return (c == at(r)).astype(bf16)


def flipped(x):
    n = x.shape[0]
    return dot(one_hot(n, lambda r: n - 1 - r), x, NN).astype(bf16)


def place():
    return lax.axis_index("seq"), lax.axis_size("seq")


def listed(fb_ref, t, shard, shards, f):
    entry = fb_ref[shard if t == 0 else shards - 1 - shard, f]
    owner = lax.shift_right_arithmetic(entry, 1)
    owner = owner if t == 0 else shards - 1 - owner
    return entry >= 0, jnp.where(entry >= 0, owner, 0)


def asked_of(fb, t, shard, shards):
    mine = shard if t == 0 else shards - 1 - shard
    inner = fb & 1
    inner = inner + 1 if t == 0 else 2 - inner
    hit = jnp.where(lax.shift_right_arithmetic(fb, 1) == mine, inner, 0)
    return jnp.sum(hit, axis=1, keepdims=True)


def pack_kernel(fb_ref, key_ref, value_ref, out_ref, kv_ref):
    shard, shards = place()
    fb = fb_ref[...]
    for which, ref in ((0, key_ref), (1, value_ref)):
        kv_ref[:, which] = ref[...]
    for t in range(2):
        asked = jnp.broadcast_to(asked_of(fb, t, shard, shards), (shards, 2 * HD))
        for d in range(shards):
            row = d if t == 0 else shards - 1 - d
            second = jnp.broadcast_to(asked[row : row + 1] == 2, (BLK, 2 * HD))
            for which, ref in ((0, key_ref), (1, value_ref)):
                out_ref[d, t, which] = jnp.where(second, ref[t, BLK:], ref[t, :BLK])


def stage(fb_ref, t, kv_ref, prev_ref, next_ref, far_ref, kbuf, vbuf):
    shard, shards = place()
    for which, buf in ((0, kbuf), (1, vbuf)):
        buf[0:128] = prev_ref[t, which]
        buf[128:256] = kv_ref[t, which]
        buf[256:384] = next_ref[t, which]
    for f in range(fb_ref.shape[1]):
        _, slot = listed(fb_ref, t, shard, shards, f)
        rows = slice(STEP + f * BLK, STEP + (f + 1) * BLK)
        kbuf[rows] = far_ref[slot, t, 0]
        vbuf[rows] = far_ref[slot, t, 1]


def biased(fb_ref, t, slopes_ref, q2, kbuf, put):
    shard, shards = place()
    cols = q2.shape[0]
    half = cols // 2
    head_col = lax.broadcasted_iota(jnp.int32, (1, cols), 1)
    slope = jnp.where(head_col < half, slopes_ref[0], slopes_ref[1])
    r = lax.broadcasted_iota(jnp.int32, (STEP, cols), 0)
    c = lax.broadcasted_iota(jnp.int32, (STEP, cols), 1)
    c = jnp.where(c < half, c, c - half)
    delta = r - 128 - c
    low = jnp.where(shard > 0, 0, 128)
    high = jnp.where(shard < shards - 1, STEP, 256)
    edge = jnp.where(c < BLK, 0, BLK)
    ok = (r >= jnp.maximum(edge, low)) & (r < jnp.minimum(edge + 320, high))
    scores = dot(kbuf[0:STEP], q2, NT) - slope * jnp.abs(delta).astype(f32)
    scores = jnp.where(ok, scores, masked_value)
    put(0, STEP, scores)
    top = jnp.max(scores, axis=0, keepdims=True)
    far_bias = slope * (-float((BAND + 1) * BLK))
    for lo in range(STEP, kbuf.shape[0], STEP):
        scores = dot(kbuf[lo : lo + STEP], q2, NT)
        parts = []
        for i in range(STEP // BLK):
            there, _ = listed(fb_ref, t, shard, shards, (lo - STEP) // BLK + i)
            row = jnp.where(there, far_bias, masked_value)
            parts.append(scores[i * BLK : (i + 1) * BLK] + row)
        scores = jnp.concatenate(parts, axis=0)
        put(lo, lo + STEP, scores)
        top = jnp.maximum(top, jnp.max(scores, axis=0, keepdims=True))
    return top


def forward_kernel(fb_ref, slopes_ref, q_ref, kv_ref, prev_ref, next_ref, far_ref, ctx_ref, rev_ref, stat_ref, kbuf, vbuf, sbuf):
    n = 2 * HD
    eye = one_hot(n, lambda r: r)
    total = kbuf.shape[0]
    for t in (1, 0):
        stage(fb_ref, t, kv_ref, prev_ref, next_ref, far_ref, kbuf, vbuf)
        q2 = two_heads(q_ref[t] * HD ** (-0.5))

        def put(lo, hi, scores):
            sbuf[lo:hi] = scores

        top = biased(fb_ref, t, slopes_ref, q2, kbuf, put)
        norm = jnp.zeros_like(top)
        for lo in range(0, total, STEP):
            w = jnp.exp(sbuf[lo : lo + STEP] - top)
            sbuf[lo : lo + STEP] = w
            norm = norm + jnp.sum(w, axis=0, keepdims=True)
        inv = 1.0 / norm
        stat_ref[t, 0:1] = top
        stat_ref[t, 1:2] = inv
        acc = jnp.zeros((n, q2.shape[0]), f32)
        for lo in range(0, total, STEP):
            low = (sbuf[lo : lo + STEP] * inv).astype(bf16)
            vt = dot(eye, vbuf[lo : lo + STEP], NT).astype(bf16)
            acc = acc + dot(vt, low, NN)
        ctx = pick_heads(acc).astype(bf16)
        if t == 1:
            rev_ref[...] = flipped(ctx)
        else:
            ctx_ref[...] = ctx


def reorder(x_ref, out_ref):
    at = lax.axis_index("tp")
    count = lax.axis_size("tp")
    rows = out_ref.shape[0] // count
    for k in range(count):
        out_ref[k * rows : (k + 1) * rows] = x_ref[lax.bitwise_xor(at, k)]


def backward_kernel(
    fb_ref, slopes_ref, q_ref, kv_ref, prev_ref, next_ref, far_ref, stat_ref, grad_ref, mirrored_ref,
    gq_ref, own_out, prev_out, next_out, far_out, kbuf, vbuf, pbuf, dbuf, rows_buf,
):
    shard, shards = place()
    n = 2 * HD
    eye = one_hot(n, lambda r: r)
    total = kbuf.shape[0]
    for t in range(2):
        stage(fb_ref, t, kv_ref, prev_ref, next_ref, far_ref, kbuf, vbuf)
        q2 = two_heads(q_ref[t] * HD ** (-0.5))
        reorder((grad_ref, mirrored_ref)[t], rows_buf)
        grad = rows_buf[...]
        g2 = two_heads(flipped(grad) if t == 1 else grad)
        cols = q2.shape[0]
        top = stat_ref[t, 0:1]
        inv = stat_ref[t, 1:2]

        def put(lo, hi, scores):
            pbuf[lo:hi] = jnp.exp(scores - top) * inv

        biased(fb_ref, t, slopes_ref, q2, kbuf, put)
        row_dot = jnp.zeros((1, cols), f32)
        for lo in range(0, total, STEP):
            gp = dot(vbuf[lo : lo + STEP], g2, NT)
            dbuf[lo : lo + STEP] = gp
            row_dot = row_dot + jnp.sum(pbuf[lo : lo + STEP] * gp, axis=0, keepdims=True)
        acc = jnp.zeros((n, cols), f32)
        for lo in range(0, total, STEP):
            p = pbuf[lo : lo + STEP]
            ds = (p * (dbuf[lo : lo + STEP] - row_dot)).astype(bf16)
            kt = dot(eye, kbuf[lo : lo + STEP], NT).astype(bf16)
            acc = acc + dot(kt, ds, NN)
            for which, x in ((0, dot(ds, q2, NN)), (1, dot(p.astype(bf16), g2, NN))):
                if lo == 0:
                    prev_out[t, which] = x[0:128].astype(bf16)
                    own_out[t, which] = x[128:256]
                    next_out[t, which] = x[256:384].astype(bf16)
                else:
                    low = x.astype(bf16)
                    for i in range(STEP // BLK):
                        there, slot = listed(fb_ref, t, shard, shards, (lo - STEP) // BLK + i)

                        @pl.when(there)
                        def _():
                            far_out[slot, t, which] = low[i * BLK : (i + 1) * BLK]

        gq_ref[t] = (pick_heads(acc) * HD ** (-0.5)).astype(bf16)


def combine_kernel(fb_ref, own_ref, prev_ref, next_ref, far_ref, gk_ref, gv_ref):
    shard, shards = place()
    fb = fb_ref[...]
    rows = 32
    for t in range(2):
        asked = jnp.broadcast_to(asked_of(fb, t, shard, shards), (shards, 2 * HD))
        for which, out_ref in ((0, gk_ref), (1, gv_ref)):
            for lo in range(0, BLK, rows):
                first = jnp.zeros((rows, 2 * HD), f32)
                second = jnp.zeros((rows, 2 * HD), f32)
                for d in range(shards):
                    row = d if t == 0 else shards - 1 - d
                    block = jnp.broadcast_to(asked[row : row + 1], (rows, 2 * HD))
                    x = far_ref[d, t, which, lo : lo + rows].astype(f32)
                    first = first + jnp.where(block == 1, x, 0.0)
                    second = second + jnp.where(block == 2, x, 0.0)
                for at, far in ((lo, first), (BLK + lo, second)):
                    here = slice(at, at + rows)
                    total = own_ref[t, which, here] + prev_ref[t, which, here].astype(f32)
                    total = total + next_ref[t, which, here].astype(f32)
                    out_ref[t, here] = (total + far).astype(bf16)


def project_kernel(ctx_ref, back_ref, weight_ref, out_ref, sum_buf):
    total = (ctx_ref[...].astype(f32) + back_ref[...].astype(f32)).astype(bf16)
    count, rows, _ = out_ref.shape
    for k in range(count):
        sum_buf[k] = total[k * rows : (k + 1) * rows]
    at = lax.axis_index("tp")
    for j in range(count):
        out_ref[j] = dot(sum_buf[lax.bitwise_xor(at, j)], weight_ref[...], NN)


def smem():
    return pl.BlockSpec(memory_space=pltpu.SMEM)


def vmem():
    return pl.BlockSpec(memory_space=pltpu.VMEM)


def shape(dims, dtype=bf16):
    return jax.ShapeDtypeStruct(dims, dtype)


def cost(flops, nbytes, exps=0):
    return pl.CostEstimate(flops=flops, bytes_accessed=nbytes, transcendentals=exps)


def swap(x, bit):
    count = lax.axis_size("tp")
    return lax.ppermute(x, "tp", [(i, i ^ bit) for i in range(count)])


def per_device(
    residual, queries, keys, values, slopes, out_weight, cotangent, far_blocks, far_count
):
    seq_count = lax.axis_size("seq")
    tp_count = lax.axis_size("tp")
    tok_rows, width = queries.shape[1:]
    total_keys = 3 * tok_rows + far_blocks.shape[1] * BLK
    model = out_weight.shape[1]
    cols = 2 * tok_rows
    both = (2, 2, tok_rows, width)
    slots = (seq_count, 2, 2, BLK, width)

    outgoing, key_value = pl.pallas_call(
        pack_kernel,
        out_shape=(shape(slots), shape(both)),
        in_specs=[vmem()] * 3,
        out_specs=(vmem(), vmem()),
        cost_estimate=cost(1_000_000, 2_500_000),
        compiler_params=pltpu.CompilerParams(vmem_limit_bytes=LIMIT),
        name="pack",
    )(far_blocks, keys, values)
    far = lax.all_to_all(outgoing, "seq", split_axis=0, concat_axis=0, tiled=True)

    up = [(i, i + 1) for i in range(seq_count - 1)]
    down = [(j, i) for i, j in up]
    mirror = [(i, seq_count - 1 - i) for i in range(seq_count)]
    from_prev = lax.ppermute(key_value, "seq", up)
    from_next = lax.ppermute(key_value, "seq", down)

    gathered = cotangent[None]
    for bit in (1, 2, 4):
        gathered = jnp.concatenate([gathered, swap(gathered, bit)], axis=0)
    grad_context = dot(gathered.reshape(tok_rows, model), out_weight, NT).astype(bf16)
    mirrored = lax.ppermute(grad_context, "seq", mirror)
    pieces = (tp_count, tok_rows // tp_count, width)

    keyed = [pltpu.VMEM((total_keys, width), bf16), pltpu.VMEM((total_keys, width), bf16)]
    context_fwd, context_rev, stats = pl.pallas_call(
        forward_kernel,
        out_shape=(shape((tok_rows, width)), shape((tok_rows, width)), shape((2, 2, cols), f32)),
        in_specs=[smem()] * 2 + [vmem()] * 5,
        out_specs=(vmem(),) * 3,
        scratch_shapes=keyed + [pltpu.VMEM((total_keys, cols), f32)],
        cost_estimate=cost(1_600_000_000, 4_000_000, 1_000_000),
        compiler_params=pltpu.CompilerParams(vmem_limit_bytes=LIMIT),
        name="attend_forward",
    )(far_blocks, slopes, queries, key_value, from_prev, from_next, far)
    context_back = lax.ppermute(context_rev, "seq", mirror)

    grad_queries, own, before, after, far_grads = pl.pallas_call(
        backward_kernel,
        out_shape=(shape((2, tok_rows, width)), shape(both, f32), shape(both), shape(both), shape(slots)),
        in_specs=[smem()] * 2 + [vmem()] * 8,
        out_specs=(vmem(),) * 5,
        scratch_shapes=keyed
        + [pltpu.VMEM((total_keys, cols), f32)] * 2
        + [pltpu.VMEM((tok_rows, width), bf16)],
        cost_estimate=cost(3_200_000_000, 8_000_000, 1_000_000),
        compiler_params=pltpu.CompilerParams(vmem_limit_bytes=LIMIT),
        name="attend_backward",
    )(
        far_blocks, slopes, queries, key_value, from_prev, from_next, far, stats,
        grad_context.reshape(pieces), mirrored.reshape(pieces),
    )
    returned = lax.all_to_all(far_grads, "seq", split_axis=0, concat_axis=0, tiled=True)
    from_prev_grad = lax.ppermute(after, "seq", up)
    from_next_grad = lax.ppermute(before, "seq", down)

    partial = pl.pallas_call(
        project_kernel,
        out_shape=shape((tp_count, tok_rows // tp_count, model), f32),
        in_specs=[vmem()] * 3,
        out_specs=vmem(),
        scratch_shapes=[pltpu.VMEM(pieces, bf16)],
        cost_estimate=cost(34_000_000, 1_000_000),
        compiler_params=pltpu.CompilerParams(vmem_limit_bytes=LIMIT),
        name="project",
    )(context_fwd, context_back, out_weight)
    held = partial
    for bit in (4, 2, 1):
        held = held[:bit] + swap(held[bit:].astype(bf16), bit).astype(f32)
    mixed = (residual.astype(f32) + held[0]).astype(bf16)

    grad_keys, grad_values = pl.pallas_call(
        combine_kernel,
        out_shape=(shape((2, tok_rows, width)),) * 2,
        in_specs=[vmem()] * 5,
        out_specs=(vmem(),) * 2,
        cost_estimate=cost(4_000_000, 3_000_000),
        compiler_params=pltpu.CompilerParams(vmem_limit_bytes=LIMIT),
        name="combine",
    )(far_blocks, own, from_prev_grad, from_next_grad, returned)
    return (mixed, grad_queries, grad_keys, grad_values)


def solution(mesh):
    return jax.shard_map(
        per_device,
        mesh=mesh,
        in_specs=(
            P(("seq", "tp"), None),
            P(None, "seq", "tp"),
            P(None, "seq", "tp"),
            P(None, "seq", "tp"),
            P("tp"),
            P("tp", None),
            P(("seq", "tp"), None),
            P(),
            P(),
        ),
        out_specs=(
            P(("seq", "tp"), None),
            P(None, "seq", "tp"),
            P(None, "seq", "tp"),
            P(None, "seq", "tp"),
        ),
        check_vma=False,
    )
```

time: 209 us -> 196 us (0.938)
  the two profiles are of different devices: /device:TPU:38 before, /device:TPU:24 now
where the time goes in v1:
time: 196 us; the launch traced here: 195 us
  waiting for transfers between devices  88.4 us (45%)
  starting transfers between devices  85.7 us (44%)
  Pallas kernels  13.7 us (7%)
  local copies, waits for them, and re-layouts  5.2 us (3%)
    ppermute x6, waiting for transfers between devices, swap(): return lax.ppermute(x, 'tp', [(i, i ^ bit) for i in range(count)])  56.9 us
    ppermute x6, starting transfers between devices, swap(): return lax.ppermute(x, 'tp', [(i, i ^ bit) for i in range(count)])  27.4 us
    ppermute x1, waiting for transfers between devices, per_device(): context_back = lax.ppermute(context_rev, 'seq', mirror)  19.5 us
    all_to_all x1, starting transfers between devices, per_device(): lax.all_to_all(outgoing, 'seq', split_axis=0, concat_axis=0, tiled=True)  14.1 us
    ppermute x1, starting transfers between devices, per_device(): mirrored = lax.ppermute(grad_context, 'seq', mirror)  10.4 us
    ppermute x1, waiting for transfers between devices, per_device(): from_next_grad = lax.ppermute(before, 'seq', down)  10.2 us
    all_to_all x1, starting transfers between devices, per_device(): lax.all_to_all(far_grads, 'seq', split_axis=0, concat_axis=0, tiled=True)  9.47 us
    ppermute x1, starting transfers between devices, per_device(): from_prev = lax.ppermute(key_value, 'seq', up)  7.88 us
  transfers between devices with their start and end apart: 14, of which 8 were waited for; matrix products, arithmetic and copies ran while one was open for 1% of the time, Pallas kernels for 2%

profile of v1, /device:TPU:24, one launch (start us, length us, event | category | flops | bytes accessed | tf_op | source)
XLA Modules:
  0.0 194.8 jit_solution(16855165910202277397)
XLA Ops:
  0.6 0.8 copy.13.fb_ref
  1.4 0.8 copy-done.3
  2.3 0.8 copy-done.4
  3.1 0.4 pack.1
  3.5 1.3 copy-done.1
  4.8 14.1 %all-to-all-start = ((bf16[32,2,2,64,128]{4,3,2,1,0:T(8,128)(2,1)}), bf16[32,2,2,64,128]{4,3,2,1,0:T(8,128)(2,1)S(1)}, u32[]{:S(2)}, u32[]{:S(2)}) async-start(bf16[32,2,2,64,128]{4,3,2,1,0:T(8,128)(2,1)} %copy-done.1), calls=%async_computation | async-start | bytes 4194304 | tf_op jit(solution)/shard_map/all_to_all | solution.py:292
  19.0 1.2 collective-permute-done.6
  20.2 1.1 collective-permute-start.7
  21.3 45.2 %collective-permute-done.7 = bf16[2,16,1024]{2,1,0:T(8,128)(2,1)S(1)} collective-permute-done((bf16[2,16,1024]{2,1,0:T(8,128)(2,1)S(1)}, bf16[2,16,1024]{2,1,0:T(8,128)(2,1)S(1)}, u32[]{:S(2)}, u32[]{:S(2)}) %collective-permute-start.7) | collective-permute-done | bytes 65568 | tf_op jit(solution)/shard_map/ppermute | solution.py:268
  66.5 0.1 collective-permute-start.8
  66.6 7.9 %collective-permute-start = (bf16[2,2,128,128]{3,2,1,0:T(8,128)(2,1)S(1)}, bf16[2,2,128,128]{3,2,1,0:T(8,128)(2,1)S(1)}, u32[]{:S(2)}, u32[]{:S(2)}) collective-permute-start(bf16[2,2,128,128]{3,2,1,0:T(8,128)(2,1)S(1)} %get-tuple-element.16.kv_ref), channel_id=1, source_target_pairs={{0,8},{8,16},{16,24},{24,32},{32,40},{40,48},{48,56},{56,64},{64,7... | collective-permute-start | bytes 393224 | tf_op jit(solution)/shard_map/ppermute | solution.py:297
  74.5 1.9 collective-permute-start.1
  76.5 0.2 convolution_convert_fusion
  76.7 10.4 %collective-permute-start.9 = (bf16[128,128]{1,0:T(8,128)(2,1)S(1)}, bf16[128,128]{1,0:T(8,128)(2,1)S(1)}, u32[]{:S(2)}, u32[]{:S(2)}) collective-permute-start(bf16[128,128]{1,0:T(8,128)(2,1)S(1)} %convolution_convert_fusion), channel_id=1, source_target_pairs={{0,248},{8,240},{16,232},{24,224},{32,216},{40,208},{48,200},{56,1... | collective-permute-start | bytes 98312 | tf_op jit(solution)/shard_map/ppermute | solution.py:304
  87.1 0.9 collective-permute-done.1.next_ref
  88.0 3.8 %attend_forward.1 = (bf16[128,128]{1,0:T(8,128)(2,1)S(1)}, bf16[128,128]{1,0:T(8,128)(2,1)S(1)}, f32[2,2,256]{2,1,0:T(2,128)S(1)}) custom-call(s32[32,24]{1,0:T(8,128)S(1)} %copy.13.fb_ref, f32[2]{0:T(128)S(1)} %copy-done.6, bf16[2,128,128]{2,1,0:T(8,128)(2,1)S(1)} %copy-done.5, bf16[2,2,128,128]{3,2,1,0:T(8,128)(2,1)S(1)} %get-tuple-element.16.kv_ref, ...), custom_call_target="tpu_custom_call" | custom-call | flops 1600000000 | bytes 4000000 | tf_op jit(solution)/shard_map/attend_forward/pallas_call | solution.py:308
  91.8 7.6 %attend_backward.1 = (bf16[2,128,128]{2,1,0:T(8,128)(2,1)}, f32[2,2,128,128]{3,2,1,0:T(8,128)S(1)}, bf16[2,2,128,128]{3,2,1,0:T(8,128)(2,1)S(1)}, bf16[2,2,128,1...) custom-call(s32[32,24]{1,0:T(8,128)S(1)} %copy.13.fb_ref, f32[2]{0:T(128)S(1)} %copy-done.6, ...), custom_call_target="tpu_custom_call" | custom-call | flops 3200000000 | bytes 8000000 | tf_op jit(solution)/shard_map/attend_backward/pallas_call | solution.py:320
  99.4 1.3 copy-done
  100.7 9.5 %all-to-all-start.1 = ((bf16[32,2,2,64,128]{4,3,2,1,0:T(8,128)(2,1)}), bf16[32,2,2,64,128]{4,3,2,1,0:T(8,128)(2,1)S(1)}, u32[]{:S(2)}, u32[]{:S(2)}) async-start(bf16[32,2,2,64,128]{4,3,2,1,0:T(8,128)(2,1)} %copy-done), calls=%async_computation.1 | async-start | bytes 4194304 | tf_op jit(solution)/shard_map/all_to_all | solution.py:335
  110.2 7.6 %collective-permute-start.2 = (bf16[128,128]{1,0:T(8,128)(2,1)S(1)}, bf16[128,128]{1,0:T(8,128)(2,1)S(1)}, u32[]{:S(2)}, u32[]{:S(2)}) collective-permute-start(bf16[128,128]{1,0:T(8,128)(2,1)S(1)} %get-tuple-element.19), channel_id=1, source_target_pairs={{0,248},{8,240},{16,232},{24,224},{32,216},{40,208},{48,200},{56,1... | collective-permute-start | bytes 98312 | tf_op jit(solution)/shard_map/ppermute | solution.py:318
  117.8 19.5 %collective-permute-done.2.back_ref = bf16[128,128]{1,0:T(8,128)(2,1)S(1)} collective-permute-done((bf16[128,128]{1,0:T(8,128)(2,1)S(1)}, bf16[128,128]{1,0:T(8,128)(2,1)S(1)}, u32[]{:S(2)}, u32[]{:S(2)}) %collective-permute-start.2) | collective-permute-done | bytes 32800 | tf_op jit(solution)/shard_map/ppermute | solution.py:318
  137.4 0.4 project.1
  137.8 25.9 %collective-permute-start.3 = (bf16[4,16,1024]{2,1,0:T(8,128)(2,1)S(1)}, bf16[4,16,1024]{2,1,0:T(8,128)(2,1)S(1)}, u32[]{:S(2)}, u32[]{:S(2)}) collective-permute-start(bf16[4,16,1024]{2,1,0:T(8,128)(2,1)S(1)} %slice.45), channel_id=1, source_target_pairs={{0,4},{1,5},{2,6},{3,7},{4,0},{5,1},{6,2},{7,3},{8,12},{9,13},{10,... | collective-permute-start | bytes 393224 | tf_op jit(solution)/shard_map/ppermute | solution.py:268
  163.7 6.3 %collective-permute-done.3 = bf16[4,16,1024]{2,1,0:T(8,128)(2,1)S(1)} collective-permute-done((bf16[4,16,1024]{2,1,0:T(8,128)(2,1)S(1)}, bf16[4,16,1024]{2,1,0:T(8,128)(2,1)S(1)}, u32[]{:S(2)}, u32[]{:S(2)}) %collective-permute-start.3) | collective-permute-done | bytes 131104 | tf_op jit(solution)/shard_map/ppermute | solution.py:268
  170.0 0.1 collective-permute-start.4
  170.1 4.3 %collective-permute-done.4 = bf16[2,16,1024]{2,1,0:T(8,128)(2,1)S(1)} collective-permute-done((bf16[2,16,1024]{2,1,0:T(8,128)(2,1)S(1)}, bf16[2,16,1024]{2,1,0:T(8,128)(2,1)S(1)}, u32[]{:S(2)}, u32[]{:S(2)}) %collective-permute-start.4) | collective-permute-done | bytes 65568 | tf_op jit(solution)/shard_map/ppermute | solution.py:268
  174.5 5.1 %collective-permute-start.10 = (bf16[2,2,128,128]{3,2,1,0:T(8,128)(2,1)S(1)}, bf16[2,2,128,128]{3,2,1,0:T(8,128)(2,1)S(1)}, u32[]{:S(2)}, u32[]{:S(2)}) collective-permute-start(bf16[2,2,128,128]{3,2,1,0:T(8,128)(2,1)S(1)} %get-tuple-element.23), channel_id=1, source_target_pairs={{0,8},{8,16},{16,24},{24,32},{32,40},{40,48},{48,56},{56,64},{64,7... | collective-permute-start | bytes 393224 | tf_op jit(solution)/shard_map/ppermute | solution.py:336
  179.6 1.9 collective-permute-start.11
  181.5 0.6 fusion.2
  182.2 0.8 collective-permute-done.10.prev_ref
  183.0 10.2 %collective-permute-done.11.next_ref = bf16[2,2,128,128]{3,2,1,0:T(8,128)(2,1)S(1)} collective-permute-done((bf16[2,2,128,128]{3,2,1,0:T(8,128)(2,1)S(1)}, bf16[2,2,128,128]{3,2,1,0:T(8,128)(2,1)S(1)}, u32[]{:S(2)}, u32[]{:S(2)}) %collective-permute-start.11) | collective-permute-done | bytes 131104 | tf_op jit(solution)/shard_map/ppermute | solution.py:337
  193.2 1.5 combine.1
  (30 shorter events, 0.4 us)
Async XLA Ops:
  1.4 0.8 copy-start.3
  2.3 0.8 copy-start.4
  3.5 1.3 copy-start.1
  4.8 14.1 %copy-start.7 = (bf16[16,1024]{1,0:T(8,128)(2,1)S(1)}, bf16[16,1024]{1,0:T(8,128)(2,1)}, u32[]{:S(2)}) copy-start(bf16[16,1024]{1,0:T(8,128)(2,1)} %param.15) | copy-start | bytes 98308
  4.8 71.7 %copy-start.2 = (bf16[128,1024]{1,0:T(8,128)(2,1)S(1)}, bf16[128,1024]{1,0:T(8,128)(2,1)}, u32[]{:S(2)}) copy-start(bf16[128,1024]{1,0:T(8,128)(2,1)} %weight_ref.1) | copy-start | bytes 786436
  4.8 83.2 %copy-start.5 = (bf16[2,128,128]{2,1,0:T(8,128)(2,1)S(1)}, bf16[2,128,128]{2,1,0:T(8,128)(2,1)}, u32[]{:S(2)}) copy-start(bf16[2,128,128]{2,1,0:T(8,128)(2,1)} %q_ref.3) | copy-start | bytes 196612
  4.8 83.2 %copy-start.6 = (f32[2]{0:T(128)S(1)}, f32[2]{0:T(128)}, u32[]{:S(2)}) copy-start(f32[2]{0:T(128)} %slopes_ref.3) | copy-start | bytes 28
  4.8 83.1 %all-to-all-start = ((bf16[32,2,2,64,128]{4,3,2,1,0:T(8,128)(2,1)}), bf16[32,2,2,64,128]{4,3,2,1,0:T(8,128)(2,1)S(1)}, u32[]{:S(2)}, u32[]{:S(2)}) async-start(bf16[32,2,2,64,128]{4,3,2,1,0:T(8,128)(2,1)} %copy-done.1), calls=%async_computation | async-start | bytes 4194304 | tf_op jit(solution)/shard_map/all_to_all | solution.py:292
  18.9 1.3 collective-permute-start.6
  20.2 46.3 %collective-permute-start.7 = (bf16[2,16,1024]{2,1,0:T(8,128)(2,1)S(1)}, bf16[2,16,1024]{2,1,0:T(8,128)(2,1)S(1)}, u32[]{:S(2)}, u32[]{:S(2)}) collective-permute-start(bf16[2,16,1024]{2,1,0:T(8,128)(2,1)S(1)} %pad_maximum_fusion.2), channel_id=1, source_target_pairs={{0,2},{1,3},{2,0},{3,1},{4,6},{5,7},{6,4},{7,5},{8,10},{9,11},{10,... | collective-permute-start | bytes 196616 | tf_op jit(solution)/shard_map/ppermute | solution.py:268
  66.5 9.9 %collective-permute-start.8 = (bf16[4,16,1024]{2,1,0:T(8,128)(2,1)S(1)}, bf16[4,16,1024]{2,1,0:T(8,128)(2,1)S(1)}, u32[]{:S(2)}, u32[]{:S(2)}) collective-permute-start(bf16[4,16,1024]{2,1,0:T(8,128)(2,1)S(1)} %pad_maximum_fusion.1), channel_id=1, source_target_pairs={{0,4},{1,5},{2,6},{3,7},{4,0},{5,1},{6,2},{7,3},{8,12},{9,13},{10,... | collective-permute-start | bytes 393224 | tf_op jit(solution)/shard_map/ppermute | solution.py:268
  66.6 20.5 %collective-permute-start = (bf16[2,2,128,128]{3,2,1,0:T(8,128)(2,1)S(1)}, bf16[2,2,128,128]{3,2,1,0:T(8,128)(2,1)S(1)}, u32[]{:S(2)}, u32[]{:S(2)}) collective-permute-start(bf16[2,2,128,128]{3,2,1,0:T(8,128)(2,1)S(1)} %get-tuple-element.16.kv_ref), channel_id=1, source_target_pairs={{0,8},{8,16},{16,24},{24,32},{32,40},{40,48},{48,56},{56,64},{64,7... | collective-permute-start | bytes 393224 | tf_op jit(solution)/shard_map/ppermute | solution.py:297
  74.5 13.5 %collective-permute-start.1 = (bf16[2,2,128,128]{3,2,1,0:T(8,128)(2,1)S(1)}, bf16[2,2,128,128]{3,2,1,0:T(8,128)(2,1)S(1)}, u32[]{:S(2)}, u32[]{:S(2)}) collective-permute-start(bf16[2,2,128,128]{3,2,1,0:T(8,128)(2,1)S(1)} %get-tuple-element.16.kv_ref), channel_id=1, source_target_pairs={{8,0},{16,8},{24,16},{32,24},{40,32},{48,40},{56,48},{64,56},{72,6... | collective-permute-start | bytes 393224 | tf_op jit(solution)/shard_map/ppermute | solution.py:298
  76.7 15.0 %collective-permute-start.9 = (bf16[128,128]{1,0:T(8,128)(2,1)S(1)}, bf16[128,128]{1,0:T(8,128)(2,1)S(1)}, u32[]{:S(2)}, u32[]{:S(2)}) collective-permute-start(bf16[128,128]{1,0:T(8,128)(2,1)S(1)} %convolution_convert_fusion), channel_id=1, source_target_pairs={{0,248},{8,240},{16,232},{24,224},{32,216},{40,208},{48,200},{56,1... | collective-permute-start | bytes 98312 | tf_op jit(solution)/shard_map/ppermute | solution.py:304
  99.4 1.3 copy-start
  100.7 92.5 %all-to-all-start.1 = ((bf16[32,2,2,64,128]{4,3,2,1,0:T(8,128)(2,1)}), bf16[32,2,2,64,128]{4,3,2,1,0:T(8,128)(2,1)S(1)}, u32[]{:S(2)}, u32[]{:S(2)}) async-start(bf16[32,2,2,64,128]{4,3,2,1,0:T(8,128)(2,1)} %copy-done), calls=%async_computation.1 | async-start | bytes 4194304 | tf_op jit(solution)/shard_map/all_to_all | solution.py:335
  110.2 71.4 %copy-start.8 = (bf16[16,1024]{1,0:T(8,128)(2,1)S(1)}, bf16[16,1024]{1,0:T(8,128)(2,1)}, u32[]{:S(2)}) copy-start(bf16[16,1024]{1,0:T(8,128)(2,1)} %param.9) | copy-start | bytes 98308
  110.2 27.2 %collective-permute-start.2 = (bf16[128,128]{1,0:T(8,128)(2,1)S(1)}, bf16[128,128]{1,0:T(8,128)(2,1)S(1)}, u32[]{:S(2)}, u32[]{:S(2)}) collective-permute-start(bf16[128,128]{1,0:T(8,128)(2,1)S(1)} %get-tuple-element.19), channel_id=1, source_target_pairs={{0,248},{8,240},{16,232},{24,224},{32,216},{40,208},{48,200},{56,1... | collective-permute-start | bytes 98312 | tf_op jit(solution)/shard_map/ppermute | solution.py:318
  137.8 32.2 %collective-permute-start.3 = (bf16[4,16,1024]{2,1,0:T(8,128)(2,1)S(1)}, bf16[4,16,1024]{2,1,0:T(8,128)(2,1)S(1)}, u32[]{:S(2)}, u32[]{:S(2)}) collective-permute-start(bf16[4,16,1024]{2,1,0:T(8,128)(2,1)S(1)} %slice.45), channel_id=1, source_target_pairs={{0,4},{1,5},{2,6},{3,7},{4,0},{5,1},{6,2},{7,3},{8,12},{9,13},{10,... | collective-permute-start | bytes 393224 | tf_op jit(solution)/shard_map/ppermute | solution.py:268
  170.0 4.4 %collective-permute-start.4 = (bf16[2,16,1024]{2,1,0:T(8,128)(2,1)S(1)}, bf16[2,16,1024]{2,1,0:T(8,128)(2,1)S(1)}, u32[]{:S(2)}, u32[]{:S(2)}) collective-permute-start(bf16[2,16,1024]{2,1,0:T(8,128)(2,1)S(1)} %slice.46), channel_id=1, source_target_pairs={{0,2},{1,3},{2,0},{3,1},{4,6},{5,7},{6,4},{7,5},{8,10},{9,11},{10,... | collective-permute-start | bytes 196616 | tf_op jit(solution)/shard_map/ppermute | solution.py:268
  174.4 7.1 %collective-permute-start.5 = (bf16[1,16,1024]{2,1,0:T(8,128)(2,1)S(1)}, bf16[1,16,1024]{2,1,0:T(8,128)(2,1)S(1)}, u32[]{:S(2)}, u32[]{:S(2)}) collective-permute-start(bf16[1,16,1024]{2,1,0:T(8,128)(2,1)S(1)} %slice.47), channel_id=1, source_target_pairs={{0,1},{1,0},{2,3},{3,2},{4,5},{5,4},{6,7},{7,6},{8,9},{9,8},{10,11... | collective-permute-start | bytes 98312 | tf_op jit(solution)/shard_map/ppermute | solution.py:268
  174.5 8.5 %collective-permute-start.10 = (bf16[2,2,128,128]{3,2,1,0:T(8,128)(2,1)S(1)}, bf16[2,2,128,128]{3,2,1,0:T(8,128)(2,1)S(1)}, u32[]{:S(2)}, u32[]{:S(2)}) collective-permute-start(bf16[2,2,128,128]{3,2,1,0:T(8,128)(2,1)S(1)} %get-tuple-element.23), channel_id=1, source_target_pairs={{0,8},{8,16},{16,24},{24,32},{32,40},{40,48},{48,56},{56,64},{64,7... | collective-permute-start | bytes 393224 | tf_op jit(solution)/shard_map/ppermute | solution.py:336
  179.6 13.6 %collective-permute-start.11 = (bf16[2,2,128,128]{3,2,1,0:T(8,128)(2,1)S(1)}, bf16[2,2,128,128]{3,2,1,0:T(8,128)(2,1)S(1)}, u32[]{:S(2)}, u32[]{:S(2)}) collective-permute-start(bf16[2,2,128,128]{3,2,1,0:T(8,128)(2,1)S(1)} %get-tuple-element.24), channel_id=1, source_target_pairs={{8,0},{16,8},{24,16},{32,24},{40,32},{48,40},{56,48},{64,56},{72,6... | collective-permute-start | bytes 393224 | tf_op jit(solution)/shard_map/ppermute | solution.py:337

commit v2 on v1

--- a/solution.py
+++ b/solution.py
@@ -48,6 +48,10 @@
 
 def place():
     return lax.axis_index("seq"), lax.axis_size("seq")
+
+
+def part(t, which):
+    return slice((2 * t + which) * BLK, (2 * t + which + 1) * BLK)
 
 
 def listed(fb_ref, t, shard, shards, f):
@@ -76,7 +80,7 @@
             row = d if t == 0 else shards - 1 - d
             second = jnp.broadcast_to(asked[row : row + 1] == 2, (BLK, 2 * HD))
             for which, ref in ((0, key_ref), (1, value_ref)):
-                out_ref[d, t, which] = jnp.where(second, ref[t, BLK:], ref[t, :BLK])
+                out_ref[d, part(t, which)] = jnp.where(second, ref[t, BLK:], ref[t, :BLK])
 
 
 def stage(fb_ref, t, kv_ref, prev_ref, next_ref, far_ref, kbuf, vbuf):
@@ -88,8 +92,8 @@
     for f in range(fb_ref.shape[1]):
         _, slot = listed(fb_ref, t, shard, shards, f)
         rows = slice(STEP + f * BLK, STEP + (f + 1) * BLK)
-        kbuf[rows] = far_ref[slot, t, 0]
-        vbuf[rows] = far_ref[slot, t, 1]
+        kbuf[rows] = far_ref[slot, part(t, 0)]
+        vbuf[rows] = far_ref[slot, part(t, 1)]
 
 
 def biased(fb_ref, t, slopes_ref, q2, kbuf, put):
@@ -156,17 +160,20 @@
             ctx_ref[...] = ctx
 
 
-def reorder(x_ref, out_ref):
+def context_grad_kernel(own_ref, ref2, ref4, ref6, weight_ref, out_ref, buf):
+    count, rows, _ = buf.shape
+    got = jnp.concatenate([ref[k] for ref in (own_ref, ref2, ref4, ref6) for k in range(2)], axis=0)
+    out = dot(got, weight_ref[...], NT).astype(bf16)
+    for k in range(count):
+        buf[k] = out[k * rows : (k + 1) * rows]
     at = lax.axis_index("tp")
-    count = lax.axis_size("tp")
-    rows = out_ref.shape[0] // count
     for k in range(count):
-        out_ref[k * rows : (k + 1) * rows] = x_ref[lax.bitwise_xor(at, k)]
+        out_ref[k * rows : (k + 1) * rows] = buf[lax.bitwise_xor(at, k)]
 
 
 def backward_kernel(
     fb_ref, slopes_ref, q_ref, kv_ref, prev_ref, next_ref, far_ref, stat_ref, grad_ref, mirrored_ref,
-    gq_ref, own_out, prev_out, next_out, far_out, kbuf, vbuf, pbuf, dbuf, rows_buf,
+    gq_ref, own_out, prev_out, next_out, far_out, kbuf, vbuf, pbuf, dbuf,
 ):
     shard, shards = place()
     n = 2 * HD
@@ -175,9 +182,7 @@
     for t in range(2):
         stage(fb_ref, t, kv_ref, prev_ref, next_ref, far_ref, kbuf, vbuf)
         q2 = two_heads(q_ref[t] * HD ** (-0.5))
-        reorder((grad_ref, mirrored_ref)[t], rows_buf)
-        grad = rows_buf[...]
-        g2 = two_heads(flipped(grad) if t == 1 else grad)
+        g2 = two_heads(flipped(mirrored_ref[...]) if t == 1 else grad_ref[...])
         cols = q2.shape[0]
         top = stat_ref[t, 0:1]
         inv = stat_ref[t, 1:2]
@@ -209,7 +214,7 @@
 
                         @pl.when(there)
                         def _():
-                            far_out[slot, t, which] = low[i * BLK : (i + 1) * BLK]
+                            far_out[slot, part(t, which)] = low[i * BLK : (i + 1) * BLK]
 
         gq_ref[t] = (pick_heads(acc) * HD ** (-0.5)).astype(bf16)
 
@@ -227,7 +232,8 @@
                 for d in range(shards):
                     row = d if t == 0 else shards - 1 - d
                     block = jnp.broadcast_to(asked[row : row + 1], (rows, 2 * HD))
-                    x = far_ref[d, t, which, lo : lo + rows].astype(f32)
+                    at = part(t, which).start + lo
+                    x = far_ref[d, at : at + rows].astype(f32)
                     first = first + jnp.where(block == 1, x, 0.0)
                     second = second + jnp.where(block == 2, x, 0.0)
                 for at, far in ((lo, first), (BLK + lo, second)):
@@ -237,14 +243,17 @@
                     out_ref[t, here] = (total + far).astype(bf16)
 
 
-def project_kernel(ctx_ref, back_ref, weight_ref, out_ref, sum_buf):
+def project_kernel(ctx_ref, back_ref, weight_ref, own_ref, ref2, ref4, ref6, sum_buf):
     total = (ctx_ref[...].astype(f32) + back_ref[...].astype(f32)).astype(bf16)
-    count, rows, _ = out_ref.shape
+    count, rows, _ = sum_buf.shape
     for k in range(count):
         sum_buf[k] = total[k * rows : (k + 1) * rows]
     at = lax.axis_index("tp")
+    blocks = jnp.concatenate([sum_buf[lax.bitwise_xor(at, j)] for j in range(count)], axis=0)
+    out = dot(blocks, weight_ref[...], NN)
     for j in range(count):
-        out_ref[j] = dot(sum_buf[lax.bitwise_xor(at, j)], weight_ref[...], NN)
+        ref = (own_ref, ref2, ref4, ref6)[j // 2]
+        ref[j % 2] = out[j * rows : (j + 1) * rows].astype(ref.dtype)
 
 
 def smem():
@@ -278,7 +287,8 @@
     model = out_weight.shape[1]
     cols = 2 * tok_rows
     both = (2, 2, tok_rows, width)
-    slots = (seq_count, 2, 2, BLK, width)
+    pieces = (tp_count, tok_rows // tp_count, width)
+    slots = (seq_count, 4 * BLK, width)
 
     outgoing, key_value = pl.pallas_call(
         pack_kernel,
@@ -289,6 +299,9 @@
         compiler_params=pltpu.CompilerParams(vmem_limit_bytes=LIMIT),
         name="pack",
     )(far_blocks, keys, values)
+    own_pair = jnp.stack([cotangent, swap(cotangent, 1)])
+    others = [swap(own_pair, bit) for bit in (2, 4, 6)]
+    outgoing, *others = lax.optimization_barrier((outgoing, *others))
     far = lax.all_to_all(outgoing, "seq", split_axis=0, concat_axis=0, tiled=True)
 
     up = [(i, i + 1) for i in range(seq_count - 1)]
@@ -297,12 +310,17 @@
     from_prev = lax.ppermute(key_value, "seq", up)
     from_next = lax.ppermute(key_value, "seq", down)
 
-    gathered = cotangent[None]
-    for bit in (1, 2, 4):
-        gathered = jnp.concatenate([gathered, swap(gathered, bit)], axis=0)
-    grad_context = dot(gathered.reshape(tok_rows, model), out_weight, NT).astype(bf16)
+    grad_context = pl.pallas_call(
+        context_grad_kernel,
+        out_shape=shape((tok_rows, width)),
+        in_specs=[vmem()] * 5,
+        out_specs=vmem(),
+        scratch_shapes=[pltpu.VMEM(pieces, bf16)],
+        cost_estimate=cost(34_000_000, 600_000),
+        compiler_params=pltpu.CompilerParams(vmem_limit_bytes=LIMIT),
+        name="context_grad",
+    )(own_pair, *others, out_weight)
     mirrored = lax.ppermute(grad_context, "seq", mirror)
-    pieces = (tp_count, tok_rows // tp_count, width)
 
     keyed = [pltpu.VMEM((total_keys, width), bf16), pltpu.VMEM((total_keys, width), bf16)]
     context_fwd, context_rev, stats = pl.pallas_call(
@@ -323,33 +341,35 @@
         in_specs=[smem()] * 2 + [vmem()] * 8,
         out_specs=(vmem(),) * 5,
         scratch_shapes=keyed
-        + [pltpu.VMEM((total_keys, cols), f32)] * 2
-        + [pltpu.VMEM((tok_rows, width), bf16)],
+        + [pltpu.VMEM((total_keys, cols), f32)] * 2,
         cost_estimate=cost(3_200_000_000, 8_000_000, 1_000_000),
         compiler_params=pltpu.CompilerParams(vmem_limit_bytes=LIMIT),
         name="attend_backward",
     )(
         far_blocks, slopes, queries, key_value, from_prev, from_next, far, stats,
-        grad_context.reshape(pieces), mirrored.reshape(pieces),
+        grad_context, mirrored,
     )
+    own_rows, *other_rows = pl.pallas_call(
+        project_kernel,
+        out_shape=(shape((2, tok_rows // tp_count, model), f32),)
+        + (shape((2, tok_rows // tp_count, model)),) * 3,
+        in_specs=[vmem()] * 3,
+        out_specs=(vmem(),) * 4,
+        scratch_shapes=[pltpu.VMEM(pieces, bf16)],
+        cost_estimate=cost(34_000_000, 1_000_000),
+        compiler_params=pltpu.CompilerParams(vmem_limit_bytes=LIMIT),
+        name="project",
+    )(context_fwd, context_back, out_weight)
+    far_grads, *other_rows = lax.optimization_barrier((far_grads, *other_rows))
     returned = lax.all_to_all(far_grads, "seq", split_axis=0, concat_axis=0, tiled=True)
     from_prev_grad = lax.ppermute(after, "seq", up)
     from_next_grad = lax.ppermute(before, "seq", down)
 
-    partial = pl.pallas_call(
-        project_kernel,
-        out_shape=shape((tp_count, tok_rows // tp_count, model), f32),
-        in_specs=[vmem()] * 3,
-        out_specs=vmem(),
-        scratch_shapes=[pltpu.VMEM(pieces, bf16)],
-        cost_estimate=cost(34_000_000, 1_000_000),
-        compiler_params=pltpu.CompilerParams(vmem_limit_bytes=LIMIT),
-        name="project",
-    )(context_fwd, context_back, out_weight)
-    held = partial
-    for bit in (4, 2, 1):
-        held = held[:bit] + swap(held[bit:].astype(bf16), bit).astype(f32)
-    mixed = (residual.astype(f32) + held[0]).astype(bf16)
+    held = own_rows
+    for bit, rows in zip((2, 4, 6), other_rows):
+        held = held + swap(rows, bit).astype(f32)
+    held, from_prev_grad, from_next_grad = lax.optimization_barrier((held, from_prev_grad, from_next_grad))
+    mixed = (residual.astype(f32) + held[0] + swap(held[1].astype(bf16), 1).astype(f32)).astype(bf16)
 
     grad_keys, grad_values = pl.pallas_call(
         combine_kernel,

time: 196 us -> 164 us (0.84)
  the two profiles are of different devices: /device:TPU:24 before, /device:TPU:7 now
where the time goes in v2:
time: 164 us; the launch traced here: 163 us
  waiting for transfers between devices  75 us (46%)
  starting transfers between devices  67 us (41%)
  Pallas kernels  13.7 us (8%)
  local copies, waits for them, and re-layouts  5.18 us (3%)
    ppermute x8, waiting for transfers between devices, swap(): return lax.ppermute(x, 'tp', [(i, i ^ bit) for i in range(count)])  34.3 us
    ppermute x1, waiting for transfers between devices, per_device(): from_next = lax.ppermute(key_value, 'seq', down)  31.4 us
    all_to_all x1, starting transfers between devices, per_device(): lax.all_to_all(outgoing, 'seq', split_axis=0, concat_axis=0, tiled=True)  13.4 us
    ppermute x8, starting transfers between devices, swap(): return lax.ppermute(x, 'tp', [(i, i ^ bit) for i in range(count)])  10.5 us
    ppermute x1, starting transfers between devices, per_device(): from_next = lax.ppermute(key_value, 'seq', down)  9.39 us
    ppermute x1, starting transfers between devices, per_device(): from_next_grad = lax.ppermute(before, 'seq', down)  9.1 us
    ppermute x1, starting transfers between devices, per_device(): mirrored = lax.ppermute(grad_context, 'seq', mirror)  8.12 us
    all_to_all x1, starting transfers between devices, per_device(): lax.all_to_all(far_grads, 'seq', split_axis=0, concat_axis=0, tiled=True)  7.83 us
  transfers between devices with their start and end apart: 16, of which 9 were waited for; matrix products, arithmetic and copies ran while one was open for 1% of the time, Pallas kernels for 7%

profile of v2, /device:TPU:7, one launch (start us, length us, event | category | flops | bytes accessed | tf_op | source)
XLA Modules:
  0.0 163.1 jit_solution(14368509540246099374)
XLA Ops:
  0.6 0.8 collective-permute-start.2
  1.4 1.1 collective-permute-done.2
  2.5 0.8 pad_maximum_fusion.own_ref
  3.2 4.3 %collective-permute-start.5 = (bf16[2,16,1024]{2,1,0:T(8,128)(2,1)S(1)}, bf16[2,16,1024]{2,1,0:T(8,128)(2,1)S(1)}, u32[]{:S(2)}, u32[]{:S(2)}) collective-permute-start(bf16[2,16,1024]{2,1,0:T(8,128)(2,1)S(1)} %pad_maximum_fusion.own_ref), channel_id=1, source_target_pairs={{0,6},{1,7},{2,4},{3,5},{4,2},{5,3},{6,0},{7,1},{8,14},{9,15},{10,... | collective-permute-start | bytes 196616 | tf_op jit(solution)/shard_map/ppermute | solution.py:277
  8.0 0.8 copy.13.fb_ref
  8.7 0.8 copy-done.3
  9.6 0.8 copy-done.4
  10.4 0.4 pack.1
  10.8 1.3 copy-done.1
  12.5 13.4 %all-to-all-start = ((bf16[32,256,128]{2,1,0:T(8,128)(2,1)}), bf16[32,256,128]{2,1,0:T(8,128)(2,1)S(1)}, u32[]{:S(2)}, u32[]{:S(2)}) async-start(bf16[32,256,128]{2,1,0:T(8,128)(2,1)} %copy-done.1), calls=%async_computation | async-start | bytes 4194304 | tf_op jit(solution)/shard_map/all_to_all | solution.py:305
  25.9 9.4 %collective-permute-start.1 = (bf16[2,2,128,128]{3,2,1,0:T(8,128)(2,1)S(1)}, bf16[2,2,128,128]{3,2,1,0:T(8,128)(2,1)S(1)}, u32[]{:S(2)}, u32[]{:S(2)}) collective-permute-start(bf16[2,2,128,128]{3,2,1,0:T(8,128)(2,1)S(1)} %get-tuple-element.31.kv_ref), channel_id=1, source_target_pairs={{8,0},{16,8},{24,16},{32,24},{40,32},{48,40},{56,48},{64,56},{72,6... | collective-permute-start | bytes 393224 | tf_op jit(solution)/shard_map/ppermute | solution.py:311
  35.3 1.9 %collective-permute-start = (bf16[2,2,128,128]{3,2,1,0:T(8,128)(2,1)S(1)}, bf16[2,2,128,128]{3,2,1,0:T(8,128)(2,1)S(1)}, u32[]{:S(2)}, u32[]{:S(2)}) collective-permute-start(bf16[2,2,128,128]{3,2,1,0:T(8,128)(2,1)S(1)} %get-tuple-element.31.kv_ref), channel_id=1, source_target_pairs={{0,8},{8,16},{16,24},{24,32},{32,40},{40,48},{48,56},{56,64},{64,7... | collective-permute-start | bytes 393224 | tf_op jit(solution)/shard_map/ppermute | solution.py:310
  37.5 8.1 %collective-permute-start.7 = (bf16[128,128]{1,0:T(8,128)(2,1)S(1)}, bf16[128,128]{1,0:T(8,128)(2,1)S(1)}, u32[]{:S(2)}, u32[]{:S(2)}) collective-permute-start(bf16[128,128]{1,0:T(8,128)(2,1)S(1)} %context_grad.1.grad_ref), channel_id=1, source_target_pairs={{0,248},{8,240},{16,232},{24,224},{32,216},{40,208},{48,200},{56,1... | collective-permute-start | bytes 98312 | tf_op jit(solution)/shard_map/ppermute | solution.py:323
  45.6 31.4 %collective-permute-done.1.next_ref = bf16[2,2,128,128]{3,2,1,0:T(8,128)(2,1)S(1)} collective-permute-done((bf16[2,2,128,128]{3,2,1,0:T(8,128)(2,1)S(1)}, bf16[2,2,128,128]{3,2,1,0:T(8,128)(2,1)S(1)}, u32[]{:S(2)}, u32[]{:S(2)}) %collective-permute-start.1) | collective-permute-done | bytes 131104 | tf_op jit(solution)/shard_map/ppermute | solution.py:311
  77.0 5.6 %collective-permute-done.prev_ref = bf16[2,2,128,128]{3,2,1,0:T(8,128)(2,1)S(1)} collective-permute-done((bf16[2,2,128,128]{3,2,1,0:T(8,128)(2,1)S(1)}, bf16[2,2,128,128]{3,2,1,0:T(8,128)(2,1)S(1)}, u32[]{:S(2)}, u32[]{:S(2)}) %collective-permute-start) | collective-permute-done | bytes 131104 | tf_op jit(solution)/shard_map/ppermute | solution.py:310
  82.6 3.8 %attend_forward.1 = (bf16[128,128]{1,0:T(8,128)(2,1)S(1)}, bf16[128,128]{1,0:T(8,128)(2,1)S(1)}, f32[2,2,256]{2,1,0:T(2,128)S(1)}) custom-call(s32[32,24]{1,0:T(8,128)S(1)} %copy.13.fb_ref, f32[2]{0:T(128)S(1)} %copy-done.6, bf16[2,128,128]{2,1,0:T(8,128)(2,1)S(1)} %copy-done.5, bf16[2,2,128,128]{3,2,1,0:T(8,128)(2,1)S(1)} %get-tuple-element.31.kv_ref, ...), custom_call_target="tpu_custom_call" | custom-call | flops 1600000000 | bytes 4000000 | tf_op jit(solution)/shard_map/attend_forward/pallas_call | solution.py:326
  86.4 3.6 %collective-permute-start.6 = (bf16[128,128]{1,0:T(8,128)(2,1)S(1)}, bf16[128,128]{1,0:T(8,128)(2,1)S(1)}, u32[]{:S(2)}, u32[]{:S(2)}) collective-permute-start(bf16[128,128]{1,0:T(8,128)(2,1)S(1)} %get-tuple-element.35), channel_id=1, source_target_pairs={{0,248},{8,240},{16,232},{24,224},{32,216},{40,208},{48,200},{56,1... | collective-permute-start | bytes 98312 | tf_op jit(solution)/shard_map/ppermute | solution.py:336
  90.0 7.6 %attend_backward.1 = (bf16[2,128,128]{2,1,0:T(8,128)(2,1)}, f32[2,2,128,128]{3,2,1,0:T(8,128)S(1)}, bf16[2,2,128,128]{3,2,1,0:T(8,128)(2,1)S(1)}, bf16[2,2,128,1...) custom-call(s32[32,24]{1,0:T(8,128)S(1)} %copy.13.fb_ref, f32[2]{0:T(128)S(1)} %copy-done.6, ...), custom_call_target="tpu_custom_call" | custom-call | flops 3200000000 | bytes 8000000 | tf_op jit(solution)/shard_map/attend_backward/pallas_call | solution.py:338
  97.6 1.4 copy-done
  99.2 7.8 %all-to-all-start.1 = ((bf16[32,256,128]{2,1,0:T(8,128)(2,1)}), bf16[32,256,128]{2,1,0:T(8,128)(2,1)S(1)}, u32[]{:S(2)}, u32[]{:S(2)}) async-start(bf16[32,256,128]{2,1,0:T(8,128)(2,1)} %copy-done), calls=%async_computation.1 | async-start | bytes 4194304 | tf_op jit(solution)/shard_map/all_to_all | solution.py:364
  107.1 2.0 %collective-permute-start.9 = (bf16[2,16,1024]{2,1,0:T(8,128)(2,1)S(1)}, bf16[2,16,1024]{2,1,0:T(8,128)(2,1)S(1)}, u32[]{:S(2)}, u32[]{:S(2)}) collective-permute-start(bf16[2,16,1024]{2,1,0:T(8,128)(2,1)S(1)} %get-tuple-element.46), channel_id=1, source_target_pairs={{0,4},{1,5},{2,6},{3,7},{4,0},{5,1},{6,2},{7,3},{8,12},{9,13},{10,... | collective-permute-start | bytes 196616 | tf_op jit(solution)/shard_map/ppermute | solution.py:277
  109.1 1.5 collective-permute-start.10
  110.6 3.1 %collective-permute-start.11 = (bf16[2,2,128,128]{3,2,1,0:T(8,128)(2,1)S(1)}, bf16[2,2,128,128]{3,2,1,0:T(8,128)(2,1)S(1)}, u32[]{:S(2)}, u32[]{:S(2)}) collective-permute-start(bf16[2,2,128,128]{3,2,1,0:T(8,128)(2,1)S(1)} %get-tuple-element.48), channel_id=1, source_target_pairs={{0,8},{8,16},{16,24},{24,32},{32,40},{40,48},{48,56},{56,64},{64,7... | collective-permute-start | bytes 393224 | tf_op jit(solution)/shard_map/ppermute | solution.py:365
  113.7 9.1 %collective-permute-start.12 = (bf16[2,2,128,128]{3,2,1,0:T(8,128)(2,1)S(1)}, bf16[2,2,128,128]{3,2,1,0:T(8,128)(2,1)S(1)}, u32[]{:S(2)}, u32[]{:S(2)}) collective-permute-start(bf16[2,2,128,128]{3,2,1,0:T(8,128)(2,1)S(1)} %get-tuple-element.49), channel_id=1, source_target_pairs={{8,0},{16,8},{24,16},{32,24},{40,32},{48,40},{56,48},{64,56},{72,6... | collective-permute-start | bytes 393224 | tf_op jit(solution)/shard_map/ppermute | solution.py:366
  122.8 25.6 %collective-permute-done.8 = bf16[2,16,1024]{2,1,0:T(8,128)(2,1)S(1)} collective-permute-done((bf16[2,16,1024]{2,1,0:T(8,128)(2,1)S(1)}, bf16[2,16,1024]{2,1,0:T(8,128)(2,1)S(1)}, u32[]{:S(2)}, u32[]{:S(2)}) %collective-permute-start.8) | collective-permute-done | bytes 65568 | tf_op jit(solution)/shard_map/ppermute | solution.py:277
  148.5 2.6 %collective-permute-done.9 = bf16[2,16,1024]{2,1,0:T(8,128)(2,1)S(1)} collective-permute-done((bf16[2,16,1024]{2,1,0:T(8,128)(2,1)S(1)}, bf16[2,16,1024]{2,1,0:T(8,128)(2,1)S(1)}, u32[]{:S(2)}, u32[]{:S(2)}) %collective-permute-start.9) | collective-permute-done | bytes 65568 | tf_op jit(solution)/shard_map/ppermute | solution.py:277
  151.1 3.9 %collective-permute-done.10 = bf16[2,16,1024]{2,1,0:T(8,128)(2,1)S(1)} collective-permute-done((bf16[2,16,1024]{2,1,0:T(8,128)(2,1)S(1)}, bf16[2,16,1024]{2,1,0:T(8,128)(2,1)S(1)}, u32[]{:S(2)}, u32[]{:S(2)}) %collective-permute-start.10) | collective-permute-done | bytes 65568 | tf_op jit(solution)/shard_map/ppermute | solution.py:277
  155.0 3.7 %collective-permute-done.11.prev_ref = bf16[2,2,128,128]{3,2,1,0:T(8,128)(2,1)S(1)} collective-permute-done((bf16[2,2,128,128]{3,2,1,0:T(8,128)(2,1)S(1)}, bf16[2,2,128,128]{3,2,1,0:T(8,128)(2,1)S(1)}, u32[]{:S(2)}, u32[]{:S(2)}) %collective-permute-start.11) | collective-permute-done | bytes 131104 | tf_op jit(solution)/shard_map/ppermute | solution.py:365
  158.7 1.4 collective-permute-start.13
  160.0 0.9 collective-permute-done.13
  160.9 0.6 fusion.1
  161.5 1.5 combine.1
  (27 shorter events, 1.3 us)
Async XLA Ops:
  0.6 1.8 %collective-permute-start.2 = (bf16[16,1024]{1,0:T(8,128)(2,1)}, bf16[16,1024]{1,0:T(8,128)(2,1)S(1)}, u32[]{:S(2)}, u32[]{:S(2)}) collective-permute-start(bf16[16,1024]{1,0:T(8,128)(2,1)} %param.15), channel_id=1, source_target_pairs={{0,1},{1,0},{2,3},{3,2},{4,5},{5,4},{6,7},{7,6},{8,9},{9,8},{10,11... | collective-permute-start | bytes 98312 | tf_op jit(solution)/shard_map/ppermute | solution.py:277
  3.2 8.9 %collective-permute-start.5 = (bf16[2,16,1024]{2,1,0:T(8,128)(2,1)S(1)}, bf16[2,16,1024]{2,1,0:T(8,128)(2,1)S(1)}, u32[]{:S(2)}, u32[]{:S(2)}) collective-permute-start(bf16[2,16,1024]{2,1,0:T(8,128)(2,1)S(1)} %pad_maximum_fusion.own_ref), channel_id=1, source_target_pairs={{0,6},{1,7},{2,4},{3,5},{4,2},{5,3},{6,0},{7,1},{8,14},{9,15},{10,... | collective-permute-start | bytes 196616 | tf_op jit(solution)/shard_map/ppermute | solution.py:277
  7.6 4.9 %collective-permute-start.4 = (bf16[2,16,1024]{2,1,0:T(8,128)(2,1)S(1)}, bf16[2,16,1024]{2,1,0:T(8,128)(2,1)S(1)}, u32[]{:S(2)}, u32[]{:S(2)}) collective-permute-start(bf16[2,16,1024]{2,1,0:T(8,128)(2,1)S(1)} %pad_maximum_fusion.own_ref), channel_id=1, source_target_pairs={{0,4},{1,5},{2,6},{3,7},{4,0},{5,1},{6,2},{7,3},{8,12},{9,13},{10,... | collective-permute-start | bytes 196616 | tf_op jit(solution)/shard_map/ppermute | solution.py:277
  7.6 4.9 %collective-permute-start.3 = (bf16[2,16,1024]{2,1,0:T(8,128)(2,1)S(1)}, bf16[2,16,1024]{2,1,0:T(8,128)(2,1)S(1)}, u32[]{:S(2)}, u32[]{:S(2)}) collective-permute-start(bf16[2,16,1024]{2,1,0:T(8,128)(2,1)S(1)} %pad_maximum_fusion.own_ref), channel_id=1, source_target_pairs={{0,2},{1,3},{2,0},{3,1},{4,6},{5,7},{6,4},{7,5},{8,10},{9,11},{10,... | collective-permute-start | bytes 196616 | tf_op jit(solution)/shard_map/ppermute | solution.py:277
  8.7 0.8 copy-start.3
  9.6 0.8 copy-start.4
  10.8 1.4 copy-start.1
  12.5 24.8 %copy-start.2 = (bf16[128,1024]{1,0:T(8,128)(2,1)S(1)}, bf16[128,1024]{1,0:T(8,128)(2,1)}, u32[]{:S(2)}) copy-start(bf16[128,1024]{1,0:T(8,128)(2,1)} %weight_ref.3) | copy-start | bytes 786436
  12.5 70.1 %copy-start.5 = (bf16[2,128,128]{2,1,0:T(8,128)(2,1)S(1)}, bf16[2,128,128]{2,1,0:T(8,128)(2,1)}, u32[]{:S(2)}) copy-start(bf16[2,128,128]{2,1,0:T(8,128)(2,1)} %q_ref.3) | copy-start | bytes 196612
  12.5 70.1 %copy-start.6 = (f32[2]{0:T(128)S(1)}, f32[2]{0:T(128)}, u32[]{:S(2)}) copy-start(f32[2]{0:T(128)} %slopes_ref.3) | copy-start | bytes 28
  12.5 70.1 %all-to-all-start = ((bf16[32,256,128]{2,1,0:T(8,128)(2,1)}), bf16[32,256,128]{2,1,0:T(8,128)(2,1)S(1)}, u32[]{:S(2)}, u32[]{:S(2)}) async-start(bf16[32,256,128]{2,1,0:T(8,128)(2,1)} %copy-done.1), calls=%async_computation | async-start | bytes 4194304 | tf_op jit(solution)/shard_map/all_to_all | solution.py:305
  25.9 51.1 %collective-permute-start.1 = (bf16[2,2,128,128]{3,2,1,0:T(8,128)(2,1)S(1)}, bf16[2,2,128,128]{3,2,1,0:T(8,128)(2,1)S(1)}, u32[]{:S(2)}, u32[]{:S(2)}) collective-permute-start(bf16[2,2,128,128]{3,2,1,0:T(8,128)(2,1)S(1)} %get-tuple-element.31.kv_ref), channel_id=1, source_target_pairs={{8,0},{16,8},{24,16},{32,24},{40,32},{48,40},{56,48},{64,56},{72,6... | collective-permute-start | bytes 393224 | tf_op jit(solution)/shard_map/ppermute | solution.py:311
  35.3 47.3 %collective-permute-start = (bf16[2,2,128,128]{3,2,1,0:T(8,128)(2,1)S(1)}, bf16[2,2,128,128]{3,2,1,0:T(8,128)(2,1)S(1)}, u32[]{:S(2)}, u32[]{:S(2)}) collective-permute-start(bf16[2,2,128,128]{3,2,1,0:T(8,128)(2,1)S(1)} %get-tuple-element.31.kv_ref), channel_id=1, source_target_pairs={{0,8},{8,16},{16,24},{24,32},{32,40},{40,48},{48,56},{56,64},{64,7... | collective-permute-start | bytes 393224 | tf_op jit(solution)/shard_map/ppermute | solution.py:310
  37.5 52.5 %collective-permute-start.7 = (bf16[128,128]{1,0:T(8,128)(2,1)S(1)}, bf16[128,128]{1,0:T(8,128)(2,1)S(1)}, u32[]{:S(2)}, u32[]{:S(2)}) collective-permute-start(bf16[128,128]{1,0:T(8,128)(2,1)S(1)} %context_grad.1.grad_ref), channel_id=1, source_target_pairs={{0,248},{8,240},{16,232},{24,224},{32,216},{40,208},{48,200},{56,1... | collective-permute-start | bytes 98312 | tf_op jit(solution)/shard_map/ppermute | solution.py:323
  86.4 12.5 %collective-permute-start.6 = (bf16[128,128]{1,0:T(8,128)(2,1)S(1)}, bf16[128,128]{1,0:T(8,128)(2,1)S(1)}, u32[]{:S(2)}, u32[]{:S(2)}) collective-permute-start(bf16[128,128]{1,0:T(8,128)(2,1)S(1)} %get-tuple-element.35), channel_id=1, source_target_pairs={{0,248},{8,240},{16,232},{24,224},{32,216},{40,208},{48,200},{56,1... | collective-permute-start | bytes 98312 | tf_op jit(solution)/shard_map/ppermute | solution.py:336
  97.6 1.4 copy-start
  99.1 61.8 %copy-start.7 = (bf16[16,1024]{1,0:T(8,128)(2,1)S(1)}, bf16[16,1024]{1,0:T(8,128)(2,1)}, u32[]{:S(2)}) copy-start(bf16[16,1024]{1,0:T(8,128)(2,1)} %param.9) | copy-start | bytes 98308
  99.2 62.4 %all-to-all-start.1 = ((bf16[32,256,128]{2,1,0:T(8,128)(2,1)}), bf16[32,256,128]{2,1,0:T(8,128)(2,1)S(1)}, u32[]{:S(2)}, u32[]{:S(2)}) async-start(bf16[32,256,128]{2,1,0:T(8,128)(2,1)} %copy-done), calls=%async_computation.1 | async-start | bytes 4194304 | tf_op jit(solution)/shard_map/all_to_all | solution.py:364
  107.0 41.5 %collective-permute-start.8 = (bf16[2,16,1024]{2,1,0:T(8,128)(2,1)S(1)}, bf16[2,16,1024]{2,1,0:T(8,128)(2,1)S(1)}, u32[]{:S(2)}, u32[]{:S(2)}) collective-permute-start(bf16[2,16,1024]{2,1,0:T(8,128)(2,1)S(1)} %get-tuple-element.45), channel_id=1, source_target_pairs={{0,2},{1,3},{2,0},{3,1},{4,6},{5,7},{6,4},{7,5},{8,10},{9,11},{10,... | collective-permute-start | bytes 196616 | tf_op jit(solution)/shard_map/ppermute | solution.py:277
  107.1 43.9 %collective-permute-start.9 = (bf16[2,16,1024]{2,1,0:T(8,128)(2,1)S(1)}, bf16[2,16,1024]{2,1,0:T(8,128)(2,1)S(1)}, u32[]{:S(2)}, u32[]{:S(2)}) collective-permute-start(bf16[2,16,1024]{2,1,0:T(8,128)(2,1)S(1)} %get-tuple-element.46), channel_id=1, source_target_pairs={{0,4},{1,5},{2,6},{3,7},{4,0},{5,1},{6,2},{7,3},{8,12},{9,13},{10,... | collective-permute-start | bytes 196616 | tf_op jit(solution)/shard_map/ppermute | solution.py:277
  109.1 45.8 %collective-permute-start.10 = (bf16[2,16,1024]{2,1,0:T(8,128)(2,1)S(1)}, bf16[2,16,1024]{2,1,0:T(8,128)(2,1)S(1)}, u32[]{:S(2)}, u32[]{:S(2)}) collective-permute-start(bf16[2,16,1024]{2,1,0:T(8,128)(2,1)S(1)} %get-tuple-element.47), channel_id=1, source_target_pairs={{0,6},{1,7},{2,4},{3,5},{4,2},{5,3},{6,0},{7,1},{8,14},{9,15},{10,... | collective-permute-start | bytes 196616 | tf_op jit(solution)/shard_map/ppermute | solution.py:277
  110.6 48.0 %collective-permute-start.11 = (bf16[2,2,128,128]{3,2,1,0:T(8,128)(2,1)S(1)}, bf16[2,2,128,128]{3,2,1,0:T(8,128)(2,1)S(1)}, u32[]{:S(2)}, u32[]{:S(2)}) collective-permute-start(bf16[2,2,128,128]{3,2,1,0:T(8,128)(2,1)S(1)} %get-tuple-element.48), channel_id=1, source_target_pairs={{0,8},{8,16},{16,24},{24,32},{32,40},{40,48},{48,56},{56,64},{64,7... | collective-permute-start | bytes 393224 | tf_op jit(solution)/shard_map/ppermute | solution.py:365
  113.7 44.9 %collective-permute-start.12 = (bf16[2,2,128,128]{3,2,1,0:T(8,128)(2,1)S(1)}, bf16[2,2,128,128]{3,2,1,0:T(8,128)(2,1)S(1)}, u32[]{:S(2)}, u32[]{:S(2)}) collective-permute-start(bf16[2,2,128,128]{3,2,1,0:T(8,128)(2,1)S(1)} %get-tuple-element.49), channel_id=1, source_target_pairs={{8,0},{16,8},{24,16},{32,24},{40,32},{48,40},{56,48},{64,56},{72,6... | collective-permute-start | bytes 393224 | tf_op jit(solution)/shard_map/ppermute | solution.py:366
  158.7 2.2 %collective-permute-start.13 = (bf16[16,1024]{1,0:T(8,128)(2,1)S(1)}, bf16[16,1024]{1,0:T(8,128)(2,1)S(1)}, u32[]{:S(2)}, u32[]{:S(2)}) collective-permute-start(bf16[16,1024]{1,0:T(8,128)(2,1)S(1)} %fusion.2), channel_id=1, source_target_pairs={{0,1},{1,0},{2,3},{3,2},{4,5},{5,4},{6,7},{7,6},{8,9},{9,8},{10,11... | collective-permute-start | bytes 98312 | tf_op jit(solution)/shard_map/ppermute | solution.py:277

commit v3 on v2

--- a/solution.py
+++ b/solution.py
@@ -46,8 +46,24 @@
     return dot(one_hot(n, lambda r: n - 1 - r), x, NN).astype(bf16)
 
 
+SEQ = ("x", "zh", "y")
+
+
 def place():
-    return lax.axis_index("seq"), lax.axis_size("seq")
+    x, zh, y = (lax.axis_index(a) for a in SEQ)
+    nx, nz, ny = (lax.axis_size(a) for a in SEQ)
+    return (x * nz + zh) * ny + y, nx * nz * ny, zh, y
+
+
+def slot_of(owner):
+    nz, ny = lax.axis_size("zh"), lax.axis_size("y")
+    xz, y = lax.div(owner, ny), lax.rem(owner, ny)
+    return (lax.div(xz, nz) * ny + y) * nz + lax.rem(xz, nz)
+
+
+def plane_readers(zh):
+    nx, nz, ny = (lax.axis_size(a) for a in SEQ)
+    return [(x * nz + zh) * ny + y for x in range(nx) for y in range(ny)]
 
 
 def part(t, which):
@@ -58,7 +74,7 @@
     entry = fb_ref[shard if t == 0 else shards - 1 - shard, f]
     owner = lax.shift_right_arithmetic(entry, 1)
     owner = owner if t == 0 else shards - 1 - owner
-    return entry >= 0, jnp.where(entry >= 0, owner, 0)
+    return entry >= 0, jnp.where(entry >= 0, slot_of(owner), 0)
 
 
 def asked_of(fb, t, shard, shards):
@@ -69,22 +85,41 @@
     return jnp.sum(hit, axis=1, keepdims=True)
 
 
-def pack_kernel(fb_ref, key_ref, value_ref, out_ref, kv_ref):
-    shard, shards = place()
+def asked_rows(fb_ref, asked_buf):
+    shard, shards, zh, y = place()
     fb = fb_ref[...]
-    for which, ref in ((0, key_ref), (1, value_ref)):
-        kv_ref[:, which] = ref[...]
-    for t in range(2):
-        asked = jnp.broadcast_to(asked_of(fb, t, shard, shards), (shards, 2 * HD))
-        for d in range(shards):
-            row = d if t == 0 else shards - 1 - d
-            second = jnp.broadcast_to(asked[row : row + 1] == 2, (BLK, 2 * HD))
-            for which, ref in ((0, key_ref), (1, value_ref)):
-                out_ref[d, part(t, which)] = jnp.where(second, ref[t, BLK:], ref[t, :BLK])
+    ny = lax.axis_size("y")
+    for z in range(lax.axis_size("zh")):
+        for t in range(2):
+            asked = asked_of(fb, t, shard + (z - zh) * ny, shards)
+            asked_buf[z, t] = jnp.broadcast_to(asked, asked_buf.shape[2:])
+
+
+def asked_by(asked_buf, z, t, reader, rows):
+    row = reader if t == 0 else asked_buf.shape[2] - 1 - reader
+    return jnp.broadcast_to(asked_buf[z, t, pl.ds(row, 1)], (rows, 2 * HD))
+
+
+def pack_kernel(fb_ref, own_ref, partner_ref, out_ref, up_ref, down_ref, asked_buf, kv_buf):
+    shard, shards, zh, y = place()
+    ny = lax.axis_size("y")
+    asked_rows(fb_ref, asked_buf)
+    kv_buf[zh] = own_ref[...]
+    kv_buf[1 - zh] = partner_ref[...]
+    up_ref[...] = kv_buf[jnp.where(y == ny - 1, 1 - zh, zh)]
+    down_ref[...] = kv_buf[jnp.where(y == 0, 1 - zh, zh)]
+    for p, reader in enumerate(plane_readers(zh)):
+        for z in range(2):
+            for t in range(2):
+                second = asked_by(asked_buf, z, t, reader, BLK) == 2
+                for which in range(2):
+                    out_ref[2 * p + z, part(t, which)] = jnp.where(
+                        second, kv_buf[z, t, which, BLK:], kv_buf[z, t, which, :BLK]
+                    )
 
 
 def stage(fb_ref, t, kv_ref, prev_ref, next_ref, far_ref, kbuf, vbuf):
-    shard, shards = place()
+    shard, shards, zh, y = place()
     for which, buf in ((0, kbuf), (1, vbuf)):
         buf[0:128] = prev_ref[t, which]
         buf[128:256] = kv_ref[t, which]
@@ -97,7 +132,7 @@
 
 
 def biased(fb_ref, t, slopes_ref, q2, kbuf, put):
-    shard, shards = place()
+    shard, shards, zh, y = place()
     cols = q2.shape[0]
     half = cols // 2
     head_col = lax.broadcasted_iota(jnp.int32, (1, cols), 1)
@@ -175,7 +210,7 @@
     fb_ref, slopes_ref, q_ref, kv_ref, prev_ref, next_ref, far_ref, stat_ref, grad_ref, mirrored_ref,
     gq_ref, own_out, prev_out, next_out, far_out, kbuf, vbuf, pbuf, dbuf,
 ):
-    shard, shards = place()
+    shard, shards, zh, y = place()
     n = 2 * HD
     eye = one_hot(n, lambda r: r)
     total = kbuf.shape[0]
@@ -219,28 +254,37 @@
         gq_ref[t] = (pick_heads(acc) * HD ** (-0.5)).astype(bf16)
 
 
-def combine_kernel(fb_ref, own_ref, prev_ref, next_ref, far_ref, gk_ref, gv_ref):
-    shard, shards = place()
-    fb = fb_ref[...]
+def combine_kernel(fb_ref, own_ref, prev_ref, next_ref, far_ref, mine_ref, other_ref, asked_buf, sum_buf):
+    shard, shards, zh, y = place()
+    last = lax.axis_size("y") - 1
+    asked_rows(fb_ref, asked_buf)
     rows = 32
-    for t in range(2):
-        asked = jnp.broadcast_to(asked_of(fb, t, shard, shards), (shards, 2 * HD))
-        for which, out_ref in ((0, gk_ref), (1, gv_ref)):
-            for lo in range(0, BLK, rows):
-                first = jnp.zeros((rows, 2 * HD), f32)
-                second = jnp.zeros((rows, 2 * HD), f32)
-                for d in range(shards):
-                    row = d if t == 0 else shards - 1 - d
-                    block = jnp.broadcast_to(asked[row : row + 1], (rows, 2 * HD))
+    for z in range(2):
+        for t in range(2):
+            for which in range(2):
+                for lo in range(0, BLK, rows):
+                    first = jnp.zeros((rows, 2 * HD), f32)
+                    second = jnp.zeros((rows, 2 * HD), f32)
                     at = part(t, which).start + lo
-                    x = far_ref[d, at : at + rows].astype(f32)
-                    first = first + jnp.where(block == 1, x, 0.0)
-                    second = second + jnp.where(block == 2, x, 0.0)
-                for at, far in ((lo, first), (BLK + lo, second)):
-                    here = slice(at, at + rows)
-                    total = own_ref[t, which, here] + prev_ref[t, which, here].astype(f32)
-                    total = total + next_ref[t, which, here].astype(f32)
-                    out_ref[t, here] = (total + far).astype(bf16)
+                    for p, reader in enumerate(plane_readers(zh)):
+                        block = asked_by(asked_buf, z, t, reader, rows)
+                        x = far_ref[2 * p + z, at : at + rows].astype(f32)
+                        first = first + jnp.where(block == 1, x, 0.0)
+                        second = second + jnp.where(block == 2, x, 0.0)
+                    sum_buf[z, t, which, lo : lo + rows] = first
+                    sum_buf[z, t, which, BLK + lo : BLK + lo + rows] = second
+    sum_buf[zh] = sum_buf[zh] + own_ref[...]
+    to = jnp.where(y == 0, 1 - zh, zh)
+    sum_buf[to] = sum_buf[to] + prev_ref[...].astype(f32)
+    to = jnp.where(y == last, 1 - zh, zh)
+    sum_buf[to] = sum_buf[to] + next_ref[...].astype(f32)
+    mine_ref[...] = sum_buf[zh]
+    other_ref[...] = sum_buf[1 - zh].astype(bf16)
+
+
+def finish_kernel(mine_ref, other_ref, gk_ref, gv_ref):
+    for which, ref in ((0, gk_ref), (1, gv_ref)):
+        ref[...] = (mine_ref[:, which] + other_ref[:, which].astype(f32)).astype(bf16)
 
 
 def project_kernel(ctx_ref, back_ref, weight_ref, own_ref, ref2, ref4, ref6, sum_buf):
@@ -280,7 +324,8 @@
 def per_device(
     residual, queries, keys, values, slopes, out_weight, cotangent, far_blocks, far_count
 ):
-    seq_count = lax.axis_size("seq")
+    nx, nz, ny = (lax.axis_size(a) for a in SEQ)
+    seq_count = nx * nz * ny
     tp_count = lax.axis_size("tp")
     tok_rows, width = queries.shape[1:]
     total_keys = 3 * tok_rows + far_blocks.shape[1] * BLK
@@ -290,25 +335,52 @@
     pieces = (tp_count, tok_rows // tp_count, width)
     slots = (seq_count, 4 * BLK, width)
 
-    outgoing, key_value = pl.pallas_call(
+    def plane_a2a(x):
+        x = x.reshape(nx * ny, nz * slots[1], width)
+        return lax.all_to_all(x, ("x", "y"), split_axis=0, concat_axis=0, tiled=True).reshape(slots)
+
+    def z_swap(x):
+        return lax.ppermute(x, "zh", [(i, nz - 1 - i) for i in range(nz)])
+
+    key_value = jnp.stack([keys, values], axis=1)
+    partner = z_swap(key_value)
+    asked = pltpu.VMEM((nz, 2, seq_count, 2 * HD), jnp.int32)
+    outgoing, to_up, to_down = pl.pallas_call(
         pack_kernel,
-        out_shape=(shape(slots), shape(both)),
+        out_shape=(shape(slots), shape(both), shape(both)),
         in_specs=[vmem()] * 3,
-        out_specs=(vmem(), vmem()),
+        out_specs=(vmem(),) * 3,
+        scratch_shapes=[asked, pltpu.VMEM((nz,) + both, bf16)],
         cost_estimate=cost(1_000_000, 2_500_000),
         compiler_params=pltpu.CompilerParams(vmem_limit_bytes=LIMIT),
         name="pack",
-    )(far_blocks, keys, values)
+    )(far_blocks, key_value, partner)
     own_pair = jnp.stack([cotangent, swap(cotangent, 1)])
     others = [swap(own_pair, bit) for bit in (2, 4, 6)]
     outgoing, *others = lax.optimization_barrier((outgoing, *others))
-    far = lax.all_to_all(outgoing, "seq", split_axis=0, concat_axis=0, tiled=True)
-
-    up = [(i, i + 1) for i in range(seq_count - 1)]
-    down = [(j, i) for i, j in up]
+    far = plane_a2a(outgoing)
+
+    def flat(x, zh, y):
+        return (x * nz + zh) * ny + y
+
+    places = [(x, zh, y) for x in range(nx) for zh in range(nz) for y in range(ny)]
+    up, down = [], []
+    for x, zh, y in places:
+        if y < ny - 1:
+            up.append((flat(x, zh, y), flat(x, zh, y + 1)))
+        elif zh == nz - 1:
+            up.append((flat(x, zh, y), flat(x, zh, 0)))
+        elif x < nx - 1:
+            up.append((flat(x, zh, y), flat(x + 1, zh, 0)))
+        if y > 0:
+            down.append((flat(x, zh, y), flat(x, zh, y - 1)))
+        elif zh == 0:
+            down.append((flat(x, zh, y), flat(x, zh, ny - 1)))
+        elif x > 0:
+            down.append((flat(x, zh, y), flat(x - 1, zh, ny - 1)))
     mirror = [(i, seq_count - 1 - i) for i in range(seq_count)]
-    from_prev = lax.ppermute(key_value, "seq", up)
-    from_next = lax.ppermute(key_value, "seq", down)
+    from_prev = lax.ppermute(to_up, SEQ, up)
+    from_next = lax.ppermute(to_down, SEQ, down)
 
     grad_context = pl.pallas_call(
         context_grad_kernel,
@@ -320,7 +392,7 @@
         compiler_params=pltpu.CompilerParams(vmem_limit_bytes=LIMIT),
         name="context_grad",
     )(own_pair, *others, out_weight)
-    mirrored = lax.ppermute(grad_context, "seq", mirror)
+    mirrored = lax.ppermute(grad_context, SEQ, mirror)
 
     keyed = [pltpu.VMEM((total_keys, width), bf16), pltpu.VMEM((total_keys, width), bf16)]
     context_fwd, context_rev, stats = pl.pallas_call(
@@ -333,7 +405,7 @@
         compiler_params=pltpu.CompilerParams(vmem_limit_bytes=LIMIT),
         name="attend_forward",
     )(far_blocks, slopes, queries, key_value, from_prev, from_next, far)
-    context_back = lax.ppermute(context_rev, "seq", mirror)
+    context_back = lax.ppermute(context_rev, SEQ, mirror)
 
     grad_queries, own, before, after, far_grads = pl.pallas_call(
         backward_kernel,
@@ -361,9 +433,9 @@
         name="project",
     )(context_fwd, context_back, out_weight)
     far_grads, *other_rows = lax.optimization_barrier((far_grads, *other_rows))
-    returned = lax.all_to_all(far_grads, "seq", split_axis=0, concat_axis=0, tiled=True)
-    from_prev_grad = lax.ppermute(after, "seq", up)
-    from_next_grad = lax.ppermute(before, "seq", down)
+    returned = plane_a2a(far_grads)
+    from_prev_grad = lax.ppermute(after, SEQ, [(b, a) for a, b in down])
+    from_next_grad = lax.ppermute(before, SEQ, [(b, a) for a, b in up])
 
     held = own_rows
     for bit, rows in zip((2, 4, 6), other_rows):
@@ -371,38 +443,36 @@
     held, from_prev_grad, from_next_grad = lax.optimization_barrier((held, from_prev_grad, from_next_grad))
     mixed = (residual.astype(f32) + held[0] + swap(held[1].astype(bf16), 1).astype(f32)).astype(bf16)
 
-    grad_keys, grad_values = pl.pallas_call(
+    mine, other = pl.pallas_call(
         combine_kernel,
-        out_shape=(shape((2, tok_rows, width)),) * 2,
+        out_shape=(shape(both, f32), shape(both)),
         in_specs=[vmem()] * 5,
         out_specs=(vmem(),) * 2,
+        scratch_shapes=[asked, pltpu.VMEM((nz,) + both, f32)],
         cost_estimate=cost(4_000_000, 3_000_000),
         compiler_params=pltpu.CompilerParams(vmem_limit_bytes=LIMIT),
         name="combine",
     )(far_blocks, own, from_prev_grad, from_next_grad, returned)
+    grad_keys, grad_values = pl.pallas_call(
+        finish_kernel,
+        out_shape=(shape((2, tok_rows, width)),) * 2,
+        in_specs=[vmem()] * 2,
+        out_specs=(vmem(),) * 2,
+        cost_estimate=cost(100_000, 500_000),
+        compiler_params=pltpu.CompilerParams(vmem_limit_bytes=LIMIT),
+        name="finish",
+    )(mine, z_swap(other))
     return (mixed, grad_queries, grad_keys, grad_values)
 
 
 def solution(mesh):
+    split = jax.sharding.Mesh(mesh.devices.reshape(4, 2, 4, -1), SEQ + ("tp",))
+    rows = P(SEQ + ("tp",), None)
+    strands = P(None, SEQ, "tp")
     return jax.shard_map(
         per_device,
-        mesh=mesh,
-        in_specs=(
-            P(("seq", "tp"), None),
-            P(None, "seq", "tp"),
-            P(None, "seq", "tp"),
-            P(None, "seq", "tp"),
-            P("tp"),
-            P("tp", None),
-            P(("seq", "tp"), None),
-            P(),
-            P(),
-        ),
-        out_specs=(
-            P(("seq", "tp"), None),
-            P(None, "seq", "tp"),
-            P(None, "seq", "tp"),
-            P(None, "seq", "tp"),
-        ),
+        mesh=split,
+        in_specs=(rows, strands, strands, strands, P("tp"), P("tp", None), rows, P(), P()),
+        out_specs=(rows, strands, strands, strands),
         check_vma=False,
     )

time: 164 us -> 126 us (0.77)
  the two profiles are of different devices: /device:TPU:7 before, /device:TPU:24 now
where the time goes in v3:
time: 126 us; the launch traced here: 125 us
  starting transfers between devices  55.2 us (44%)
  waiting for transfers between devices  48.3 us (38%)
  Pallas kernels  14.7 us (12%)
  local copies, waits for them, and re-layouts  3.48 us (3%)
  other arithmetic  2.32 us (2%)
    ppermute x1, waiting for transfers between devices, per_device(): from_prev = lax.ppermute(to_up, SEQ, up)  13.8 us
    all_to_all x2, starting transfers between devices, plane_a2a(): lax.all_to_all(x, ('x', 'y'), split_axis=0, concat_axis=0, tiled=True)  13.4 us
    ppermute x1, waiting for transfers between devices, per_device(): from_prev_grad = lax.ppermute(after, SEQ, [(b, a) for a, b in down])  12.3 us
    ppermute x2, starting transfers between devices, z_swap(): return lax.ppermute(x, 'zh', [(i, nz - 1 - i) for i in range(nz)])  9.06 us
    ppermute x2, waiting for transfers between devices, z_swap(): return lax.ppermute(x, 'zh', [(i, nz - 1 - i) for i in range(nz)])  9.01 us
    ppermute x8, starting transfers between devices, swap(): return lax.ppermute(x, 'tp', [(i, i ^ bit) for i in range(count)])  8.95 us
    pallas_call x1, Pallas kernels, per_device(): pl.pallas_call(backward_kernel, out_shape=(shape((2, tok_rows, width)), s...  8.18 us
    ppermute x1, starting transfers between devices, per_device(): mirrored = lax.ppermute(grad_context, SEQ, mirror)  6.3 us
  transfers between devices with their start and end apart: 18, of which 8 were waited for; matrix products, arithmetic and copies ran while one was open for 2% of the time, Pallas kernels for 11%

profile of v3, /device:TPU:24, one launch (start us, length us, event | category | flops | bytes accessed | tf_op | source)
XLA Modules:
  0.0 124.8 jit_solution(16160393570916402709)
XLA Ops:
  0.7 0.9 pad_maximum_fusion.own_ref.kv_ref
  1.6 7.3 %collective-permute-start = (bf16[2,2,128,128]{3,2,1,0:T(8,128)(2,1)S(1)}, bf16[2,2,128,128]{3,2,1,0:T(8,128)(2,1)S(1)}, u32[]{:S(2)}, u32[]{:S(2)}) collective-permute-start(bf16[2,2,128,128]{3,2,1,0:T(8,128)(2,1)S(1)} %pad_maximum_fusion.own_ref.kv_ref), channel_id=1, source_target_pairs={{0,32},{32,0},{1,33},{33,1},{2,34},{34,2},{3,35},{35,3},{4,36},{36... | collective-permute-start | bytes 393224 | tf_op jit(solution)/shard_map/ppermute | solution.py:343
  8.9 0.8 pad_maximum_fusion.1.own_ref
  9.7 1.9 %collective-permute-start.6 = (bf16[2,16,1024]{2,1,0:T(8,128)(2,1)S(1)}, bf16[2,16,1024]{2,1,0:T(8,128)(2,1)S(1)}, u32[]{:S(2)}, u32[]{:S(2)}) collective-permute-start(bf16[2,16,1024]{2,1,0:T(8,128)(2,1)S(1)} %pad_maximum_fusion.1.own_ref), channel_id=1, source_target_pairs={{0,6},{1,7},{2,4},{3,5},{4,2},{5,3},{6,0},{7,1},{8,14},{9,15},{10,... | collective-permute-start | bytes 196616 | tf_op jit(solution)/shard_map/ppermute | solution.py:321
  12.2 1.9 %collective-permute-start.4 = (bf16[2,16,1024]{2,1,0:T(8,128)(2,1)S(1)}, bf16[2,16,1024]{2,1,0:T(8,128)(2,1)S(1)}, u32[]{:S(2)}, u32[]{:S(2)}) collective-permute-start(bf16[2,16,1024]{2,1,0:T(8,128)(2,1)S(1)} %pad_maximum_fusion.1.own_ref), channel_id=1, source_target_pairs={{0,2},{1,3},{2,0},{3,1},{4,6},{5,7},{6,4},{7,5},{8,10},{9,11},{10,... | collective-permute-start | bytes 196616 | tf_op jit(solution)/shard_map/ppermute | solution.py:321
  14.1 0.8 copy.13.fb_ref
  14.8 0.6 pack.1
  15.5 1.3 %copy-done.1 = bf16[32,256,128]{2,1,0:T(8,128)(2,1)} copy-done((bf16[32,256,128]{2,1,0:T(8,128)(2,1)}, bf16[32,256,128]{2,1,0:T(8,128)(2,1)S(1)}, u32[]{:S(2)}) %copy-start.1) | copy-done | bytes 2097176
  16.8 1.1 collective-permute-done.6.ref6
  17.9 4.1 %collective-permute-done.5.ref4 = bf16[2,16,1024]{2,1,0:T(8,128)(2,1)S(1)} collective-permute-done((bf16[2,16,1024]{2,1,0:T(8,128)(2,1)S(1)}, bf16[2,16,1024]{2,1,0:T(8,128)(2,1)S(1)}, u32[]{:S(2)}, u32[]{:S(2)}) %collective-permute-start.5) | collective-permute-done | bytes 65568 | tf_op jit(solution)/shard_map/ppermute | solution.py:321
  21.9 7.3 %all-to-all-start = ((bf16[16,512,128]{2,1,0:T(8,128)(2,1)}), bf16[16,512,128]{2,1,0:T(8,128)(2,1)S(1)}, u32[]{:S(2)}, u32[]{:S(2)}) async-start(bf16[16,512,128]{2,1,0:T(8,128)(2,1)} %bitcast.20), calls=%async_computation | async-start | bytes 4194304 | tf_op jit(solution)/shard_map/all_to_all | solution.py:340
  29.3 3.4 %collective-permute-start.1 = (bf16[2,2,128,128]{3,2,1,0:T(8,128)(2,1)S(1)}, bf16[2,2,128,128]{3,2,1,0:T(8,128)(2,1)S(1)}, u32[]{:S(2)}, u32[]{:S(2)}) collective-permute-start(bf16[2,2,128,128]{3,2,1,0:T(8,128)(2,1)S(1)} %get-tuple-element.34), channel_id=1, source_target_pairs={{0,8},{8,16},{16,24},{24,64},{32,40},{40,48},{48,56},{56,32},{64,7... | collective-permute-start | bytes 393224 | tf_op jit(solution)/shard_map/ppermute | solution.py:382
  32.6 2.5 %collective-permute-start.2 = (bf16[2,2,128,128]{3,2,1,0:T(8,128)(2,1)S(1)}, bf16[2,2,128,128]{3,2,1,0:T(8,128)(2,1)S(1)}, u32[]{:S(2)}, u32[]{:S(2)}) collective-permute-start(bf16[2,2,128,128]{3,2,1,0:T(8,128)(2,1)S(1)} %get-tuple-element.35), channel_id=1, source_target_pairs={{0,24},{8,0},{16,8},{24,16},{40,32},{48,40},{56,48},{64,88},{72,64... | collective-permute-start | bytes 393224 | tf_op jit(solution)/shard_map/ppermute | solution.py:383
  35.4 6.3 %collective-permute-start.8 = (bf16[128,128]{1,0:T(8,128)(2,1)S(1)}, bf16[128,128]{1,0:T(8,128)(2,1)S(1)}, u32[]{:S(2)}, u32[]{:S(2)}) collective-permute-start(bf16[128,128]{1,0:T(8,128)(2,1)S(1)} %context_grad.1.grad_ref), channel_id=1, source_target_pairs={{0,248},{8,240},{16,232},{24,224},{32,216},{40,208},{48,200},{56,1... | collective-permute-start | bytes 98312 | tf_op jit(solution)/shard_map/ppermute | solution.py:395
  41.7 13.8 %collective-permute-done.1.prev_ref = bf16[2,2,128,128]{3,2,1,0:T(8,128)(2,1)S(1)} collective-permute-done((bf16[2,2,128,128]{3,2,1,0:T(8,128)(2,1)S(1)}, bf16[2,2,128,128]{3,2,1,0:T(8,128)(2,1)S(1)}, u32[]{:S(2)}, u32[]{:S(2)}) %collective-permute-start.1) | collective-permute-done | bytes 131104 | tf_op jit(solution)/shard_map/ppermute | solution.py:382
  55.5 2.1 %collective-permute-done.2.next_ref = bf16[2,2,128,128]{3,2,1,0:T(8,128)(2,1)S(1)} collective-permute-done((bf16[2,2,128,128]{3,2,1,0:T(8,128)(2,1)S(1)}, bf16[2,2,128,128]{3,2,1,0:T(8,128)(2,1)S(1)}, u32[]{:S(2)}, u32[]{:S(2)}) %collective-permute-start.2) | collective-permute-done | bytes 131104 | tf_op jit(solution)/shard_map/ppermute | solution.py:383
  57.8 3.8 %attend_forward.1 = (bf16[128,128]{1,0:T(8,128)(2,1)S(1)}, bf16[128,128]{1,0:T(8,128)(2,1)S(1)}, f32[2,2,256]{2,1,0:T(2,128)S(1)}) custom-call(s32[32,24]{1,0:T(8,128)S(1)} %copy.13.fb_ref, f32[2]{0:T(128)S(1)} %copy-done.4, bf16[2,128,128]{2,1,0:T(8,128)(2,1)S(1)} %copy-done.3, bf16[2,2,128,128]{3,2,1,0:T(8,128)(2,1)S(1)} %pad_maximum_fusion.own_ref.kv_ref, ...), custom_call_target="tpu_custom_call" | custom-call | flops 1600000000 | bytes 4000000 | tf_op jit(solution)/shard_map/attend_forward/pallas_call | solution.py:398
  61.6 5.8 %collective-permute-start.7 = (bf16[128,128]{1,0:T(8,128)(2,1)S(1)}, bf16[128,128]{1,0:T(8,128)(2,1)S(1)}, u32[]{:S(2)}, u32[]{:S(2)}) collective-permute-start(bf16[128,128]{1,0:T(8,128)(2,1)S(1)} %get-tuple-element.39), channel_id=1, source_target_pairs={{0,248},{8,240},{16,232},{24,224},{32,216},{40,208},{48,200},{56,1... | collective-permute-start | bytes 98312 | tf_op jit(solution)/shard_map/ppermute | solution.py:408
  67.4 8.2 %attend_backward.1 = (bf16[2,128,128]{2,1,0:T(8,128)(2,1)}, f32[2,2,128,128]{3,2,1,0:T(8,128)S(1)}, bf16[2,2,128,128]{3,2,1,0:T(8,128)(2,1)S(1)}, bf16[2,2,128,1...) custom-call(s32[32,24]{1,0:T(8,128)S(1)} %copy.13.fb_ref, f32[2]{0:T(128)S(1)} %copy-done.4, ...), custom_call_target="tpu_custom_call" | custom-call | flops 3200000000 | bytes 8000000 | tf_op jit(solution)/shard_map/attend_backward/pallas_call | solution.py:410
  75.6 1.3 %copy-done = bf16[32,256,128]{2,1,0:T(8,128)(2,1)} copy-done((bf16[32,256,128]{2,1,0:T(8,128)(2,1)}, bf16[32,256,128]{2,1,0:T(8,128)(2,1)S(1)}, u32[]{:S(2)}) %copy-start) | copy-done | bytes 2097176
  77.2 6.1 %all-to-all-start.1 = ((bf16[16,512,128]{2,1,0:T(8,128)(2,1)}), bf16[16,512,128]{2,1,0:T(8,128)(2,1)S(1)}, u32[]{:S(2)}, u32[]{:S(2)}) async-start(bf16[16,512,128]{2,1,0:T(8,128)(2,1)} %bitcast.17), calls=%async_computation.1 | async-start | bytes 4194304 | tf_op jit(solution)/shard_map/all_to_all | solution.py:340
  83.4 1.4 %collective-permute-start.10 = (bf16[2,16,1024]{2,1,0:T(8,128)(2,1)S(1)}, bf16[2,16,1024]{2,1,0:T(8,128)(2,1)S(1)}, u32[]{:S(2)}, u32[]{:S(2)}) collective-permute-start(bf16[2,16,1024]{2,1,0:T(8,128)(2,1)S(1)} %get-tuple-element.50), channel_id=1, source_target_pairs={{0,4},{1,5},{2,6},{3,7},{4,0},{5,1},{6,2},{7,3},{8,12},{9,13},{10,... | collective-permute-start | bytes 196616 | tf_op jit(solution)/shard_map/ppermute | solution.py:321
  84.8 3.0 %collective-permute-start.11 = (bf16[2,16,1024]{2,1,0:T(8,128)(2,1)S(1)}, bf16[2,16,1024]{2,1,0:T(8,128)(2,1)S(1)}, u32[]{:S(2)}, u32[]{:S(2)}) collective-permute-start(bf16[2,16,1024]{2,1,0:T(8,128)(2,1)S(1)} %get-tuple-element.51), channel_id=1, source_target_pairs={{0,6},{1,7},{2,4},{3,5},{4,2},{5,3},{6,0},{7,1},{8,14},{9,15},{10,... | collective-permute-start | bytes 196616 | tf_op jit(solution)/shard_map/ppermute | solution.py:321
  87.8 2.0 %collective-permute-start.12 = (bf16[2,2,128,128]{3,2,1,0:T(8,128)(2,1)S(1)}, bf16[2,2,128,128]{3,2,1,0:T(8,128)(2,1)S(1)}, u32[]{:S(2)}, u32[]{:S(2)}) collective-permute-start(bf16[2,2,128,128]{3,2,1,0:T(8,128)(2,1)S(1)} %get-tuple-element.52), channel_id=1, source_target_pairs={{24,0},{0,8},{8,16},{16,24},{32,40},{40,48},{48,56},{88,64},{64,72... | collective-permute-start | bytes 393224 | tf_op jit(solution)/shard_map/ppermute | solution.py:437
  89.8 3.8 %collective-permute-start.13 = (bf16[2,2,128,128]{3,2,1,0:T(8,128)(2,1)S(1)}, bf16[2,2,128,128]{3,2,1,0:T(8,128)(2,1)S(1)}, u32[]{:S(2)}, u32[]{:S(2)}) collective-permute-start(bf16[2,2,128,128]{3,2,1,0:T(8,128)(2,1)S(1)} %get-tuple-element.53), channel_id=1, source_target_pairs={{8,0},{16,8},{24,16},{64,24},{40,32},{48,40},{56,48},{32,56},{72,6... | collective-permute-start | bytes 393224 | tf_op jit(solution)/shard_map/ppermute | solution.py:438
  93.7 12.3 %collective-permute-done.12.prev_ref = bf16[2,2,128,128]{3,2,1,0:T(8,128)(2,1)S(1)} collective-permute-done((bf16[2,2,128,128]{3,2,1,0:T(8,128)(2,1)S(1)}, bf16[2,2,128,128]{3,2,1,0:T(8,128)(2,1)S(1)}, u32[]{:S(2)}, u32[]{:S(2)}) %collective-permute-start.12) | collective-permute-done | bytes 131104 | tf_op jit(solution)/shard_map/ppermute | solution.py:437
  106.0 5.7 %collective-permute-done.13.next_ref = bf16[2,2,128,128]{3,2,1,0:T(8,128)(2,1)S(1)} collective-permute-done((bf16[2,2,128,128]{3,2,1,0:T(8,128)(2,1)S(1)}, bf16[2,2,128,128]{3,2,1,0:T(8,128)(2,1)S(1)}, u32[]{:S(2)}, u32[]{:S(2)}) %collective-permute-start.13) | collective-permute-done | bytes 131104 | tf_op jit(solution)/shard_map/ppermute | solution.py:438
  111.8 1.0 combine.1
  112.7 1.8 %collective-permute-start.15 = (bf16[2,2,128,128]{3,2,1,0:T(8,128)(2,1)S(1)}, bf16[2,2,128,128]{3,2,1,0:T(8,128)(2,1)S(1)}, u32[]{:S(2)}, u32[]{:S(2)}) collective-permute-start(bf16[2,2,128,128]{3,2,1,0:T(8,128)(2,1)S(1)} %get-tuple-element.61), channel_id=1, source_target_pairs={{0,32},{32,0},{1,33},{33,1},{2,34},{34,2},{3,35},{35,3},{4,36},{36... | collective-permute-start | bytes 393224 | tf_op jit(solution)/shard_map/ppermute | solution.py:343
  114.5 0.6 fusion.1
  115.2 9.0 %collective-permute-done.15.other_ref = bf16[2,2,128,128]{3,2,1,0:T(8,128)(2,1)S(1)} collective-permute-done((bf16[2,2,128,128]{3,2,1,0:T(8,128)(2,1)S(1)}, bf16[2,2,128,128]{3,2,1,0:T(8,128)(2,1)S(1)}, u32[]{:S(2)}, u32[]{:S(2)}) %collective-permute-start.15) | collective-permute-done | bytes 131104 | tf_op jit(solution)/shard_map/ppermute | solution.py:343
  124.2 0.7 finish.1
  (29 shorter events, 1.5 us)
Async XLA Ops:
  0.6 8.3 %collective-permute-start.3 = (bf16[16,1024]{1,0:T(8,128)(2,1)}, bf16[16,1024]{1,0:T(8,128)(2,1)S(1)}, u32[]{:S(2)}, u32[]{:S(2)}) collective-permute-start(bf16[16,1024]{1,0:T(8,128)(2,1)} %param.15), channel_id=1, source_target_pairs={{0,1},{1,0},{2,3},{3,2},{4,5},{5,4},{6,7},{7,6},{8,9},{9,8},{10,11... | collective-permute-start | bytes 98312 | tf_op jit(solution)/shard_map/ppermute | solution.py:321
  1.6 13.2 %collective-permute-start = (bf16[2,2,128,128]{3,2,1,0:T(8,128)(2,1)S(1)}, bf16[2,2,128,128]{3,2,1,0:T(8,128)(2,1)S(1)}, u32[]{:S(2)}, u32[]{:S(2)}) collective-permute-start(bf16[2,2,128,128]{3,2,1,0:T(8,128)(2,1)S(1)} %pad_maximum_fusion.own_ref.kv_ref), channel_id=1, source_target_pairs={{0,32},{32,0},{1,33},{33,1},{2,34},{34,2},{3,35},{35,3},{4,36},{36... | collective-permute-start | bytes 393224 | tf_op jit(solution)/shard_map/ppermute | solution.py:343
  9.7 8.2 %collective-permute-start.6 = (bf16[2,16,1024]{2,1,0:T(8,128)(2,1)S(1)}, bf16[2,16,1024]{2,1,0:T(8,128)(2,1)S(1)}, u32[]{:S(2)}, u32[]{:S(2)}) collective-permute-start(bf16[2,16,1024]{2,1,0:T(8,128)(2,1)S(1)} %pad_maximum_fusion.1.own_ref), channel_id=1, source_target_pairs={{0,6},{1,7},{2,4},{3,5},{4,2},{5,3},{6,0},{7,1},{8,14},{9,15},{10,... | collective-permute-start | bytes 196616 | tf_op jit(solution)/shard_map/ppermute | solution.py:321
  11.6 10.3 %collective-permute-start.5 = (bf16[2,16,1024]{2,1,0:T(8,128)(2,1)S(1)}, bf16[2,16,1024]{2,1,0:T(8,128)(2,1)S(1)}, u32[]{:S(2)}, u32[]{:S(2)}) collective-permute-start(bf16[2,16,1024]{2,1,0:T(8,128)(2,1)S(1)} %pad_maximum_fusion.1.own_ref), channel_id=1, source_target_pairs={{0,4},{1,5},{2,6},{3,7},{4,0},{5,1},{6,2},{7,3},{8,12},{9,13},{10,... | collective-permute-start | bytes 196616 | tf_op jit(solution)/shard_map/ppermute | solution.py:321
  12.2 9.8 %collective-permute-start.4 = (bf16[2,16,1024]{2,1,0:T(8,128)(2,1)S(1)}, bf16[2,16,1024]{2,1,0:T(8,128)(2,1)S(1)}, u32[]{:S(2)}, u32[]{:S(2)}) collective-permute-start(bf16[2,16,1024]{2,1,0:T(8,128)(2,1)S(1)} %pad_maximum_fusion.1.own_ref), channel_id=1, source_target_pairs={{0,2},{1,3},{2,0},{3,1},{4,6},{5,7},{6,4},{7,5},{8,10},{9,11},{10,... | collective-permute-start | bytes 196616 | tf_op jit(solution)/shard_map/ppermute | solution.py:321
  15.4 1.3 %copy-start.1 = (bf16[32,256,128]{2,1,0:T(8,128)(2,1)}, bf16[32,256,128]{2,1,0:T(8,128)(2,1)S(1)}, u32[]{:S(2)}) copy-start(bf16[32,256,128]{2,1,0:T(8,128)(2,1)S(1)} %get-tuple-element.37) | copy-start | bytes 6291460
  21.9 13.2 %copy-start.2 = (bf16[128,1024]{1,0:T(8,128)(2,1)S(1)}, bf16[128,1024]{1,0:T(8,128)(2,1)}, u32[]{:S(2)}) copy-start(bf16[128,1024]{1,0:T(8,128)(2,1)} %weight_ref.3) | copy-start | bytes 786436
  21.9 35.8 %copy-start.3 = (bf16[2,128,128]{2,1,0:T(8,128)(2,1)S(1)}, bf16[2,128,128]{2,1,0:T(8,128)(2,1)}, u32[]{:S(2)}) copy-start(bf16[2,128,128]{2,1,0:T(8,128)(2,1)} %q_ref.3) | copy-start | bytes 196612
  21.9 35.8 %copy-start.4 = (f32[2]{0:T(128)S(1)}, f32[2]{0:T(128)}, u32[]{:S(2)}) copy-start(f32[2]{0:T(128)} %slopes_ref.3) | copy-start | bytes 28
  21.9 35.8 %all-to-all-start = ((bf16[16,512,128]{2,1,0:T(8,128)(2,1)}), bf16[16,512,128]{2,1,0:T(8,128)(2,1)S(1)}, u32[]{:S(2)}, u32[]{:S(2)}) async-start(bf16[16,512,128]{2,1,0:T(8,128)(2,1)} %bitcast.20), calls=%async_computation | async-start | bytes 4194304 | tf_op jit(solution)/shard_map/all_to_all | solution.py:340
  29.3 26.2 %collective-permute-start.1 = (bf16[2,2,128,128]{3,2,1,0:T(8,128)(2,1)S(1)}, bf16[2,2,128,128]{3,2,1,0:T(8,128)(2,1)S(1)}, u32[]{:S(2)}, u32[]{:S(2)}) collective-permute-start(bf16[2,2,128,128]{3,2,1,0:T(8,128)(2,1)S(1)} %get-tuple-element.34), channel_id=1, source_target_pairs={{0,8},{8,16},{16,24},{24,64},{32,40},{40,48},{48,56},{56,32},{64,7... | collective-permute-start | bytes 393224 | tf_op jit(solution)/shard_map/ppermute | solution.py:382
  32.6 24.9 %collective-permute-start.2 = (bf16[2,2,128,128]{3,2,1,0:T(8,128)(2,1)S(1)}, bf16[2,2,128,128]{3,2,1,0:T(8,128)(2,1)S(1)}, u32[]{:S(2)}, u32[]{:S(2)}) collective-permute-start(bf16[2,2,128,128]{3,2,1,0:T(8,128)(2,1)S(1)} %get-tuple-element.35), channel_id=1, source_target_pairs={{0,24},{8,0},{16,8},{24,16},{40,32},{48,40},{56,48},{64,88},{72,64... | collective-permute-start | bytes 393224 | tf_op jit(solution)/shard_map/ppermute | solution.py:383
  35.4 32.1 %collective-permute-start.8 = (bf16[128,128]{1,0:T(8,128)(2,1)S(1)}, bf16[128,128]{1,0:T(8,128)(2,1)S(1)}, u32[]{:S(2)}, u32[]{:S(2)}) collective-permute-start(bf16[128,128]{1,0:T(8,128)(2,1)S(1)} %context_grad.1.grad_ref), channel_id=1, source_target_pairs={{0,248},{8,240},{16,232},{24,224},{32,216},{40,208},{48,200},{56,1... | collective-permute-start | bytes 98312 | tf_op jit(solution)/shard_map/ppermute | solution.py:395
  61.6 15.4 %collective-permute-start.7 = (bf16[128,128]{1,0:T(8,128)(2,1)S(1)}, bf16[128,128]{1,0:T(8,128)(2,1)S(1)}, u32[]{:S(2)}, u32[]{:S(2)}) collective-permute-start(bf16[128,128]{1,0:T(8,128)(2,1)S(1)} %get-tuple-element.39), channel_id=1, source_target_pairs={{0,248},{8,240},{16,232},{24,224},{32,216},{40,208},{48,200},{56,1... | collective-permute-start | bytes 98312 | tf_op jit(solution)/shard_map/ppermute | solution.py:408
  75.6 1.3 %copy-start = (bf16[32,256,128]{2,1,0:T(8,128)(2,1)}, bf16[32,256,128]{2,1,0:T(8,128)(2,1)S(1)}, u32[]{:S(2)}) copy-start(bf16[32,256,128]{2,1,0:T(8,128)(2,1)S(1)} %get-tuple-element.59) | copy-start | bytes 6291460
  77.2 34.6 %all-to-all-start.1 = ((bf16[16,512,128]{2,1,0:T(8,128)(2,1)}), bf16[16,512,128]{2,1,0:T(8,128)(2,1)S(1)}, u32[]{:S(2)}, u32[]{:S(2)}) async-start(bf16[16,512,128]{2,1,0:T(8,128)(2,1)} %bitcast.17), calls=%async_computation.1 | async-start | bytes 4194304 | tf_op jit(solution)/shard_map/all_to_all | solution.py:340
  83.3 31.2 %copy-start.5 = (bf16[16,1024]{1,0:T(8,128)(2,1)S(1)}, bf16[16,1024]{1,0:T(8,128)(2,1)}, u32[]{:S(2)}) copy-start(bf16[16,1024]{1,0:T(8,128)(2,1)} %param.9) | copy-start | bytes 98308
  83.3 10.3 %collective-permute-start.9 = (bf16[2,16,1024]{2,1,0:T(8,128)(2,1)S(1)}, bf16[2,16,1024]{2,1,0:T(8,128)(2,1)S(1)}, u32[]{:S(2)}, u32[]{:S(2)}) collective-permute-start(bf16[2,16,1024]{2,1,0:T(8,128)(2,1)S(1)} %get-tuple-element.49), channel_id=1, source_target_pairs={{0,2},{1,3},{2,0},{3,1},{4,6},{5,7},{6,4},{7,5},{8,10},{9,11},{10,... | collective-permute-start | bytes 196616 | tf_op jit(solution)/shard_map/ppermute | solution.py:321
  83.4 10.2 %collective-permute-start.10 = (bf16[2,16,1024]{2,1,0:T(8,128)(2,1)S(1)}, bf16[2,16,1024]{2,1,0:T(8,128)(2,1)S(1)}, u32[]{:S(2)}, u32[]{:S(2)}) collective-permute-start(bf16[2,16,1024]{2,1,0:T(8,128)(2,1)S(1)} %get-tuple-element.50), channel_id=1, source_target_pairs={{0,4},{1,5},{2,6},{3,7},{4,0},{5,1},{6,2},{7,3},{8,12},{9,13},{10,... | collective-permute-start | bytes 196616 | tf_op jit(solution)/shard_map/ppermute | solution.py:321
  84.8 8.9 %collective-permute-start.11 = (bf16[2,16,1024]{2,1,0:T(8,128)(2,1)S(1)}, bf16[2,16,1024]{2,1,0:T(8,128)(2,1)S(1)}, u32[]{:S(2)}, u32[]{:S(2)}) collective-permute-start(bf16[2,16,1024]{2,1,0:T(8,128)(2,1)S(1)} %get-tuple-element.51), channel_id=1, source_target_pairs={{0,6},{1,7},{2,4},{3,5},{4,2},{5,3},{6,0},{7,1},{8,14},{9,15},{10,... | collective-permute-start | bytes 196616 | tf_op jit(solution)/shard_map/ppermute | solution.py:321
  87.8 18.2 %collective-permute-start.12 = (bf16[2,2,128,128]{3,2,1,0:T(8,128)(2,1)S(1)}, bf16[2,2,128,128]{3,2,1,0:T(8,128)(2,1)S(1)}, u32[]{:S(2)}, u32[]{:S(2)}) collective-permute-start(bf16[2,2,128,128]{3,2,1,0:T(8,128)(2,1)S(1)} %get-tuple-element.52), channel_id=1, source_target_pairs={{24,0},{0,8},{8,16},{16,24},{32,40},{40,48},{48,56},{88,64},{64,72... | collective-permute-start | bytes 393224 | tf_op jit(solution)/shard_map/ppermute | solution.py:437
  89.8 21.9 %collective-permute-start.13 = (bf16[2,2,128,128]{3,2,1,0:T(8,128)(2,1)S(1)}, bf16[2,2,128,128]{3,2,1,0:T(8,128)(2,1)S(1)}, u32[]{:S(2)}, u32[]{:S(2)}) collective-permute-start(bf16[2,2,128,128]{3,2,1,0:T(8,128)(2,1)S(1)} %get-tuple-element.53), channel_id=1, source_target_pairs={{8,0},{16,8},{24,16},{64,24},{40,32},{48,40},{56,48},{32,56},{72,6... | collective-permute-start | bytes 393224 | tf_op jit(solution)/shard_map/ppermute | solution.py:438
  111.7 2.8 %collective-permute-start.14 = (bf16[16,1024]{1,0:T(8,128)(2,1)S(1)}, bf16[16,1024]{1,0:T(8,128)(2,1)S(1)}, u32[]{:S(2)}, u32[]{:S(2)}) collective-permute-start(bf16[16,1024]{1,0:T(8,128)(2,1)S(1)} %fusion.2), channel_id=1, source_target_pairs={{0,1},{1,0},{2,3},{3,2},{4,5},{5,4},{6,7},{7,6},{8,9},{9,8},{10,11... | collective-permute-start | bytes 98312 | tf_op jit(solution)/shard_map/ppermute | solution.py:321
  112.7 11.4 %collective-permute-start.15 = (bf16[2,2,128,128]{3,2,1,0:T(8,128)(2,1)S(1)}, bf16[2,2,128,128]{3,2,1,0:T(8,128)(2,1)S(1)}, u32[]{:S(2)}, u32[]{:S(2)}) collective-permute-start(bf16[2,2,128,128]{3,2,1,0:T(8,128)(2,1)S(1)} %get-tuple-element.61), channel_id=1, source_target_pairs={{0,32},{32,0},{1,33},{33,1},{2,34},{34,2},{3,35},{35,3},{4,36},{36... | collective-permute-start | bytes 393224 | tf_op jit(solution)/shard_map/ppermute | solution.py:343

commit v4 on v3

--- a/solution.py
+++ b/solution.py
@@ -100,7 +100,7 @@
     return jnp.broadcast_to(asked_buf[z, t, pl.ds(row, 1)], (rows, 2 * HD))
 
 
-def pack_kernel(fb_ref, own_ref, partner_ref, out_ref, up_ref, down_ref, asked_buf, kv_buf):
+def pack_kernel(fb_ref, own_ref, partner_ref, out_ref, up_ref, down_ref, asked_buf, kv_buf, out_buf, sems):
     shard, shards, zh, y = place()
     ny = lax.axis_size("y")
     asked_rows(fb_ref, asked_buf)
@@ -108,14 +108,21 @@
     kv_buf[1 - zh] = partner_ref[...]
     up_ref[...] = kv_buf[jnp.where(y == ny - 1, 1 - zh, zh)]
     down_ref[...] = kv_buf[jnp.where(y == 0, 1 - zh, zh)]
+    copies = []
     for p, reader in enumerate(plane_readers(zh)):
         for z in range(2):
             for t in range(2):
                 second = asked_by(asked_buf, z, t, reader, BLK) == 2
                 for which in range(2):
-                    out_ref[2 * p + z, part(t, which)] = jnp.where(
+                    out_buf[2 * p + z, part(t, which)] = jnp.where(
                         second, kv_buf[z, t, which, BLK:], kv_buf[z, t, which, :BLK]
                     )
+        if p % 4 == 3:
+            done = pl.ds(2 * p - 6, 8)
+            copies.append(pltpu.make_async_copy(out_buf.at[done], out_ref.at[done], sems.at[p // 4]))
+            copies[-1].start()
+    for copy in copies:
+        copy.wait()
 
 
 def stage(fb_ref, t, kv_ref, prev_ref, next_ref, far_ref, kbuf, vbuf):
@@ -163,41 +170,10 @@
     return top
 
 
-def forward_kernel(fb_ref, slopes_ref, q_ref, kv_ref, prev_ref, next_ref, far_ref, ctx_ref, rev_ref, stat_ref, kbuf, vbuf, sbuf):
-    n = 2 * HD
-    eye = one_hot(n, lambda r: r)
-    total = kbuf.shape[0]
-    for t in (1, 0):
-        stage(fb_ref, t, kv_ref, prev_ref, next_ref, far_ref, kbuf, vbuf)
-        q2 = two_heads(q_ref[t] * HD ** (-0.5))
-
-        def put(lo, hi, scores):
-            sbuf[lo:hi] = scores
-
-        top = biased(fb_ref, t, slopes_ref, q2, kbuf, put)
-        norm = jnp.zeros_like(top)
-        for lo in range(0, total, STEP):
-            w = jnp.exp(sbuf[lo : lo + STEP] - top)
-            sbuf[lo : lo + STEP] = w
-            norm = norm + jnp.sum(w, axis=0, keepdims=True)
-        inv = 1.0 / norm
-        stat_ref[t, 0:1] = top
-        stat_ref[t, 1:2] = inv
-        acc = jnp.zeros((n, q2.shape[0]), f32)
-        for lo in range(0, total, STEP):
-            low = (sbuf[lo : lo + STEP] * inv).astype(bf16)
-            vt = dot(eye, vbuf[lo : lo + STEP], NT).astype(bf16)
-            acc = acc + dot(vt, low, NN)
-        ctx = pick_heads(acc).astype(bf16)
-        if t == 1:
-            rev_ref[...] = flipped(ctx)
-        else:
-            ctx_ref[...] = ctx
-
-
-def context_grad_kernel(own_ref, ref2, ref4, ref6, weight_ref, out_ref, buf):
+def context_grad_kernel(ref0, ref2, ref4, ref6, odd_ref, weight_ref, out_ref, buf):
     count, rows, _ = buf.shape
-    got = jnp.concatenate([ref[k] for ref in (own_ref, ref2, ref4, ref6) for k in range(2)], axis=0)
+    got = [x for k, ref in enumerate((ref0, ref2, ref4, ref6)) for x in (ref[...], odd_ref[k])]
+    got = jnp.concatenate(got, axis=0)
     out = dot(got, weight_ref[...], NT).astype(bf16)
     for k in range(count):
         buf[k] = out[k * rows : (k + 1) * rows]
@@ -206,52 +182,72 @@
         out_ref[k * rows : (k + 1) * rows] = buf[lax.bitwise_xor(at, k)]
 
 
-def backward_kernel(
-    fb_ref, slopes_ref, q_ref, kv_ref, prev_ref, next_ref, far_ref, stat_ref, grad_ref, mirrored_ref,
-    gq_ref, own_out, prev_out, next_out, far_out, kbuf, vbuf, pbuf, dbuf,
+def attend_kernel(
+    fb_ref, slopes_ref, q_ref, kv_ref, prev_ref, next_ref, far_ref, grad_ref, mirrored_ref,
+    ctx_ref, rev_ref, gq_ref, own_out, prev_out, next_out, far_out,
+    kbuf, vbuf, pbuf, dbuf, far_buf0, far_buf1, sems,
 ):
     shard, shards, zh, y = place()
     n = 2 * HD
     eye = one_hot(n, lambda r: r)
     total = kbuf.shape[0]
+    copies = []
     for t in range(2):
+        far_buf = (far_buf0, far_buf1)[t]
         stage(fb_ref, t, kv_ref, prev_ref, next_ref, far_ref, kbuf, vbuf)
         q2 = two_heads(q_ref[t] * HD ** (-0.5))
         g2 = two_heads(flipped(mirrored_ref[...]) if t == 1 else grad_ref[...])
         cols = q2.shape[0]
-        top = stat_ref[t, 0:1]
-        inv = stat_ref[t, 1:2]
 
         def put(lo, hi, scores):
-            pbuf[lo:hi] = jnp.exp(scores - top) * inv
-
-        biased(fb_ref, t, slopes_ref, q2, kbuf, put)
+            pbuf[lo:hi] = scores
+
+        top = biased(fb_ref, t, slopes_ref, q2, kbuf, put)
+        norm = jnp.zeros((1, cols), f32)
         row_dot = jnp.zeros((1, cols), f32)
         for lo in range(0, total, STEP):
+            w = jnp.exp(pbuf[lo : lo + STEP] - top)
             gp = dot(vbuf[lo : lo + STEP], g2, NT)
+            pbuf[lo : lo + STEP] = w
             dbuf[lo : lo + STEP] = gp
-            row_dot = row_dot + jnp.sum(pbuf[lo : lo + STEP] * gp, axis=0, keepdims=True)
-        acc = jnp.zeros((n, cols), f32)
+            norm = norm + jnp.sum(w, axis=0, keepdims=True)
+            row_dot = row_dot + jnp.sum(w * gp, axis=0, keepdims=True)
+        inv = 1.0 / norm
+        row_dot = row_dot * inv
+        gq_acc = jnp.zeros((n, cols), f32)
+        ctx_acc = jnp.zeros((n, cols), f32)
         for lo in range(0, total, STEP):
-            p = pbuf[lo : lo + STEP]
+            p = pbuf[lo : lo + STEP] * inv
+            low = p.astype(bf16)
             ds = (p * (dbuf[lo : lo + STEP] - row_dot)).astype(bf16)
+            vt = dot(eye, vbuf[lo : lo + STEP], NT).astype(bf16)
+            ctx_acc = ctx_acc + dot(vt, low, NN)
             kt = dot(eye, kbuf[lo : lo + STEP], NT).astype(bf16)
-            acc = acc + dot(kt, ds, NN)
-            for which, x in ((0, dot(ds, q2, NN)), (1, dot(p.astype(bf16), g2, NN))):
+            gq_acc = gq_acc + dot(kt, ds, NN)
+            for which, x in ((0, dot(ds, q2, NN)), (1, dot(low, g2, NN))):
                 if lo == 0:
                     prev_out[t, which] = x[0:128].astype(bf16)
                     own_out[t, which] = x[128:256]
                     next_out[t, which] = x[256:384].astype(bf16)
                 else:
-                    low = x.astype(bf16)
+                    x = x.astype(bf16)
                     for i in range(STEP // BLK):
                         there, slot = listed(fb_ref, t, shard, shards, (lo - STEP) // BLK + i)
 
                         @pl.when(there)
                         def _():
-                            far_out[slot, part(t, which)] = low[i * BLK : (i + 1) * BLK]
-
-        gq_ref[t] = (pick_heads(acc) * HD ** (-0.5)).astype(bf16)
+                            far_buf[slot, which * BLK : (which + 1) * BLK] = x[i * BLK : (i + 1) * BLK]
+
+        copies.append(pltpu.make_async_copy(far_buf, far_out.at[:, 2 * t * BLK : 2 * (t + 1) * BLK], sems.at[t]))
+        copies[-1].start()
+        gq_ref[t] = (pick_heads(gq_acc) * HD ** (-0.5)).astype(bf16)
+        ctx = pick_heads(ctx_acc).astype(bf16)
+        if t == 1:
+            rev_ref[...] = flipped(ctx)
+        else:
+            ctx_ref[...] = ctx
+    for copy in copies:
+        copy.wait()
 
 
 def combine_kernel(fb_ref, own_ref, prev_ref, next_ref, far_ref, mine_ref, other_ref, asked_buf, sum_buf):
@@ -287,7 +283,7 @@
         ref[...] = (mine_ref[:, which] + other_ref[:, which].astype(f32)).astype(bf16)
 
 
-def project_kernel(ctx_ref, back_ref, weight_ref, own_ref, ref2, ref4, ref6, sum_buf):
+def project_kernel(ctx_ref, back_ref, weight_ref, even_ref, odd_ref, sum_buf):
     total = (ctx_ref[...].astype(f32) + back_ref[...].astype(f32)).astype(bf16)
     count, rows, _ = sum_buf.shape
     for k in range(count):
@@ -296,8 +292,8 @@
     blocks = jnp.concatenate([sum_buf[lax.bitwise_xor(at, j)] for j in range(count)], axis=0)
     out = dot(blocks, weight_ref[...], NN)
     for j in range(count):
-        ref = (own_ref, ref2, ref4, ref6)[j // 2]
-        ref[j % 2] = out[j * rows : (j + 1) * rows].astype(ref.dtype)
+        ref = (even_ref, odd_ref)[j % 2]
+        ref[j // 2] = out[j * rows : (j + 1) * rows].astype(ref.dtype)
 
 
 def smem():
@@ -306,6 +302,10 @@
 
 def vmem():
     return pl.BlockSpec(memory_space=pltpu.VMEM)
+
+
+def hbm():
+    return pl.BlockSpec(memory_space=pltpu.HBM)
 
 
 def shape(dims, dtype=bf16):
@@ -347,17 +347,20 @@
     asked = pltpu.VMEM((nz, 2, seq_count, 2 * HD), jnp.int32)
     outgoing, to_up, to_down = pl.pallas_call(
         pack_kernel,
-        out_shape=(shape(slots), shape(both), shape(both)),
+        out_shape=(pltpu.HBM(slots, bf16), shape(both), shape(both)),
         in_specs=[vmem()] * 3,
-        out_specs=(vmem(),) * 3,
-        scratch_shapes=[asked, pltpu.VMEM((nz,) + both, bf16)],
+        out_specs=(hbm(), vmem(), vmem()),
+        scratch_shapes=[
+            asked, pltpu.VMEM((nz,) + both, bf16), pltpu.VMEM(slots, bf16),
+            pltpu.SemaphoreType.DMA((nx * ny // 4,)),
+        ],
         cost_estimate=cost(1_000_000, 2_500_000),
         compiler_params=pltpu.CompilerParams(vmem_limit_bytes=LIMIT),
         name="pack",
     )(far_blocks, key_value, partner)
-    own_pair = jnp.stack([cotangent, swap(cotangent, 1)])
-    others = [swap(own_pair, bit) for bit in (2, 4, 6)]
-    outgoing, *others = lax.optimization_barrier((outgoing, *others))
+    same_core = [cotangent] + [swap(cotangent, bit) for bit in (2, 4, 6)]
+    other_core = swap(jnp.stack(same_core), 1)
+    outgoing, other_core = lax.optimization_barrier((outgoing, other_core))
     far = plane_a2a(outgoing)
 
     def flat(x, zh, y):
@@ -385,63 +388,57 @@
     grad_context = pl.pallas_call(
         context_grad_kernel,
         out_shape=shape((tok_rows, width)),
-        in_specs=[vmem()] * 5,
+        in_specs=[vmem()] * 6,
         out_specs=vmem(),
         scratch_shapes=[pltpu.VMEM(pieces, bf16)],
         cost_estimate=cost(34_000_000, 600_000),
         compiler_params=pltpu.CompilerParams(vmem_limit_bytes=LIMIT),
         name="context_grad",
-    )(own_pair, *others, out_weight)
+    )(*same_core, other_core, out_weight)
     mirrored = lax.ppermute(grad_context, SEQ, mirror)
 
-    keyed = [pltpu.VMEM((total_keys, width), bf16), pltpu.VMEM((total_keys, width), bf16)]
-    context_fwd, context_rev, stats = pl.pallas_call(
-        forward_kernel,
-        out_shape=(shape((tok_rows, width)), shape((tok_rows, width)), shape((2, 2, cols), f32)),
-        in_specs=[smem()] * 2 + [vmem()] * 5,
-        out_specs=(vmem(),) * 3,
-        scratch_shapes=keyed + [pltpu.VMEM((total_keys, cols), f32)],
-        cost_estimate=cost(1_600_000_000, 4_000_000, 1_000_000),
-        compiler_params=pltpu.CompilerParams(vmem_limit_bytes=LIMIT),
-        name="attend_forward",
-    )(far_blocks, slopes, queries, key_value, from_prev, from_next, far)
+    square = shape((tok_rows, width))
+    half = pltpu.VMEM((seq_count, 2 * BLK, width), bf16)
+    context_fwd, context_rev, grad_queries, own, before, after, far_grads = pl.pallas_call(
+        attend_kernel,
+        out_shape=(square, square, shape((2, tok_rows, width)), shape(both, f32), shape(both), shape(both), pltpu.HBM(slots, bf16)),
+        in_specs=[smem()] * 2 + [vmem()] * 7,
+        out_specs=(vmem(),) * 6 + (hbm(),),
+        scratch_shapes=[pltpu.VMEM((total_keys, width), bf16)] * 2
+        + [pltpu.VMEM((total_keys, cols), f32)] * 2
+        + [half, half, pltpu.SemaphoreType.DMA((2,))],
+        cost_estimate=cost(4_000_000_000, 8_000_000, 1_000_000),
+        compiler_params=pltpu.CompilerParams(vmem_limit_bytes=LIMIT),
+        name="attend",
+    )(far_blocks, slopes, queries, key_value, from_prev, from_next, far, grad_context, mirrored)
     context_back = lax.ppermute(context_rev, SEQ, mirror)
 
-    grad_queries, own, before, after, far_grads = pl.pallas_call(
-        backward_kernel,
-        out_shape=(shape((2, tok_rows, width)), shape(both, f32), shape(both), shape(both), shape(slots)),
-        in_specs=[smem()] * 2 + [vmem()] * 8,
-        out_specs=(vmem(),) * 5,
-        scratch_shapes=keyed
-        + [pltpu.VMEM((total_keys, cols), f32)] * 2,
-        cost_estimate=cost(3_200_000_000, 8_000_000, 1_000_000),
-        compiler_params=pltpu.CompilerParams(vmem_limit_bytes=LIMIT),
-        name="attend_backward",
-    )(
-        far_blocks, slopes, queries, key_value, from_prev, from_next, far, stats,
-        grad_context, mirrored,
-    )
-    own_rows, *other_rows = pl.pallas_call(
-        project_kernel,
-        out_shape=(shape((2, tok_rows // tp_count, model), f32),)
-        + (shape((2, tok_rows // tp_count, model)),) * 3,
-        in_specs=[vmem()] * 3,
-        out_specs=(vmem(),) * 4,
-        scratch_shapes=[pltpu.VMEM(pieces, bf16)],
-        cost_estimate=cost(34_000_000, 1_000_000),
-        compiler_params=pltpu.CompilerParams(vmem_limit_bytes=LIMIT),
-        name="project",
-    )(context_fwd, context_back, out_weight)
-    far_grads, *other_rows = lax.optimization_barrier((far_grads, *other_rows))
     returned = plane_a2a(far_grads)
     from_prev_grad = lax.ppermute(after, SEQ, [(b, a) for a, b in down])
     from_next_grad = lax.ppermute(before, SEQ, [(b, a) for a, b in up])
-
-    held = own_rows
-    for bit, rows in zip((2, 4, 6), other_rows):
-        held = held + swap(rows, bit).astype(f32)
-    held, from_prev_grad, from_next_grad = lax.optimization_barrier((held, from_prev_grad, from_next_grad))
-    mixed = (residual.astype(f32) + held[0] + swap(held[1].astype(bf16), 1).astype(f32)).astype(bf16)
+    context_back, from_prev_grad, from_next_grad = lax.optimization_barrier(
+        (context_back, from_prev_grad, from_next_grad)
+    )
+
+    even, odd = pl.pallas_call(
+        project_kernel,
+        out_shape=(
+            shape((tp_count // 2, tok_rows // tp_count, model), f32),
+            shape((tp_count // 2, tok_rows // tp_count, model)),
+        ),
+        in_specs=[vmem()] * 3,
+        out_specs=(vmem(),) * 2,
+        scratch_shapes=[pltpu.VMEM(pieces, bf16)],
+        cost_estimate=cost(34_000_000, 1_000_000),
+        compiler_params=pltpu.CompilerParams(vmem_limit_bytes=LIMIT),
+        name="project",
+    )(context_fwd, context_back, out_weight)
+    held = even + swap(odd, 1).astype(f32)
+    parts = [swap(held[k].astype(bf16), 2 * k) for k in range(1, tp_count // 2)]
+    total = residual.astype(f32) + held[0]
+    for part_here in parts:
+        total = total + part_here.astype(f32)
+    mixed = total.astype(bf16)
 
     mine, other = pl.pallas_call(
         combine_kernel,

time: 126 us -> 121 us (0.960)
  waiting for transfers between devices: 48.3 us -> 37.3 us
  starting transfers between devices: 55.2 us -> 63.4 us
  local copies, waits for them, and re-layouts: 3.48 us -> 1.47 us
    ppermute x1, waiting for transfers between devices: 13.8 us -> 5.08 us  [per_device(): from_prev = lax.ppermute(to_up, SEQ, up)]
    ppermute x1, waiting for transfers between devices: 12.3 us -> 5.48 us  [per_device(): from_prev_grad = lax.ppermute(after, SEQ, [(b, a) for a, b in down])]
    ppermute x1, starting transfers between devices: 5.82 us -> 9.78 us  [per_device(): context_back = lax.ppermute(context_rev, SEQ, mirror)]
    ppermute x1, starting transfers between devices: 6.3 us -> 10.1 us  [per_device(): mirrored = lax.ppermute(grad_context, SEQ, mirror)]
    ppermute x2, waiting for transfers between devices: 9.01 us -> 5.28 us  [z_swap(): return lax.ppermute(x, 'zh', [(i, nz - 1 - i) for i in range(nz)])]
    ppermute x1, waiting for transfers between devices: 0.01 us -> 3 us  [per_device(): context_back = lax.ppermute(context_rev, SEQ, mirror)]
    ppermute x1, waiting for transfers between devices: 0.01 us -> 2.68 us  [per_device(): mirrored = lax.ppermute(grad_context, SEQ, mirror)]
    ppermute x8, starting transfers between devices: 8.95 us -> 11.6 us  [swap(): return lax.ppermute(x, 'tp', [(i, i ^ bit) for i in range(count)])]
  transfers between devices with their start and end apart: 18 -> 18, of which waited for: 8 -> 11; matrix products, arithmetic and copies ran while one was open for 2% -> 3% of each run, Pallas kernels for 11% -> 3%
where the time goes in v4:
time: 121 us; the launch traced here: 119 us
  starting transfers between devices  63.4 us (52%)
  waiting for transfers between devices  37.3 us (31%)
  Pallas kernels  13.7 us (11%)
  other arithmetic  2.33 us (2%)
  local copies, waits for them, and re-layouts  1.47 us (1%)
    all_to_all x2, starting transfers between devices, plane_a2a(): lax.all_to_all(x, ('x', 'y'), split_axis=0, concat_axis=0, tiled=True)  13.7 us
    ppermute x8, starting transfers between devices, swap(): return lax.ppermute(x, 'tp', [(i, i ^ bit) for i in range(count)])  11.6 us
    ppermute x1, starting transfers between devices, per_device(): mirrored = lax.ppermute(grad_context, SEQ, mirror)  10.1 us
    pallas_call x1, Pallas kernels, per_device(): pl.pallas_call(attend_kernel, out_shape=(square, square, shape((2, tok_ro...  10.1 us
    ppermute x1, starting transfers between devices, per_device(): context_back = lax.ppermute(context_rev, SEQ, mirror)  9.78 us
    ppermute x8, waiting for transfers between devices, swap(): return lax.ppermute(x, 'tp', [(i, i ^ bit) for i in range(count)])  7.24 us
    ppermute x2, starting transfers between devices, z_swap(): return lax.ppermute(x, 'zh', [(i, nz - 1 - i) for i in range(nz)])  6.57 us
    ppermute x1, waiting for transfers between devices, per_device(): from_next_grad = lax.ppermute(before, SEQ, [(b, a) for a, b in up])  6.01 us
  transfers between devices with their start and end apart: 18, of which 11 were waited for; matrix products, arithmetic and copies ran while one was open for 3% of the time, Pallas kernels for 3%

profile of v4, /device:TPU:24, one launch (start us, length us, event | category | flops | bytes accessed | tf_op | source)
XLA Modules:
  0.0 119.0 jit_solution(2612735501987824819)
XLA Ops:
  0.6 3.4 %collective-permute-start.4 = (bf16[16,1024]{1,0:T(8,128)(2,1)}, bf16[16,1024]{1,0:T(8,128)(2,1)S(1)}, u32[]{:S(2)}, u32[]{:S(2)}) collective-permute-start(bf16[16,1024]{1,0:T(8,128)(2,1)} %ref0.1), channel_id=1, source_target_pairs={{0,4},{1,5},{2,6},{3,7},{4,0},{5,1},{6,2},{7,3},{8,12},{9,13},{10,... | collective-permute-start | bytes 98312 | tf_op jit(solution)/shard_map/ppermute | solution.py:321
  4.0 1.9 %collective-permute-start.3 = (bf16[16,1024]{1,0:T(8,128)(2,1)}, bf16[16,1024]{1,0:T(8,128)(2,1)S(1)}, u32[]{:S(2)}, u32[]{:S(2)}) collective-permute-start(bf16[16,1024]{1,0:T(8,128)(2,1)} %ref0.1), channel_id=1, source_target_pairs={{0,2},{1,3},{2,0},{3,1},{4,6},{5,7},{6,4},{7,5},{8,10},{9,11},{10,... | collective-permute-start | bytes 98312 | tf_op jit(solution)/shard_map/ppermute | solution.py:321
  5.9 0.9 pad_maximum_fusion.own_ref.kv_ref
  6.8 6.5 %collective-permute-start = (bf16[2,2,128,128]{3,2,1,0:T(8,128)(2,1)S(1)}, bf16[2,2,128,128]{3,2,1,0:T(8,128)(2,1)S(1)}, u32[]{:S(2)}, u32[]{:S(2)}) collective-permute-start(bf16[2,2,128,128]{3,2,1,0:T(8,128)(2,1)S(1)} %pad_maximum_fusion.own_ref.kv_ref), channel_id=1, source_target_pairs={{0,32},{32,0},{1,33},{33,1},{2,34},{34,2},{3,35},{35,3},{4,36},{36... | collective-permute-start | bytes 393224 | tf_op jit(solution)/shard_map/ppermute | solution.py:343
  13.3 0.8 pad_maximum_fusion.1
  14.2 0.8 copy.13.fb_ref
  14.9 2.6 %collective-permute-done.partner_ref = bf16[2,2,128,128]{3,2,1,0:T(8,128)(2,1)S(1)} collective-permute-done((bf16[2,2,128,128]{3,2,1,0:T(8,128)(2,1)S(1)}, bf16[2,2,128,128]{3,2,1,0:T(8,128)(2,1)S(1)}, u32[]{:S(2)}, u32[]{:S(2)}) %collective-permute-start) | collective-permute-done | bytes 131104 | tf_op jit(solution)/shard_map/ppermute | solution.py:343
  17.5 1.6 %pack.1 = (bf16[32,256,128]{2,1,0:T(8,128)(2,1)}, bf16[2,2,128,128]{3,2,1,0:T(8,128)(2,1)S(1)}, bf16[2,2,128,128]{3,2,1,0:T(8,128)(2,1)S(1)}) custom-call(s32[32,24]{1,0:T(8,128)S(1)} %copy.13.fb_ref, bf16[2,2,128,128]{3,2,1,0:T(8,128)(2,1)S(1)} %pad_maximum_fusion.own_ref.kv_ref, bf16[2,2,128,128]{3,2,1,0:T(8,128)(2,1)S(1)} %collective-permute-done.partner_ref), custom_call_target="tpu_custom_call" | custom-call | flops 1000000 | bytes 2500000 | tf_op jit(solution)/shard_map/pack/pallas_call | solution.py:348
  19.2 7.3 %all-to-all-start = ((bf16[16,512,128]{2,1,0:T(8,128)(2,1)}), bf16[16,512,128]{2,1,0:T(8,128)(2,1)S(1)}, u32[]{:S(2)}, u32[]{:S(2)}) async-start(bf16[16,512,128]{2,1,0:T(8,128)(2,1)} %bitcast.35), calls=%async_computation | async-start | bytes 4194304 | tf_op jit(solution)/shard_map/all_to_all | solution.py:340
  26.5 3.4 %collective-permute-start.1 = (bf16[2,2,128,128]{3,2,1,0:T(8,128)(2,1)S(1)}, bf16[2,2,128,128]{3,2,1,0:T(8,128)(2,1)S(1)}, u32[]{:S(2)}, u32[]{:S(2)}) collective-permute-start(bf16[2,2,128,128]{3,2,1,0:T(8,128)(2,1)S(1)} %get-tuple-element.25), channel_id=1, source_target_pairs={{0,8},{8,16},{16,24},{24,64},{32,40},{40,48},{48,56},{56,32},{64,7... | collective-permute-start | bytes 393224 | tf_op jit(solution)/shard_map/ppermute | solution.py:385
  29.9 2.5 %collective-permute-start.2 = (bf16[2,2,128,128]{3,2,1,0:T(8,128)(2,1)S(1)}, bf16[2,2,128,128]{3,2,1,0:T(8,128)(2,1)S(1)}, u32[]{:S(2)}, u32[]{:S(2)}) collective-permute-start(bf16[2,2,128,128]{3,2,1,0:T(8,128)(2,1)S(1)} %get-tuple-element.26), channel_id=1, source_target_pairs={{0,24},{8,0},{16,8},{24,16},{40,32},{48,40},{56,48},{64,88},{72,64... | collective-permute-start | bytes 393224 | tf_op jit(solution)/shard_map/ppermute | solution.py:386
  32.6 10.1 %collective-permute-start.7 = (bf16[128,128]{1,0:T(8,128)(2,1)S(1)}, bf16[128,128]{1,0:T(8,128)(2,1)S(1)}, u32[]{:S(2)}, u32[]{:S(2)}) collective-permute-start(bf16[128,128]{1,0:T(8,128)(2,1)S(1)} %context_grad.1.grad_ref), channel_id=1, source_target_pairs={{0,248},{8,240},{16,232},{24,224},{32,216},{40,208},{48,200},{56,1... | collective-permute-start | bytes 98312 | tf_op jit(solution)/shard_map/ppermute | solution.py:398
  42.7 2.7 %collective-permute-done.7.mirrored_ref = bf16[128,128]{1,0:T(8,128)(2,1)S(1)} collective-permute-done((bf16[128,128]{1,0:T(8,128)(2,1)S(1)}, bf16[128,128]{1,0:T(8,128)(2,1)S(1)}, u32[]{:S(2)}, u32[]{:S(2)}) %collective-permute-start.7) | collective-permute-done | bytes 32800 | tf_op jit(solution)/shard_map/ppermute | solution.py:398
  45.4 5.1 %collective-permute-done.1.prev_ref = bf16[2,2,128,128]{3,2,1,0:T(8,128)(2,1)S(1)} collective-permute-done((bf16[2,2,128,128]{3,2,1,0:T(8,128)(2,1)S(1)}, bf16[2,2,128,128]{3,2,1,0:T(8,128)(2,1)S(1)}, u32[]{:S(2)}, u32[]{:S(2)}) %collective-permute-start.1) | collective-permute-done | bytes 131104 | tf_op jit(solution)/shard_map/ppermute | solution.py:385
  50.5 2.5 %collective-permute-done.2.next_ref = bf16[2,2,128,128]{3,2,1,0:T(8,128)(2,1)S(1)} collective-permute-done((bf16[2,2,128,128]{3,2,1,0:T(8,128)(2,1)S(1)}, bf16[2,2,128,128]{3,2,1,0:T(8,128)(2,1)S(1)}, u32[]{:S(2)}, u32[]{:S(2)}) %collective-permute-start.2) | collective-permute-done | bytes 131104 | tf_op jit(solution)/shard_map/ppermute | solution.py:386
  52.9 0.7 copy-done.3
  53.6 10.1 %attend.1 = (bf16[128,128]{1,0:T(8,128)(2,1)S(1)}, bf16[128,128]{1,0:T(8,128)(2,1)S(1)}, bf16[2,128,128]{2,1,0:T(8,128)(2,1)}, f32[2,2,128,128]{3,2,1,0:T(8,128)...) custom-call(s32[32,24]{1,0:T(8,128)S(1)} %copy.13.fb_ref, ...), custom_call_target="tpu_custom_call" | custom-call | flops 4000000000 | bytes 8000000 | tf_op jit(solution)/shard_map/attend/pallas_call | solution.py:402
  63.7 6.4 %all-to-all-start.1 = ((bf16[16,512,128]{2,1,0:T(8,128)(2,1)}), bf16[16,512,128]{2,1,0:T(8,128)(2,1)S(1)}, u32[]{:S(2)}, u32[]{:S(2)}) async-start(bf16[16,512,128]{2,1,0:T(8,128)(2,1)} %bitcast.34), calls=%async_computation.1 | async-start | bytes 4194304 | tf_op jit(solution)/shard_map/all_to_all | solution.py:340
  70.1 2.0 %collective-permute-start.9 = (bf16[2,2,128,128]{3,2,1,0:T(8,128)(2,1)S(1)}, bf16[2,2,128,128]{3,2,1,0:T(8,128)(2,1)S(1)}, u32[]{:S(2)}, u32[]{:S(2)}) collective-permute-start(bf16[2,2,128,128]{3,2,1,0:T(8,128)(2,1)S(1)} %get-tuple-element.32), channel_id=1, source_target_pairs={{24,0},{0,8},{8,16},{16,24},{32,40},{40,48},{48,56},{88,64},{64,72... | collective-permute-start | bytes 393224 | tf_op jit(solution)/shard_map/ppermute | solution.py:417
  72.1 3.8 %collective-permute-start.10 = (bf16[2,2,128,128]{3,2,1,0:T(8,128)(2,1)S(1)}, bf16[2,2,128,128]{3,2,1,0:T(8,128)(2,1)S(1)}, u32[]{:S(2)}, u32[]{:S(2)}) collective-permute-start(bf16[2,2,128,128]{3,2,1,0:T(8,128)(2,1)S(1)} %get-tuple-element.33), channel_id=1, source_target_pairs={{8,0},{16,8},{24,16},{64,24},{40,32},{48,40},{56,48},{32,56},{72,6... | collective-permute-start | bytes 393224 | tf_op jit(solution)/shard_map/ppermute | solution.py:418
  75.9 9.8 %collective-permute-start.8 = (bf16[128,128]{1,0:T(8,128)(2,1)S(1)}, bf16[128,128]{1,0:T(8,128)(2,1)S(1)}, u32[]{:S(2)}, u32[]{:S(2)}) collective-permute-start(bf16[128,128]{1,0:T(8,128)(2,1)S(1)} %get-tuple-element.31), channel_id=1, source_target_pairs={{0,248},{8,240},{16,232},{24,224},{32,216},{40,208},{48,200},{56,1... | collective-permute-start | bytes 98312 | tf_op jit(solution)/shard_map/ppermute | solution.py:414
  85.7 3.0 %collective-permute-done.8.back_ref = bf16[128,128]{1,0:T(8,128)(2,1)S(1)} collective-permute-done((bf16[128,128]{1,0:T(8,128)(2,1)S(1)}, bf16[128,128]{1,0:T(8,128)(2,1)S(1)}, u32[]{:S(2)}, u32[]{:S(2)}) %collective-permute-start.8) | collective-permute-done | bytes 32800 | tf_op jit(solution)/shard_map/ppermute | solution.py:414
  88.7 5.5 %collective-permute-done.9.prev_ref = bf16[2,2,128,128]{3,2,1,0:T(8,128)(2,1)S(1)} collective-permute-done((bf16[2,2,128,128]{3,2,1,0:T(8,128)(2,1)S(1)}, bf16[2,2,128,128]{3,2,1,0:T(8,128)(2,1)S(1)}, u32[]{:S(2)}, u32[]{:S(2)}) %collective-permute-start.9) | collective-permute-done | bytes 131104 | tf_op jit(solution)/shard_map/ppermute | solution.py:417
  94.2 6.0 %collective-permute-done.10.next_ref = bf16[2,2,128,128]{3,2,1,0:T(8,128)(2,1)S(1)} collective-permute-done((bf16[2,2,128,128]{3,2,1,0:T(8,128)(2,1)S(1)}, bf16[2,2,128,128]{3,2,1,0:T(8,128)(2,1)S(1)}, u32[]{:S(2)}, u32[]{:S(2)}) %collective-permute-start.10) | collective-permute-done | bytes 131104 | tf_op jit(solution)/shard_map/ppermute | solution.py:418
  100.7 1.3 %collective-permute-done.11 = bf16[4,16,1024]{2,1,0:T(8,128)(2,1)S(1)} collective-permute-done((bf16[4,16,1024]{2,1,0:T(8,128)(2,1)S(1)}, bf16[4,16,1024]{2,1,0:T(8,128)(2,1)S(1)}, u32[]{:S(2)}, u32[]{:S(2)}) %collective-permute-start.11) | collective-permute-done | bytes 131104 | tf_op jit(solution)/shard_map/ppermute | solution.py:321
  102.2 5.8 %collective-permute-start.14 = (bf16[16,1024]{1,0:T(8,128)(2,1)S(1)}, bf16[16,1024]{1,0:T(8,128)(2,1)S(1)}, u32[]{:S(2)}, u32[]{:S(2)}) collective-permute-start(bf16[16,1024]{1,0:T(8,128)(2,1)S(1)} %get-tuple-element.49), channel_id=1, source_target_pairs={{0,6},{1,7},{2,4},{3,5},{4,2},{5,3},{6,0},{7,1},{8,14},{9,15},{10,... | collective-permute-start | bytes 98312 | tf_op jit(solution)/shard_map/ppermute | solution.py:321
  108.0 1.0 combine.1
  109.1 1.4 %collective-permute-done.14 = bf16[16,1024]{1,0:T(8,128)(2,1)S(1)} collective-permute-done((bf16[16,1024]{1,0:T(8,128)(2,1)S(1)}, bf16[16,1024]{1,0:T(8,128)(2,1)S(1)}, u32[]{:S(2)}, u32[]{:S(2)}) %collective-permute-start.14) | collective-permute-done | bytes 32800 | tf_op jit(solution)/shard_map/ppermute | solution.py:321
  110.6 4.4 %collective-permute-done.13 = bf16[16,1024]{1,0:T(8,128)(2,1)S(1)} collective-permute-done((bf16[16,1024]{1,0:T(8,128)(2,1)S(1)}, bf16[16,1024]{1,0:T(8,128)(2,1)S(1)}, u32[]{:S(2)}, u32[]{:S(2)}) %collective-permute-start.13) | collective-permute-done | bytes 32800 | tf_op jit(solution)/shard_map/ppermute | solution.py:321
  115.0 0.6 fusion.4
  115.7 2.7 %collective-permute-done.15.other_ref = bf16[2,2,128,128]{3,2,1,0:T(8,128)(2,1)S(1)} collective-permute-done((bf16[2,2,128,128]{3,2,1,0:T(8,128)(2,1)S(1)}, bf16[2,2,128,128]{3,2,1,0:T(8,128)(2,1)S(1)}, u32[]{:S(2)}, u32[]{:S(2)}) %collective-permute-start.15) | collective-permute-done | bytes 131104 | tf_op jit(solution)/shard_map/ppermute | solution.py:343
  118.3 0.7 finish.1
  (26 shorter events, 1.1 us)
Async XLA Ops:
  0.6 12.6 %collective-permute-start.4 = (bf16[16,1024]{1,0:T(8,128)(2,1)}, bf16[16,1024]{1,0:T(8,128)(2,1)S(1)}, u32[]{:S(2)}, u32[]{:S(2)}) collective-permute-start(bf16[16,1024]{1,0:T(8,128)(2,1)} %ref0.1), channel_id=1, source_target_pairs={{0,4},{1,5},{2,6},{3,7},{4,0},{5,1},{6,2},{7,3},{8,12},{9,13},{10,... | collective-permute-start | bytes 98312 | tf_op jit(solution)/shard_map/ppermute | solution.py:321
  4.0 9.3 %collective-permute-start.3 = (bf16[16,1024]{1,0:T(8,128)(2,1)}, bf16[16,1024]{1,0:T(8,128)(2,1)S(1)}, u32[]{:S(2)}, u32[]{:S(2)}) collective-permute-start(bf16[16,1024]{1,0:T(8,128)(2,1)} %ref0.1), channel_id=1, source_target_pairs={{0,2},{1,3},{2,0},{3,1},{4,6},{5,7},{6,4},{7,5},{8,10},{9,11},{10,... | collective-permute-start | bytes 98312 | tf_op jit(solution)/shard_map/ppermute | solution.py:321
  5.9 7.4 %collective-permute-start.5 = (bf16[16,1024]{1,0:T(8,128)(2,1)}, bf16[16,1024]{1,0:T(8,128)(2,1)S(1)}, u32[]{:S(2)}, u32[]{:S(2)}) collective-permute-start(bf16[16,1024]{1,0:T(8,128)(2,1)} %ref0.1), channel_id=1, source_target_pairs={{0,6},{1,7},{2,4},{3,5},{4,2},{5,3},{6,0},{7,1},{8,14},{9,15},{10,... | collective-permute-start | bytes 98312 | tf_op jit(solution)/shard_map/ppermute | solution.py:321
  6.8 10.7 %collective-permute-start = (bf16[2,2,128,128]{3,2,1,0:T(8,128)(2,1)S(1)}, bf16[2,2,128,128]{3,2,1,0:T(8,128)(2,1)S(1)}, u32[]{:S(2)}, u32[]{:S(2)}) collective-permute-start(bf16[2,2,128,128]{3,2,1,0:T(8,128)(2,1)S(1)} %pad_maximum_fusion.own_ref.kv_ref), channel_id=1, source_target_pairs={{0,32},{32,0},{1,33},{33,1},{2,34},{34,2},{3,35},{35,3},{4,36},{36... | collective-permute-start | bytes 393224 | tf_op jit(solution)/shard_map/ppermute | solution.py:343
  14.1 5.1 %collective-permute-start.6 = (bf16[4,16,1024]{2,1,0:T(8,128)(2,1)S(1)}, bf16[4,16,1024]{2,1,0:T(8,128)(2,1)S(1)}, u32[]{:S(2)}, u32[]{:S(2)}) collective-permute-start(bf16[4,16,1024]{2,1,0:T(8,128)(2,1)S(1)} %pad_maximum_fusion.1), channel_id=1, source_target_pairs={{0,1},{1,0},{2,3},{3,2},{4,5},{5,4},{6,7},{7,6},{8,9},{9,8},{10,11... | collective-permute-start | bytes 393224 | tf_op jit(solution)/shard_map/ppermute | solution.py:321
  19.1 13.2 %copy-start = (bf16[128,1024]{1,0:T(8,128)(2,1)S(1)}, bf16[128,1024]{1,0:T(8,128)(2,1)}, u32[]{:S(2)}) copy-start(bf16[128,1024]{1,0:T(8,128)(2,1)} %weight_ref.3) | copy-start | bytes 786436
  19.2 13.2 %copy-start.1 = (bf16[16,1024]{1,0:T(8,128)(2,1)S(1)}, bf16[16,1024]{1,0:T(8,128)(2,1)}, u32[]{:S(2)}) copy-start(bf16[16,1024]{1,0:T(8,128)(2,1)} %ref0.1) | copy-start | bytes 98308
  19.2 33.8 %copy-start.2 = (bf16[2,128,128]{2,1,0:T(8,128)(2,1)S(1)}, bf16[2,128,128]{2,1,0:T(8,128)(2,1)}, u32[]{:S(2)}) copy-start(bf16[2,128,128]{2,1,0:T(8,128)(2,1)} %q_ref.1) | copy-start | bytes 196612
  19.2 33.7 %all-to-all-start = ((bf16[16,512,128]{2,1,0:T(8,128)(2,1)}), bf16[16,512,128]{2,1,0:T(8,128)(2,1)S(1)}, u32[]{:S(2)}, u32[]{:S(2)}) async-start(bf16[16,512,128]{2,1,0:T(8,128)(2,1)} %bitcast.35), calls=%async_computation | async-start | bytes 4194304 | tf_op jit(solution)/shard_map/all_to_all | solution.py:340
  26.5 24.0 %collective-permute-start.1 = (bf16[2,2,128,128]{3,2,1,0:T(8,128)(2,1)S(1)}, bf16[2,2,128,128]{3,2,1,0:T(8,128)(2,1)S(1)}, u32[]{:S(2)}, u32[]{:S(2)}) collective-permute-start(bf16[2,2,128,128]{3,2,1,0:T(8,128)(2,1)S(1)} %get-tuple-element.25), channel_id=1, source_target_pairs={{0,8},{8,16},{16,24},{24,64},{32,40},{40,48},{48,56},{56,32},{64,7... | collective-permute-start | bytes 393224 | tf_op jit(solution)/shard_map/ppermute | solution.py:385
  29.9 23.1 %collective-permute-start.2 = (bf16[2,2,128,128]{3,2,1,0:T(8,128)(2,1)S(1)}, bf16[2,2,128,128]{3,2,1,0:T(8,128)(2,1)S(1)}, u32[]{:S(2)}, u32[]{:S(2)}) collective-permute-start(bf16[2,2,128,128]{3,2,1,0:T(8,128)(2,1)S(1)} %get-tuple-element.26), channel_id=1, source_target_pairs={{0,24},{8,0},{16,8},{24,16},{40,32},{48,40},{56,48},{64,88},{72,64... | collective-permute-start | bytes 393224 | tf_op jit(solution)/shard_map/ppermute | solution.py:386
  32.6 12.8 %collective-permute-start.7 = (bf16[128,128]{1,0:T(8,128)(2,1)S(1)}, bf16[128,128]{1,0:T(8,128)(2,1)S(1)}, u32[]{:S(2)}, u32[]{:S(2)}) collective-permute-start(bf16[128,128]{1,0:T(8,128)(2,1)S(1)} %context_grad.1.grad_ref), channel_id=1, source_target_pairs={{0,248},{8,240},{16,232},{24,224},{32,216},{40,208},{48,200},{56,1... | collective-permute-start | bytes 98312 | tf_op jit(solution)/shard_map/ppermute | solution.py:398
  52.9 0.7 copy-start.3
  63.7 44.4 %all-to-all-start.1 = ((bf16[16,512,128]{2,1,0:T(8,128)(2,1)}), bf16[16,512,128]{2,1,0:T(8,128)(2,1)S(1)}, u32[]{:S(2)}, u32[]{:S(2)}) async-start(bf16[16,512,128]{2,1,0:T(8,128)(2,1)} %bitcast.34), calls=%async_computation.1 | async-start | bytes 4194304 | tf_op jit(solution)/shard_map/all_to_all | solution.py:340
  70.1 45.0 %copy-start.4 = (bf16[16,1024]{1,0:T(8,128)(2,1)S(1)}, bf16[16,1024]{1,0:T(8,128)(2,1)}, u32[]{:S(2)}) copy-start(bf16[16,1024]{1,0:T(8,128)(2,1)} %param.9) | copy-start | bytes 98308
  70.1 24.1 %collective-permute-start.9 = (bf16[2,2,128,128]{3,2,1,0:T(8,128)(2,1)S(1)}, bf16[2,2,128,128]{3,2,1,0:T(8,128)(2,1)S(1)}, u32[]{:S(2)}, u32[]{:S(2)}) collective-permute-start(bf16[2,2,128,128]{3,2,1,0:T(8,128)(2,1)S(1)} %get-tuple-element.32), channel_id=1, source_target_pairs={{24,0},{0,8},{8,16},{16,24},{32,40},{40,48},{48,56},{88,64},{64,72... | collective-permute-start | bytes 393224 | tf_op jit(solution)/shard_map/ppermute | solution.py:417
  72.1 28.1 %collective-permute-start.10 = (bf16[2,2,128,128]{3,2,1,0:T(8,128)(2,1)S(1)}, bf16[2,2,128,128]{3,2,1,0:T(8,128)(2,1)S(1)}, u32[]{:S(2)}, u32[]{:S(2)}) collective-permute-start(bf16[2,2,128,128]{3,2,1,0:T(8,128)(2,1)S(1)} %get-tuple-element.33), channel_id=1, source_target_pairs={{8,0},{16,8},{24,16},{64,24},{40,32},{48,40},{56,48},{32,56},{72,6... | collective-permute-start | bytes 393224 | tf_op jit(solution)/shard_map/ppermute | solution.py:418
  75.9 12.8 %collective-permute-start.8 = (bf16[128,128]{1,0:T(8,128)(2,1)S(1)}, bf16[128,128]{1,0:T(8,128)(2,1)S(1)}, u32[]{:S(2)}, u32[]{:S(2)}) collective-permute-start(bf16[128,128]{1,0:T(8,128)(2,1)S(1)} %get-tuple-element.31), channel_id=1, source_target_pairs={{0,248},{8,240},{16,232},{24,224},{32,216},{40,208},{48,200},{56,1... | collective-permute-start | bytes 98312 | tf_op jit(solution)/shard_map/ppermute | solution.py:414
  100.4 1.6 %collective-permute-start.11 = (bf16[4,16,1024]{2,1,0:T(8,128)(2,1)S(1)}, bf16[4,16,1024]{2,1,0:T(8,128)(2,1)S(1)}, u32[]{:S(2)}, u32[]{:S(2)}) collective-permute-start(bf16[4,16,1024]{2,1,0:T(8,128)(2,1)S(1)} %get-tuple-element.36), channel_id=1, source_target_pairs={{0,1},{1,0},{2,3},{3,2},{4,5},{5,4},{6,7},{7,6},{8,9},{9,8},{10,11... | collective-permute-start | bytes 393224 | tf_op jit(solution)/shard_map/ppermute | solution.py:321
  102.1 7.0 %collective-permute-start.12 = (bf16[16,1024]{1,0:T(8,128)(2,1)S(1)}, bf16[16,1024]{1,0:T(8,128)(2,1)S(1)}, u32[]{:S(2)}, u32[]{:S(2)}) collective-permute-start(bf16[16,1024]{1,0:T(8,128)(2,1)S(1)} %get-tuple-element.48), channel_id=1, source_target_pairs={{0,2},{1,3},{2,0},{3,1},{4,6},{5,7},{6,4},{7,5},{8,10},{9,11},{10,... | collective-permute-start | bytes 98312 | tf_op jit(solution)/shard_map/ppermute | solution.py:321
  102.2 8.4 %collective-permute-start.14 = (bf16[16,1024]{1,0:T(8,128)(2,1)S(1)}, bf16[16,1024]{1,0:T(8,128)(2,1)S(1)}, u32[]{:S(2)}, u32[]{:S(2)}) collective-permute-start(bf16[16,1024]{1,0:T(8,128)(2,1)S(1)} %get-tuple-element.49), channel_id=1, source_target_pairs={{0,6},{1,7},{2,4},{3,5},{4,2},{5,3},{6,0},{7,1},{8,14},{9,15},{10,... | collective-permute-start | bytes 98312 | tf_op jit(solution)/shard_map/ppermute | solution.py:321
  108.0 7.0 %collective-permute-start.13 = (bf16[16,1024]{1,0:T(8,128)(2,1)S(1)}, bf16[16,1024]{1,0:T(8,128)(2,1)S(1)}, u32[]{:S(2)}, u32[]{:S(2)}) collective-permute-start(bf16[16,1024]{1,0:T(8,128)(2,1)S(1)} %get-tuple-element.50), channel_id=1, source_target_pairs={{0,4},{1,5},{2,6},{3,7},{4,0},{5,1},{6,2},{7,3},{8,12},{9,13},{10,... | collective-permute-start | bytes 98312 | tf_op jit(solution)/shard_map/ppermute | solution.py:321
  109.0 9.3 %collective-permute-start.15 = (bf16[2,2,128,128]{3,2,1,0:T(8,128)(2,1)S(1)}, bf16[2,2,128,128]{3,2,1,0:T(8,128)(2,1)S(1)}, u32[]{:S(2)}, u32[]{:S(2)}) collective-permute-start(bf16[2,2,128,128]{3,2,1,0:T(8,128)(2,1)S(1)} %get-tuple-element.43), channel_id=1, source_target_pairs={{0,32},{32,0},{1,33},{33,1},{2,34},{34,2},{3,35},{35,3},{4,36},{36... | collective-permute-start | bytes 393224 | tf_op jit(solution)/shard_map/ppermute | solution.py:343

commit v5 on v4

--- a/solution.py
+++ b/solution.py
@@ -55,10 +55,11 @@
     return (x * nz + zh) * ny + y, nx * nz * ny, zh, y
 
 
-def slot_of(owner):
-    nz, ny = lax.axis_size("zh"), lax.axis_size("y")
+def slot_of(owner, zh):
+    nx, nz, ny = (lax.axis_size(a) for a in SEQ)
     xz, y = lax.div(owner, ny), lax.rem(owner, ny)
-    return (lax.div(xz, nz) * ny + y) * nz + lax.rem(xz, nz)
+    x, z = lax.div(xz, nz), lax.rem(xz, nz)
+    return jnp.where(z == zh, 0, nx * ny) + x * ny + y
 
 
 def plane_readers(zh):
@@ -70,11 +71,11 @@
     return slice((2 * t + which) * BLK, (2 * t + which + 1) * BLK)
 
 
-def listed(fb_ref, t, shard, shards, f):
+def listed(fb_ref, t, shard, shards, zh, f):
     entry = fb_ref[shard if t == 0 else shards - 1 - shard, f]
     owner = lax.shift_right_arithmetic(entry, 1)
     owner = owner if t == 0 else shards - 1 - owner
-    return entry >= 0, jnp.where(entry >= 0, slot_of(owner), 0)
+    return entry >= 0, jnp.where(entry >= 0, slot_of(owner, zh), 0)
 
 
 def asked_of(fb, t, shard, shards):
@@ -85,57 +86,65 @@
     return jnp.sum(hit, axis=1, keepdims=True)
 
 
-def asked_rows(fb_ref, asked_buf):
-    shard, shards, zh, y = place()
+def asked_rows(fb_ref, asked_buf, rel):
+    shard, shards, zh, y = place()
+    target = shard + rel * (1 - 2 * zh) * lax.axis_size("y")
     fb = fb_ref[...]
-    ny = lax.axis_size("y")
-    for z in range(lax.axis_size("zh")):
-        for t in range(2):
-            asked = asked_of(fb, t, shard + (z - zh) * ny, shards)
-            asked_buf[z, t] = jnp.broadcast_to(asked, asked_buf.shape[2:])
-
-
-def asked_by(asked_buf, z, t, reader, rows):
-    row = reader if t == 0 else asked_buf.shape[2] - 1 - reader
-    return jnp.broadcast_to(asked_buf[z, t, pl.ds(row, 1)], (rows, 2 * HD))
-
-
-def pack_kernel(fb_ref, own_ref, partner_ref, out_ref, up_ref, down_ref, asked_buf, kv_buf, out_buf, sems):
-    shard, shards, zh, y = place()
-    ny = lax.axis_size("y")
-    asked_rows(fb_ref, asked_buf)
-    kv_buf[zh] = own_ref[...]
-    kv_buf[1 - zh] = partner_ref[...]
-    up_ref[...] = kv_buf[jnp.where(y == ny - 1, 1 - zh, zh)]
-    down_ref[...] = kv_buf[jnp.where(y == 0, 1 - zh, zh)]
+    for t in range(2):
+        asked_buf[t] = jnp.broadcast_to(asked_of(fb, t, target, shards), asked_buf.shape[1:])
+
+
+def asked_by(asked_buf, t, reader, rows):
+    row = reader if t == 0 else asked_buf.shape[1] - 1 - reader
+    return jnp.broadcast_to(asked_buf[t, pl.ds(row, 1)], (rows, 2 * HD))
+
+
+def pack(fb_ref, kv_ref, out_ref, asked_buf, out_buf, sems, rel):
+    shard, shards, zh, y = place()
+    asked_rows(fb_ref, asked_buf, rel)
     copies = []
     for p, reader in enumerate(plane_readers(zh)):
-        for z in range(2):
-            for t in range(2):
-                second = asked_by(asked_buf, z, t, reader, BLK) == 2
-                for which in range(2):
-                    out_buf[2 * p + z, part(t, which)] = jnp.where(
-                        second, kv_buf[z, t, which, BLK:], kv_buf[z, t, which, :BLK]
-                    )
+        for t in range(2):
+            second = asked_by(asked_buf, t, reader, BLK) == 2
+            for which in range(2):
+                out_buf[p, part(t, which)] = jnp.where(second, kv_ref[t, which, BLK:], kv_ref[t, which, :BLK])
         if p % 4 == 3:
-            done = pl.ds(2 * p - 6, 8)
+            done = pl.ds(p - 3, 4)
             copies.append(pltpu.make_async_copy(out_buf.at[done], out_ref.at[done], sems.at[p // 4]))
             copies[-1].start()
+    return copies
+
+
+def pack_own_kernel(fb_ref, key_ref, value_ref, out_ref, kv_ref, asked_buf, out_buf, sems):
+    kv_ref[:, 0] = key_ref[...]
+    kv_ref[:, 1] = value_ref[...]
+    for copy in pack(fb_ref, kv_ref, out_ref, asked_buf, out_buf, sems, 0):
+        copy.wait()
+
+
+def pack_partner_kernel(fb_ref, own_ref, partner_ref, out_ref, up_ref, down_ref, asked_buf, out_buf, sems):
+    shard, shards, zh, y = place()
+    copies = pack(fb_ref, partner_ref, out_ref, asked_buf, out_buf, sems, 1)
+    up_ref[...] = jnp.where(y == lax.axis_size("y") - 1, partner_ref[...], own_ref[...])
+    down_ref[...] = jnp.where(y == 0, partner_ref[...], own_ref[...])
     for copy in copies:
         copy.wait()
 
 
-def stage(fb_ref, t, kv_ref, prev_ref, next_ref, far_ref, kbuf, vbuf):
-    shard, shards, zh, y = place()
+def stage(fb_ref, t, kv_ref, prev_ref, next_ref, far_refs, kbuf, vbuf):
+    shard, shards, zh, y = place()
+    plane = far_refs[0].shape[0]
     for which, buf in ((0, kbuf), (1, vbuf)):
         buf[0:128] = prev_ref[t, which]
         buf[128:256] = kv_ref[t, which]
         buf[256:384] = next_ref[t, which]
     for f in range(fb_ref.shape[1]):
-        _, slot = listed(fb_ref, t, shard, shards, f)
+        _, slot = listed(fb_ref, t, shard, shards, zh, f)
         rows = slice(STEP + f * BLK, STEP + (f + 1) * BLK)
-        kbuf[rows] = far_ref[slot, part(t, 0)]
-        vbuf[rows] = far_ref[slot, part(t, 1)]
+        here = slot < plane
+        at = jnp.where(here, slot, slot - plane)
+        for which, buf in ((0, kbuf), (1, vbuf)):
+            buf[rows] = jnp.where(here, *(ref[at, part(t, which)] for ref in far_refs))
 
 
 def biased(fb_ref, t, slopes_ref, q2, kbuf, put):
@@ -161,7 +170,7 @@
         scores = dot(kbuf[lo : lo + STEP], q2, NT)
         parts = []
         for i in range(STEP // BLK):
-            there, _ = listed(fb_ref, t, shard, shards, (lo - STEP) // BLK + i)
+            there, _ = listed(fb_ref, t, shard, shards, zh, (lo - STEP) // BLK + i)
             row = jnp.where(there, far_bias, masked_value)
             parts.append(scores[i * BLK : (i + 1) * BLK] + row)
         scores = jnp.concatenate(parts, axis=0)
@@ -183,8 +192,8 @@
 
 
 def attend_kernel(
-    fb_ref, slopes_ref, q_ref, kv_ref, prev_ref, next_ref, far_ref, grad_ref, mirrored_ref,
-    ctx_ref, rev_ref, gq_ref, own_out, prev_out, next_out, far_out,
+    fb_ref, slopes_ref, q_ref, kv_ref, prev_ref, next_ref, far_own, far_partner, grad_ref, mirrored_ref,
+    ctx_ref, rev_ref, gq_ref, own_out, prev_out, next_out, partner_out, here_out,
     kbuf, vbuf, pbuf, dbuf, far_buf0, far_buf1, sems,
 ):
     shard, shards, zh, y = place()
@@ -194,7 +203,7 @@
     copies = []
     for t in range(2):
         far_buf = (far_buf0, far_buf1)[t]
-        stage(fb_ref, t, kv_ref, prev_ref, next_ref, far_ref, kbuf, vbuf)
+        stage(fb_ref, t, kv_ref, prev_ref, next_ref, (far_own, far_partner), kbuf, vbuf)
         q2 = two_heads(q_ref[t] * HD ** (-0.5))
         g2 = two_heads(flipped(mirrored_ref[...]) if t == 1 else grad_ref[...])
         cols = q2.shape[0]
@@ -232,14 +241,17 @@
                 else:
                     x = x.astype(bf16)
                     for i in range(STEP // BLK):
-                        there, slot = listed(fb_ref, t, shard, shards, (lo - STEP) // BLK + i)
+                        there, slot = listed(fb_ref, t, shard, shards, zh, (lo - STEP) // BLK + i)
 
                         @pl.when(there)
                         def _():
                             far_buf[slot, which * BLK : (which + 1) * BLK] = x[i * BLK : (i + 1) * BLK]
 
-        copies.append(pltpu.make_async_copy(far_buf, far_out.at[:, 2 * t * BLK : 2 * (t + 1) * BLK], sems.at[t]))
-        copies[-1].start()
+        plane = far_own.shape[0]
+        for k, (out, rows) in enumerate(((here_out, pl.ds(0, plane)), (partner_out, pl.ds(plane, plane)))):
+            to = out.at[:, 2 * t * BLK : 2 * (t + 1) * BLK]
+            copies.append(pltpu.make_async_copy(far_buf.at[rows], to, sems.at[t, k]))
+            copies[-1].start()
         gq_ref[t] = (pick_heads(gq_acc) * HD ** (-0.5)).astype(bf16)
         ctx = pick_heads(ctx_acc).astype(bf16)
         if t == 1:
@@ -250,37 +262,48 @@
         copy.wait()
 
 
-def combine_kernel(fb_ref, own_ref, prev_ref, next_ref, far_ref, mine_ref, other_ref, asked_buf, sum_buf):
+def combine(fb_ref, far_ref, asked_buf, rel, put):
+    shard, shards, zh, y = place()
+    asked_rows(fb_ref, asked_buf, rel)
+    rows = 32
+    for t in range(2):
+        for which in range(2):
+            for lo in range(0, BLK, rows):
+                first = jnp.zeros((rows, 2 * HD), f32)
+                second = jnp.zeros((rows, 2 * HD), f32)
+                at = part(t, which).start + lo
+                for p, reader in enumerate(plane_readers(zh)):
+                    block = asked_by(asked_buf, t, reader, rows)
+                    x = far_ref[p, at : at + rows].astype(f32)
+                    first = first + jnp.where(block == 1, x, 0.0)
+                    second = second + jnp.where(block == 2, x, 0.0)
+                put(t, which, slice(lo, lo + rows), first)
+                put(t, which, slice(BLK + lo, BLK + lo + rows), second)
+
+
+def combine_partner_kernel(fb_ref, prev_ref, next_ref, far_ref, out_ref, asked_buf):
     shard, shards, zh, y = place()
     last = lax.axis_size("y") - 1
-    asked_rows(fb_ref, asked_buf)
-    rows = 32
-    for z in range(2):
-        for t in range(2):
-            for which in range(2):
-                for lo in range(0, BLK, rows):
-                    first = jnp.zeros((rows, 2 * HD), f32)
-                    second = jnp.zeros((rows, 2 * HD), f32)
-                    at = part(t, which).start + lo
-                    for p, reader in enumerate(plane_readers(zh)):
-                        block = asked_by(asked_buf, z, t, reader, rows)
-                        x = far_ref[2 * p + z, at : at + rows].astype(f32)
-                        first = first + jnp.where(block == 1, x, 0.0)
-                        second = second + jnp.where(block == 2, x, 0.0)
-                    sum_buf[z, t, which, lo : lo + rows] = first
-                    sum_buf[z, t, which, BLK + lo : BLK + lo + rows] = second
-    sum_buf[zh] = sum_buf[zh] + own_ref[...]
-    to = jnp.where(y == 0, 1 - zh, zh)
-    sum_buf[to] = sum_buf[to] + prev_ref[...].astype(f32)
-    to = jnp.where(y == last, 1 - zh, zh)
-    sum_buf[to] = sum_buf[to] + next_ref[...].astype(f32)
-    mine_ref[...] = sum_buf[zh]
-    other_ref[...] = sum_buf[1 - zh].astype(bf16)
-
-
-def finish_kernel(mine_ref, other_ref, gk_ref, gv_ref):
-    for which, ref in ((0, gk_ref), (1, gv_ref)):
-        ref[...] = (mine_ref[:, which] + other_ref[:, which].astype(f32)).astype(bf16)
+
+    def put(t, which, rows, far):
+        far = far + jnp.where(y == 0, prev_ref[t, which, rows].astype(f32), 0.0)
+        far = far + jnp.where(y == last, next_ref[t, which, rows].astype(f32), 0.0)
+        out_ref[t, which, rows] = far.astype(bf16)
+
+    combine(fb_ref, far_ref, asked_buf, 1, put)
+
+
+def combine_own_kernel(fb_ref, own_ref, prev_ref, next_ref, other_ref, far_ref, gk_ref, gv_ref, asked_buf):
+    shard, shards, zh, y = place()
+    last = lax.axis_size("y") - 1
+
+    def put(t, which, rows, far):
+        total = own_ref[t, which, rows] + jnp.where(y == 0, 0.0, prev_ref[t, which, rows].astype(f32))
+        total = total + jnp.where(y == last, 0.0, next_ref[t, which, rows].astype(f32))
+        total = total + other_ref[t, which, rows].astype(f32) + far
+        (gk_ref, gv_ref)[which][t, rows] = total.astype(bf16)
+
+    combine(fb_ref, far_ref, asked_buf, 0, put)
 
 
 def project_kernel(ctx_ref, back_ref, weight_ref, even_ref, odd_ref, sum_buf):
@@ -333,35 +356,42 @@
     cols = 2 * tok_rows
     both = (2, 2, tok_rows, width)
     pieces = (tp_count, tok_rows // tp_count, width)
-    slots = (seq_count, 4 * BLK, width)
+    slots = (nx * ny, 4 * BLK, width)
 
     def plane_a2a(x):
-        x = x.reshape(nx * ny, nz * slots[1], width)
-        return lax.all_to_all(x, ("x", "y"), split_axis=0, concat_axis=0, tiled=True).reshape(slots)
+        return lax.all_to_all(x, ("x", "y"), split_axis=0, concat_axis=0, tiled=True)
 
     def z_swap(x):
         return lax.ppermute(x, "zh", [(i, nz - 1 - i) for i in range(nz)])
 
-    key_value = jnp.stack([keys, values], axis=1)
+    asked = pltpu.VMEM((2, seq_count, 2 * HD), jnp.int32)
+    packed = [asked, pltpu.VMEM(slots, bf16), pltpu.SemaphoreType.DMA((nx * ny // 4,))]
+    outgoing, key_value = pl.pallas_call(
+        pack_own_kernel,
+        out_shape=(pltpu.HBM(slots, bf16), shape(both)),
+        in_specs=[vmem()] * 3,
+        out_specs=(hbm(), vmem()),
+        scratch_shapes=packed,
+        cost_estimate=cost(500_000, 1_500_000),
+        compiler_params=pltpu.CompilerParams(vmem_limit_bytes=LIMIT),
+        name="pack_own",
+    )(far_blocks, keys, values)
+    far_own = plane_a2a(outgoing)
     partner = z_swap(key_value)
-    asked = pltpu.VMEM((nz, 2, seq_count, 2 * HD), jnp.int32)
     outgoing, to_up, to_down = pl.pallas_call(
-        pack_kernel,
+        pack_partner_kernel,
         out_shape=(pltpu.HBM(slots, bf16), shape(both), shape(both)),
         in_specs=[vmem()] * 3,
         out_specs=(hbm(), vmem(), vmem()),
-        scratch_shapes=[
-            asked, pltpu.VMEM((nz,) + both, bf16), pltpu.VMEM(slots, bf16),
-            pltpu.SemaphoreType.DMA((nx * ny // 4,)),
-        ],
-        cost_estimate=cost(1_000_000, 2_500_000),
-        compiler_params=pltpu.CompilerParams(vmem_limit_bytes=LIMIT),
-        name="pack",
+        scratch_shapes=packed,
+        cost_estimate=cost(500_000, 1_500_000),
+        compiler_params=pltpu.CompilerParams(vmem_limit_bytes=LIMIT),
+        name="pack_partner",
     )(far_blocks, key_value, partner)
     same_core = [cotangent] + [swap(cotangent, bit) for bit in (2, 4, 6)]
     other_core = swap(jnp.stack(same_core), 1)
     outgoing, other_core = lax.optimization_barrier((outgoing, other_core))
-    far = plane_a2a(outgoing)
+    far_partner = plane_a2a(outgoing)
 
     def flat(x, zh, y):
         return (x * nz + zh) * ny + y
@@ -399,26 +429,40 @@
 
     square = shape((tok_rows, width))
     half = pltpu.VMEM((seq_count, 2 * BLK, width), bf16)
-    context_fwd, context_rev, grad_queries, own, before, after, far_grads = pl.pallas_call(
+    context_fwd, context_rev, grad_queries, own, before, after, partner_grads, here_grads = pl.pallas_call(
         attend_kernel,
-        out_shape=(square, square, shape((2, tok_rows, width)), shape(both, f32), shape(both), shape(both), pltpu.HBM(slots, bf16)),
-        in_specs=[smem()] * 2 + [vmem()] * 7,
-        out_specs=(vmem(),) * 6 + (hbm(),),
+        out_shape=(square, square, shape((2, tok_rows, width)), shape(both, f32), shape(both), shape(both))
+        + (pltpu.HBM(slots, bf16),) * 2,
+        in_specs=[smem()] * 2 + [vmem()] * 8,
+        out_specs=(vmem(),) * 6 + (hbm(),) * 2,
         scratch_shapes=[pltpu.VMEM((total_keys, width), bf16)] * 2
         + [pltpu.VMEM((total_keys, cols), f32)] * 2
-        + [half, half, pltpu.SemaphoreType.DMA((2,))],
+        + [half, half, pltpu.SemaphoreType.DMA((2, 2))],
         cost_estimate=cost(4_000_000_000, 8_000_000, 1_000_000),
         compiler_params=pltpu.CompilerParams(vmem_limit_bytes=LIMIT),
         name="attend",
-    )(far_blocks, slopes, queries, key_value, from_prev, from_next, far, grad_context, mirrored)
+    )(far_blocks, slopes, queries, key_value, from_prev, from_next, far_own, far_partner, grad_context, mirrored)
     context_back = lax.ppermute(context_rev, SEQ, mirror)
 
-    returned = plane_a2a(far_grads)
+    returned_partner = plane_a2a(partner_grads)
     from_prev_grad = lax.ppermute(after, SEQ, [(b, a) for a, b in down])
     from_next_grad = lax.ppermute(before, SEQ, [(b, a) for a, b in up])
-    context_back, from_prev_grad, from_next_grad = lax.optimization_barrier(
-        (context_back, from_prev_grad, from_next_grad)
+    here_grads, returned_partner, context_back = lax.optimization_barrier(
+        (here_grads, returned_partner, context_back)
     )
+    returned_own = plane_a2a(here_grads)
+    other = pl.pallas_call(
+        combine_partner_kernel,
+        out_shape=shape(both),
+        in_specs=[vmem()] * 4,
+        out_specs=vmem(),
+        scratch_shapes=[asked],
+        cost_estimate=cost(2_000_000, 1_500_000),
+        compiler_params=pltpu.CompilerParams(vmem_limit_bytes=LIMIT),
+        name="combine_partner",
+    )(far_blocks, from_prev_grad, from_next_grad, returned_partner)
+    other, context_back = lax.optimization_barrier((other, context_back))
+    other = z_swap(other)
 
     even, odd = pl.pallas_call(
         project_kernel,
@@ -440,25 +484,16 @@
         total = total + part_here.astype(f32)
     mixed = total.astype(bf16)
 
-    mine, other = pl.pallas_call(
-        combine_kernel,
-        out_shape=(shape(both, f32), shape(both)),
-        in_specs=[vmem()] * 5,
+    grad_keys, grad_values = pl.pallas_call(
+        combine_own_kernel,
+        out_shape=(shape((2, tok_rows, width)),) * 2,
+        in_specs=[vmem()] * 6,
         out_specs=(vmem(),) * 2,
-        scratch_shapes=[asked, pltpu.VMEM((nz,) + both, f32)],
-        cost_estimate=cost(4_000_000, 3_000_000),
-        compiler_params=pltpu.CompilerParams(vmem_limit_bytes=LIMIT),
-        name="combine",
-    )(far_blocks, own, from_prev_grad, from_next_grad, returned)
-    grad_keys, grad_values = pl.pallas_call(
-        finish_kernel,
-        out_shape=(shape((2, tok_rows, width)),) * 2,
-        in_specs=[vmem()] * 2,
-        out_specs=(vmem(),) * 2,
-        cost_estimate=cost(100_000, 500_000),
-        compiler_params=pltpu.CompilerParams(vmem_limit_bytes=LIMIT),
-        name="finish",
-    )(mine, z_swap(other))
+        scratch_shapes=[asked],
+        cost_estimate=cost(2_000_000, 1_500_000),
+        compiler_params=pltpu.CompilerParams(vmem_limit_bytes=LIMIT),
+        name="combine_own",
+    )(far_blocks, own, from_prev_grad, from_next_grad, other, returned_own)
     return (mixed, grad_queries, grad_keys, grad_values)
 
 

time: 121 us -> 115 us (0.950); the launches traced: 119 us -> 115 us
  waiting for transfers between devices: 37.3 us -> 20.9 us
  starting transfers between devices: 63.4 us -> 74.1 us
  local copies, waits for them, and re-layouts: 1.47 us -> 3.15 us
  other arithmetic: 2.33 us -> 0.69 us
    all_to_all x2 -> x4, starting transfers between devices: 13.7 us -> 27.5 us  [plane_a2a(): lax.all_to_all(x, ('x', 'y'), split_axis=0, concat_axis=0, tiled=True)]
    ppermute x1, waiting for transfers between devices: 5.48 us -> 0.01 us  [per_device(): from_prev_grad = lax.ppermute(after, SEQ, [(b, a) for a, b in down])]
    ppermute x1, waiting for transfers between devices: 5.08 us -> 0.01 us  [per_device(): from_prev = lax.ppermute(to_up, SEQ, up)]
    ppermute x2, waiting for transfers between devices: 5.28 us -> 8.88 us  [z_swap(): return lax.ppermute(x, 'zh', [(i, nz - 1 - i) for i in range(nz)])]
    ppermute x1, waiting for transfers between devices: 6.01 us -> 3 us  [per_device(): from_next_grad = lax.ppermute(before, SEQ, [(b, a) for a, b in up])]
    ppermute x1, waiting for transfers between devices: 3 us -> 0.01 us  [per_device(): context_back = lax.ppermute(context_rev, SEQ, mirror)]
    ppermute x1, starting transfers between devices: 2.01 us -> 4.57 us  [per_device(): from_prev_grad = lax.ppermute(after, SEQ, [(b, a) for a, b in down])]
    ppermute x8, starting transfers between devices: 11.6 us -> 9.04 us  [swap(): return lax.ppermute(x, 'tp', [(i, i ^ bit) for i in range(count)])]
  transfers between devices with their start and end apart: 18 -> 20, of which waited for: 11 -> 8; matrix products, arithmetic and copies ran while one was open for 3% -> 1% of each run, Pallas kernels for 3% -> 2%
where the time goes in v5:
time: 115 us
  starting transfers between devices  74.1 us (64%)
  waiting for transfers between devices  20.9 us (18%)
  Pallas kernels  14.9 us (13%)
  local copies, waits for them, and re-layouts  3.15 us (3%)
    all_to_all x4, starting transfers between devices, plane_a2a(): lax.all_to_all(x, ('x', 'y'), split_axis=0, concat_axis=0, tiled=True)  27.5 us
    pallas_call x1, Pallas kernels, per_device(): pl.pallas_call(attend_kernel, out_shape=(square, square, shape((2, tok_ro...  10.4 us
    ppermute x1, starting transfers between devices, per_device(): mirrored = lax.ppermute(grad_context, SEQ, mirror)  9.32 us
    ppermute x8, starting transfers between devices, swap(): return lax.ppermute(x, 'tp', [(i, i ^ bit) for i in range(count)])  9.04 us
    ppermute x2, waiting for transfers between devices, z_swap(): return lax.ppermute(x, 'zh', [(i, nz - 1 - i) for i in range(nz)])  8.88 us
    ppermute x1, starting transfers between devices, per_device(): context_back = lax.ppermute(context_rev, SEQ, mirror)  8.06 us
    ppermute x2, starting transfers between devices, z_swap(): return lax.ppermute(x, 'zh', [(i, nz - 1 - i) for i in range(nz)])  7.72 us
    ppermute x8, waiting for transfers between devices, swap(): return lax.ppermute(x, 'tp', [(i, i ^ bit) for i in range(count)])  6.16 us
  transfers between devices with their start and end apart: 20, of which 8 were waited for; matrix products, arithmetic and copies ran while one was open for 1% of the time, Pallas kernels for 2%

profile of v5, /device:TPU:24, one launch (start us, length us, event | category | flops | bytes accessed | tf_op | source)
XLA Modules:
  0.0 114.5 jit_solution(9959665608697482454)
XLA Ops:
  0.6 0.8 copy.14.fb_ref
  1.4 0.8 copy-done.2
  2.3 0.8 copy-done.3
  3.1 1.1 %pack_own.1 = (bf16[16,256,128]{2,1,0:T(8,128)(2,1)}, bf16[2,2,128,128]{3,2,1,0:T(8,128)(2,1)S(1)}) custom-call(s32[32,24]{1,0:T(8,128)S(1)} %copy.14.fb_ref, bf16[2,128,128]{2,1,0:T(8,128)(2,1)S(1)} %copy-done.2, bf16[2,128,128]{2,1,0:T(8,128)(2,1)S(1)} %copy-done.3), custom_call_target="tpu_custom_call" | custom-call | flops 500000 | bytes 1500000 | tf_op jit(solution)/shard_map/pack_own/pallas_call | solution.py:369
  4.3 7.2 %all-to-all-start = ((bf16[16,256,128]{2,1,0:T(8,128)(2,1)}), bf16[16,256,128]{2,1,0:T(8,128)(2,1)S(1)}, u32[]{:S(2)}, u32[]{:S(2)}) async-start(bf16[16,256,128]{2,1,0:T(8,128)(2,1)} %get-tuple-element.31), calls=%async_computation | async-start | bytes 2097152 | tf_op jit(solution)/shard_map/all_to_all | solution.py:362
  11.4 3.4 %collective-permute-start.4 = (bf16[16,1024]{1,0:T(8,128)(2,1)S(1)}, bf16[16,1024]{1,0:T(8,128)(2,1)S(1)}, u32[]{:S(2)}, u32[]{:S(2)}) collective-permute-start(bf16[16,1024]{1,0:T(8,128)(2,1)S(1)} %copy-done.1), channel_id=1, source_target_pairs={{0,4},{1,5},{2,6},{3,7},{4,0},{5,1},{6,2},{7,3},{8,12},{9,13},{10,... | collective-permute-start | bytes 98312 | tf_op jit(solution)/shard_map/ppermute | solution.py:344
  14.8 1.9 %collective-permute-start.3 = (bf16[16,1024]{1,0:T(8,128)(2,1)S(1)}, bf16[16,1024]{1,0:T(8,128)(2,1)S(1)}, u32[]{:S(2)}, u32[]{:S(2)}) collective-permute-start(bf16[16,1024]{1,0:T(8,128)(2,1)S(1)} %copy-done.1), channel_id=1, source_target_pairs={{0,2},{1,3},{2,0},{3,1},{4,6},{5,7},{6,4},{7,5},{8,10},{9,11},{10,... | collective-permute-start | bytes 98312 | tf_op jit(solution)/shard_map/ppermute | solution.py:344
  16.7 6.4 %collective-permute-start = (bf16[2,2,128,128]{3,2,1,0:T(8,128)(2,1)S(1)}, bf16[2,2,128,128]{3,2,1,0:T(8,128)(2,1)S(1)}, u32[]{:S(2)}, u32[]{:S(2)}) collective-permute-start(bf16[2,2,128,128]{3,2,1,0:T(8,128)(2,1)S(1)} %get-tuple-element.28.own_ref.kv_ref), channel_id=1, source_target_pairs={{0,32},{32,0},{1,33},{33,1},{2,34},{34,2},{3,35},{35,3},{4,36},{36... | collective-permute-start | bytes 393224 | tf_op jit(solution)/shard_map/ppermute | solution.py:365
  23.3 4.6 %collective-permute-done.partner_ref = bf16[2,2,128,128]{3,2,1,0:T(8,128)(2,1)S(1)} collective-permute-done((bf16[2,2,128,128]{3,2,1,0:T(8,128)(2,1)S(1)}, bf16[2,2,128,128]{3,2,1,0:T(8,128)(2,1)S(1)}, u32[]{:S(2)}, u32[]{:S(2)}) %collective-permute-start) | collective-permute-done | bytes 131104 | tf_op jit(solution)/shard_map/ppermute | solution.py:365
  28.0 1.1 pack_partner.1
  29.1 7.4 %all-to-all-start.1 = ((bf16[16,256,128]{2,1,0:T(8,128)(2,1)}), bf16[16,256,128]{2,1,0:T(8,128)(2,1)S(1)}, u32[]{:S(2)}, u32[]{:S(2)}) async-start(bf16[16,256,128]{2,1,0:T(8,128)(2,1)} %get-tuple-element.33), calls=%async_computation.1 | async-start | bytes 2097152 | tf_op jit(solution)/shard_map/all_to_all | solution.py:362
  36.5 3.4 %collective-permute-start.1 = (bf16[2,2,128,128]{3,2,1,0:T(8,128)(2,1)S(1)}, bf16[2,2,128,128]{3,2,1,0:T(8,128)(2,1)S(1)}, u32[]{:S(2)}, u32[]{:S(2)}) collective-permute-start(bf16[2,2,128,128]{3,2,1,0:T(8,128)(2,1)S(1)} %get-tuple-element.29), channel_id=1, source_target_pairs={{0,8},{8,16},{16,24},{24,64},{32,40},{40,48},{48,56},{56,32},{64,7... | collective-permute-start | bytes 393224 | tf_op jit(solution)/shard_map/ppermute | solution.py:415
  39.9 2.6 %collective-permute-start.2 = (bf16[2,2,128,128]{3,2,1,0:T(8,128)(2,1)S(1)}, bf16[2,2,128,128]{3,2,1,0:T(8,128)(2,1)S(1)}, u32[]{:S(2)}, u32[]{:S(2)}) collective-permute-start(bf16[2,2,128,128]{3,2,1,0:T(8,128)(2,1)S(1)} %get-tuple-element.30), channel_id=1, source_target_pairs={{0,24},{8,0},{16,8},{24,16},{40,32},{48,40},{56,48},{64,88},{72,64... | collective-permute-start | bytes 393224 | tf_op jit(solution)/shard_map/ppermute | solution.py:416
  42.8 9.3 %collective-permute-start.7 = (bf16[128,128]{1,0:T(8,128)(2,1)S(1)}, bf16[128,128]{1,0:T(8,128)(2,1)S(1)}, u32[]{:S(2)}, u32[]{:S(2)}) collective-permute-start(bf16[128,128]{1,0:T(8,128)(2,1)S(1)} %context_grad.1.grad_ref), channel_id=1, source_target_pairs={{0,248},{8,240},{16,232},{24,224},{32,216},{40,208},{48,200},{56,1... | collective-permute-start | bytes 98312 | tf_op jit(solution)/shard_map/ppermute | solution.py:428
  52.1 2.8 %collective-permute-done.7.mirrored_ref = bf16[128,128]{1,0:T(8,128)(2,1)S(1)} collective-permute-done((bf16[128,128]{1,0:T(8,128)(2,1)S(1)}, bf16[128,128]{1,0:T(8,128)(2,1)S(1)}, u32[]{:S(2)}, u32[]{:S(2)}) %collective-permute-start.7) | collective-permute-done | bytes 32800 | tf_op jit(solution)/shard_map/ppermute | solution.py:428
  54.9 0.6 copy-done.5
  55.6 10.4 %attend.1 = (bf16[128,128]{1,0:T(8,128)(2,1)S(1)}, bf16[128,128]{1,0:T(8,128)(2,1)}, bf16[2,128,128]{2,1,0:T(8,128)(2,1)}, f32[2,2,128,128]{3,2,1,0:T(8,128)S(1)...) custom-call(s32[32,24]{1,0:T(8,128)S(1)} %copy.14.fb_ref, ...), custom_call_target="tpu_custom_call" | custom-call | flops 4000000000 | bytes 8000000 | tf_op jit(solution)/shard_map/attend/pallas_call | solution.py:432
  66.0 6.7 %all-to-all-start.2 = ((bf16[16,256,128]{2,1,0:T(8,128)(2,1)}), bf16[16,256,128]{2,1,0:T(8,128)(2,1)S(1)}, u32[]{:S(2)}, u32[]{:S(2)}) async-start(bf16[16,256,128]{2,1,0:T(8,128)(2,1)} %get-tuple-element.39), calls=%async_computation.2 | async-start | bytes 2097152 | tf_op jit(solution)/shard_map/all_to_all | solution.py:362
  72.7 8.1 %collective-permute-start.10 = (bf16[128,128]{1,0:T(8,128)(2,1)}, bf16[128,128]{1,0:T(8,128)(2,1)S(1)}, u32[]{:S(2)}, u32[]{:S(2)}) collective-permute-start(bf16[128,128]{1,0:T(8,128)(2,1)} %get-tuple-element.40), channel_id=1, source_target_pairs={{0,248},{8,240},{16,232},{24,224},{32,216},{40,208},{48,200},{56,1... | collective-permute-start | bytes 98312 | tf_op jit(solution)/shard_map/ppermute | solution.py:445
  80.7 4.6 %collective-permute-start.8 = (bf16[2,2,128,128]{3,2,1,0:T(8,128)(2,1)S(1)}, bf16[2,2,128,128]{3,2,1,0:T(8,128)(2,1)S(1)}, u32[]{:S(2)}, u32[]{:S(2)}) collective-permute-start(bf16[2,2,128,128]{3,2,1,0:T(8,128)(2,1)S(1)} %get-tuple-element.36), channel_id=1, source_target_pairs={{24,0},{0,8},{8,16},{16,24},{32,40},{40,48},{48,56},{88,64},{64,72... | collective-permute-start | bytes 393224 | tf_op jit(solution)/shard_map/ppermute | solution.py:448
  85.3 1.9 %collective-permute-start.9 = (bf16[2,2,128,128]{3,2,1,0:T(8,128)(2,1)S(1)}, bf16[2,2,128,128]{3,2,1,0:T(8,128)(2,1)S(1)}, u32[]{:S(2)}, u32[]{:S(2)}) collective-permute-start(bf16[2,2,128,128]{3,2,1,0:T(8,128)(2,1)S(1)} %get-tuple-element.37), channel_id=1, source_target_pairs={{8,0},{16,8},{24,16},{64,24},{40,32},{48,40},{56,48},{32,56},{72,6... | collective-permute-start | bytes 393224 | tf_op jit(solution)/shard_map/ppermute | solution.py:449
  87.2 6.3 %all-to-all-start.3 = ((bf16[16,256,128]{2,1,0:T(8,128)(2,1)}), bf16[16,256,128]{2,1,0:T(8,128)(2,1)S(1)}, u32[]{:S(2)}, u32[]{:S(2)}) async-start(bf16[16,256,128]{2,1,0:T(8,128)(2,1)} %get-tuple-element.49), calls=%async_computation.3 | async-start | bytes 2097152 | tf_op jit(solution)/shard_map/all_to_all | solution.py:362
  93.5 3.0 %collective-permute-done.9.next_ref = bf16[2,2,128,128]{3,2,1,0:T(8,128)(2,1)S(1)} collective-permute-done((bf16[2,2,128,128]{3,2,1,0:T(8,128)(2,1)S(1)}, bf16[2,2,128,128]{3,2,1,0:T(8,128)(2,1)S(1)}, u32[]{:S(2)}, u32[]{:S(2)}) %collective-permute-start.9) | collective-permute-done | bytes 131104 | tf_op jit(solution)/shard_map/ppermute | solution.py:449
  97.4 1.3 %collective-permute-done.11 = bf16[4,16,1024]{2,1,0:T(8,128)(2,1)S(1)} collective-permute-done((bf16[4,16,1024]{2,1,0:T(8,128)(2,1)S(1)}, bf16[4,16,1024]{2,1,0:T(8,128)(2,1)S(1)}, u32[]{:S(2)}, u32[]{:S(2)}) %collective-permute-start.11) | collective-permute-done | bytes 131104 | tf_op jit(solution)/shard_map/ppermute | solution.py:344
  99.1 0.8 collective-permute-start.14
  99.9 2.4 %collective-permute-start.13 = (bf16[16,1024]{1,0:T(8,128)(2,1)S(1)}, bf16[16,1024]{1,0:T(8,128)(2,1)S(1)}, u32[]{:S(2)}, u32[]{:S(2)}) collective-permute-start(bf16[16,1024]{1,0:T(8,128)(2,1)S(1)} %get-tuple-element.56), channel_id=1, source_target_pairs={{0,4},{1,5},{2,6},{3,7},{4,0},{5,1},{6,2},{7,3},{8,12},{9,13},{10,... | collective-permute-start | bytes 98312 | tf_op jit(solution)/shard_map/ppermute | solution.py:344
  102.4 1.3 %collective-permute-start.15 = (bf16[2,2,128,128]{3,2,1,0:T(8,128)(2,1)S(1)}, bf16[2,2,128,128]{3,2,1,0:T(8,128)(2,1)S(1)}, u32[]{:S(2)}, u32[]{:S(2)}) collective-permute-start(bf16[2,2,128,128]{3,2,1,0:T(8,128)(2,1)S(1)} %combine_partner.1), channel_id=1, source_target_pairs={{0,32},{32,0},{1,33},{33,1},{2,34},{34,2},{3,35},{35,3},{4,36},{36... | collective-permute-start | bytes 393224 | tf_op jit(solution)/shard_map/ppermute | solution.py:365
  103.7 1.2 %collective-permute-done.14 = bf16[16,1024]{1,0:T(8,128)(2,1)S(1)} collective-permute-done((bf16[16,1024]{1,0:T(8,128)(2,1)S(1)}, bf16[16,1024]{1,0:T(8,128)(2,1)S(1)}, u32[]{:S(2)}, u32[]{:S(2)}) %collective-permute-start.14) | collective-permute-done | bytes 32800 | tf_op jit(solution)/shard_map/ppermute | solution.py:344
  104.9 3.5 %collective-permute-done.13 = bf16[16,1024]{1,0:T(8,128)(2,1)S(1)} collective-permute-done((bf16[16,1024]{1,0:T(8,128)(2,1)S(1)}, bf16[16,1024]{1,0:T(8,128)(2,1)S(1)}, u32[]{:S(2)}, u32[]{:S(2)}) %collective-permute-start.13) | collective-permute-done | bytes 32800 | tf_op jit(solution)/shard_map/ppermute | solution.py:344
  108.4 0.6 fusion.4
  109.1 4.2 %collective-permute-done.15.other_ref = bf16[2,2,128,128]{3,2,1,0:T(8,128)(2,1)S(1)} collective-permute-done((bf16[2,2,128,128]{3,2,1,0:T(8,128)(2,1)S(1)}, bf16[2,2,128,128]{3,2,1,0:T(8,128)(2,1)S(1)}, u32[]{:S(2)}, u32[]{:S(2)}) %collective-permute-start.15) | collective-permute-done | bytes 131104 | tf_op jit(solution)/shard_map/ppermute | solution.py:365
  113.3 1.2 %combine_own.1 = (bf16[2,128,128]{2,1,0:T(8,128)(2,1)}, bf16[2,128,128]{2,1,0:T(8,128)(2,1)}) custom-call(s32[32,24]{1,0:T(8,128)S(1)} %copy.14.fb_ref, f32[2,2,128,128]{3,2,1,0:T(8,128)S(1)} %get-tuple-element.47.own_ref, bf16[2,2,128,128]{3,2,1,0:T(8,128)(2,1)S(1)} %collective-permute-done.8.prev_ref, ...), custom_call_target="tpu_custom_call" | custom-call | flops 2000000 | bytes 1500000 | tf_op jit(solution)/shard_map/combine_own/pallas_call | solution.py:487
  (34 shorter events, 1.7 us)
Async XLA Ops:
  1.4 0.8 copy-start.2
  2.3 0.8 copy-start.3
  4.2 7.2 %copy-start.1 = (bf16[16,1024]{1,0:T(8,128)(2,1)S(1)}, bf16[16,1024]{1,0:T(8,128)(2,1)}, u32[]{:S(2)}) copy-start(bf16[16,1024]{1,0:T(8,128)(2,1)} %ref0.1) | copy-start | bytes 98308
  4.3 24.9 %all-to-all-start = ((bf16[16,256,128]{2,1,0:T(8,128)(2,1)}), bf16[16,256,128]{2,1,0:T(8,128)(2,1)S(1)}, u32[]{:S(2)}, u32[]{:S(2)}) async-start(bf16[16,256,128]{2,1,0:T(8,128)(2,1)} %get-tuple-element.31), calls=%async_computation | async-start | bytes 2097152 | tf_op jit(solution)/shard_map/all_to_all | solution.py:362
  11.4 11.7 %collective-permute-start.4 = (bf16[16,1024]{1,0:T(8,128)(2,1)S(1)}, bf16[16,1024]{1,0:T(8,128)(2,1)S(1)}, u32[]{:S(2)}, u32[]{:S(2)}) collective-permute-start(bf16[16,1024]{1,0:T(8,128)(2,1)S(1)} %copy-done.1), channel_id=1, source_target_pairs={{0,4},{1,5},{2,6},{3,7},{4,0},{5,1},{6,2},{7,3},{8,12},{9,13},{10,... | collective-permute-start | bytes 98312 | tf_op jit(solution)/shard_map/ppermute | solution.py:344
  14.8 8.3 %collective-permute-start.3 = (bf16[16,1024]{1,0:T(8,128)(2,1)S(1)}, bf16[16,1024]{1,0:T(8,128)(2,1)S(1)}, u32[]{:S(2)}, u32[]{:S(2)}) collective-permute-start(bf16[16,1024]{1,0:T(8,128)(2,1)S(1)} %copy-done.1), channel_id=1, source_target_pairs={{0,2},{1,3},{2,0},{3,1},{4,6},{5,7},{6,4},{7,5},{8,10},{9,11},{10,... | collective-permute-start | bytes 98312 | tf_op jit(solution)/shard_map/ppermute | solution.py:344
  16.7 6.5 %collective-permute-start.5 = (bf16[16,1024]{1,0:T(8,128)(2,1)S(1)}, bf16[16,1024]{1,0:T(8,128)(2,1)S(1)}, u32[]{:S(2)}, u32[]{:S(2)}) collective-permute-start(bf16[16,1024]{1,0:T(8,128)(2,1)S(1)} %copy-done.1), channel_id=1, source_target_pairs={{0,6},{1,7},{2,4},{3,5},{4,2},{5,3},{6,0},{7,1},{8,14},{9,15},{10,... | collective-permute-start | bytes 98312 | tf_op jit(solution)/shard_map/ppermute | solution.py:344
  16.7 11.2 %collective-permute-start = (bf16[2,2,128,128]{3,2,1,0:T(8,128)(2,1)S(1)}, bf16[2,2,128,128]{3,2,1,0:T(8,128)(2,1)S(1)}, u32[]{:S(2)}, u32[]{:S(2)}) collective-permute-start(bf16[2,2,128,128]{3,2,1,0:T(8,128)(2,1)S(1)} %get-tuple-element.28.own_ref.kv_ref), channel_id=1, source_target_pairs={{0,32},{32,0},{1,33},{33,1},{2,34},{34,2},{3,35},{35,3},{4,36},{36... | collective-permute-start | bytes 393224 | tf_op jit(solution)/shard_map/ppermute | solution.py:365
  23.2 5.9 %collective-permute-start.6 = (bf16[4,16,1024]{2,1,0:T(8,128)(2,1)S(1)}, bf16[4,16,1024]{2,1,0:T(8,128)(2,1)S(1)}, u32[]{:S(2)}, u32[]{:S(2)}) collective-permute-start(bf16[4,16,1024]{2,1,0:T(8,128)(2,1)S(1)} %pad_maximum_fusion), channel_id=1, source_target_pairs={{0,1},{1,0},{2,3},{3,2},{4,5},{5,4},{6,7},{7,6},{8,9},{9,8},{10,11... | collective-permute-start | bytes 393224 | tf_op jit(solution)/shard_map/ppermute | solution.py:344
  29.1 13.4 %copy-start = (bf16[128,1024]{1,0:T(8,128)(2,1)S(1)}, bf16[128,1024]{1,0:T(8,128)(2,1)}, u32[]{:S(2)}) copy-start(bf16[128,1024]{1,0:T(8,128)(2,1)} %weight_ref.3) | copy-start | bytes 786436
  29.1 25.8 %all-to-all-start.1 = ((bf16[16,256,128]{2,1,0:T(8,128)(2,1)}), bf16[16,256,128]{2,1,0:T(8,128)(2,1)S(1)}, u32[]{:S(2)}, u32[]{:S(2)}) async-start(bf16[16,256,128]{2,1,0:T(8,128)(2,1)} %get-tuple-element.33), calls=%async_computation.1 | async-start | bytes 2097152 | tf_op jit(solution)/shard_map/all_to_all | solution.py:362
  36.5 18.4 %collective-permute-start.1 = (bf16[2,2,128,128]{3,2,1,0:T(8,128)(2,1)S(1)}, bf16[2,2,128,128]{3,2,1,0:T(8,128)(2,1)S(1)}, u32[]{:S(2)}, u32[]{:S(2)}) collective-permute-start(bf16[2,2,128,128]{3,2,1,0:T(8,128)(2,1)S(1)} %get-tuple-element.29), channel_id=1, source_target_pairs={{0,8},{8,16},{16,24},{24,64},{32,40},{40,48},{48,56},{56,32},{64,7... | collective-permute-start | bytes 393224 | tf_op jit(solution)/shard_map/ppermute | solution.py:415
  39.9 15.0 %copy-start.4 = (bf16[2,128,128]{2,1,0:T(8,128)(2,1)S(1)}, bf16[2,128,128]{2,1,0:T(8,128)(2,1)}, u32[]{:S(2)}) copy-start(bf16[2,128,128]{2,1,0:T(8,128)(2,1)} %q_ref.1) | copy-start | bytes 196612
  39.9 15.0 %collective-permute-start.2 = (bf16[2,2,128,128]{3,2,1,0:T(8,128)(2,1)S(1)}, bf16[2,2,128,128]{3,2,1,0:T(8,128)(2,1)S(1)}, u32[]{:S(2)}, u32[]{:S(2)}) collective-permute-start(bf16[2,2,128,128]{3,2,1,0:T(8,128)(2,1)S(1)} %get-tuple-element.30), channel_id=1, source_target_pairs={{0,24},{8,0},{16,8},{24,16},{40,32},{48,40},{56,48},{64,88},{72,64... | collective-permute-start | bytes 393224 | tf_op jit(solution)/shard_map/ppermute | solution.py:416
  42.8 12.1 %collective-permute-start.7 = (bf16[128,128]{1,0:T(8,128)(2,1)S(1)}, bf16[128,128]{1,0:T(8,128)(2,1)S(1)}, u32[]{:S(2)}, u32[]{:S(2)}) collective-permute-start(bf16[128,128]{1,0:T(8,128)(2,1)S(1)} %context_grad.1.grad_ref), channel_id=1, source_target_pairs={{0,248},{8,240},{16,232},{24,224},{32,216},{40,208},{48,200},{56,1... | collective-permute-start | bytes 98312 | tf_op jit(solution)/shard_map/ppermute | solution.py:428
  54.9 0.7 copy-start.5
  66.0 21.2 %all-to-all-start.2 = ((bf16[16,256,128]{2,1,0:T(8,128)(2,1)}), bf16[16,256,128]{2,1,0:T(8,128)(2,1)S(1)}, u32[]{:S(2)}, u32[]{:S(2)}) async-start(bf16[16,256,128]{2,1,0:T(8,128)(2,1)} %get-tuple-element.39), calls=%async_computation.2 | async-start | bytes 2097152 | tf_op jit(solution)/shard_map/all_to_all | solution.py:362
  72.7 14.6 %collective-permute-start.10 = (bf16[128,128]{1,0:T(8,128)(2,1)}, bf16[128,128]{1,0:T(8,128)(2,1)S(1)}, u32[]{:S(2)}, u32[]{:S(2)}) collective-permute-start(bf16[128,128]{1,0:T(8,128)(2,1)} %get-tuple-element.40), channel_id=1, source_target_pairs={{0,248},{8,240},{16,232},{24,224},{32,216},{40,208},{48,200},{56,1... | collective-permute-start | bytes 98312 | tf_op jit(solution)/shard_map/ppermute | solution.py:445
  80.7 12.8 %collective-permute-start.8 = (bf16[2,2,128,128]{3,2,1,0:T(8,128)(2,1)S(1)}, bf16[2,2,128,128]{3,2,1,0:T(8,128)(2,1)S(1)}, u32[]{:S(2)}, u32[]{:S(2)}) collective-permute-start(bf16[2,2,128,128]{3,2,1,0:T(8,128)(2,1)S(1)} %get-tuple-element.36), channel_id=1, source_target_pairs={{24,0},{0,8},{8,16},{16,24},{32,40},{40,48},{48,56},{88,64},{64,72... | collective-permute-start | bytes 393224 | tf_op jit(solution)/shard_map/ppermute | solution.py:448
  85.3 11.2 %collective-permute-start.9 = (bf16[2,2,128,128]{3,2,1,0:T(8,128)(2,1)S(1)}, bf16[2,2,128,128]{3,2,1,0:T(8,128)(2,1)S(1)}, u32[]{:S(2)}, u32[]{:S(2)}) collective-permute-start(bf16[2,2,128,128]{3,2,1,0:T(8,128)(2,1)S(1)} %get-tuple-element.37), channel_id=1, source_target_pairs={{8,0},{16,8},{24,16},{64,24},{40,32},{48,40},{56,48},{32,56},{72,6... | collective-permute-start | bytes 393224 | tf_op jit(solution)/shard_map/ppermute | solution.py:449
  87.2 26.1 %all-to-all-start.3 = ((bf16[16,256,128]{2,1,0:T(8,128)(2,1)}), bf16[16,256,128]{2,1,0:T(8,128)(2,1)S(1)}, u32[]{:S(2)}, u32[]{:S(2)}) async-start(bf16[16,256,128]{2,1,0:T(8,128)(2,1)} %get-tuple-element.49), calls=%async_computation.3 | async-start | bytes 2097152 | tf_op jit(solution)/shard_map/all_to_all | solution.py:362
  97.3 1.4 %collective-permute-start.11 = (bf16[4,16,1024]{2,1,0:T(8,128)(2,1)S(1)}, bf16[4,16,1024]{2,1,0:T(8,128)(2,1)S(1)}, u32[]{:S(2)}, u32[]{:S(2)}) collective-permute-start(bf16[4,16,1024]{2,1,0:T(8,128)(2,1)S(1)} %get-tuple-element.45), channel_id=1, source_target_pairs={{0,1},{1,0},{2,3},{3,2},{4,5},{5,4},{6,7},{7,6},{8,9},{9,8},{10,11... | collective-permute-start | bytes 393224 | tf_op jit(solution)/shard_map/ppermute | solution.py:344
  98.8 9.7 %copy-start.6 = (bf16[16,1024]{1,0:T(8,128)(2,1)S(1)}, bf16[16,1024]{1,0:T(8,128)(2,1)}, u32[]{:S(2)}) copy-start(bf16[16,1024]{1,0:T(8,128)(2,1)} %param.9) | copy-start | bytes 98308
  98.8 4.9 %collective-permute-start.12 = (bf16[16,1024]{1,0:T(8,128)(2,1)S(1)}, bf16[16,1024]{1,0:T(8,128)(2,1)S(1)}, u32[]{:S(2)}, u32[]{:S(2)}) collective-permute-start(bf16[16,1024]{1,0:T(8,128)(2,1)S(1)} %get-tuple-element.54), channel_id=1, source_target_pairs={{0,2},{1,3},{2,0},{3,1},{4,6},{5,7},{6,4},{7,5},{8,10},{9,11},{10,... | collective-permute-start | bytes 98312 | tf_op jit(solution)/shard_map/ppermute | solution.py:344
  99.1 5.8 %collective-permute-start.14 = (bf16[16,1024]{1,0:T(8,128)(2,1)S(1)}, bf16[16,1024]{1,0:T(8,128)(2,1)S(1)}, u32[]{:S(2)}, u32[]{:S(2)}) collective-permute-start(bf16[16,1024]{1,0:T(8,128)(2,1)S(1)} %get-tuple-element.55), channel_id=1, source_target_pairs={{0,6},{1,7},{2,4},{3,5},{4,2},{5,3},{6,0},{7,1},{8,14},{9,15},{10,... | collective-permute-start | bytes 98312 | tf_op jit(solution)/shard_map/ppermute | solution.py:344
  99.9 8.5 %collective-permute-start.13 = (bf16[16,1024]{1,0:T(8,128)(2,1)S(1)}, bf16[16,1024]{1,0:T(8,128)(2,1)S(1)}, u32[]{:S(2)}, u32[]{:S(2)}) collective-permute-start(bf16[16,1024]{1,0:T(8,128)(2,1)S(1)} %get-tuple-element.56), channel_id=1, source_target_pairs={{0,4},{1,5},{2,6},{3,7},{4,0},{5,1},{6,2},{7,3},{8,12},{9,13},{10,... | collective-permute-start | bytes 98312 | tf_op jit(solution)/shard_map/ppermute | solution.py:344
  102.4 11.0 %collective-permute-start.15 = (bf16[2,2,128,128]{3,2,1,0:T(8,128)(2,1)S(1)}, bf16[2,2,128,128]{3,2,1,0:T(8,128)(2,1)S(1)}, u32[]{:S(2)}, u32[]{:S(2)}) collective-permute-start(bf16[2,2,128,128]{3,2,1,0:T(8,128)(2,1)S(1)} %combine_partner.1), channel_id=1, source_target_pairs={{0,32},{32,0},{1,33},{33,1},{2,34},{34,2},{3,35},{35,3},{4,36},{36... | collective-permute-start | bytes 393224 | tf_op jit(solution)/shard_map/ppermute | solution.py:365

commit v6 on v5

v6 whole, which is shorter than its diff:
```python
import jax
import jax.numpy as jnp
from jax import lax
from jax.experimental import pallas as pl
from jax.experimental.pallas import tpu as pltpu
from jax.sharding import PartitionSpec as P

HD = 64
BLK = 64
BAND = 2
STEP = 384
LIMIT = 24 << 20

masked_value = -1e30
f32 = jnp.float32
bf16 = jnp.bfloat16

NT = (((1,), (1,)), ((), ()))
NN = (((1,), (0,)), ((), ()))


def dot(a, b, dims):
    return lax.dot_general(a, b, dims, preferred_element_type=f32)


def two_heads(x):
    first = lax.broadcasted_iota(jnp.int32, x.shape, 1) < HD
    zero = jnp.zeros_like(x)
    return jnp.concatenate([jnp.where(first, x, zero), jnp.where(first, zero, x)], axis=0)


def pick_heads(xt):
    rows = xt.shape[1] // 2
    own = jnp.concatenate([xt[:HD, :rows], xt[HD:, rows:]], axis=0)
    return own.T


def one_hot(n, at):
    r = lax.broadcasted_iota(jnp.int32, (n, n), 0)
    c = lax.broadcasted_iota(jnp.int32, (n, n), 1)
    return (c == at(r)).astype(bf16)


def flipped(x):
    n = x.shape[0]
    return dot(one_hot(n, lambda r: n - 1 - r), x, NN).astype(bf16)


SEQ = ("x", "zh", "y")


def place():
    x, zh, y = (lax.axis_index(a) for a in SEQ)
    nx, nz, ny = (lax.axis_size(a) for a in SEQ)
    return (x * nz + zh) * ny + y, nx * nz * ny, zh, y


def slot_of(owner, zh):
    nz, ny = lax.axis_size("zh"), lax.axis_size("y")
    xz, y = lax.div(owner, ny), lax.rem(owner, ny)
    x, z = lax.div(xz, nz), lax.rem(xz, nz)
    return 2 * (x * ny + y) + jnp.where(z == zh, 0, 1)


def plane_readers(zh):
    nx, nz, ny = (lax.axis_size(a) for a in SEQ)
    return [(x * nz + zh) * ny + y for x in range(nx) for y in range(ny)]


def part(t, which):
    return slice((2 * t + which) * BLK, (2 * t + which + 1) * BLK)


def listed(fb_ref, t, shard, shards, zh, f):
    entry = fb_ref[shard if t == 0 else shards - 1 - shard, f]
    owner = lax.shift_right_arithmetic(entry, 1)
    owner = owner if t == 0 else shards - 1 - owner
    return entry >= 0, jnp.where(entry >= 0, slot_of(owner, zh), 0)


def asked_of(fb, t, shard, shards):
    mine = shard if t == 0 else shards - 1 - shard
    inner = fb & 1
    inner = inner + 1 if t == 0 else 2 - inner
    hit = jnp.where(lax.shift_right_arithmetic(fb, 1) == mine, inner, 0)
    return jnp.sum(hit, axis=1, keepdims=True)


def asked_rows(fb_ref, asked_buf, rel):
    shard, shards, zh, y = place()
    target = shard + rel * (1 - 2 * zh) * lax.axis_size("y")
    fb = fb_ref[...]
    for t in range(2):
        asked_buf[t] = jnp.broadcast_to(asked_of(fb, t, target, shards), asked_buf.shape[1:])


def asked_by(asked_buf, t, reader, rows):
    row = reader if t == 0 else asked_buf.shape[1] - 1 - reader
    return jnp.broadcast_to(asked_buf[t, pl.ds(row, 1)], (rows, 2 * HD))


def load_kernel(key_ref, value_ref, cot_ref, out_ref, sems):
    rows, lanes = cot_ref.shape[0], out_ref.shape[2]
    copies = []
    for t in range(2):
        for which, ref in ((0, key_ref), (1, value_ref)):
            copies.append((ref.at[t], out_ref.at[2 * t + which]))
    for k in range(cot_ref.shape[1] // lanes):
        copies.append((cot_ref.at[:, pl.ds(k * lanes, lanes)], out_ref.at[4, pl.ds(k * rows, rows)]))
    copies = [pltpu.make_async_copy(a, b, sems.at[n]) for n, (a, b) in enumerate(copies)]
    for copy in copies:
        copy.start()
    for copy in copies:
        copy.wait()


def pack_kernel(fb_ref, own_ref, partner_ref, out_ref, up_ref, down_ref, asked_buf, out_buf, sems):
    shard, shards, zh, y = place()
    readers = plane_readers(zh)
    copies = []
    for rel, kv_ref in ((0, own_ref), (1, partner_ref)):
        asked_rows(fb_ref, asked_buf, rel)
        for p, reader in enumerate(readers):
            for t in range(2):
                second = asked_by(asked_buf, t, reader, BLK) == 2
                for which in range(2):
                    kv = kv_ref.at[2 * t + which]
                    out_buf[2 * p + rel, part(t, which)] = jnp.where(second, kv[BLK:], kv[:BLK])
            if rel == 1 and p % 4 == 3:
                done = pl.ds(2 * p - 6, 8)
                copies.append(pltpu.make_async_copy(out_buf.at[done], out_ref.at[done], sems.at[p // 4]))
                copies[-1].start()
    for k in range(4):
        up_ref[k] = jnp.where(y == lax.axis_size("y") - 1, partner_ref[k], own_ref[k])
        down_ref[k] = jnp.where(y == 0, partner_ref[k], own_ref[k])
    for copy in copies:
        copy.wait()


def stage(fb_ref, t, kv_ref, prev_ref, next_ref, far_ref, kbuf, vbuf):
    shard, shards, zh, y = place()
    for which, buf in ((0, kbuf), (1, vbuf)):
        buf[0:128] = prev_ref[2 * t + which]
        buf[128:256] = kv_ref[2 * t + which]
        buf[256:384] = next_ref[2 * t + which]
    for f in range(fb_ref.shape[1]):
        _, slot = listed(fb_ref, t, shard, shards, zh, f)
        rows = slice(STEP + f * BLK, STEP + (f + 1) * BLK)
        for which, buf in ((0, kbuf), (1, vbuf)):
            buf[rows] = far_ref[slot, part(t, which)]


def biased(fb_ref, t, slopes_ref, q2, kbuf, put):
    shard, shards, zh, y = place()
    cols = q2.shape[0]
    half = cols // 2
    head_col = lax.broadcasted_iota(jnp.int32, (1, cols), 1)
    slope = jnp.where(head_col < half, slopes_ref[0], slopes_ref[1])
    r = lax.broadcasted_iota(jnp.int32, (STEP, cols), 0)
    c = lax.broadcasted_iota(jnp.int32, (STEP, cols), 1)
    c = jnp.where(c < half, c, c - half)
    delta = r - 128 - c
    low = jnp.where(shard > 0, 0, 128)
    high = jnp.where(shard < shards - 1, STEP, 256)
    edge = jnp.where(c < BLK, 0, BLK)
    ok = (r >= jnp.maximum(edge, low)) & (r < jnp.minimum(edge + 320, high))
    scores = dot(kbuf[0:STEP], q2, NT) - slope * jnp.abs(delta).astype(f32)
    scores = jnp.where(ok, scores, masked_value)
    put(0, STEP, scores)
    top = jnp.max(scores, axis=0, keepdims=True)
    far_bias = slope * (-float((BAND + 1) * BLK))
    for lo in range(STEP, kbuf.shape[0], STEP):
        scores = dot(kbuf[lo : lo + STEP], q2, NT)
        parts = []
        for i in range(STEP // BLK):
            there, _ = listed(fb_ref, t, shard, shards, zh, (lo - STEP) // BLK + i)
            row = jnp.where(there, far_bias, masked_value)
            parts.append(scores[i * BLK : (i + 1) * BLK] + row)
        scores = jnp.concatenate(parts, axis=0)
        put(lo, lo + STEP, scores)
        top = jnp.maximum(top, jnp.max(scores, axis=0, keepdims=True))
    return top


def context_grad_kernel(ref0, ref2, ref4, ref6, odd_ref, weight_ref, own_ref, mirrored_ref, buf):
    _, count, rows, lanes = buf.shape
    pieces = [x for k, ref in enumerate((ref0, ref2, ref4, ref6)) for x in (ref, odd_ref.at[k])]
    out = jnp.zeros((2 * count * rows, lanes), f32)
    for k in range(pieces[0].shape[1] // rows):
        here = [piece[which, k * rows : (k + 1) * rows] for which in range(2) for piece in pieces]
        out = out + dot(jnp.concatenate(here, axis=0), weight_ref[:, k * lanes : (k + 1) * lanes], NT)
    out = out.astype(bf16)
    for which in range(2):
        for j in range(count):
            at = (which * count + j) * rows
            buf[which, j] = out[at : at + rows]
    at = lax.axis_index("tp")
    for which, ref in ((0, own_ref), (1, mirrored_ref)):
        for k in range(count):
            ref[k * rows : (k + 1) * rows] = buf[which, lax.bitwise_xor(at, k)]


def attend_kernel(
    fb_ref, slopes_ref, q_ref, kv_ref, prev_ref, next_ref, far_ref, grad_ref, mirrored_ref,
    ctx_ref, rev_ref, gq_ref, own_out, prev_out, next_out, far_out,
    kbuf, vbuf, pbuf, dbuf, far_buf0, far_buf1, sems,
):
    shard, shards, zh, y = place()
    n = 2 * HD
    eye = one_hot(n, lambda r: r)
    total = kbuf.shape[0]
    copies = []
    for t in range(2):
        far_buf = (far_buf0, far_buf1)[t]
        stage(fb_ref, t, kv_ref, prev_ref, next_ref, far_ref, kbuf, vbuf)
        q2 = two_heads(q_ref[t] * HD ** (-0.5))
        g2 = two_heads(flipped(mirrored_ref[...]) if t == 1 else grad_ref[...])
        cols = q2.shape[0]

        def put(lo, hi, scores):
            pbuf[lo:hi] = scores

        top = biased(fb_ref, t, slopes_ref, q2, kbuf, put)
        norm = jnp.zeros((1, cols), f32)
        row_dot = jnp.zeros((1, cols), f32)
        for lo in range(0, total, STEP):
            w = jnp.exp(pbuf[lo : lo + STEP] - top)
            gp = dot(vbuf[lo : lo + STEP], g2, NT)
            pbuf[lo : lo + STEP] = w
            dbuf[lo : lo + STEP] = gp
            norm = norm + jnp.sum(w, axis=0, keepdims=True)
            row_dot = row_dot + jnp.sum(w * gp, axis=0, keepdims=True)
        inv = 1.0 / norm
        row_dot = row_dot * inv
        gq_acc = jnp.zeros((n, cols), f32)
        ctx_acc = jnp.zeros((n, cols), f32)
        for lo in range(0, total, STEP):
            p = pbuf[lo : lo + STEP] * inv
            low = p.astype(bf16)
            ds = (p * (dbuf[lo : lo + STEP] - row_dot)).astype(bf16)
            vt = dot(eye, vbuf[lo : lo + STEP], NT).astype(bf16)
            ctx_acc = ctx_acc + dot(vt, low, NN)
            kt = dot(eye, kbuf[lo : lo + STEP], NT).astype(bf16)
            gq_acc = gq_acc + dot(kt, ds, NN)
            for which, x in ((0, dot(ds, q2, NN)), (1, dot(low, g2, NN))):
                if lo == 0:
                    prev_out[t, which] = x[0:128].astype(bf16)
                    own_out[t, which] = x[128:256]
                    next_out[t, which] = x[256:384].astype(bf16)
                else:
                    x = x.astype(bf16)
                    for i in range(STEP // BLK):
                        there, slot = listed(fb_ref, t, shard, shards, zh, (lo - STEP) // BLK + i)

                        @pl.when(there)
                        def _():
                            far_buf[slot, which * BLK : (which + 1) * BLK] = x[i * BLK : (i + 1) * BLK]

        copies.append(pltpu.make_async_copy(far_buf, far_out.at[:, 2 * t * BLK : 2 * (t + 1) * BLK], sems.at[t]))
        copies[-1].start()
        gq_ref[t] = (pick_heads(gq_acc) * HD ** (-0.5)).astype(bf16)
        ctx = pick_heads(ctx_acc).astype(bf16)
        if t == 1:
            rev_ref[...] = flipped(ctx)
        else:
            ctx_ref[...] = ctx
    for copy in copies:
        copy.wait()


def combine(fb_ref, far_ref, asked_buf, rel, put):
    shard, shards, zh, y = place()
    asked_rows(fb_ref, asked_buf, rel)
    rows = 32
    for t in range(2):
        for which in range(2):
            for lo in range(0, BLK, rows):
                first = jnp.zeros((rows, 2 * HD), f32)
                second = jnp.zeros((rows, 2 * HD), f32)
                at = part(t, which).start + lo
                for p, reader in enumerate(plane_readers(zh)):
                    block = asked_by(asked_buf, t, reader, rows)
                    x = far_ref[2 * p + rel, at : at + rows].astype(f32)
                    first = first + jnp.where(block == 1, x, 0.0)
                    second = second + jnp.where(block == 2, x, 0.0)
                put(t, which, slice(lo, lo + rows), first)
                put(t, which, slice(BLK + lo, BLK + lo + rows), second)


def combine_partner_kernel(fb_ref, prev_ref, next_ref, far_ref, rows_ref, out_ref, asked_buf):
    shard, shards, zh, y = place()
    last = lax.axis_size("y") - 1

    def put(t, which, rows, far):
        far = far + jnp.where(y == 0, prev_ref[t, which, rows].astype(f32), 0.0)
        far = far + jnp.where(y == last, next_ref[t, which, rows].astype(f32), 0.0)
        out_ref[2 * t + which, rows] = far.astype(bf16)

    combine(fb_ref, far_ref, asked_buf, 1, put)
    rows, lanes = rows_ref.shape[0], out_ref.shape[2]
    for k in range(rows_ref.shape[1] // lanes):
        out_ref[4, k * rows : (k + 1) * rows] = rows_ref[:, k * lanes : (k + 1) * lanes]


def combine_own_kernel(fb_ref, own_ref, prev_ref, next_ref, far_ref, out_ref, asked_buf):
    shard, shards, zh, y = place()
    last = lax.axis_size("y") - 1

    def put(t, which, rows, far):
        total = own_ref[t, which, rows] + jnp.where(y == 0, 0.0, prev_ref[t, which, rows].astype(f32))
        total = total + jnp.where(y == last, 0.0, next_ref[t, which, rows].astype(f32))
        out_ref[t, which, rows] = total + far

    combine(fb_ref, far_ref, asked_buf, 0, put)


def finish_kernel(mine_ref, other_ref, residual_ref, rows_ref, gk_ref, gv_ref, mixed_ref):
    for t in range(2):
        for which, ref in ((0, gk_ref), (1, gv_ref)):
            ref[t] = (mine_ref[t, which] + other_ref[2 * t + which].astype(f32)).astype(bf16)
    rows, lanes = residual_ref.shape[0], other_ref.shape[2]
    for k in range(residual_ref.shape[1] // lanes):
        cols = slice(k * lanes, (k + 1) * lanes)
        total = residual_ref[:, cols].astype(f32) + rows_ref[:, cols]
        total = total + other_ref[4, k * rows : (k + 1) * rows].astype(f32)
        mixed_ref[:, cols] = total.astype(bf16)


def project_kernel(ctx_ref, rev_ref, weight_ref, even_ref, odd_ref, buf):
    _, count, rows, _ = buf.shape
    for which, ref in ((0, ctx_ref), (1, rev_ref)):
        for k in range(count):
            buf[which, k] = ref[k * rows : (k + 1) * rows]
    at = lax.axis_index("tp")
    blocks = [buf[which, lax.bitwise_xor(at, j)] for which in range(2) for j in range(count)]
    out = dot(jnp.concatenate(blocks, axis=0), weight_ref[...], NN)
    for which in range(2):
        for j in range(count):
            ref = (even_ref, odd_ref)[j % 2]
            row = (which * count + j) * rows
            ref[j // 2, which] = out[row : row + rows].astype(ref.dtype)


def smem():
    return pl.BlockSpec(memory_space=pltpu.SMEM)


def vmem():
    return pl.BlockSpec(memory_space=pltpu.VMEM)


def hbm():
    return pl.BlockSpec(memory_space=pltpu.HBM)


def shape(dims, dtype=bf16):
    return jax.ShapeDtypeStruct(dims, dtype)


def cost(flops, nbytes, exps=0):
    return pl.CostEstimate(flops=flops, bytes_accessed=nbytes, transcendentals=exps)


def swap(x, bit):
    count = lax.axis_size("tp")
    return lax.ppermute(x, "tp", [(i, i ^ bit) for i in range(count)])


def per_device(
    residual, queries, keys, values, slopes, out_weight, cotangent, far_blocks, far_count
):
    nx, nz, ny = (lax.axis_size(a) for a in SEQ)
    seq_count = nx * nz * ny
    tp_count = lax.axis_size("tp")
    tok_rows, width = queries.shape[1:]
    total_keys = 3 * tok_rows + far_blocks.shape[1] * BLK
    model = out_weight.shape[1]
    cols = 2 * tok_rows
    both = (2, 2, tok_rows, width)
    pieces = (tp_count, tok_rows // tp_count, width)
    slots = (nx * ny, 4 * BLK, width)

    def plane_a2a(x):
        halves = x.reshape(slots[0], 2 * slots[1], width)
        return lax.all_to_all(halves, ("x", "y"), split_axis=0, concat_axis=0, tiled=True).reshape(x.shape)

    def z_swap(x):
        return lax.ppermute(x, "zh", [(i, nz - 1 - i) for i in range(nz)])

    asked = pltpu.VMEM((2, seq_count, 2 * HD), jnp.int32)
    tile = (tok_rows, width)
    loaded = pl.pallas_call(
        load_kernel,
        out_shape=shape((5,) + tile),
        in_specs=[hbm()] * 3,
        out_specs=vmem(),
        scratch_shapes=[pltpu.SemaphoreType.DMA((4 + model // width,))],
        cost_estimate=cost(1_000, 320_000),
        compiler_params=pltpu.CompilerParams(vmem_limit_bytes=LIMIT),
        name="load",
    )(*(pltpu.with_memory_space_constraint(x, pltpu.HBM) for x in (keys, values, cotangent)))
    partner = z_swap(loaded)
    outgoing, to_up, to_down = pl.pallas_call(
        pack_kernel,
        out_shape=(pltpu.HBM((2 * slots[0],) + slots[1:], bf16), shape((4,) + tile), shape((4,) + tile)),
        in_specs=[vmem()] * 3,
        out_specs=(hbm(), vmem(), vmem()),
        scratch_shapes=[
            asked, pltpu.VMEM((2 * slots[0],) + slots[1:], bf16), pltpu.SemaphoreType.DMA((slots[0] // 4,)),
        ],
        cost_estimate=cost(1_000_000, 2_500_000),
        compiler_params=pltpu.CompilerParams(vmem_limit_bytes=LIMIT),
        name="pack",
    )(far_blocks, loaded, partner)
    far = plane_a2a(outgoing)

    turn = [
        ((x * nz + zh) * ny + y, ((nx - 1 - x) * nz + zh) * ny + ny - 1 - y)
        for x in range(nx)
        for zh in range(nz)
        for y in range(ny)
    ]
    both_cot = jnp.stack([loaded[4], lax.ppermute(partner[4], SEQ, turn)])
    same_core = [both_cot] + [swap(both_cot, bit) for bit in (2, 4, 6)]
    other_core = swap(jnp.stack(same_core), 1)

    def flat(x, zh, y):
        return (x * nz + zh) * ny + y

    places = [(x, zh, y) for x in range(nx) for zh in range(nz) for y in range(ny)]
    up, down = [], []
    for x, zh, y in places:
        if y < ny - 1:
            up.append((flat(x, zh, y), flat(x, zh, y + 1)))
        elif zh == nz - 1:
            up.append((flat(x, zh, y), flat(x, zh, 0)))
        elif x < nx - 1:
            up.append((flat(x, zh, y), flat(x + 1, zh, 0)))
        if y > 0:
            down.append((flat(x, zh, y), flat(x, zh, y - 1)))
        elif zh == 0:
            down.append((flat(x, zh, y), flat(x, zh, ny - 1)))
        elif x > 0:
            down.append((flat(x, zh, y), flat(x - 1, zh, ny - 1)))
    from_prev = lax.ppermute(to_up, SEQ, up)
    from_next = lax.ppermute(to_down, SEQ, down)

    grad_context, mirrored = pl.pallas_call(
        context_grad_kernel,
        out_shape=(shape(tile), shape(tile)),
        in_specs=[vmem()] * 6,
        out_specs=(vmem(), vmem()),
        scratch_shapes=[pltpu.VMEM((2,) + pieces, bf16)],
        cost_estimate=cost(68_000_000, 900_000),
        compiler_params=pltpu.CompilerParams(vmem_limit_bytes=LIMIT),
        name="context_grad",
    )(*same_core, other_core, out_weight)

    square = shape((tok_rows, width))
    half = pltpu.VMEM((seq_count, 2 * BLK, width), bf16)
    context_fwd, context_rev, grad_queries, own, before, after, far_grads = pl.pallas_call(
        attend_kernel,
        out_shape=(square, square, shape((2, tok_rows, width)), shape(both, f32), shape(both), shape(both))
        + (pltpu.HBM(outgoing.shape, bf16),),
        in_specs=[smem()] * 2 + [vmem()] * 7,
        out_specs=(vmem(),) * 6 + (hbm(),),
        scratch_shapes=[pltpu.VMEM((total_keys, width), bf16)] * 2
        + [pltpu.VMEM((total_keys, cols), f32)] * 2
        + [half, half, pltpu.SemaphoreType.DMA((2,))],
        cost_estimate=cost(4_000_000_000, 8_000_000, 1_000_000),
        compiler_params=pltpu.CompilerParams(vmem_limit_bytes=LIMIT),
        name="attend",
    )(far_blocks, slopes, queries, loaded, from_prev, from_next, far, grad_context, mirrored)
    returned = plane_a2a(far_grads)
    from_prev_grad = lax.ppermute(after, SEQ, [(b, a) for a, b in down])
    from_next_grad = lax.ppermute(before, SEQ, [(b, a) for a, b in up])
    rows = (tp_count // 2, 2, tok_rows // tp_count, model)
    even, odd = pl.pallas_call(
        project_kernel,
        out_shape=(shape(rows, f32), shape(rows)),
        in_specs=[vmem()] * 3,
        out_specs=(vmem(),) * 2,
        scratch_shapes=[pltpu.VMEM((2,) + pieces, bf16)],
        cost_estimate=cost(68_000_000, 1_500_000),
        compiler_params=pltpu.CompilerParams(vmem_limit_bytes=LIMIT),
        name="project",
    )(context_fwd, context_rev, out_weight)
    held = even + swap(odd, 1).astype(f32)
    parts = [swap(held[k].astype(bf16), 2 * k) for k in range(1, tp_count // 2)]
    summed = held[0] + sum(here.astype(f32) for here in parts)
    turned = lax.ppermute(summed[1].astype(bf16), SEQ, turn)

    other = pl.pallas_call(
        combine_partner_kernel,
        out_shape=shape((5,) + tile),
        in_specs=[vmem()] * 5,
        out_specs=vmem(),
        scratch_shapes=[asked],
        cost_estimate=cost(2_000_000, 1_500_000),
        compiler_params=pltpu.CompilerParams(vmem_limit_bytes=LIMIT),
        name="combine_partner",
    )(far_blocks, from_prev_grad, from_next_grad, returned, turned)
    mine = pl.pallas_call(
        combine_own_kernel,
        out_shape=shape(both, f32),
        in_specs=[vmem()] * 5,
        out_specs=vmem(),
        scratch_shapes=[asked],
        cost_estimate=cost(2_000_000, 1_500_000),
        compiler_params=pltpu.CompilerParams(vmem_limit_bytes=LIMIT),
        name="combine_own",
    )(far_blocks, own, from_prev_grad, from_next_grad, returned)
    grad_keys, grad_values, mixed = pl.pallas_call(
        finish_kernel,
        out_shape=(shape((2,) + tile),) * 2 + (shape(residual.shape),),
        in_specs=[vmem()] * 4,
        out_specs=(vmem(),) * 3,
        cost_estimate=cost(200_000, 900_000),
        compiler_params=pltpu.CompilerParams(vmem_limit_bytes=LIMIT),
        name="finish",
    )(mine, z_swap(other), residual, summed[0])
    return (mixed, grad_queries, grad_keys, grad_values)


def solution(mesh):
    split = jax.sharding.Mesh(mesh.devices.reshape(4, 2, 4, -1), SEQ + ("tp",))
    rows = P(SEQ + ("tp",), None)
    strands = P(None, SEQ, "tp")
    return jax.shard_map(
        per_device,
        mesh=split,
        in_specs=(rows, strands, strands, strands, P("tp"), P("tp", None), rows, P(), P()),
        out_specs=(rows, strands, strands, strands),
        check_vma=False,
    )
```

time: 115 us -> 131 us (1.14); the launches traced: 115 us -> 129 us
  waiting for transfers between devices: 20.9 us -> 56.7 us
  starting transfers between devices: 74.1 us -> 55.2 us
  local copies, waits for them, and re-layouts: 3.15 us -> 0.84 us
    ppermute x2, waiting for transfers between devices: 2.82 us -> 23.4 us  [the longest x1 23.4 us: per_device(): both_cot = jnp.stack([loaded[4], lax.ppermute(partner[4], SEQ, turn)])]
    all_to_all x4 -> x2, starting transfers between devices: 27.5 us -> 12.8 us  [plane_a2a(): lax.all_to_all(halves, ('x', 'y'), split_axis=0, concat_axis=0, tiled=True)]
    ppermute x2, starting transfers between devices: 17.4 us -> 6.45 us  [the longest x1 3.69 us: per_device(): turned = lax.ppermute(summed[1].astype(bf16), SEQ, turn)]
    ppermute x1, waiting for transfers between devices: 0.01 us -> 7.62 us  [per_device(): from_prev_grad = lax.ppermute(after, SEQ, [(b, a) for a, b in down])]
    ppermute x2, starting transfers between devices: 7.72 us -> 13.9 us  [z_swap(): return lax.ppermute(x, 'zh', [(i, nz - 1 - i) for i in range(nz)])]
    ppermute x1, waiting for transfers between devices: 0.01 us -> 5.33 us  [per_device(): from_next = lax.ppermute(to_down, SEQ, down)]
    ppermute x1, starting transfers between devices: 4.57 us -> 1.99 us  [per_device(): from_prev_grad = lax.ppermute(after, SEQ, [(b, a) for a, b in down])]
    ppermute x1, waiting for transfers between devices: 3 us -> 5.56 us  [per_device(): from_next_grad = lax.ppermute(before, SEQ, [(b, a) for a, b in up])]
  transfers between devices with their start and end apart: 20 -> 18, of which waited for: 8 -> 12; matrix products, arithmetic and copies ran while one was open for 1% -> 1% of each run, Pallas kernels for 2% -> 1%
where the time goes in v6:
time: 131 us; the launch traced here: 129 us
  waiting for transfers between devices  56.7 us (43%)
  starting transfers between devices  55.2 us (42%)
  Pallas kernels  15.2 us (12%)
    ppermute x1, waiting for transfers between devices, per_device(): both_cot = jnp.stack([loaded[4], lax.ppermute(partner[4], SEQ, turn)])  23.4 us
    ppermute x2, starting transfers between devices, z_swap(): return lax.ppermute(x, 'zh', [(i, nz - 1 - i) for i in range(nz)])  13.9 us
    all_to_all x2, starting transfers between devices, plane_a2a(): lax.all_to_all(halves, ('x', 'y'), split_axis=0, concat_axis=0, tiled=True)  12.8 us
    pallas_call x1, Pallas kernels, per_device(): pl.pallas_call(attend_kernel, out_shape=(square, square, shape((2, tok_ro...  10.2 us
    ppermute x8, starting transfers between devices, swap(): return lax.ppermute(x, 'tp', [(i, i ^ bit) for i in range(count)])  9.98 us
    ppermute x1, waiting for transfers between devices, per_device(): from_prev_grad = lax.ppermute(after, SEQ, [(b, a) for a, b in down])  7.62 us
    ppermute x2, waiting for transfers between devices, z_swap(): return lax.ppermute(x, 'zh', [(i, nz - 1 - i) for i in range(nz)])  7.51 us
    ppermute x8, waiting for transfers between devices, swap(): return lax.ppermute(x, 'tp', [(i, i ^ bit) for i in range(count)])  6.09 us
  transfers between devices with their start and end apart: 18, of which 12 were waited for; matrix products, arithmetic and copies ran while one was open for 1% of the time, Pallas kernels for 1%

profile of v6, /device:TPU:24, one launch (start us, length us, event | category | flops | bytes accessed | tf_op | source)
XLA Modules:
  0.0 128.9 jit_solution(12420030915376493383)
XLA Ops:
  0.6 0.9 load.1.own_ref.kv_ref
  1.6 7.3 %collective-permute-start = (bf16[5,128,128]{2,1,0:T(8,128)(2,1)S(1)}, bf16[5,128,128]{2,1,0:T(8,128)(2,1)S(1)}, u32[]{:S(2)}, u32[]{:S(2)}) collective-permute-start(bf16[5,128,128]{2,1,0:T(8,128)(2,1)S(1)} %load.1.own_ref.kv_ref), channel_id=1, source_target_pairs={{0,32},{32,0},{1,33},{33,1},{2,34},{34,2},{3,35},{35,3},{4,36},{36... | collective-permute-start | bytes 491528 | tf_op jit(solution)/shard_map/ppermute | solution.py:388
  8.8 0.8 copy.14.fb_ref
  9.6 3.5 %collective-permute-done.partner_ref = bf16[5,128,128]{2,1,0:T(8,128)(2,1)S(1)} collective-permute-done((bf16[5,128,128]{2,1,0:T(8,128)(2,1)S(1)}, bf16[5,128,128]{2,1,0:T(8,128)(2,1)S(1)}, u32[]{:S(2)}, u32[]{:S(2)}) %collective-permute-start) | collective-permute-done | bytes 163872 | tf_op jit(solution)/shard_map/ppermute | solution.py:388
  13.2 1.7 %pack.1 = (bf16[32,256,128]{2,1,0:T(8,128)(2,1)}, bf16[4,128,128]{2,1,0:T(8,128)(2,1)S(1)}, bf16[4,128,128]{2,1,0:T(8,128)(2,1)S(1)}) custom-call(s32[32,24]{1,0:T(8,128)S(1)} %copy.14.fb_ref, bf16[5,128,128]{2,1,0:T(8,128)(2,1)S(1)} %load.1.own_ref.kv_ref, bf16[5,128,128]{2,1,0:T(8,128)(2,1)S(1)} %collective-permute-done.partner_ref), custom_call_target="tpu_custom_call" | custom-call | flops 1000000 | bytes 2500000 | tf_op jit(solution)/shard_map/pack/pallas_call | solution.py:403
  14.9 7.3 %all-to-all-start = ((bf16[16,512,128]{2,1,0:T(8,128)(2,1)}), bf16[16,512,128]{2,1,0:T(8,128)(2,1)S(1)}, u32[]{:S(2)}, u32[]{:S(2)}) async-start(bf16[16,512,128]{2,1,0:T(8,128)(2,1)} %bitcast.33), calls=%async_computation | async-start | bytes 4194304 | tf_op jit(solution)/shard_map/all_to_all | solution.py:385
  22.2 2.8 %collective-permute-start.3 = (bf16[128,128]{1,0:T(8,128)(2,1)S(1)}, bf16[128,128]{1,0:T(8,128)(2,1)S(1)}, u32[]{:S(2)}, u32[]{:S(2)}) collective-permute-start(bf16[128,128]{1,0:T(8,128)(2,1)S(1)} %slice_bitcast_fusion.5), channel_id=1, source_target_pairs={{0,216},{8,208},{16,200},{24,192},{32,248},{40,240},{48,232},{56,2... | collective-permute-start | bytes 98312 | tf_op jit(solution)/shard_map/ppermute | solution.py:423
  25.0 23.4 %collective-permute-done.3 = bf16[128,128]{1,0:T(8,128)(2,1)S(1)} collective-permute-done((bf16[128,128]{1,0:T(8,128)(2,1)S(1)}, bf16[128,128]{1,0:T(8,128)(2,1)S(1)}, u32[]{:S(2)}, u32[]{:S(2)}) %collective-permute-start.3) | collective-permute-done | bytes 32800 | tf_op jit(solution)/shard_map/ppermute | solution.py:423
  48.4 0.8 collective-permute-start.6
  49.2 4.9 %collective-permute-start.5 = (bf16[2,128,128]{2,1,0:T(8,128)(2,1)S(1)}, bf16[2,128,128]{2,1,0:T(8,128)(2,1)S(1)}, u32[]{:S(2)}, u32[]{:S(2)}) collective-permute-start(bf16[2,128,128]{2,1,0:T(8,128)(2,1)S(1)} %get-tuple-element.44.ref0), channel_id=1, source_target_pairs={{0,4},{1,5},{2,6},{3,7},{4,0},{5,1},{6,2},{7,3},{8,12},{9,13},{10,... | collective-permute-start | bytes 196616 | tf_op jit(solution)/shard_map/ppermute | solution.py:366
  54.6 2.5 %collective-permute-done.5.ref4 = bf16[2,128,128]{2,1,0:T(8,128)(2,1)S(1)} collective-permute-done((bf16[2,128,128]{2,1,0:T(8,128)(2,1)S(1)}, bf16[2,128,128]{2,1,0:T(8,128)(2,1)S(1)}, u32[]{:S(2)}, u32[]{:S(2)}) %collective-permute-start.5) | collective-permute-done | bytes 65568 | tf_op jit(solution)/shard_map/ppermute | solution.py:366
  57.1 1.3 %collective-permute-done.4.ref2 = bf16[2,128,128]{2,1,0:T(8,128)(2,1)S(1)} collective-permute-done((bf16[2,128,128]{2,1,0:T(8,128)(2,1)S(1)}, bf16[2,128,128]{2,1,0:T(8,128)(2,1)S(1)}, u32[]{:S(2)}, u32[]{:S(2)}) %collective-permute-start.4) | collective-permute-done | bytes 65568 | tf_op jit(solution)/shard_map/ppermute | solution.py:366
  58.5 4.4 %collective-permute-start.1 = (bf16[4,128,128]{2,1,0:T(8,128)(2,1)S(1)}, bf16[4,128,128]{2,1,0:T(8,128)(2,1)S(1)}, u32[]{:S(2)}, u32[]{:S(2)}) collective-permute-start(bf16[4,128,128]{2,1,0:T(8,128)(2,1)S(1)} %get-tuple-element.21), channel_id=1, source_target_pairs={{0,8},{8,16},{16,24},{24,64},{32,40},{40,48},{48,56},{56,32},{64,7... | collective-permute-start | bytes 393224 | tf_op jit(solution)/shard_map/ppermute | solution.py:445
  62.9 1.9 %collective-permute-start.2 = (bf16[4,128,128]{2,1,0:T(8,128)(2,1)S(1)}, bf16[4,128,128]{2,1,0:T(8,128)(2,1)S(1)}, u32[]{:S(2)}, u32[]{:S(2)}) collective-permute-start(bf16[4,128,128]{2,1,0:T(8,128)(2,1)S(1)} %get-tuple-element.22), channel_id=1, source_target_pairs={{0,24},{8,0},{16,8},{24,16},{40,32},{48,40},{56,48},{64,88},{72,64... | collective-permute-start | bytes 393224 | tf_op jit(solution)/shard_map/ppermute | solution.py:446
  65.2 1.1 collective-permute-done.1.prev_ref
  66.3 5.3 %collective-permute-done.2.next_ref = bf16[4,128,128]{2,1,0:T(8,128)(2,1)S(1)} collective-permute-done((bf16[4,128,128]{2,1,0:T(8,128)(2,1)S(1)}, bf16[4,128,128]{2,1,0:T(8,128)(2,1)S(1)}, u32[]{:S(2)}, u32[]{:S(2)}) %collective-permute-start.2) | collective-permute-done | bytes 131104 | tf_op jit(solution)/shard_map/ppermute | solution.py:446
  71.7 10.2 %attend.1 = (bf16[128,128]{1,0:T(8,128)(2,1)S(1)}, bf16[128,128]{1,0:T(8,128)(2,1)S(1)}, bf16[2,128,128]{2,1,0:T(8,128)(2,1)}, f32[2,2,128,128]{3,2,1,0:T(8,128)...) custom-call(s32[32,24]{1,0:T(8,128)S(1)} %copy.14.fb_ref, ...), custom_call_target="tpu_custom_call" | custom-call | flops 4000000000 | bytes 8000000 | tf_op jit(solution)/shard_map/attend/pallas_call | solution.py:461
  81.9 5.5 %all-to-all-start.1 = ((bf16[16,512,128]{2,1,0:T(8,128)(2,1)}), bf16[16,512,128]{2,1,0:T(8,128)(2,1)S(1)}, u32[]{:S(2)}, u32[]{:S(2)}) async-start(bf16[16,512,128]{2,1,0:T(8,128)(2,1)} %bitcast.32), calls=%async_computation.1 | async-start | bytes 4194304 | tf_op jit(solution)/shard_map/all_to_all | solution.py:385
  87.9 1.5 %collective-permute-done.10 = bf16[4,2,16,1024]{3,2,1,0:T(8,128)(2,1)S(1)} collective-permute-done((bf16[4,2,16,1024]{3,2,1,0:T(8,128)(2,1)S(1)}, bf16[4,2,16,1024]{3,2,1,0:T(8,128)(2,1)S(1)}, u32[]{:S(2)}, u32[]{:S(2)}) %collective-permute-start.10) | collective-permute-done | bytes 262176 | tf_op jit(solution)/shard_map/ppermute | solution.py:366
  89.5 1.3 collective-permute-start.11
  90.8 2.1 %collective-permute-start.13 = (bf16[2,16,1024]{2,1,0:T(8,128)(2,1)S(1)}, bf16[2,16,1024]{2,1,0:T(8,128)(2,1)S(1)}, u32[]{:S(2)}, u32[]{:S(2)}) collective-permute-start(bf16[2,16,1024]{2,1,0:T(8,128)(2,1)S(1)} %get-tuple-element.41), channel_id=1, source_target_pairs={{0,6},{1,7},{2,4},{3,5},{4,2},{5,3},{6,0},{7,1},{8,14},{9,15},{10,... | collective-permute-start | bytes 196616 | tf_op jit(solution)/shard_map/ppermute | solution.py:366
  93.1 2.0 %collective-permute-start.8 = (bf16[2,2,128,128]{3,2,1,0:T(8,128)(2,1)S(1)}, bf16[2,2,128,128]{3,2,1,0:T(8,128)(2,1)S(1)}, u32[]{:S(2)}, u32[]{:S(2)}) collective-permute-start(bf16[2,2,128,128]{3,2,1,0:T(8,128)(2,1)S(1)} %get-tuple-element.27), channel_id=1, source_target_pairs={{24,0},{0,8},{8,16},{16,24},{32,40},{40,48},{48,56},{88,64},{64,72... | collective-permute-start | bytes 393224 | tf_op jit(solution)/shard_map/ppermute | solution.py:475
  95.1 3.8 %collective-permute-start.9 = (bf16[2,2,128,128]{3,2,1,0:T(8,128)(2,1)S(1)}, bf16[2,2,128,128]{3,2,1,0:T(8,128)(2,1)S(1)}, u32[]{:S(2)}, u32[]{:S(2)}) collective-permute-start(bf16[2,2,128,128]{3,2,1,0:T(8,128)(2,1)S(1)} %get-tuple-element.28), channel_id=1, source_target_pairs={{8,0},{16,8},{24,16},{64,24},{40,32},{48,40},{56,48},{32,56},{72,6... | collective-permute-start | bytes 393224 | tf_op jit(solution)/shard_map/ppermute | solution.py:476
  99.0 0.6 collective-permute-done.12
  99.6 3.7 %collective-permute-start.14 = (bf16[16,1024]{1,0:T(8,128)(2,1)S(1)}, bf16[16,1024]{1,0:T(8,128)(2,1)S(1)}, u32[]{:S(2)}, u32[]{:S(2)}) collective-permute-start(bf16[16,1024]{1,0:T(8,128)(2,1)S(1)} %fusion.1), channel_id=1, source_target_pairs={{0,216},{8,208},{16,200},{24,192},{32,248},{40,240},{48,232},{56,2... | collective-permute-start | bytes 98312 | tf_op jit(solution)/shard_map/ppermute | solution.py:491
  103.3 7.6 %collective-permute-done.8.prev_ref = bf16[2,2,128,128]{3,2,1,0:T(8,128)(2,1)S(1)} collective-permute-done((bf16[2,2,128,128]{3,2,1,0:T(8,128)(2,1)S(1)}, bf16[2,2,128,128]{3,2,1,0:T(8,128)(2,1)S(1)}, u32[]{:S(2)}, u32[]{:S(2)}) %collective-permute-start.8) | collective-permute-done | bytes 131104 | tf_op jit(solution)/shard_map/ppermute | solution.py:475
  111.0 5.6 %collective-permute-done.9.next_ref = bf16[2,2,128,128]{3,2,1,0:T(8,128)(2,1)S(1)} collective-permute-done((bf16[2,2,128,128]{3,2,1,0:T(8,128)(2,1)S(1)}, bf16[2,2,128,128]{3,2,1,0:T(8,128)(2,1)S(1)}, u32[]{:S(2)}, u32[]{:S(2)}) %collective-permute-start.9) | collective-permute-done | bytes 131104 | tf_op jit(solution)/shard_map/ppermute | solution.py:476
  116.5 0.5 combine_partner.1
  117.1 6.6 %collective-permute-start.15 = (bf16[5,128,128]{2,1,0:T(8,128)(2,1)S(1)}, bf16[5,128,128]{2,1,0:T(8,128)(2,1)S(1)}, u32[]{:S(2)}, u32[]{:S(2)}) collective-permute-start(bf16[5,128,128]{2,1,0:T(8,128)(2,1)S(1)} %combine_partner.1), channel_id=1, source_target_pairs={{0,32},{32,0},{1,33},{33,1},{2,34},{34,2},{3,35},{35,3},{4,36},{36... | collective-permute-start | bytes 491528 | tf_op jit(solution)/shard_map/ppermute | solution.py:388
  123.7 0.5 combine_own.1.mine_ref
  124.2 4.0 %collective-permute-done.15.other_ref = bf16[5,128,128]{2,1,0:T(8,128)(2,1)S(1)} collective-permute-done((bf16[5,128,128]{2,1,0:T(8,128)(2,1)S(1)}, bf16[5,128,128]{2,1,0:T(8,128)(2,1)S(1)}, u32[]{:S(2)}, u32[]{:S(2)}) %collective-permute-start.15) | collective-permute-done | bytes 163872 | tf_op jit(solution)/shard_map/ppermute | solution.py:388
  128.2 0.7 finish.1
  (30 shorter events, 1.8 us)
Async XLA Ops:
  1.6 11.6 %collective-permute-start = (bf16[5,128,128]{2,1,0:T(8,128)(2,1)S(1)}, bf16[5,128,128]{2,1,0:T(8,128)(2,1)S(1)}, u32[]{:S(2)}, u32[]{:S(2)}) collective-permute-start(bf16[5,128,128]{2,1,0:T(8,128)(2,1)S(1)} %load.1.own_ref.kv_ref), channel_id=1, source_target_pairs={{0,32},{32,0},{1,33},{33,1},{2,34},{34,2},{3,35},{35,3},{4,36},{36... | collective-permute-start | bytes 491528 | tf_op jit(solution)/shard_map/ppermute | solution.py:388
  14.9 50.0 %copy-start = (bf16[128,1024]{1,0:T(8,128)(2,1)S(1)}, bf16[128,1024]{1,0:T(8,128)(2,1)}, u32[]{:S(2)}) copy-start(bf16[128,1024]{1,0:T(8,128)(2,1)} %weight_ref.3) | copy-start | bytes 786436
  14.9 56.8 %copy-start.2 = (bf16[2,128,128]{2,1,0:T(8,128)(2,1)S(1)}, bf16[2,128,128]{2,1,0:T(8,128)(2,1)}, u32[]{:S(2)}) copy-start(bf16[2,128,128]{2,1,0:T(8,128)(2,1)} %q_ref.1) | copy-start | bytes 196612
  14.9 56.7 %copy-start.3 = (f32[2]{0:T(128)S(1)}, f32[2]{0:T(128)}, u32[]{:S(2)}) copy-start(f32[2]{0:T(128)} %slopes_ref.1) | copy-start | bytes 28
  14.9 56.7 %all-to-all-start = ((bf16[16,512,128]{2,1,0:T(8,128)(2,1)}), bf16[16,512,128]{2,1,0:T(8,128)(2,1)S(1)}, u32[]{:S(2)}, u32[]{:S(2)}) async-start(bf16[16,512,128]{2,1,0:T(8,128)(2,1)} %bitcast.33), calls=%async_computation | async-start | bytes 4194304 | tf_op jit(solution)/shard_map/all_to_all | solution.py:385
  22.2 26.2 %collective-permute-start.3 = (bf16[128,128]{1,0:T(8,128)(2,1)S(1)}, bf16[128,128]{1,0:T(8,128)(2,1)S(1)}, u32[]{:S(2)}, u32[]{:S(2)}) collective-permute-start(bf16[128,128]{1,0:T(8,128)(2,1)S(1)} %slice_bitcast_fusion.5), channel_id=1, source_target_pairs={{0,216},{8,208},{16,200},{24,192},{32,248},{40,240},{48,232},{56,2... | collective-permute-start | bytes 98312 | tf_op jit(solution)/shard_map/ppermute | solution.py:423
  48.4 6.2 %collective-permute-start.6 = (bf16[2,128,128]{2,1,0:T(8,128)(2,1)S(1)}, bf16[2,128,128]{2,1,0:T(8,128)(2,1)S(1)}, u32[]{:S(2)}, u32[]{:S(2)}) collective-permute-start(bf16[2,128,128]{2,1,0:T(8,128)(2,1)S(1)} %get-tuple-element.44.ref0), channel_id=1, source_target_pairs={{0,6},{1,7},{2,4},{3,5},{4,2},{5,3},{6,0},{7,1},{8,14},{9,15},{10,... | collective-permute-start | bytes 196616 | tf_op jit(solution)/shard_map/ppermute | solution.py:366
  49.2 7.9 %collective-permute-start.5 = (bf16[2,128,128]{2,1,0:T(8,128)(2,1)S(1)}, bf16[2,128,128]{2,1,0:T(8,128)(2,1)S(1)}, u32[]{:S(2)}, u32[]{:S(2)}) collective-permute-start(bf16[2,128,128]{2,1,0:T(8,128)(2,1)S(1)} %get-tuple-element.44.ref0), channel_id=1, source_target_pairs={{0,4},{1,5},{2,6},{3,7},{4,0},{5,1},{6,2},{7,3},{8,12},{9,13},{10,... | collective-permute-start | bytes 196616 | tf_op jit(solution)/shard_map/ppermute | solution.py:366
  54.1 4.3 %collective-permute-start.4 = (bf16[2,128,128]{2,1,0:T(8,128)(2,1)S(1)}, bf16[2,128,128]{2,1,0:T(8,128)(2,1)S(1)}, u32[]{:S(2)}, u32[]{:S(2)}) collective-permute-start(bf16[2,128,128]{2,1,0:T(8,128)(2,1)S(1)} %get-tuple-element.44.ref0), channel_id=1, source_target_pairs={{0,2},{1,3},{2,0},{3,1},{4,6},{5,7},{6,4},{7,5},{8,10},{9,11},{10,... | collective-permute-start | bytes 196616 | tf_op jit(solution)/shard_map/ppermute | solution.py:366
  58.4 6.4 %collective-permute-start.7 = (bf16[4,2,128,128]{3,2,1,0:T(8,128)(2,1)S(1)}, bf16[4,2,128,128]{3,2,1,0:T(8,128)(2,1)S(1)}, u32[]{:S(2)}, u32[]{:S(2)}) collective-permute-start(bf16[4,2,128,128]{3,2,1,0:T(8,128)(2,1)S(1)} %pad_maximum_fusion), channel_id=1, source_target_pairs={{0,1},{1,0},{2,3},{3,2},{4,5},{5,4},{6,7},{7,6},{8,9},{9,8},{10,11... | collective-permute-start | bytes 786440 | tf_op jit(solution)/shard_map/ppermute | solution.py:366
  58.5 7.8 %collective-permute-start.1 = (bf16[4,128,128]{2,1,0:T(8,128)(2,1)S(1)}, bf16[4,128,128]{2,1,0:T(8,128)(2,1)S(1)}, u32[]{:S(2)}, u32[]{:S(2)}) collective-permute-start(bf16[4,128,128]{2,1,0:T(8,128)(2,1)S(1)} %get-tuple-element.21), channel_id=1, source_target_pairs={{0,8},{8,16},{16,24},{24,64},{32,40},{40,48},{48,56},{56,32},{64,7... | collective-permute-start | bytes 393224 | tf_op jit(solution)/shard_map/ppermute | solution.py:445
  62.9 8.7 %collective-permute-start.2 = (bf16[4,128,128]{2,1,0:T(8,128)(2,1)S(1)}, bf16[4,128,128]{2,1,0:T(8,128)(2,1)S(1)}, u32[]{:S(2)}, u32[]{:S(2)}) collective-permute-start(bf16[4,128,128]{2,1,0:T(8,128)(2,1)S(1)} %get-tuple-element.22), channel_id=1, source_target_pairs={{0,24},{8,0},{16,8},{24,16},{40,32},{48,40},{56,48},{64,88},{72,64... | collective-permute-start | bytes 393224 | tf_op jit(solution)/shard_map/ppermute | solution.py:446
  81.9 34.7 %all-to-all-start.1 = ((bf16[16,512,128]{2,1,0:T(8,128)(2,1)}), bf16[16,512,128]{2,1,0:T(8,128)(2,1)S(1)}, u32[]{:S(2)}, u32[]{:S(2)}) async-start(bf16[16,512,128]{2,1,0:T(8,128)(2,1)} %bitcast.32), calls=%async_computation.1 | async-start | bytes 4194304 | tf_op jit(solution)/shard_map/all_to_all | solution.py:385
  87.6 1.8 %collective-permute-start.10 = (bf16[4,2,16,1024]{3,2,1,0:T(8,128)(2,1)S(1)}, bf16[4,2,16,1024]{3,2,1,0:T(8,128)(2,1)S(1)}, u32[]{:S(2)}, u32[]{:S(2)}) collective-permute-start(bf16[4,2,16,1024]{3,2,1,0:T(8,128)(2,1)S(1)} %get-tuple-element.33), channel_id=1, source_target_pairs={{0,1},{1,0},{2,3},{3,2},{4,5},{5,4},{6,7},{7,6},{8,9},{9,8},{10,11... | collective-permute-start | bytes 786440 | tf_op jit(solution)/shard_map/ppermute | solution.py:366
  89.5 9.5 %collective-permute-start.11 = (bf16[2,16,1024]{2,1,0:T(8,128)(2,1)S(1)}, bf16[2,16,1024]{2,1,0:T(8,128)(2,1)S(1)}, u32[]{:S(2)}, u32[]{:S(2)}) collective-permute-start(bf16[2,16,1024]{2,1,0:T(8,128)(2,1)S(1)} %get-tuple-element.40), channel_id=1, source_target_pairs={{0,2},{1,3},{2,0},{3,1},{4,6},{5,7},{6,4},{7,5},{8,10},{9,11},{10,... | collective-permute-start | bytes 196616 | tf_op jit(solution)/shard_map/ppermute | solution.py:366
  90.8 8.2 %collective-permute-start.13 = (bf16[2,16,1024]{2,1,0:T(8,128)(2,1)S(1)}, bf16[2,16,1024]{2,1,0:T(8,128)(2,1)S(1)}, u32[]{:S(2)}, u32[]{:S(2)}) collective-permute-start(bf16[2,16,1024]{2,1,0:T(8,128)(2,1)S(1)} %get-tuple-element.41), channel_id=1, source_target_pairs={{0,6},{1,7},{2,4},{3,5},{4,2},{5,3},{6,0},{7,1},{8,14},{9,15},{10,... | collective-permute-start | bytes 196616 | tf_op jit(solution)/shard_map/ppermute | solution.py:366
  92.9 6.7 %collective-permute-start.12 = (bf16[2,16,1024]{2,1,0:T(8,128)(2,1)S(1)}, bf16[2,16,1024]{2,1,0:T(8,128)(2,1)S(1)}, u32[]{:S(2)}, u32[]{:S(2)}) collective-permute-start(bf16[2,16,1024]{2,1,0:T(8,128)(2,1)S(1)} %get-tuple-element.42), channel_id=1, source_target_pairs={{0,4},{1,5},{2,6},{3,7},{4,0},{5,1},{6,2},{7,3},{8,12},{9,13},{10,... | collective-permute-start | bytes 196616 | tf_op jit(solution)/shard_map/ppermute | solution.py:366
  93.1 17.8 %collective-permute-start.8 = (bf16[2,2,128,128]{3,2,1,0:T(8,128)(2,1)S(1)}, bf16[2,2,128,128]{3,2,1,0:T(8,128)(2,1)S(1)}, u32[]{:S(2)}, u32[]{:S(2)}) collective-permute-start(bf16[2,2,128,128]{3,2,1,0:T(8,128)(2,1)S(1)} %get-tuple-element.27), channel_id=1, source_target_pairs={{24,0},{0,8},{8,16},{16,24},{32,40},{40,48},{48,56},{88,64},{64,72... | collective-permute-start | bytes 393224 | tf_op jit(solution)/shard_map/ppermute | solution.py:475
  95.1 21.4 %collective-permute-start.9 = (bf16[2,2,128,128]{3,2,1,0:T(8,128)(2,1)S(1)}, bf16[2,2,128,128]{3,2,1,0:T(8,128)(2,1)S(1)}, u32[]{:S(2)}, u32[]{:S(2)}) collective-permute-start(bf16[2,2,128,128]{3,2,1,0:T(8,128)(2,1)S(1)} %get-tuple-element.28), channel_id=1, source_target_pairs={{8,0},{16,8},{24,16},{64,24},{40,32},{48,40},{56,48},{32,56},{72,6... | collective-permute-start | bytes 393224 | tf_op jit(solution)/shard_map/ppermute | solution.py:476
  99.6 16.9 %collective-permute-start.14 = (bf16[16,1024]{1,0:T(8,128)(2,1)S(1)}, bf16[16,1024]{1,0:T(8,128)(2,1)S(1)}, u32[]{:S(2)}, u32[]{:S(2)}) collective-permute-start(bf16[16,1024]{1,0:T(8,128)(2,1)S(1)} %fusion.1), channel_id=1, source_target_pairs={{0,216},{8,208},{16,200},{24,192},{32,248},{40,240},{48,232},{56,2... | collective-permute-start | bytes 98312 | tf_op jit(solution)/shard_map/ppermute | solution.py:491
  117.1 11.2 %copy-start.1 = (bf16[16,1024]{1,0:T(8,128)(2,1)S(1)}, bf16[16,1024]{1,0:T(8,128)(2,1)}, u32[]{:S(2)}) copy-start(bf16[16,1024]{1,0:T(8,128)(2,1)} %residual_ref.1) | copy-start | bytes 98308
  117.1 11.1 %collective-permute-start.15 = (bf16[5,128,128]{2,1,0:T(8,128)(2,1)S(1)}, bf16[5,128,128]{2,1,0:T(8,128)(2,1)S(1)}, u32[]{:S(2)}, u32[]{:S(2)}) collective-permute-start(bf16[5,128,128]{2,1,0:T(8,128)(2,1)S(1)} %combine_partner.1), channel_id=1, source_target_pairs={{0,32},{32,0},{1,33},{33,1},{2,34},{34,2},{3,35},{35,3},{4,36},{36... | collective-permute-start | bytes 491528 | tf_op jit(solution)/shard_map/ppermute | solution.py:388

commit v7 on v5

--- a/solution.py
+++ b/solution.py
@@ -9,6 +9,7 @@
 BLK = 64
 BAND = 2
 STEP = 384
+FAR_STEP = 256
 LIMIT = 24 << 20
 
 masked_value = -1e30
@@ -17,6 +18,7 @@
 
 NT = (((1,), (1,)), ((), ()))
 NN = (((1,), (0,)), ((), ()))
+TN = (((0,), (0,)), ((), ()))
 
 
 def dot(a, b, dims):
@@ -115,9 +117,16 @@
     return copies
 
 
-def pack_own_kernel(fb_ref, key_ref, value_ref, out_ref, kv_ref, asked_buf, out_buf, sems):
-    kv_ref[:, 0] = key_ref[...]
-    kv_ref[:, 1] = value_ref[...]
+def pack_own_kernel(fb_ref, key_ref, value_ref, out_ref, kv_ref, asked_buf, out_buf, sems, in_sems):
+    loads = [
+        pltpu.make_async_copy(ref.at[t], kv_ref.at[t, which], in_sems.at[t, which])
+        for t in range(2)
+        for which, ref in ((0, key_ref), (1, value_ref))
+    ]
+    for copy in loads:
+        copy.start()
+    for copy in loads:
+        copy.wait()
     for copy in pack(fb_ref, kv_ref, out_ref, asked_buf, out_buf, sems, 0):
         copy.wait()
 
@@ -166,15 +175,15 @@
     put(0, STEP, scores)
     top = jnp.max(scores, axis=0, keepdims=True)
     far_bias = slope * (-float((BAND + 1) * BLK))
-    for lo in range(STEP, kbuf.shape[0], STEP):
-        scores = dot(kbuf[lo : lo + STEP], q2, NT)
+    for lo in range(STEP, kbuf.shape[0], FAR_STEP):
+        scores = dot(kbuf[lo : lo + FAR_STEP], q2, NT)
         parts = []
-        for i in range(STEP // BLK):
+        for i in range(FAR_STEP // BLK):
             there, _ = listed(fb_ref, t, shard, shards, zh, (lo - STEP) // BLK + i)
             row = jnp.where(there, far_bias, masked_value)
             parts.append(scores[i * BLK : (i + 1) * BLK] + row)
         scores = jnp.concatenate(parts, axis=0)
-        put(lo, lo + STEP, scores)
+        put(lo, lo + FAR_STEP, scores)
         top = jnp.maximum(top, jnp.max(scores, axis=0, keepdims=True))
     return top
 
@@ -192,19 +201,26 @@
 
 
 def attend_kernel(
-    fb_ref, slopes_ref, q_ref, kv_ref, prev_ref, next_ref, far_own, far_partner, grad_ref, mirrored_ref,
+    fb_ref, slopes_hbm, q_ref, kv_ref, prev_ref, next_ref, far_own, far_partner, grad_ref, mirrored_ref,
     ctx_ref, rev_ref, gq_ref, own_out, prev_out, next_out, partner_out, here_out,
-    kbuf, vbuf, pbuf, dbuf, far_buf0, far_buf1, sems,
+    kbuf, vbuf, pbuf, dbuf, far_buf0, far_buf1, sems, slopes_ref, slopes_sem,
 ):
     shard, shards, zh, y = place()
     n = 2 * HD
     eye = one_hot(n, lambda r: r)
     total = kbuf.shape[0]
+    slopes_copy = pltpu.make_async_copy(slopes_hbm, slopes_ref, slopes_sem)
+    slopes_copy.start()
     copies = []
     for t in range(2):
         far_buf = (far_buf0, far_buf1)[t]
+        spare = far_buf.shape[0] - 1
+        to = [listed(fb_ref, t, shard, shards, zh, f) for f in range(fb_ref.shape[1])]
+        to = [jnp.where(there, slot, spare) for there, slot in to]
         stage(fb_ref, t, kv_ref, prev_ref, next_ref, (far_own, far_partner), kbuf, vbuf)
         q2 = two_heads(q_ref[t] * HD ** (-0.5))
+        if t == 0:
+            slopes_copy.wait()
         g2 = two_heads(flipped(mirrored_ref[...]) if t == 1 else grad_ref[...])
         cols = q2.shape[0]
 
@@ -214,11 +230,11 @@
         top = biased(fb_ref, t, slopes_ref, q2, kbuf, put)
         norm = jnp.zeros((1, cols), f32)
         row_dot = jnp.zeros((1, cols), f32)
-        for lo in range(0, total, STEP):
-            w = jnp.exp(pbuf[lo : lo + STEP] - top)
-            gp = dot(vbuf[lo : lo + STEP], g2, NT)
-            pbuf[lo : lo + STEP] = w
-            dbuf[lo : lo + STEP] = gp
+        for lo in range(0, total, FAR_STEP):
+            w = jnp.exp(pbuf[lo : lo + FAR_STEP] - top)
+            gp = dot(vbuf[lo : lo + FAR_STEP], g2, NT)
+            pbuf[lo : lo + FAR_STEP] = w
+            dbuf[lo : lo + FAR_STEP] = gp
             norm = norm + jnp.sum(w, axis=0, keepdims=True)
             row_dot = row_dot + jnp.sum(w * gp, axis=0, keepdims=True)
         inv = 1.0 / norm
@@ -229,10 +245,8 @@
             p = pbuf[lo : lo + STEP] * inv
             low = p.astype(bf16)
             ds = (p * (dbuf[lo : lo + STEP] - row_dot)).astype(bf16)
-            vt = dot(eye, vbuf[lo : lo + STEP], NT).astype(bf16)
-            ctx_acc = ctx_acc + dot(vt, low, NN)
-            kt = dot(eye, kbuf[lo : lo + STEP], NT).astype(bf16)
-            gq_acc = gq_acc + dot(kt, ds, NN)
+            ctx_acc = ctx_acc + dot(vbuf[lo : lo + STEP], low, TN)
+            gq_acc = gq_acc + dot(kbuf[lo : lo + STEP], ds, TN)
             for which, x in ((0, dot(ds, q2, NN)), (1, dot(low, g2, NN))):
                 if lo == 0:
                     prev_out[t, which] = x[0:128].astype(bf16)
@@ -241,11 +255,7 @@
                 else:
                     x = x.astype(bf16)
                     for i in range(STEP // BLK):
-                        there, slot = listed(fb_ref, t, shard, shards, zh, (lo - STEP) // BLK + i)
-
-                        @pl.when(there)
-                        def _():
-                            far_buf[slot, which * BLK : (which + 1) * BLK] = x[i * BLK : (i + 1) * BLK]
+                        far_buf[to[(lo - STEP) // BLK + i], which * BLK : (which + 1) * BLK] = x[i * BLK : (i + 1) * BLK]
 
         plane = far_own.shape[0]
         for k, (out, rows) in enumerate(((here_out, pl.ds(0, plane)), (partner_out, pl.ds(plane, plane)))):
@@ -369,13 +379,13 @@
     outgoing, key_value = pl.pallas_call(
         pack_own_kernel,
         out_shape=(pltpu.HBM(slots, bf16), shape(both)),
-        in_specs=[vmem()] * 3,
+        in_specs=[vmem(), hbm(), hbm()],
         out_specs=(hbm(), vmem()),
-        scratch_shapes=packed,
+        scratch_shapes=packed + [pltpu.SemaphoreType.DMA((2, 2))],
         cost_estimate=cost(500_000, 1_500_000),
         compiler_params=pltpu.CompilerParams(vmem_limit_bytes=LIMIT),
         name="pack_own",
-    )(far_blocks, keys, values)
+    )(far_blocks, *(pltpu.with_memory_space_constraint(x, pltpu.HBM) for x in (keys, values)))
     far_own = plane_a2a(outgoing)
     partner = z_swap(key_value)
     outgoing, to_up, to_down = pl.pallas_call(
@@ -428,27 +438,28 @@
     mirrored = lax.ppermute(grad_context, SEQ, mirror)
 
     square = shape((tok_rows, width))
-    half = pltpu.VMEM((seq_count, 2 * BLK, width), bf16)
+    half = pltpu.VMEM((seq_count + 1, 2 * BLK, width), bf16)
     context_fwd, context_rev, grad_queries, own, before, after, partner_grads, here_grads = pl.pallas_call(
         attend_kernel,
         out_shape=(square, square, shape((2, tok_rows, width)), shape(both, f32), shape(both), shape(both))
         + (pltpu.HBM(slots, bf16),) * 2,
-        in_specs=[smem()] * 2 + [vmem()] * 8,
+        in_specs=[smem(), hbm()] + [vmem()] * 8,
         out_specs=(vmem(),) * 6 + (hbm(),) * 2,
         scratch_shapes=[pltpu.VMEM((total_keys, width), bf16)] * 2
         + [pltpu.VMEM((total_keys, cols), f32)] * 2
-        + [half, half, pltpu.SemaphoreType.DMA((2, 2))],
+        + [half, half, pltpu.SemaphoreType.DMA((2, 2)), pltpu.SMEM(slopes.shape, f32), pltpu.SemaphoreType.DMA(())],
         cost_estimate=cost(4_000_000_000, 8_000_000, 1_000_000),
         compiler_params=pltpu.CompilerParams(vmem_limit_bytes=LIMIT),
         name="attend",
-    )(far_blocks, slopes, queries, key_value, from_prev, from_next, far_own, far_partner, grad_context, mirrored)
+    )(
+        far_blocks, pltpu.with_memory_space_constraint(slopes, pltpu.HBM), queries, key_value, from_prev, from_next, far_own, far_partner, grad_context, mirrored)
     context_back = lax.ppermute(context_rev, SEQ, mirror)
 
     returned_partner = plane_a2a(partner_grads)
     from_prev_grad = lax.ppermute(after, SEQ, [(b, a) for a, b in down])
     from_next_grad = lax.ppermute(before, SEQ, [(b, a) for a, b in up])
-    here_grads, returned_partner, context_back = lax.optimization_barrier(
-        (here_grads, returned_partner, context_back)
+    here_grads, returned_partner, context_back, from_prev_grad, from_next_grad = lax.optimization_barrier(
+        (here_grads, returned_partner, context_back, from_prev_grad, from_next_grad)
     )
     returned_own = plane_a2a(here_grads)
     other = pl.pallas_call(
@@ -478,12 +489,8 @@
         name="project",
     )(context_fwd, context_back, out_weight)
     held = even + swap(odd, 1).astype(f32)
+    held, other = lax.optimization_barrier((held, other))
     parts = [swap(held[k].astype(bf16), 2 * k) for k in range(1, tp_count // 2)]
-    total = residual.astype(f32) + held[0]
-    for part_here in parts:
-        total = total + part_here.astype(f32)
-    mixed = total.astype(bf16)
-
     grad_keys, grad_values = pl.pallas_call(
         combine_own_kernel,
         out_shape=(shape((2, tok_rows, width)),) * 2,
@@ -494,6 +501,11 @@
         compiler_params=pltpu.CompilerParams(vmem_limit_bytes=LIMIT),
         name="combine_own",
     )(far_blocks, own, from_prev_grad, from_next_grad, other, returned_own)
+    grad_keys, grad_values, *parts = lax.optimization_barrier((grad_keys, grad_values, *parts))
+    total = residual.astype(f32) + held[0]
+    for part_here in parts:
+        total = total + part_here.astype(f32)
+    mixed = total.astype(bf16)
     return (mixed, grad_queries, grad_keys, grad_values)
 
 

time: 115 us -> 118 us (1.026)
  starting transfers between devices: 74.1 us -> 80 us
  local copies, waits for them, and re-layouts: 3.15 us -> 1.42 us
  Pallas kernels: 14.9 us -> 13.2 us
    ppermute x2, starting transfers between devices: 7.72 us -> 12.7 us  [z_swap(): return lax.ppermute(x, 'zh', [(i, nz - 1 - i) for i in range(nz)])]
    ppermute x1, waiting for transfers between devices: 0.01 us -> 4.25 us  [per_device(): context_back = lax.ppermute(context_rev, SEQ, mirror)]
    ppermute x8, waiting for transfers between devices: 6.16 us -> 1.97 us  [swap(): return lax.ppermute(x, 'tp', [(i, i ^ bit) for i in range(count)])]
    ppermute x1, waiting for transfers between devices: 3 us -> 0.01 us  [per_device(): from_next_grad = lax.ppermute(before, SEQ, [(b, a) for a, b in up])]
    ppermute x1, starting transfers between devices: 4.57 us -> 2.01 us  [per_device(): from_prev_grad = lax.ppermute(after, SEQ, [(b, a) for a, b in down])]
    pallas_call x1, Pallas kernels: 10.4 us -> 7.91 us  [per_device(): pl.pallas_call(attend_kernel, out_shape=(square, square, shape((2, tok_ro...]
    ppermute x2, waiting for transfers between devices: 8.88 us -> 11.4 us  [z_swap(): return lax.ppermute(x, 'zh', [(i, nz - 1 - i) for i in range(nz)])]
    ppermute x1, starting transfers between devices: 1.92 us -> 3.82 us  [per_device(): from_next_grad = lax.ppermute(before, SEQ, [(b, a) for a, b in up])]
  transfers between devices with their start and end apart: 20 -> 20, of which waited for: 8 -> 7; matrix products, arithmetic and copies ran while one was open for 1% -> 0% of each run, Pallas kernels for 2% -> 3%
where the time goes in v7:
time: 118 us; the launch traced here: 117 us
  starting transfers between devices  80 us (68%)
  waiting for transfers between devices  20.4 us (17%)
  Pallas kernels  13.2 us (11%)
  local copies, waits for them, and re-layouts  1.42 us (1%)
    all_to_all x4, starting transfers between devices, plane_a2a(): lax.all_to_all(x, ('x', 'y'), split_axis=0, concat_axis=0, tiled=True)  27.9 us
    ppermute x2, starting transfers between devices, z_swap(): return lax.ppermute(x, 'zh', [(i, nz - 1 - i) for i in range(nz)])  12.7 us
    ppermute x2, waiting for transfers between devices, z_swap(): return lax.ppermute(x, 'zh', [(i, nz - 1 - i) for i in range(nz)])  11.4 us
    ppermute x8, starting transfers between devices, swap(): return lax.ppermute(x, 'tp', [(i, i ^ bit) for i in range(count)])  10.1 us
    ppermute x1, starting transfers between devices, per_device(): mirrored = lax.ppermute(grad_context, SEQ, mirror)  9.33 us
    ppermute x1, starting transfers between devices, per_device(): context_back = lax.ppermute(context_rev, SEQ, mirror)  8.19 us
    pallas_call x1, Pallas kernels, per_device(): pl.pallas_call(attend_kernel, out_shape=(square, square, shape((2, tok_ro...  7.91 us
    ppermute x1, waiting for transfers between devices, per_device(): context_back = lax.ppermute(context_rev, SEQ, mirror)  4.25 us
  transfers between devices with their start and end apart: 20, of which 7 were waited for; matrix products, arithmetic and copies ran while one was open for 0% of the time, Pallas kernels for 3%

profile of v7, /device:TPU:24, one launch (start us, length us, event | category | flops | bytes accessed | tf_op | source)
XLA Modules:
  0.0 116.5 jit_solution(3713451791724905893)
XLA Ops:
  0.6 0.8 copy.14.fb_ref
  1.4 2.0 %pack_own.1 = (bf16[16,256,128]{2,1,0:T(8,128)(2,1)}, bf16[2,2,128,128]{3,2,1,0:T(8,128)(2,1)S(1)}) custom-call(s32[32,24]{1,0:T(8,128)S(1)} %copy.14.fb_ref, bf16[2,128,128]{2,1,0:T(8,128)(2,1)} %key_ref.1, bf16[2,128,128]{2,1,0:T(8,128)(2,1)} %value_ref.1), custom_call_target="tpu_custom_call" | custom-call | flops 500000 | bytes 1500000 | tf_op jit(solution)/shard_map/pack_own/pallas_call | solution.py:379
  3.4 7.2 %all-to-all-start = ((bf16[16,256,128]{2,1,0:T(8,128)(2,1)}), bf16[16,256,128]{2,1,0:T(8,128)(2,1)S(1)}, u32[]{:S(2)}, u32[]{:S(2)}) async-start(bf16[16,256,128]{2,1,0:T(8,128)(2,1)} %get-tuple-element.40), calls=%async_computation | async-start | bytes 2097152 | tf_op jit(solution)/shard_map/all_to_all | solution.py:372
  10.6 3.4 %collective-permute-start.4 = (bf16[16,1024]{1,0:T(8,128)(2,1)S(1)}, bf16[16,1024]{1,0:T(8,128)(2,1)S(1)}, u32[]{:S(2)}, u32[]{:S(2)}) collective-permute-start(bf16[16,1024]{1,0:T(8,128)(2,1)S(1)} %copy-done.1), channel_id=1, source_target_pairs={{0,4},{1,5},{2,6},{3,7},{4,0},{5,1},{6,2},{7,3},{8,12},{9,13},{10,... | collective-permute-start | bytes 98312 | tf_op jit(solution)/shard_map/ppermute | solution.py:354
  14.0 1.9 %collective-permute-start.3 = (bf16[16,1024]{1,0:T(8,128)(2,1)S(1)}, bf16[16,1024]{1,0:T(8,128)(2,1)S(1)}, u32[]{:S(2)}, u32[]{:S(2)}) collective-permute-start(bf16[16,1024]{1,0:T(8,128)(2,1)S(1)} %copy-done.1), channel_id=1, source_target_pairs={{0,2},{1,3},{2,0},{3,1},{4,6},{5,7},{6,4},{7,5},{8,10},{9,11},{10,... | collective-permute-start | bytes 98312 | tf_op jit(solution)/shard_map/ppermute | solution.py:354
  15.9 6.4 %collective-permute-start = (bf16[2,2,128,128]{3,2,1,0:T(8,128)(2,1)S(1)}, bf16[2,2,128,128]{3,2,1,0:T(8,128)(2,1)S(1)}, u32[]{:S(2)}, u32[]{:S(2)}) collective-permute-start(bf16[2,2,128,128]{3,2,1,0:T(8,128)(2,1)S(1)} %get-tuple-element.37.own_ref.kv_ref), channel_id=1, source_target_pairs={{0,32},{32,0},{1,33},{33,1},{2,34},{34,2},{3,35},{35,3},{4,36},{36... | collective-permute-start | bytes 393224 | tf_op jit(solution)/shard_map/ppermute | solution.py:375
  22.5 4.6 %collective-permute-done.partner_ref = bf16[2,2,128,128]{3,2,1,0:T(8,128)(2,1)S(1)} collective-permute-done((bf16[2,2,128,128]{3,2,1,0:T(8,128)(2,1)S(1)}, bf16[2,2,128,128]{3,2,1,0:T(8,128)(2,1)S(1)}, u32[]{:S(2)}, u32[]{:S(2)}) %collective-permute-start) | collective-permute-done | bytes 131104 | tf_op jit(solution)/shard_map/ppermute | solution.py:375
  27.1 1.1 pack_partner.1
  28.3 7.4 %all-to-all-start.1 = ((bf16[16,256,128]{2,1,0:T(8,128)(2,1)}), bf16[16,256,128]{2,1,0:T(8,128)(2,1)S(1)}, u32[]{:S(2)}, u32[]{:S(2)}) async-start(bf16[16,256,128]{2,1,0:T(8,128)(2,1)} %get-tuple-element.42), calls=%async_computation.1 | async-start | bytes 2097152 | tf_op jit(solution)/shard_map/all_to_all | solution.py:372
  35.7 3.4 %collective-permute-start.1 = (bf16[2,2,128,128]{3,2,1,0:T(8,128)(2,1)S(1)}, bf16[2,2,128,128]{3,2,1,0:T(8,128)(2,1)S(1)}, u32[]{:S(2)}, u32[]{:S(2)}) collective-permute-start(bf16[2,2,128,128]{3,2,1,0:T(8,128)(2,1)S(1)} %get-tuple-element.38), channel_id=1, source_target_pairs={{0,8},{8,16},{16,24},{24,64},{32,40},{40,48},{48,56},{56,32},{64,7... | collective-permute-start | bytes 393224 | tf_op jit(solution)/shard_map/ppermute | solution.py:425
  39.1 2.6 %collective-permute-start.2 = (bf16[2,2,128,128]{3,2,1,0:T(8,128)(2,1)S(1)}, bf16[2,2,128,128]{3,2,1,0:T(8,128)(2,1)S(1)}, u32[]{:S(2)}, u32[]{:S(2)}) collective-permute-start(bf16[2,2,128,128]{3,2,1,0:T(8,128)(2,1)S(1)} %get-tuple-element.39), channel_id=1, source_target_pairs={{0,24},{8,0},{16,8},{24,16},{40,32},{48,40},{56,48},{64,88},{72,64... | collective-permute-start | bytes 393224 | tf_op jit(solution)/shard_map/ppermute | solution.py:426
  41.7 0.2 context_grad.1.grad_ref
  41.9 9.3 %collective-permute-start.7 = (bf16[128,128]{1,0:T(8,128)(2,1)S(1)}, bf16[128,128]{1,0:T(8,128)(2,1)S(1)}, u32[]{:S(2)}, u32[]{:S(2)}) collective-permute-start(bf16[128,128]{1,0:T(8,128)(2,1)S(1)} %context_grad.1.grad_ref), channel_id=1, source_target_pairs={{0,248},{8,240},{16,232},{24,224},{32,216},{40,208},{48,200},{56,1... | collective-permute-start | bytes 98312 | tf_op jit(solution)/shard_map/ppermute | solution.py:438
  51.3 2.8 %collective-permute-done.7.mirrored_ref = bf16[128,128]{1,0:T(8,128)(2,1)S(1)} collective-permute-done((bf16[128,128]{1,0:T(8,128)(2,1)S(1)}, bf16[128,128]{1,0:T(8,128)(2,1)S(1)}, u32[]{:S(2)}, u32[]{:S(2)}) %collective-permute-start.7) | collective-permute-done | bytes 32800 | tf_op jit(solution)/shard_map/ppermute | solution.py:438
  54.1 7.9 %attend.1 = (bf16[128,128]{1,0:T(8,128)(2,1)S(1)}, bf16[128,128]{1,0:T(8,128)(2,1)S(1)}, bf16[2,128,128]{2,1,0:T(8,128)(2,1)}, f32[2,2,128,128]{3,2,1,0:T(8,128)...) custom-call(s32[32,24]{1,0:T(8,128)S(1)} %copy.14.fb_ref, ...), custom_call_target="tpu_custom_call" | custom-call | flops 4000000000 | bytes 8000000 | tf_op jit(solution)/shard_map/attend/pallas_call | solution.py:442
  62.0 0.6 copy-done.3
  62.6 6.6 %all-to-all-start.2 = ((bf16[16,256,128]{2,1,0:T(8,128)(2,1)}), bf16[16,256,128]{2,1,0:T(8,128)(2,1)S(1)}, u32[]{:S(2)}, u32[]{:S(2)}) async-start(bf16[16,256,128]{2,1,0:T(8,128)(2,1)} %get-tuple-element.46), calls=%async_computation.2 | async-start | bytes 2097152 | tf_op jit(solution)/shard_map/all_to_all | solution.py:372
  69.3 2.0 %collective-permute-start.9 = (bf16[2,2,128,128]{3,2,1,0:T(8,128)(2,1)S(1)}, bf16[2,2,128,128]{3,2,1,0:T(8,128)(2,1)S(1)}, u32[]{:S(2)}, u32[]{:S(2)}) collective-permute-start(bf16[2,2,128,128]{3,2,1,0:T(8,128)(2,1)S(1)} %get-tuple-element.48), channel_id=1, source_target_pairs={{24,0},{0,8},{8,16},{16,24},{32,40},{40,48},{48,56},{88,64},{64,72... | collective-permute-start | bytes 393224 | tf_op jit(solution)/shard_map/ppermute | solution.py:459
  71.3 3.8 %collective-permute-start.10 = (bf16[2,2,128,128]{3,2,1,0:T(8,128)(2,1)S(1)}, bf16[2,2,128,128]{3,2,1,0:T(8,128)(2,1)S(1)}, u32[]{:S(2)}, u32[]{:S(2)}) collective-permute-start(bf16[2,2,128,128]{3,2,1,0:T(8,128)(2,1)S(1)} %get-tuple-element.49), channel_id=1, source_target_pairs={{8,0},{16,8},{24,16},{64,24},{40,32},{48,40},{56,48},{32,56},{72,6... | collective-permute-start | bytes 393224 | tf_op jit(solution)/shard_map/ppermute | solution.py:460
  75.1 8.2 %collective-permute-start.8 = (bf16[128,128]{1,0:T(8,128)(2,1)}, bf16[128,128]{1,0:T(8,128)(2,1)S(1)}, u32[]{:S(2)}, u32[]{:S(2)}) collective-permute-start(bf16[128,128]{1,0:T(8,128)(2,1)} %copy-done.3), channel_id=1, source_target_pairs={{0,248},{8,240},{16,232},{24,224},{32,216},{40,208},{48,200},{56,1... | collective-permute-start | bytes 98312 | tf_op jit(solution)/shard_map/ppermute | solution.py:456
  83.3 4.2 %collective-permute-done.8.back_ref = bf16[128,128]{1,0:T(8,128)(2,1)S(1)} collective-permute-done((bf16[128,128]{1,0:T(8,128)(2,1)}, bf16[128,128]{1,0:T(8,128)(2,1)S(1)}, u32[]{:S(2)}, u32[]{:S(2)}) %collective-permute-start.8) | collective-permute-done | bytes 32800 | tf_op jit(solution)/shard_map/ppermute | solution.py:456
  87.6 6.7 %all-to-all-start.3 = ((bf16[16,256,128]{2,1,0:T(8,128)(2,1)}), bf16[16,256,128]{2,1,0:T(8,128)(2,1)S(1)}, u32[]{:S(2)}, u32[]{:S(2)}) async-start(bf16[16,256,128]{2,1,0:T(8,128)(2,1)} %get-tuple-element.61), calls=%async_computation.3 | async-start | bytes 2097152 | tf_op jit(solution)/shard_map/all_to_all | solution.py:372
  94.3 0.5 combine_partner.1
  95.0 0.3 collective-permute-start.11
  95.3 6.3 %collective-permute-start.12 = (bf16[2,2,128,128]{3,2,1,0:T(8,128)(2,1)S(1)}, bf16[2,2,128,128]{3,2,1,0:T(8,128)(2,1)S(1)}, u32[]{:S(2)}, u32[]{:S(2)}) collective-permute-start(bf16[2,2,128,128]{3,2,1,0:T(8,128)(2,1)S(1)} %combine_partner.1), channel_id=1, source_target_pairs={{0,32},{32,0},{1,33},{33,1},{2,34},{34,2},{3,35},{35,3},{4,36},{36... | collective-permute-start | bytes 393224 | tf_op jit(solution)/shard_map/ppermute | solution.py:375
  101.6 6.7 %collective-permute-done.12.other_ref = bf16[2,2,128,128]{3,2,1,0:T(8,128)(2,1)S(1)} collective-permute-done((bf16[2,2,128,128]{3,2,1,0:T(8,128)(2,1)S(1)}, bf16[2,2,128,128]{3,2,1,0:T(8,128)(2,1)S(1)}, u32[]{:S(2)}, u32[]{:S(2)}) %collective-permute-start.12) | collective-permute-done | bytes 131104 | tf_op jit(solution)/shard_map/ppermute | solution.py:375
  108.4 2.4 %collective-permute-start.15 = (bf16[16,1024]{1,0:T(8,128)(2,1)S(1)}, bf16[16,1024]{1,0:T(8,128)(2,1)S(1)}, u32[]{:S(2)}, u32[]{:S(2)}) collective-permute-start(bf16[16,1024]{1,0:T(8,128)(2,1)S(1)} %get-tuple-element.70), channel_id=1, source_target_pairs={{0,6},{1,7},{2,4},{3,5},{4,2},{5,3},{6,0},{7,1},{8,14},{9,15},{10,... | collective-permute-start | bytes 98312 | tf_op jit(solution)/shard_map/ppermute | solution.py:354
  110.8 2.0 %collective-permute-start.13 = (bf16[16,1024]{1,0:T(8,128)(2,1)S(1)}, bf16[16,1024]{1,0:T(8,128)(2,1)S(1)}, u32[]{:S(2)}, u32[]{:S(2)}) collective-permute-start(bf16[16,1024]{1,0:T(8,128)(2,1)S(1)} %get-tuple-element.72), channel_id=1, source_target_pairs={{0,2},{1,3},{2,0},{3,1},{4,6},{5,7},{6,4},{7,5},{8,10},{9,11},{10,... | collective-permute-start | bytes 98312 | tf_op jit(solution)/shard_map/ppermute | solution.py:354
  112.9 1.2 %combine_own.1 = (bf16[2,128,128]{2,1,0:T(8,128)(2,1)}, bf16[2,128,128]{2,1,0:T(8,128)(2,1)}) custom-call(s32[32,24]{1,0:T(8,128)S(1)} %copy.14.fb_ref, f32[2,2,128,128]{3,2,1,0:T(8,128)S(1)} %get-tuple-element.59.own_ref, bf16[2,2,128,128]{3,2,1,0:T(8,128)(2,1)S(1)} %collective-permute-done.9.prev_ref, ...), custom_call_target="tpu_custom_call" | custom-call | flops 2000000 | bytes 1500000 | tf_op jit(solution)/shard_map/combine_own/pallas_call | solution.py:494
  114.0 0.4 collective-permute-done.15
  114.4 1.5 %collective-permute-done.14 = bf16[16,1024]{1,0:T(8,128)(2,1)S(1)} collective-permute-done((bf16[16,1024]{1,0:T(8,128)(2,1)S(1)}, bf16[16,1024]{1,0:T(8,128)(2,1)S(1)}, u32[]{:S(2)}, u32[]{:S(2)}) %collective-permute-start.14) | collective-permute-done | bytes 32800 | tf_op jit(solution)/shard_map/ppermute | solution.py:354
  115.9 0.6 fusion.3
  (31 shorter events, 0.5 us)
Async XLA Ops:
  3.4 7.2 %copy-start.1 = (bf16[16,1024]{1,0:T(8,128)(2,1)S(1)}, bf16[16,1024]{1,0:T(8,128)(2,1)}, u32[]{:S(2)}) copy-start(bf16[16,1024]{1,0:T(8,128)(2,1)} %ref0.1) | copy-start | bytes 98308
  3.4 24.9 %all-to-all-start = ((bf16[16,256,128]{2,1,0:T(8,128)(2,1)}), bf16[16,256,128]{2,1,0:T(8,128)(2,1)S(1)}, u32[]{:S(2)}, u32[]{:S(2)}) async-start(bf16[16,256,128]{2,1,0:T(8,128)(2,1)} %get-tuple-element.40), calls=%async_computation | async-start | bytes 2097152 | tf_op jit(solution)/shard_map/all_to_all | solution.py:372
  10.6 11.7 %collective-permute-start.4 = (bf16[16,1024]{1,0:T(8,128)(2,1)S(1)}, bf16[16,1024]{1,0:T(8,128)(2,1)S(1)}, u32[]{:S(2)}, u32[]{:S(2)}) collective-permute-start(bf16[16,1024]{1,0:T(8,128)(2,1)S(1)} %copy-done.1), channel_id=1, source_target_pairs={{0,4},{1,5},{2,6},{3,7},{4,0},{5,1},{6,2},{7,3},{8,12},{9,13},{10,... | collective-permute-start | bytes 98312 | tf_op jit(solution)/shard_map/ppermute | solution.py:354
  14.0 8.3 %collective-permute-start.3 = (bf16[16,1024]{1,0:T(8,128)(2,1)S(1)}, bf16[16,1024]{1,0:T(8,128)(2,1)S(1)}, u32[]{:S(2)}, u32[]{:S(2)}) collective-permute-start(bf16[16,1024]{1,0:T(8,128)(2,1)S(1)} %copy-done.1), channel_id=1, source_target_pairs={{0,2},{1,3},{2,0},{3,1},{4,6},{5,7},{6,4},{7,5},{8,10},{9,11},{10,... | collective-permute-start | bytes 98312 | tf_op jit(solution)/shard_map/ppermute | solution.py:354
  15.9 6.5 %collective-permute-start.5 = (bf16[16,1024]{1,0:T(8,128)(2,1)S(1)}, bf16[16,1024]{1,0:T(8,128)(2,1)S(1)}, u32[]{:S(2)}, u32[]{:S(2)}) collective-permute-start(bf16[16,1024]{1,0:T(8,128)(2,1)S(1)} %copy-done.1), channel_id=1, source_target_pairs={{0,6},{1,7},{2,4},{3,5},{4,2},{5,3},{6,0},{7,1},{8,14},{9,15},{10,... | collective-permute-start | bytes 98312 | tf_op jit(solution)/shard_map/ppermute | solution.py:354
  15.9 11.2 %collective-permute-start = (bf16[2,2,128,128]{3,2,1,0:T(8,128)(2,1)S(1)}, bf16[2,2,128,128]{3,2,1,0:T(8,128)(2,1)S(1)}, u32[]{:S(2)}, u32[]{:S(2)}) collective-permute-start(bf16[2,2,128,128]{3,2,1,0:T(8,128)(2,1)S(1)} %get-tuple-element.37.own_ref.kv_ref), channel_id=1, source_target_pairs={{0,32},{32,0},{1,33},{33,1},{2,34},{34,2},{3,35},{35,3},{4,36},{36... | collective-permute-start | bytes 393224 | tf_op jit(solution)/shard_map/ppermute | solution.py:375
  22.4 5.9 %collective-permute-start.6 = (bf16[4,16,1024]{2,1,0:T(8,128)(2,1)S(1)}, bf16[4,16,1024]{2,1,0:T(8,128)(2,1)S(1)}, u32[]{:S(2)}, u32[]{:S(2)}) collective-permute-start(bf16[4,16,1024]{2,1,0:T(8,128)(2,1)S(1)} %pad_maximum_fusion), channel_id=1, source_target_pairs={{0,1},{1,0},{2,3},{3,2},{4,5},{5,4},{6,7},{7,6},{8,9},{9,8},{10,11... | collective-permute-start | bytes 393224 | tf_op jit(solution)/shard_map/ppermute | solution.py:354
  28.3 13.4 %copy-start = (bf16[128,1024]{1,0:T(8,128)(2,1)S(1)}, bf16[128,1024]{1,0:T(8,128)(2,1)}, u32[]{:S(2)}) copy-start(bf16[128,1024]{1,0:T(8,128)(2,1)} %weight_ref.3) | copy-start | bytes 786436
  28.3 25.8 %all-to-all-start.1 = ((bf16[16,256,128]{2,1,0:T(8,128)(2,1)}), bf16[16,256,128]{2,1,0:T(8,128)(2,1)S(1)}, u32[]{:S(2)}, u32[]{:S(2)}) async-start(bf16[16,256,128]{2,1,0:T(8,128)(2,1)} %get-tuple-element.42), calls=%async_computation.1 | async-start | bytes 2097152 | tf_op jit(solution)/shard_map/all_to_all | solution.py:372
  35.7 18.4 %collective-permute-start.1 = (bf16[2,2,128,128]{3,2,1,0:T(8,128)(2,1)S(1)}, bf16[2,2,128,128]{3,2,1,0:T(8,128)(2,1)S(1)}, u32[]{:S(2)}, u32[]{:S(2)}) collective-permute-start(bf16[2,2,128,128]{3,2,1,0:T(8,128)(2,1)S(1)} %get-tuple-element.38), channel_id=1, source_target_pairs={{0,8},{8,16},{16,24},{24,64},{32,40},{40,48},{48,56},{56,32},{64,7... | collective-permute-start | bytes 393224 | tf_op jit(solution)/shard_map/ppermute | solution.py:425
  39.1 15.0 %copy-start.2 = (bf16[2,128,128]{2,1,0:T(8,128)(2,1)S(1)}, bf16[2,128,128]{2,1,0:T(8,128)(2,1)}, u32[]{:S(2)}) copy-start(bf16[2,128,128]{2,1,0:T(8,128)(2,1)} %q_ref.1) | copy-start | bytes 196612
  39.1 15.0 %collective-permute-start.2 = (bf16[2,2,128,128]{3,2,1,0:T(8,128)(2,1)S(1)}, bf16[2,2,128,128]{3,2,1,0:T(8,128)(2,1)S(1)}, u32[]{:S(2)}, u32[]{:S(2)}) collective-permute-start(bf16[2,2,128,128]{3,2,1,0:T(8,128)(2,1)S(1)} %get-tuple-element.39), channel_id=1, source_target_pairs={{0,24},{8,0},{16,8},{24,16},{40,32},{48,40},{56,48},{64,88},{72,64... | collective-permute-start | bytes 393224 | tf_op jit(solution)/shard_map/ppermute | solution.py:426
  41.9 12.1 %collective-permute-start.7 = (bf16[128,128]{1,0:T(8,128)(2,1)S(1)}, bf16[128,128]{1,0:T(8,128)(2,1)S(1)}, u32[]{:S(2)}, u32[]{:S(2)}) collective-permute-start(bf16[128,128]{1,0:T(8,128)(2,1)S(1)} %context_grad.1.grad_ref), channel_id=1, source_target_pairs={{0,248},{8,240},{16,232},{24,224},{32,216},{40,208},{48,200},{56,1... | collective-permute-start | bytes 98312 | tf_op jit(solution)/shard_map/ppermute | solution.py:438
  62.0 0.6 copy-start.3
  62.6 24.9 %all-to-all-start.2 = ((bf16[16,256,128]{2,1,0:T(8,128)(2,1)}), bf16[16,256,128]{2,1,0:T(8,128)(2,1)S(1)}, u32[]{:S(2)}, u32[]{:S(2)}) async-start(bf16[16,256,128]{2,1,0:T(8,128)(2,1)} %get-tuple-element.46), calls=%async_computation.2 | async-start | bytes 2097152 | tf_op jit(solution)/shard_map/all_to_all | solution.py:372
  69.3 18.3 %collective-permute-start.9 = (bf16[2,2,128,128]{3,2,1,0:T(8,128)(2,1)S(1)}, bf16[2,2,128,128]{3,2,1,0:T(8,128)(2,1)S(1)}, u32[]{:S(2)}, u32[]{:S(2)}) collective-permute-start(bf16[2,2,128,128]{3,2,1,0:T(8,128)(2,1)S(1)} %get-tuple-element.48), channel_id=1, source_target_pairs={{24,0},{0,8},{8,16},{16,24},{32,40},{40,48},{48,56},{88,64},{64,72... | collective-permute-start | bytes 393224 | tf_op jit(solution)/shard_map/ppermute | solution.py:459
  71.3 16.3 %collective-permute-start.10 = (bf16[2,2,128,128]{3,2,1,0:T(8,128)(2,1)S(1)}, bf16[2,2,128,128]{3,2,1,0:T(8,128)(2,1)S(1)}, u32[]{:S(2)}, u32[]{:S(2)}) collective-permute-start(bf16[2,2,128,128]{3,2,1,0:T(8,128)(2,1)S(1)} %get-tuple-element.49), channel_id=1, source_target_pairs={{8,0},{16,8},{24,16},{64,24},{40,32},{48,40},{56,48},{32,56},{72,6... | collective-permute-start | bytes 393224 | tf_op jit(solution)/shard_map/ppermute | solution.py:460
  75.1 12.4 %collective-permute-start.8 = (bf16[128,128]{1,0:T(8,128)(2,1)}, bf16[128,128]{1,0:T(8,128)(2,1)S(1)}, u32[]{:S(2)}, u32[]{:S(2)}) collective-permute-start(bf16[128,128]{1,0:T(8,128)(2,1)} %copy-done.3), channel_id=1, source_target_pairs={{0,248},{8,240},{16,232},{24,224},{32,216},{40,208},{48,200},{56,1... | collective-permute-start | bytes 98312 | tf_op jit(solution)/shard_map/ppermute | solution.py:456
  87.6 25.3 %all-to-all-start.3 = ((bf16[16,256,128]{2,1,0:T(8,128)(2,1)}), bf16[16,256,128]{2,1,0:T(8,128)(2,1)S(1)}, u32[]{:S(2)}, u32[]{:S(2)}) async-start(bf16[16,256,128]{2,1,0:T(8,128)(2,1)} %get-tuple-element.61), calls=%async_computation.3 | async-start | bytes 2097152 | tf_op jit(solution)/shard_map/all_to_all | solution.py:372
  95.0 6.6 %collective-permute-start.11 = (bf16[4,16,1024]{2,1,0:T(8,128)(2,1)S(1)}, bf16[4,16,1024]{2,1,0:T(8,128)(2,1)S(1)}, u32[]{:S(2)}, u32[]{:S(2)}) collective-permute-start(bf16[4,16,1024]{2,1,0:T(8,128)(2,1)S(1)} %get-tuple-element.56), channel_id=1, source_target_pairs={{0,1},{1,0},{2,3},{3,2},{4,5},{5,4},{6,7},{7,6},{8,9},{9,8},{10,11... | collective-permute-start | bytes 393224 | tf_op jit(solution)/shard_map/ppermute | solution.py:354
  95.3 13.0 %collective-permute-start.12 = (bf16[2,2,128,128]{3,2,1,0:T(8,128)(2,1)S(1)}, bf16[2,2,128,128]{3,2,1,0:T(8,128)(2,1)S(1)}, u32[]{:S(2)}, u32[]{:S(2)}) collective-permute-start(bf16[2,2,128,128]{3,2,1,0:T(8,128)(2,1)S(1)} %combine_partner.1), channel_id=1, source_target_pairs={{0,32},{32,0},{1,33},{33,1},{2,34},{34,2},{3,35},{35,3},{4,36},{36... | collective-permute-start | bytes 393224 | tf_op jit(solution)/shard_map/ppermute | solution.py:375
  108.4 6.1 %collective-permute-start.15 = (bf16[16,1024]{1,0:T(8,128)(2,1)S(1)}, bf16[16,1024]{1,0:T(8,128)(2,1)S(1)}, u32[]{:S(2)}, u32[]{:S(2)}) collective-permute-start(bf16[16,1024]{1,0:T(8,128)(2,1)S(1)} %get-tuple-element.70), channel_id=1, source_target_pairs={{0,6},{1,7},{2,4},{3,5},{4,2},{5,3},{6,0},{7,1},{8,14},{9,15},{10,... | collective-permute-start | bytes 98312 | tf_op jit(solution)/shard_map/ppermute | solution.py:354
  110.8 5.1 %collective-permute-start.14 = (bf16[16,1024]{1,0:T(8,128)(2,1)S(1)}, bf16[16,1024]{1,0:T(8,128)(2,1)S(1)}, u32[]{:S(2)}, u32[]{:S(2)}) collective-permute-start(bf16[16,1024]{1,0:T(8,128)(2,1)S(1)} %get-tuple-element.71), channel_id=1, source_target_pairs={{0,4},{1,5},{2,6},{3,7},{4,0},{5,1},{6,2},{7,3},{8,12},{9,13},{10,... | collective-permute-start | bytes 98312 | tf_op jit(solution)/shard_map/ppermute | solution.py:354
  110.8 5.1 %collective-permute-start.13 = (bf16[16,1024]{1,0:T(8,128)(2,1)S(1)}, bf16[16,1024]{1,0:T(8,128)(2,1)S(1)}, u32[]{:S(2)}, u32[]{:S(2)}) collective-permute-start(bf16[16,1024]{1,0:T(8,128)(2,1)S(1)} %get-tuple-element.72), channel_id=1, source_target_pairs={{0,2},{1,3},{2,0},{3,1},{4,6},{5,7},{6,4},{7,5},{8,10},{9,11},{10,... | collective-permute-start | bytes 98312 | tf_op jit(solution)/shard_map/ppermute | solution.py:354
  112.8 3.1 %copy-start.4 = (bf16[16,1024]{1,0:T(8,128)(2,1)S(1)}, bf16[16,1024]{1,0:T(8,128)(2,1)}, u32[]{:S(2)}) copy-start(bf16[16,1024]{1,0:T(8,128)(2,1)} %param.9) | copy-start | bytes 98308

commit v8 on v7

--- a/solution.py
+++ b/solution.py
@@ -458,8 +458,8 @@
     returned_partner = plane_a2a(partner_grads)
     from_prev_grad = lax.ppermute(after, SEQ, [(b, a) for a, b in down])
     from_next_grad = lax.ppermute(before, SEQ, [(b, a) for a, b in up])
-    here_grads, returned_partner, context_back, from_prev_grad, from_next_grad = lax.optimization_barrier(
-        (here_grads, returned_partner, context_back, from_prev_grad, from_next_grad)
+    here_grads, returned_partner, context_back = lax.optimization_barrier(
+        (here_grads, returned_partner, context_back)
     )
     returned_own = plane_a2a(here_grads)
     other = pl.pallas_call(
@@ -489,8 +489,12 @@
         name="project",
     )(context_fwd, context_back, out_weight)
     held = even + swap(odd, 1).astype(f32)
-    held, other = lax.optimization_barrier((held, other))
     parts = [swap(held[k].astype(bf16), 2 * k) for k in range(1, tp_count // 2)]
+    total = residual.astype(f32) + held[0]
+    for part_here in parts:
+        total = total + part_here.astype(f32)
+    mixed = total.astype(bf16)
+
     grad_keys, grad_values = pl.pallas_call(
         combine_own_kernel,
         out_shape=(shape((2, tok_rows, width)),) * 2,
@@ -501,11 +505,6 @@
         compiler_params=pltpu.CompilerParams(vmem_limit_bytes=LIMIT),
         name="combine_own",
     )(far_blocks, own, from_prev_grad, from_next_grad, other, returned_own)
-    grad_keys, grad_values, *parts = lax.optimization_barrier((grad_keys, grad_values, *parts))
-    total = residual.astype(f32) + held[0]
-    for part_here in parts:
-        total = total + part_here.astype(f32)
-    mixed = total.astype(bf16)
     return (mixed, grad_queries, grad_keys, grad_values)
 
 

time: 118 us -> 112 us (0.949)
  starting transfers between devices: 80 us -> 74.4 us
    ppermute x2, starting transfers between devices: 12.7 us -> 7.82 us  [z_swap(): return lax.ppermute(x, 'zh', [(i, nz - 1 - i) for i in range(nz)])]
    ppermute x1, waiting for transfers between devices: 4.25 us -> 0.01 us  [per_device(): context_back = lax.ppermute(context_rev, SEQ, mirror)]
    ppermute x8, waiting for transfers between devices: 1.97 us -> 6.06 us  [swap(): return lax.ppermute(x, 'tp', [(i, i ^ bit) for i in range(count)])]
    ppermute x1, waiting for transfers between devices: 0.01 us -> 2.98 us  [per_device(): from_next_grad = lax.ppermute(before, SEQ, [(b, a) for a, b in up])]
    ppermute x1, starting transfers between devices: 2.01 us -> 4.57 us  [per_device(): from_prev_grad = lax.ppermute(after, SEQ, [(b, a) for a, b in down])]
    ppermute x2, waiting for transfers between devices: 11.4 us -> 8.91 us  [z_swap(): return lax.ppermute(x, 'zh', [(i, nz - 1 - i) for i in range(nz)])]
    ppermute x1, starting transfers between devices: 3.82 us -> 1.92 us  [per_device(): from_next_grad = lax.ppermute(before, SEQ, [(b, a) for a, b in up])]
  transfers between devices with their start and end apart: 20 -> 20, of which waited for: 7 -> 8; matrix products, arithmetic and copies ran while one was open for 0% -> 1% of each run, Pallas kernels for 3% -> 2%
where the time goes in v8:
time: 112 us; the launch traced here: 111 us
  starting transfers between devices  74.4 us (66%)
  waiting for transfers between devices  20.8 us (19%)
  Pallas kernels  13.2 us (12%)
    all_to_all x4, starting transfers between devices, plane_a2a(): lax.all_to_all(x, ('x', 'y'), split_axis=0, concat_axis=0, tiled=True)  27.5 us
    ppermute x1, starting transfers between devices, per_device(): mirrored = lax.ppermute(grad_context, SEQ, mirror)  9.33 us
    ppermute x8, starting transfers between devices, swap(): return lax.ppermute(x, 'tp', [(i, i ^ bit) for i in range(count)])  9.22 us
    ppermute x2, waiting for transfers between devices, z_swap(): return lax.ppermute(x, 'zh', [(i, nz - 1 - i) for i in range(nz)])  8.91 us
    ppermute x1, starting transfers between devices, per_device(): context_back = lax.ppermute(context_rev, SEQ, mirror)  8.08 us
    pallas_call x1, Pallas kernels, per_device(): pl.pallas_call(attend_kernel, out_shape=(square, square, shape((2, tok_ro...  7.92 us
    ppermute x2, starting transfers between devices, z_swap(): return lax.ppermute(x, 'zh', [(i, nz - 1 - i) for i in range(nz)])  7.82 us
    ppermute x8, waiting for transfers between devices, swap(): return lax.ppermute(x, 'tp', [(i, i ^ bit) for i in range(count)])  6.06 us
  transfers between devices with their start and end apart: 20, of which 8 were waited for; matrix products, arithmetic and copies ran while one was open for 1% of the time, Pallas kernels for 2%

profile of v8, /device:TPU:24, one launch (start us, length us, event | category | flops | bytes accessed | tf_op | source)
XLA Modules:
  0.0 110.7 jit_solution(5462386864212037000)
XLA Ops:
  0.6 0.8 copy.14.fb_ref
  1.4 2.0 %pack_own.1 = (bf16[16,256,128]{2,1,0:T(8,128)(2,1)}, bf16[2,2,128,128]{3,2,1,0:T(8,128)(2,1)S(1)}) custom-call(s32[32,24]{1,0:T(8,128)S(1)} %copy.14.fb_ref, bf16[2,128,128]{2,1,0:T(8,128)(2,1)} %key_ref.1, bf16[2,128,128]{2,1,0:T(8,128)(2,1)} %value_ref.1), custom_call_target="tpu_custom_call" | custom-call | flops 500000 | bytes 1500000 | tf_op jit(solution)/shard_map/pack_own/pallas_call | solution.py:379
  3.4 7.2 %all-to-all-start = ((bf16[16,256,128]{2,1,0:T(8,128)(2,1)}), bf16[16,256,128]{2,1,0:T(8,128)(2,1)S(1)}, u32[]{:S(2)}, u32[]{:S(2)}) async-start(bf16[16,256,128]{2,1,0:T(8,128)(2,1)} %get-tuple-element.31), calls=%async_computation | async-start | bytes 2097152 | tf_op jit(solution)/shard_map/all_to_all | solution.py:372
  10.6 3.4 %collective-permute-start.4 = (bf16[16,1024]{1,0:T(8,128)(2,1)S(1)}, bf16[16,1024]{1,0:T(8,128)(2,1)S(1)}, u32[]{:S(2)}, u32[]{:S(2)}) collective-permute-start(bf16[16,1024]{1,0:T(8,128)(2,1)S(1)} %copy-done.1), channel_id=1, source_target_pairs={{0,4},{1,5},{2,6},{3,7},{4,0},{5,1},{6,2},{7,3},{8,12},{9,13},{10,... | collective-permute-start | bytes 98312 | tf_op jit(solution)/shard_map/ppermute | solution.py:354
  14.0 1.9 %collective-permute-start.3 = (bf16[16,1024]{1,0:T(8,128)(2,1)S(1)}, bf16[16,1024]{1,0:T(8,128)(2,1)S(1)}, u32[]{:S(2)}, u32[]{:S(2)}) collective-permute-start(bf16[16,1024]{1,0:T(8,128)(2,1)S(1)} %copy-done.1), channel_id=1, source_target_pairs={{0,2},{1,3},{2,0},{3,1},{4,6},{5,7},{6,4},{7,5},{8,10},{9,11},{10,... | collective-permute-start | bytes 98312 | tf_op jit(solution)/shard_map/ppermute | solution.py:354
  15.9 6.4 %collective-permute-start = (bf16[2,2,128,128]{3,2,1,0:T(8,128)(2,1)S(1)}, bf16[2,2,128,128]{3,2,1,0:T(8,128)(2,1)S(1)}, u32[]{:S(2)}, u32[]{:S(2)}) collective-permute-start(bf16[2,2,128,128]{3,2,1,0:T(8,128)(2,1)S(1)} %get-tuple-element.28.own_ref.kv_ref), channel_id=1, source_target_pairs={{0,32},{32,0},{1,33},{33,1},{2,34},{34,2},{3,35},{35,3},{4,36},{36... | collective-permute-start | bytes 393224 | tf_op jit(solution)/shard_map/ppermute | solution.py:375
  22.5 4.6 %collective-permute-done.partner_ref = bf16[2,2,128,128]{3,2,1,0:T(8,128)(2,1)S(1)} collective-permute-done((bf16[2,2,128,128]{3,2,1,0:T(8,128)(2,1)S(1)}, bf16[2,2,128,128]{3,2,1,0:T(8,128)(2,1)S(1)}, u32[]{:S(2)}, u32[]{:S(2)}) %collective-permute-start) | collective-permute-done | bytes 131104 | tf_op jit(solution)/shard_map/ppermute | solution.py:375
  27.1 1.1 %pack_partner.1 = (bf16[16,256,128]{2,1,0:T(8,128)(2,1)}, bf16[2,2,128,128]{3,2,1,0:T(8,128)(2,1)S(1)}, bf16[2,2,128,128]{3,2,1,0:T(8,128)(2,1)S(1)}) custom-call(s32[32,24]{1,0:T(8,128)S(1)} %copy.14.fb_ref, bf16[2,2,128,128]{3,2,1,0:T(8,128)(2,1)S(1)} %get-tuple-element.28.own_ref.kv_ref, bf16[2,2,128,128]{3,2,1,0:T(8,128)(2,1)S(1)} %collective-permute-done.partner_ref), custom_call_target="tpu_custom_call" | custom-call | flops 500000 | bytes 1500000 | tf_op jit(solution)/shard_map/pack_partner/pallas_call | solution.py:391
  28.3 7.4 %all-to-all-start.1 = ((bf16[16,256,128]{2,1,0:T(8,128)(2,1)}), bf16[16,256,128]{2,1,0:T(8,128)(2,1)S(1)}, u32[]{:S(2)}, u32[]{:S(2)}) async-start(bf16[16,256,128]{2,1,0:T(8,128)(2,1)} %get-tuple-element.33), calls=%async_computation.1 | async-start | bytes 2097152 | tf_op jit(solution)/shard_map/all_to_all | solution.py:372
  35.7 3.4 %collective-permute-start.1 = (bf16[2,2,128,128]{3,2,1,0:T(8,128)(2,1)S(1)}, bf16[2,2,128,128]{3,2,1,0:T(8,128)(2,1)S(1)}, u32[]{:S(2)}, u32[]{:S(2)}) collective-permute-start(bf16[2,2,128,128]{3,2,1,0:T(8,128)(2,1)S(1)} %get-tuple-element.29), channel_id=1, source_target_pairs={{0,8},{8,16},{16,24},{24,64},{32,40},{40,48},{48,56},{56,32},{64,7... | collective-permute-start | bytes 393224 | tf_op jit(solution)/shard_map/ppermute | solution.py:425
  39.1 2.6 %collective-permute-start.2 = (bf16[2,2,128,128]{3,2,1,0:T(8,128)(2,1)S(1)}, bf16[2,2,128,128]{3,2,1,0:T(8,128)(2,1)S(1)}, u32[]{:S(2)}, u32[]{:S(2)}) collective-permute-start(bf16[2,2,128,128]{3,2,1,0:T(8,128)(2,1)S(1)} %get-tuple-element.30), channel_id=1, source_target_pairs={{0,24},{8,0},{16,8},{24,16},{40,32},{48,40},{56,48},{64,88},{72,64... | collective-permute-start | bytes 393224 | tf_op jit(solution)/shard_map/ppermute | solution.py:426
  41.9 9.3 %collective-permute-start.7 = (bf16[128,128]{1,0:T(8,128)(2,1)S(1)}, bf16[128,128]{1,0:T(8,128)(2,1)S(1)}, u32[]{:S(2)}, u32[]{:S(2)}) collective-permute-start(bf16[128,128]{1,0:T(8,128)(2,1)S(1)} %context_grad.1.grad_ref), channel_id=1, source_target_pairs={{0,248},{8,240},{16,232},{24,224},{32,216},{40,208},{48,200},{56,1... | collective-permute-start | bytes 98312 | tf_op jit(solution)/shard_map/ppermute | solution.py:438
  51.3 2.8 %collective-permute-done.7.mirrored_ref = bf16[128,128]{1,0:T(8,128)(2,1)S(1)} collective-permute-done((bf16[128,128]{1,0:T(8,128)(2,1)S(1)}, bf16[128,128]{1,0:T(8,128)(2,1)S(1)}, u32[]{:S(2)}, u32[]{:S(2)}) %collective-permute-start.7) | collective-permute-done | bytes 32800 | tf_op jit(solution)/shard_map/ppermute | solution.py:438
  54.1 7.9 %attend.1 = (bf16[128,128]{1,0:T(8,128)(2,1)S(1)}, bf16[128,128]{1,0:T(8,128)(2,1)}, bf16[2,128,128]{2,1,0:T(8,128)(2,1)}, f32[2,2,128,128]{3,2,1,0:T(8,128)S(1)...) custom-call(s32[32,24]{1,0:T(8,128)S(1)} %copy.14.fb_ref, ...), custom_call_target="tpu_custom_call" | custom-call | flops 4000000000 | bytes 8000000 | tf_op jit(solution)/shard_map/attend/pallas_call | solution.py:442
  62.0 6.6 %all-to-all-start.2 = ((bf16[16,256,128]{2,1,0:T(8,128)(2,1)}), bf16[16,256,128]{2,1,0:T(8,128)(2,1)S(1)}, u32[]{:S(2)}, u32[]{:S(2)}) async-start(bf16[16,256,128]{2,1,0:T(8,128)(2,1)} %get-tuple-element.39), calls=%async_computation.2 | async-start | bytes 2097152 | tf_op jit(solution)/shard_map/all_to_all | solution.py:372
  68.7 8.1 %collective-permute-start.10 = (bf16[128,128]{1,0:T(8,128)(2,1)}, bf16[128,128]{1,0:T(8,128)(2,1)S(1)}, u32[]{:S(2)}, u32[]{:S(2)}) collective-permute-start(bf16[128,128]{1,0:T(8,128)(2,1)} %get-tuple-element.40), channel_id=1, source_target_pairs={{0,248},{8,240},{16,232},{24,224},{32,216},{40,208},{48,200},{56,1... | collective-permute-start | bytes 98312 | tf_op jit(solution)/shard_map/ppermute | solution.py:456
  76.8 4.6 %collective-permute-start.8 = (bf16[2,2,128,128]{3,2,1,0:T(8,128)(2,1)S(1)}, bf16[2,2,128,128]{3,2,1,0:T(8,128)(2,1)S(1)}, u32[]{:S(2)}, u32[]{:S(2)}) collective-permute-start(bf16[2,2,128,128]{3,2,1,0:T(8,128)(2,1)S(1)} %get-tuple-element.36), channel_id=1, source_target_pairs={{24,0},{0,8},{8,16},{16,24},{32,40},{40,48},{48,56},{88,64},{64,72... | collective-permute-start | bytes 393224 | tf_op jit(solution)/shard_map/ppermute | solution.py:459
  81.3 1.9 %collective-permute-start.9 = (bf16[2,2,128,128]{3,2,1,0:T(8,128)(2,1)S(1)}, bf16[2,2,128,128]{3,2,1,0:T(8,128)(2,1)S(1)}, u32[]{:S(2)}, u32[]{:S(2)}) collective-permute-start(bf16[2,2,128,128]{3,2,1,0:T(8,128)(2,1)S(1)} %get-tuple-element.37), channel_id=1, source_target_pairs={{8,0},{16,8},{24,16},{64,24},{40,32},{48,40},{56,48},{32,56},{72,6... | collective-permute-start | bytes 393224 | tf_op jit(solution)/shard_map/ppermute | solution.py:460
  83.3 6.3 %all-to-all-start.3 = ((bf16[16,256,128]{2,1,0:T(8,128)(2,1)}), bf16[16,256,128]{2,1,0:T(8,128)(2,1)S(1)}, u32[]{:S(2)}, u32[]{:S(2)}) async-start(bf16[16,256,128]{2,1,0:T(8,128)(2,1)} %get-tuple-element.49), calls=%async_computation.3 | async-start | bytes 2097152 | tf_op jit(solution)/shard_map/all_to_all | solution.py:372
  89.6 3.0 %collective-permute-done.9.next_ref = bf16[2,2,128,128]{3,2,1,0:T(8,128)(2,1)S(1)} collective-permute-done((bf16[2,2,128,128]{3,2,1,0:T(8,128)(2,1)S(1)}, bf16[2,2,128,128]{3,2,1,0:T(8,128)(2,1)S(1)}, u32[]{:S(2)}, u32[]{:S(2)}) %collective-permute-start.9) | collective-permute-done | bytes 131104 | tf_op jit(solution)/shard_map/ppermute | solution.py:460
  92.5 0.5 combine_partner.1
  93.3 0.3 collective-permute-start.11
  93.6 1.3 %collective-permute-done.11 = bf16[4,16,1024]{2,1,0:T(8,128)(2,1)S(1)} collective-permute-done((bf16[4,16,1024]{2,1,0:T(8,128)(2,1)S(1)}, bf16[4,16,1024]{2,1,0:T(8,128)(2,1)S(1)}, u32[]{:S(2)}, u32[]{:S(2)}) %collective-permute-start.11) | collective-permute-done | bytes 131104 | tf_op jit(solution)/shard_map/ppermute | solution.py:354
  95.0 0.3 collective-permute-start.12
  95.3 0.9 collective-permute-start.14
  96.2 2.4 %collective-permute-start.13 = (bf16[16,1024]{1,0:T(8,128)(2,1)S(1)}, bf16[16,1024]{1,0:T(8,128)(2,1)S(1)}, u32[]{:S(2)}, u32[]{:S(2)}) collective-permute-start(bf16[16,1024]{1,0:T(8,128)(2,1)S(1)} %get-tuple-element.56), channel_id=1, source_target_pairs={{0,4},{1,5},{2,6},{3,7},{4,0},{5,1},{6,2},{7,3},{8,12},{9,13},{10,... | collective-permute-start | bytes 98312 | tf_op jit(solution)/shard_map/ppermute | solution.py:354
  98.6 1.4 %collective-permute-start.15 = (bf16[2,2,128,128]{3,2,1,0:T(8,128)(2,1)S(1)}, bf16[2,2,128,128]{3,2,1,0:T(8,128)(2,1)S(1)}, u32[]{:S(2)}, u32[]{:S(2)}) collective-permute-start(bf16[2,2,128,128]{3,2,1,0:T(8,128)(2,1)S(1)} %combine_partner.1), channel_id=1, source_target_pairs={{0,32},{32,0},{1,33},{33,1},{2,34},{34,2},{3,35},{35,3},{4,36},{36... | collective-permute-start | bytes 393224 | tf_op jit(solution)/shard_map/ppermute | solution.py:375
  100.0 1.1 collective-permute-done.14
  101.1 3.6 %collective-permute-done.13 = bf16[16,1024]{1,0:T(8,128)(2,1)S(1)} collective-permute-done((bf16[16,1024]{1,0:T(8,128)(2,1)S(1)}, bf16[16,1024]{1,0:T(8,128)(2,1)S(1)}, u32[]{:S(2)}, u32[]{:S(2)}) %collective-permute-start.13) | collective-permute-done | bytes 32800 | tf_op jit(solution)/shard_map/ppermute | solution.py:354
  104.6 0.6 fusion.4
  105.3 4.3 %collective-permute-done.15.other_ref = bf16[2,2,128,128]{3,2,1,0:T(8,128)(2,1)S(1)} collective-permute-done((bf16[2,2,128,128]{3,2,1,0:T(8,128)(2,1)S(1)}, bf16[2,2,128,128]{3,2,1,0:T(8,128)(2,1)S(1)}, u32[]{:S(2)}, u32[]{:S(2)}) %collective-permute-start.15) | collective-permute-done | bytes 131104 | tf_op jit(solution)/shard_map/ppermute | solution.py:375
  109.5 1.2 %combine_own.1 = (bf16[2,128,128]{2,1,0:T(8,128)(2,1)}, bf16[2,128,128]{2,1,0:T(8,128)(2,1)}) custom-call(s32[32,24]{1,0:T(8,128)S(1)} %copy.14.fb_ref, f32[2,2,128,128]{3,2,1,0:T(8,128)S(1)} %get-tuple-element.47.own_ref, bf16[2,2,128,128]{3,2,1,0:T(8,128)(2,1)S(1)} %collective-permute-done.8.prev_ref, ...), custom_call_target="tpu_custom_call" | custom-call | flops 2000000 | bytes 1500000 | tf_op jit(solution)/shard_map/combine_own/pallas_call | solution.py:498
  (28 shorter events, 0.7 us)
Async XLA Ops:
  3.4 7.2 %copy-start.1 = (bf16[16,1024]{1,0:T(8,128)(2,1)S(1)}, bf16[16,1024]{1,0:T(8,128)(2,1)}, u32[]{:S(2)}) copy-start(bf16[16,1024]{1,0:T(8,128)(2,1)} %ref0.1) | copy-start | bytes 98308
  3.4 24.9 %all-to-all-start = ((bf16[16,256,128]{2,1,0:T(8,128)(2,1)}), bf16[16,256,128]{2,1,0:T(8,128)(2,1)S(1)}, u32[]{:S(2)}, u32[]{:S(2)}) async-start(bf16[16,256,128]{2,1,0:T(8,128)(2,1)} %get-tuple-element.31), calls=%async_computation | async-start | bytes 2097152 | tf_op jit(solution)/shard_map/all_to_all | solution.py:372
  10.6 11.7 %collective-permute-start.4 = (bf16[16,1024]{1,0:T(8,128)(2,1)S(1)}, bf16[16,1024]{1,0:T(8,128)(2,1)S(1)}, u32[]{:S(2)}, u32[]{:S(2)}) collective-permute-start(bf16[16,1024]{1,0:T(8,128)(2,1)S(1)} %copy-done.1), channel_id=1, source_target_pairs={{0,4},{1,5},{2,6},{3,7},{4,0},{5,1},{6,2},{7,3},{8,12},{9,13},{10,... | collective-permute-start | bytes 98312 | tf_op jit(solution)/shard_map/ppermute | solution.py:354
  14.0 8.3 %collective-permute-start.3 = (bf16[16,1024]{1,0:T(8,128)(2,1)S(1)}, bf16[16,1024]{1,0:T(8,128)(2,1)S(1)}, u32[]{:S(2)}, u32[]{:S(2)}) collective-permute-start(bf16[16,1024]{1,0:T(8,128)(2,1)S(1)} %copy-done.1), channel_id=1, source_target_pairs={{0,2},{1,3},{2,0},{3,1},{4,6},{5,7},{6,4},{7,5},{8,10},{9,11},{10,... | collective-permute-start | bytes 98312 | tf_op jit(solution)/shard_map/ppermute | solution.py:354
  15.9 6.5 %collective-permute-start.5 = (bf16[16,1024]{1,0:T(8,128)(2,1)S(1)}, bf16[16,1024]{1,0:T(8,128)(2,1)S(1)}, u32[]{:S(2)}, u32[]{:S(2)}) collective-permute-start(bf16[16,1024]{1,0:T(8,128)(2,1)S(1)} %copy-done.1), channel_id=1, source_target_pairs={{0,6},{1,7},{2,4},{3,5},{4,2},{5,3},{6,0},{7,1},{8,14},{9,15},{10,... | collective-permute-start | bytes 98312 | tf_op jit(solution)/shard_map/ppermute | solution.py:354
  15.9 11.2 %collective-permute-start = (bf16[2,2,128,128]{3,2,1,0:T(8,128)(2,1)S(1)}, bf16[2,2,128,128]{3,2,1,0:T(8,128)(2,1)S(1)}, u32[]{:S(2)}, u32[]{:S(2)}) collective-permute-start(bf16[2,2,128,128]{3,2,1,0:T(8,128)(2,1)S(1)} %get-tuple-element.28.own_ref.kv_ref), channel_id=1, source_target_pairs={{0,32},{32,0},{1,33},{33,1},{2,34},{34,2},{3,35},{35,3},{4,36},{36... | collective-permute-start | bytes 393224 | tf_op jit(solution)/shard_map/ppermute | solution.py:375
  22.4 5.9 %collective-permute-start.6 = (bf16[4,16,1024]{2,1,0:T(8,128)(2,1)S(1)}, bf16[4,16,1024]{2,1,0:T(8,128)(2,1)S(1)}, u32[]{:S(2)}, u32[]{:S(2)}) collective-permute-start(bf16[4,16,1024]{2,1,0:T(8,128)(2,1)S(1)} %pad_maximum_fusion), channel_id=1, source_target_pairs={{0,1},{1,0},{2,3},{3,2},{4,5},{5,4},{6,7},{7,6},{8,9},{9,8},{10,11... | collective-permute-start | bytes 393224 | tf_op jit(solution)/shard_map/ppermute | solution.py:354
  28.3 13.4 %copy-start = (bf16[128,1024]{1,0:T(8,128)(2,1)S(1)}, bf16[128,1024]{1,0:T(8,128)(2,1)}, u32[]{:S(2)}) copy-start(bf16[128,1024]{1,0:T(8,128)(2,1)} %weight_ref.3) | copy-start | bytes 786436
  28.3 25.8 %all-to-all-start.1 = ((bf16[16,256,128]{2,1,0:T(8,128)(2,1)}), bf16[16,256,128]{2,1,0:T(8,128)(2,1)S(1)}, u32[]{:S(2)}, u32[]{:S(2)}) async-start(bf16[16,256,128]{2,1,0:T(8,128)(2,1)} %get-tuple-element.33), calls=%async_computation.1 | async-start | bytes 2097152 | tf_op jit(solution)/shard_map/all_to_all | solution.py:372
  35.7 18.4 %collective-permute-start.1 = (bf16[2,2,128,128]{3,2,1,0:T(8,128)(2,1)S(1)}, bf16[2,2,128,128]{3,2,1,0:T(8,128)(2,1)S(1)}, u32[]{:S(2)}, u32[]{:S(2)}) collective-permute-start(bf16[2,2,128,128]{3,2,1,0:T(8,128)(2,1)S(1)} %get-tuple-element.29), channel_id=1, source_target_pairs={{0,8},{8,16},{16,24},{24,64},{32,40},{40,48},{48,56},{56,32},{64,7... | collective-permute-start | bytes 393224 | tf_op jit(solution)/shard_map/ppermute | solution.py:425
  39.1 15.0 %copy-start.2 = (bf16[2,128,128]{2,1,0:T(8,128)(2,1)S(1)}, bf16[2,128,128]{2,1,0:T(8,128)(2,1)}, u32[]{:S(2)}) copy-start(bf16[2,128,128]{2,1,0:T(8,128)(2,1)} %q_ref.1) | copy-start | bytes 196612
  39.1 15.0 %collective-permute-start.2 = (bf16[2,2,128,128]{3,2,1,0:T(8,128)(2,1)S(1)}, bf16[2,2,128,128]{3,2,1,0:T(8,128)(2,1)S(1)}, u32[]{:S(2)}, u32[]{:S(2)}) collective-permute-start(bf16[2,2,128,128]{3,2,1,0:T(8,128)(2,1)S(1)} %get-tuple-element.30), channel_id=1, source_target_pairs={{0,24},{8,0},{16,8},{24,16},{40,32},{48,40},{56,48},{64,88},{72,64... | collective-permute-start | bytes 393224 | tf_op jit(solution)/shard_map/ppermute | solution.py:426
  41.9 12.1 %collective-permute-start.7 = (bf16[128,128]{1,0:T(8,128)(2,1)S(1)}, bf16[128,128]{1,0:T(8,128)(2,1)S(1)}, u32[]{:S(2)}, u32[]{:S(2)}) collective-permute-start(bf16[128,128]{1,0:T(8,128)(2,1)S(1)} %context_grad.1.grad_ref), channel_id=1, source_target_pairs={{0,248},{8,240},{16,232},{24,224},{32,216},{40,208},{48,200},{56,1... | collective-permute-start | bytes 98312 | tf_op jit(solution)/shard_map/ppermute | solution.py:438
  62.0 21.2 %all-to-all-start.2 = ((bf16[16,256,128]{2,1,0:T(8,128)(2,1)}), bf16[16,256,128]{2,1,0:T(8,128)(2,1)S(1)}, u32[]{:S(2)}, u32[]{:S(2)}) async-start(bf16[16,256,128]{2,1,0:T(8,128)(2,1)} %get-tuple-element.39), calls=%async_computation.2 | async-start | bytes 2097152 | tf_op jit(solution)/shard_map/all_to_all | solution.py:372
  68.7 14.6 %collective-permute-start.10 = (bf16[128,128]{1,0:T(8,128)(2,1)}, bf16[128,128]{1,0:T(8,128)(2,1)S(1)}, u32[]{:S(2)}, u32[]{:S(2)}) collective-permute-start(bf16[128,128]{1,0:T(8,128)(2,1)} %get-tuple-element.40), channel_id=1, source_target_pairs={{0,248},{8,240},{16,232},{24,224},{32,216},{40,208},{48,200},{56,1... | collective-permute-start | bytes 98312 | tf_op jit(solution)/shard_map/ppermute | solution.py:456
  76.8 12.8 %collective-permute-start.8 = (bf16[2,2,128,128]{3,2,1,0:T(8,128)(2,1)S(1)}, bf16[2,2,128,128]{3,2,1,0:T(8,128)(2,1)S(1)}, u32[]{:S(2)}, u32[]{:S(2)}) collective-permute-start(bf16[2,2,128,128]{3,2,1,0:T(8,128)(2,1)S(1)} %get-tuple-element.36), channel_id=1, source_target_pairs={{24,0},{0,8},{8,16},{16,24},{32,40},{40,48},{48,56},{88,64},{64,72... | collective-permute-start | bytes 393224 | tf_op jit(solution)/shard_map/ppermute | solution.py:459
  81.3 11.2 %collective-permute-start.9 = (bf16[2,2,128,128]{3,2,1,0:T(8,128)(2,1)S(1)}, bf16[2,2,128,128]{3,2,1,0:T(8,128)(2,1)S(1)}, u32[]{:S(2)}, u32[]{:S(2)}) collective-permute-start(bf16[2,2,128,128]{3,2,1,0:T(8,128)(2,1)S(1)} %get-tuple-element.37), channel_id=1, source_target_pairs={{8,0},{16,8},{24,16},{64,24},{40,32},{48,40},{56,48},{32,56},{72,6... | collective-permute-start | bytes 393224 | tf_op jit(solution)/shard_map/ppermute | solution.py:460
  83.3 26.3 %all-to-all-start.3 = ((bf16[16,256,128]{2,1,0:T(8,128)(2,1)}), bf16[16,256,128]{2,1,0:T(8,128)(2,1)S(1)}, u32[]{:S(2)}, u32[]{:S(2)}) async-start(bf16[16,256,128]{2,1,0:T(8,128)(2,1)} %get-tuple-element.49), calls=%async_computation.3 | async-start | bytes 2097152 | tf_op jit(solution)/shard_map/all_to_all | solution.py:372
  93.3 1.6 %collective-permute-start.11 = (bf16[4,16,1024]{2,1,0:T(8,128)(2,1)S(1)}, bf16[4,16,1024]{2,1,0:T(8,128)(2,1)S(1)}, u32[]{:S(2)}, u32[]{:S(2)}) collective-permute-start(bf16[4,16,1024]{2,1,0:T(8,128)(2,1)S(1)} %get-tuple-element.45), channel_id=1, source_target_pairs={{0,1},{1,0},{2,3},{3,2},{4,5},{5,4},{6,7},{7,6},{8,9},{9,8},{10,11... | collective-permute-start | bytes 393224 | tf_op jit(solution)/shard_map/ppermute | solution.py:354
  95.0 9.7 %copy-start.3 = (bf16[16,1024]{1,0:T(8,128)(2,1)S(1)}, bf16[16,1024]{1,0:T(8,128)(2,1)}, u32[]{:S(2)}) copy-start(bf16[16,1024]{1,0:T(8,128)(2,1)} %param.9) | copy-start | bytes 98308
  95.0 5.0 %collective-permute-start.12 = (bf16[16,1024]{1,0:T(8,128)(2,1)S(1)}, bf16[16,1024]{1,0:T(8,128)(2,1)S(1)}, u32[]{:S(2)}, u32[]{:S(2)}) collective-permute-start(bf16[16,1024]{1,0:T(8,128)(2,1)S(1)} %get-tuple-element.54), channel_id=1, source_target_pairs={{0,2},{1,3},{2,0},{3,1},{4,6},{5,7},{6,4},{7,5},{8,10},{9,11},{10,... | collective-permute-start | bytes 98312 | tf_op jit(solution)/shard_map/ppermute | solution.py:354
  95.3 5.8 %collective-permute-start.14 = (bf16[16,1024]{1,0:T(8,128)(2,1)S(1)}, bf16[16,1024]{1,0:T(8,128)(2,1)S(1)}, u32[]{:S(2)}, u32[]{:S(2)}) collective-permute-start(bf16[16,1024]{1,0:T(8,128)(2,1)S(1)} %get-tuple-element.55), channel_id=1, source_target_pairs={{0,6},{1,7},{2,4},{3,5},{4,2},{5,3},{6,0},{7,1},{8,14},{9,15},{10,... | collective-permute-start | bytes 98312 | tf_op jit(solution)/shard_map/ppermute | solution.py:354
  96.2 8.4 %collective-permute-start.13 = (bf16[16,1024]{1,0:T(8,128)(2,1)S(1)}, bf16[16,1024]{1,0:T(8,128)(2,1)S(1)}, u32[]{:S(2)}, u32[]{:S(2)}) collective-permute-start(bf16[16,1024]{1,0:T(8,128)(2,1)S(1)} %get-tuple-element.56), channel_id=1, source_target_pairs={{0,4},{1,5},{2,6},{3,7},{4,0},{5,1},{6,2},{7,3},{8,12},{9,13},{10,... | collective-permute-start | bytes 98312 | tf_op jit(solution)/shard_map/ppermute | solution.py:354
  98.6 11.0 %collective-permute-start.15 = (bf16[2,2,128,128]{3,2,1,0:T(8,128)(2,1)S(1)}, bf16[2,2,128,128]{3,2,1,0:T(8,128)(2,1)S(1)}, u32[]{:S(2)}, u32[]{:S(2)}) collective-permute-start(bf16[2,2,128,128]{3,2,1,0:T(8,128)(2,1)S(1)} %combine_partner.1), channel_id=1, source_target_pairs={{0,32},{32,0},{1,33},{33,1},{2,34},{34,2},{3,35},{35,3},{4,36},{36... | collective-permute-start | bytes 393224 | tf_op jit(solution)/shard_map/ppermute | solution.py:375

commit v9 on v8

--- a/solution.py
+++ b/solution.py
@@ -458,23 +458,6 @@
     returned_partner = plane_a2a(partner_grads)
     from_prev_grad = lax.ppermute(after, SEQ, [(b, a) for a, b in down])
     from_next_grad = lax.ppermute(before, SEQ, [(b, a) for a, b in up])
-    here_grads, returned_partner, context_back = lax.optimization_barrier(
-        (here_grads, returned_partner, context_back)
-    )
-    returned_own = plane_a2a(here_grads)
-    other = pl.pallas_call(
-        combine_partner_kernel,
-        out_shape=shape(both),
-        in_specs=[vmem()] * 4,
-        out_specs=vmem(),
-        scratch_shapes=[asked],
-        cost_estimate=cost(2_000_000, 1_500_000),
-        compiler_params=pltpu.CompilerParams(vmem_limit_bytes=LIMIT),
-        name="combine_partner",
-    )(far_blocks, from_prev_grad, from_next_grad, returned_partner)
-    other, context_back = lax.optimization_barrier((other, context_back))
-    other = z_swap(other)
-
     even, odd = pl.pallas_call(
         project_kernel,
         out_shape=(
@@ -488,6 +471,21 @@
         compiler_params=pltpu.CompilerParams(vmem_limit_bytes=LIMIT),
         name="project",
     )(context_fwd, context_back, out_weight)
+    here_grads, returned_partner, even, odd = lax.optimization_barrier((here_grads, returned_partner, even, odd))
+    returned_own = plane_a2a(here_grads)
+    other = pl.pallas_call(
+        combine_partner_kernel,
+        out_shape=shape(both),
+        in_specs=[vmem()] * 4,
+        out_specs=vmem(),
+        scratch_shapes=[asked],
+        cost_estimate=cost(2_000_000, 1_500_000),
+        compiler_params=pltpu.CompilerParams(vmem_limit_bytes=LIMIT),
+        name="combine_partner",
+    )(far_blocks, from_prev_grad, from_next_grad, returned_partner)
+    other, odd = lax.optimization_barrier((other, odd))
+    other = z_swap(other)
+
     held = even + swap(odd, 1).astype(f32)
     parts = [swap(held[k].astype(bf16), 2 * k) for k in range(1, tp_count // 2)]
     total = residual.astype(f32) + held[0]

time: 112 us -> 111 us (level)
  no operation moved by 1% of the time
where the time goes in v9:
time: 111 us
  starting transfers between devices  74.1 us (67%)
  waiting for transfers between devices  21.1 us (19%)
  Pallas kernels  13.2 us (12%)
    all_to_all x4, starting transfers between devices, plane_a2a(): lax.all_to_all(x, ('x', 'y'), split_axis=0, concat_axis=0, tiled=True)  27.5 us
    ppermute x1, starting transfers between devices, per_device(): mirrored = lax.ppermute(grad_context, SEQ, mirror)  9.33 us
    ppermute x8, starting transfers between devices, swap(): return lax.ppermute(x, 'tp', [(i, i ^ bit) for i in range(count)])  9.21 us
    ppermute x2, waiting for transfers between devices, z_swap(): return lax.ppermute(x, 'zh', [(i, nz - 1 - i) for i in range(nz)])  8.8 us
    ppermute x1, starting transfers between devices, per_device(): context_back = lax.ppermute(context_rev, SEQ, mirror)  8.08 us
    pallas_call x1, Pallas kernels, per_device(): pl.pallas_call(attend_kernel, out_shape=(square, square, shape((2, tok_ro...  7.91 us
    ppermute x2, starting transfers between devices, z_swap(): return lax.ppermute(x, 'zh', [(i, nz - 1 - i) for i in range(nz)])  7.53 us
    ppermute x8, waiting for transfers between devices, swap(): return lax.ppermute(x, 'tp', [(i, i ^ bit) for i in range(count)])  6.44 us
  transfers between devices with their start and end apart: 20, of which 8 were waited for; matrix products, arithmetic and copies ran while one was open for 1% of the time, Pallas kernels for 2%

profile of v9, /device:TPU:24, one launch (start us, length us, event | category | flops | bytes accessed | tf_op | source)
XLA Modules:
  0.0 110.7 jit_solution(11567982565943772917)
XLA Ops:
  0.6 0.8 copy.14.fb_ref
  1.4 2.0 %pack_own.1 = (bf16[16,256,128]{2,1,0:T(8,128)(2,1)}, bf16[2,2,128,128]{3,2,1,0:T(8,128)(2,1)S(1)}) custom-call(s32[32,24]{1,0:T(8,128)S(1)} %copy.14.fb_ref, bf16[2,128,128]{2,1,0:T(8,128)(2,1)} %key_ref.1, bf16[2,128,128]{2,1,0:T(8,128)(2,1)} %value_ref.1), custom_call_target="tpu_custom_call" | custom-call | flops 500000 | bytes 1500000 | tf_op jit(solution)/shard_map/pack_own/pallas_call | solution.py:379
  3.4 7.2 %all-to-all-start = ((bf16[16,256,128]{2,1,0:T(8,128)(2,1)}), bf16[16,256,128]{2,1,0:T(8,128)(2,1)S(1)}, u32[]{:S(2)}, u32[]{:S(2)}) async-start(bf16[16,256,128]{2,1,0:T(8,128)(2,1)} %get-tuple-element.32), calls=%async_computation | async-start | bytes 2097152 | tf_op jit(solution)/shard_map/all_to_all | solution.py:372
  10.6 3.4 %collective-permute-start.4 = (bf16[16,1024]{1,0:T(8,128)(2,1)S(1)}, bf16[16,1024]{1,0:T(8,128)(2,1)S(1)}, u32[]{:S(2)}, u32[]{:S(2)}) collective-permute-start(bf16[16,1024]{1,0:T(8,128)(2,1)S(1)} %copy-done.1), channel_id=1, source_target_pairs={{0,4},{1,5},{2,6},{3,7},{4,0},{5,1},{6,2},{7,3},{8,12},{9,13},{10,... | collective-permute-start | bytes 98312 | tf_op jit(solution)/shard_map/ppermute | solution.py:354
  14.0 1.9 %collective-permute-start.3 = (bf16[16,1024]{1,0:T(8,128)(2,1)S(1)}, bf16[16,1024]{1,0:T(8,128)(2,1)S(1)}, u32[]{:S(2)}, u32[]{:S(2)}) collective-permute-start(bf16[16,1024]{1,0:T(8,128)(2,1)S(1)} %copy-done.1), channel_id=1, source_target_pairs={{0,2},{1,3},{2,0},{3,1},{4,6},{5,7},{6,4},{7,5},{8,10},{9,11},{10,... | collective-permute-start | bytes 98312 | tf_op jit(solution)/shard_map/ppermute | solution.py:354
  15.9 6.4 %collective-permute-start = (bf16[2,2,128,128]{3,2,1,0:T(8,128)(2,1)S(1)}, bf16[2,2,128,128]{3,2,1,0:T(8,128)(2,1)S(1)}, u32[]{:S(2)}, u32[]{:S(2)}) collective-permute-start(bf16[2,2,128,128]{3,2,1,0:T(8,128)(2,1)S(1)} %get-tuple-element.29.own_ref.kv_ref), channel_id=1, source_target_pairs={{0,32},{32,0},{1,33},{33,1},{2,34},{34,2},{3,35},{35,3},{4,36},{36... | collective-permute-start | bytes 393224 | tf_op jit(solution)/shard_map/ppermute | solution.py:375
  22.5 4.6 %collective-permute-done.partner_ref = bf16[2,2,128,128]{3,2,1,0:T(8,128)(2,1)S(1)} collective-permute-done((bf16[2,2,128,128]{3,2,1,0:T(8,128)(2,1)S(1)}, bf16[2,2,128,128]{3,2,1,0:T(8,128)(2,1)S(1)}, u32[]{:S(2)}, u32[]{:S(2)}) %collective-permute-start) | collective-permute-done | bytes 131104 | tf_op jit(solution)/shard_map/ppermute | solution.py:375
  27.1 1.1 %pack_partner.1 = (bf16[16,256,128]{2,1,0:T(8,128)(2,1)}, bf16[2,2,128,128]{3,2,1,0:T(8,128)(2,1)S(1)}, bf16[2,2,128,128]{3,2,1,0:T(8,128)(2,1)S(1)}) custom-call(s32[32,24]{1,0:T(8,128)S(1)} %copy.14.fb_ref, bf16[2,2,128,128]{3,2,1,0:T(8,128)(2,1)S(1)} %get-tuple-element.29.own_ref.kv_ref, bf16[2,2,128,128]{3,2,1,0:T(8,128)(2,1)S(1)} %collective-permute-done.partner_ref), custom_call_target="tpu_custom_call" | custom-call | flops 500000 | bytes 1500000 | tf_op jit(solution)/shard_map/pack_partner/pallas_call | solution.py:391
  28.3 7.4 %all-to-all-start.1 = ((bf16[16,256,128]{2,1,0:T(8,128)(2,1)}), bf16[16,256,128]{2,1,0:T(8,128)(2,1)S(1)}, u32[]{:S(2)}, u32[]{:S(2)}) async-start(bf16[16,256,128]{2,1,0:T(8,128)(2,1)} %get-tuple-element.34), calls=%async_computation.1 | async-start | bytes 2097152 | tf_op jit(solution)/shard_map/all_to_all | solution.py:372
  35.7 3.4 %collective-permute-start.1 = (bf16[2,2,128,128]{3,2,1,0:T(8,128)(2,1)S(1)}, bf16[2,2,128,128]{3,2,1,0:T(8,128)(2,1)S(1)}, u32[]{:S(2)}, u32[]{:S(2)}) collective-permute-start(bf16[2,2,128,128]{3,2,1,0:T(8,128)(2,1)S(1)} %get-tuple-element.30), channel_id=1, source_target_pairs={{0,8},{8,16},{16,24},{24,64},{32,40},{40,48},{48,56},{56,32},{64,7... | collective-permute-start | bytes 393224 | tf_op jit(solution)/shard_map/ppermute | solution.py:425
  39.1 2.6 %collective-permute-start.2 = (bf16[2,2,128,128]{3,2,1,0:T(8,128)(2,1)S(1)}, bf16[2,2,128,128]{3,2,1,0:T(8,128)(2,1)S(1)}, u32[]{:S(2)}, u32[]{:S(2)}) collective-permute-start(bf16[2,2,128,128]{3,2,1,0:T(8,128)(2,1)S(1)} %get-tuple-element.31), channel_id=1, source_target_pairs={{0,24},{8,0},{16,8},{24,16},{40,32},{48,40},{56,48},{64,88},{72,64... | collective-permute-start | bytes 393224 | tf_op jit(solution)/shard_map/ppermute | solution.py:426
  41.7 0.2 context_grad.1.grad_ref
  41.9 9.3 %collective-permute-start.7 = (bf16[128,128]{1,0:T(8,128)(2,1)S(1)}, bf16[128,128]{1,0:T(8,128)(2,1)S(1)}, u32[]{:S(2)}, u32[]{:S(2)}) collective-permute-start(bf16[128,128]{1,0:T(8,128)(2,1)S(1)} %context_grad.1.grad_ref), channel_id=1, source_target_pairs={{0,248},{8,240},{16,232},{24,224},{32,216},{40,208},{48,200},{56,1... | collective-permute-start | bytes 98312 | tf_op jit(solution)/shard_map/ppermute | solution.py:438
  51.3 2.8 %collective-permute-done.7.mirrored_ref = bf16[128,128]{1,0:T(8,128)(2,1)S(1)} collective-permute-done((bf16[128,128]{1,0:T(8,128)(2,1)S(1)}, bf16[128,128]{1,0:T(8,128)(2,1)S(1)}, u32[]{:S(2)}, u32[]{:S(2)}) %collective-permute-start.7) | collective-permute-done | bytes 32800 | tf_op jit(solution)/shard_map/ppermute | solution.py:438
  54.1 7.9 %attend.1 = (bf16[128,128]{1,0:T(8,128)(2,1)S(1)}, bf16[128,128]{1,0:T(8,128)(2,1)S(1)}, bf16[2,128,128]{2,1,0:T(8,128)(2,1)}, f32[2,2,128,128]{3,2,1,0:T(8,128)...) custom-call(s32[32,24]{1,0:T(8,128)S(1)} %copy.14.fb_ref, ...), custom_call_target="tpu_custom_call" | custom-call | flops 4000000000 | bytes 8000000 | tf_op jit(solution)/shard_map/attend/pallas_call | solution.py:442
  62.0 6.6 %all-to-all-start.2 = ((bf16[16,256,128]{2,1,0:T(8,128)(2,1)}), bf16[16,256,128]{2,1,0:T(8,128)(2,1)S(1)}, u32[]{:S(2)}, u32[]{:S(2)}) async-start(bf16[16,256,128]{2,1,0:T(8,128)(2,1)} %get-tuple-element.37), calls=%async_computation.2 | async-start | bytes 2097152 | tf_op jit(solution)/shard_map/all_to_all | solution.py:372
  68.7 8.1 %collective-permute-start.8 = (bf16[128,128]{1,0:T(8,128)(2,1)S(1)}, bf16[128,128]{1,0:T(8,128)(2,1)S(1)}, u32[]{:S(2)}, u32[]{:S(2)}) collective-permute-start(bf16[128,128]{1,0:T(8,128)(2,1)S(1)} %get-tuple-element.39), channel_id=1, source_target_pairs={{0,248},{8,240},{16,232},{24,224},{32,216},{40,208},{48,200},{56,1... | collective-permute-start | bytes 98312 | tf_op jit(solution)/shard_map/ppermute | solution.py:456
  76.7 4.6 %collective-permute-start.9 = (bf16[2,2,128,128]{3,2,1,0:T(8,128)(2,1)S(1)}, bf16[2,2,128,128]{3,2,1,0:T(8,128)(2,1)S(1)}, u32[]{:S(2)}, u32[]{:S(2)}) collective-permute-start(bf16[2,2,128,128]{3,2,1,0:T(8,128)(2,1)S(1)} %get-tuple-element.43), channel_id=1, source_target_pairs={{24,0},{0,8},{8,16},{16,24},{32,40},{40,48},{48,56},{88,64},{64,72... | collective-permute-start | bytes 393224 | tf_op jit(solution)/shard_map/ppermute | solution.py:459
  81.3 1.9 %collective-permute-start.10 = (bf16[2,2,128,128]{3,2,1,0:T(8,128)(2,1)S(1)}, bf16[2,2,128,128]{3,2,1,0:T(8,128)(2,1)S(1)}, u32[]{:S(2)}, u32[]{:S(2)}) collective-permute-start(bf16[2,2,128,128]{3,2,1,0:T(8,128)(2,1)S(1)} %get-tuple-element.44), channel_id=1, source_target_pairs={{8,0},{16,8},{24,16},{64,24},{40,32},{48,40},{56,48},{32,56},{72,6... | collective-permute-start | bytes 393224 | tf_op jit(solution)/shard_map/ppermute | solution.py:460
  83.5 6.3 %all-to-all-start.3 = ((bf16[16,256,128]{2,1,0:T(8,128)(2,1)}), bf16[16,256,128]{2,1,0:T(8,128)(2,1)S(1)}, u32[]{:S(2)}, u32[]{:S(2)}) async-start(bf16[16,256,128]{2,1,0:T(8,128)(2,1)} %get-tuple-element.51), calls=%async_computation.3 | async-start | bytes 2097152 | tf_op jit(solution)/shard_map/all_to_all | solution.py:372
  89.8 3.0 %collective-permute-done.10.next_ref = bf16[2,2,128,128]{3,2,1,0:T(8,128)(2,1)S(1)} collective-permute-done((bf16[2,2,128,128]{3,2,1,0:T(8,128)(2,1)S(1)}, bf16[2,2,128,128]{3,2,1,0:T(8,128)(2,1)S(1)}, u32[]{:S(2)}, u32[]{:S(2)}) %collective-permute-start.10) | collective-permute-done | bytes 131104 | tf_op jit(solution)/shard_map/ppermute | solution.py:460
  92.8 0.5 combine_partner.1
  93.3 0.3 collective-permute-start.11
  93.6 1.3 %collective-permute-done.11 = bf16[4,16,1024]{2,1,0:T(8,128)(2,1)S(1)} collective-permute-done((bf16[4,16,1024]{2,1,0:T(8,128)(2,1)S(1)}, bf16[4,16,1024]{2,1,0:T(8,128)(2,1)S(1)}, u32[]{:S(2)}, u32[]{:S(2)}) %collective-permute-start.11) | collective-permute-done | bytes 131104 | tf_op jit(solution)/shard_map/ppermute | solution.py:354
  95.1 1.3 %collective-permute-start.14 = (bf16[16,1024]{1,0:T(8,128)(2,1)S(1)}, bf16[16,1024]{1,0:T(8,128)(2,1)S(1)}, u32[]{:S(2)}, u32[]{:S(2)}) collective-permute-start(bf16[16,1024]{1,0:T(8,128)(2,1)S(1)} %get-tuple-element.57), channel_id=1, source_target_pairs={{0,6},{1,7},{2,4},{3,5},{4,2},{5,3},{6,0},{7,1},{8,14},{9,15},{10,... | collective-permute-start | bytes 98312 | tf_op jit(solution)/shard_map/ppermute | solution.py:354
  96.4 2.2 %collective-permute-start.13 = (bf16[16,1024]{1,0:T(8,128)(2,1)S(1)}, bf16[16,1024]{1,0:T(8,128)(2,1)S(1)}, u32[]{:S(2)}, u32[]{:S(2)}) collective-permute-start(bf16[16,1024]{1,0:T(8,128)(2,1)S(1)} %get-tuple-element.58), channel_id=1, source_target_pairs={{0,4},{1,5},{2,6},{3,7},{4,0},{5,1},{6,2},{7,3},{8,12},{9,13},{10,... | collective-permute-start | bytes 98312 | tf_op jit(solution)/shard_map/ppermute | solution.py:354
  98.6 1.1 %collective-permute-start.15 = (bf16[2,2,128,128]{3,2,1,0:T(8,128)(2,1)S(1)}, bf16[2,2,128,128]{3,2,1,0:T(8,128)(2,1)S(1)}, u32[]{:S(2)}, u32[]{:S(2)}) collective-permute-start(bf16[2,2,128,128]{3,2,1,0:T(8,128)(2,1)S(1)} %combine_partner.1), channel_id=1, source_target_pairs={{0,32},{32,0},{1,33},{33,1},{2,34},{34,2},{3,35},{35,3},{4,36},{36... | collective-permute-start | bytes 393224 | tf_op jit(solution)/shard_map/ppermute | solution.py:375
  99.7 1.4 %collective-permute-done.14 = bf16[16,1024]{1,0:T(8,128)(2,1)S(1)} collective-permute-done((bf16[16,1024]{1,0:T(8,128)(2,1)S(1)}, bf16[16,1024]{1,0:T(8,128)(2,1)S(1)}, u32[]{:S(2)}, u32[]{:S(2)}) %collective-permute-start.14) | collective-permute-done | bytes 32800 | tf_op jit(solution)/shard_map/ppermute | solution.py:354
  101.1 3.6 %collective-permute-done.13 = bf16[16,1024]{1,0:T(8,128)(2,1)S(1)} collective-permute-done((bf16[16,1024]{1,0:T(8,128)(2,1)S(1)}, bf16[16,1024]{1,0:T(8,128)(2,1)S(1)}, u32[]{:S(2)}, u32[]{:S(2)}) %collective-permute-start.13) | collective-permute-done | bytes 32800 | tf_op jit(solution)/shard_map/ppermute | solution.py:354
  104.7 0.6 fusion.4
  105.4 4.2 %collective-permute-done.15.other_ref = bf16[2,2,128,128]{3,2,1,0:T(8,128)(2,1)S(1)} collective-permute-done((bf16[2,2,128,128]{3,2,1,0:T(8,128)(2,1)S(1)}, bf16[2,2,128,128]{3,2,1,0:T(8,128)(2,1)S(1)}, u32[]{:S(2)}, u32[]{:S(2)}) %collective-permute-start.15) | collective-permute-done | bytes 131104 | tf_op jit(solution)/shard_map/ppermute | solution.py:375
  109.5 1.2 %combine_own.1 = (bf16[2,128,128]{2,1,0:T(8,128)(2,1)}, bf16[2,128,128]{2,1,0:T(8,128)(2,1)}) custom-call(s32[32,24]{1,0:T(8,128)S(1)} %copy.14.fb_ref, f32[2,2,128,128]{3,2,1,0:T(8,128)S(1)} %get-tuple-element.49.own_ref, bf16[2,2,128,128]{3,2,1,0:T(8,128)(2,1)S(1)} %collective-permute-done.9.prev_ref, ...), custom_call_target="tpu_custom_call" | custom-call | flops 2000000 | bytes 1500000 | tf_op jit(solution)/shard_map/combine_own/pallas_call | solution.py:496
  (28 shorter events, 0.6 us)
Async XLA Ops:
  3.4 7.2 %copy-start.1 = (bf16[16,1024]{1,0:T(8,128)(2,1)S(1)}, bf16[16,1024]{1,0:T(8,128)(2,1)}, u32[]{:S(2)}) copy-start(bf16[16,1024]{1,0:T(8,128)(2,1)} %ref0.1) | copy-start | bytes 98308
  3.4 24.9 %all-to-all-start = ((bf16[16,256,128]{2,1,0:T(8,128)(2,1)}), bf16[16,256,128]{2,1,0:T(8,128)(2,1)S(1)}, u32[]{:S(2)}, u32[]{:S(2)}) async-start(bf16[16,256,128]{2,1,0:T(8,128)(2,1)} %get-tuple-element.32), calls=%async_computation | async-start | bytes 2097152 | tf_op jit(solution)/shard_map/all_to_all | solution.py:372
  10.6 11.7 %collective-permute-start.4 = (bf16[16,1024]{1,0:T(8,128)(2,1)S(1)}, bf16[16,1024]{1,0:T(8,128)(2,1)S(1)}, u32[]{:S(2)}, u32[]{:S(2)}) collective-permute-start(bf16[16,1024]{1,0:T(8,128)(2,1)S(1)} %copy-done.1), channel_id=1, source_target_pairs={{0,4},{1,5},{2,6},{3,7},{4,0},{5,1},{6,2},{7,3},{8,12},{9,13},{10,... | collective-permute-start | bytes 98312 | tf_op jit(solution)/shard_map/ppermute | solution.py:354
  14.0 8.3 %collective-permute-start.3 = (bf16[16,1024]{1,0:T(8,128)(2,1)S(1)}, bf16[16,1024]{1,0:T(8,128)(2,1)S(1)}, u32[]{:S(2)}, u32[]{:S(2)}) collective-permute-start(bf16[16,1024]{1,0:T(8,128)(2,1)S(1)} %copy-done.1), channel_id=1, source_target_pairs={{0,2},{1,3},{2,0},{3,1},{4,6},{5,7},{6,4},{7,5},{8,10},{9,11},{10,... | collective-permute-start | bytes 98312 | tf_op jit(solution)/shard_map/ppermute | solution.py:354
  15.9 6.5 %collective-permute-start.5 = (bf16[16,1024]{1,0:T(8,128)(2,1)S(1)}, bf16[16,1024]{1,0:T(8,128)(2,1)S(1)}, u32[]{:S(2)}, u32[]{:S(2)}) collective-permute-start(bf16[16,1024]{1,0:T(8,128)(2,1)S(1)} %copy-done.1), channel_id=1, source_target_pairs={{0,6},{1,7},{2,4},{3,5},{4,2},{5,3},{6,0},{7,1},{8,14},{9,15},{10,... | collective-permute-start | bytes 98312 | tf_op jit(solution)/shard_map/ppermute | solution.py:354
  15.9 11.2 %collective-permute-start = (bf16[2,2,128,128]{3,2,1,0:T(8,128)(2,1)S(1)}, bf16[2,2,128,128]{3,2,1,0:T(8,128)(2,1)S(1)}, u32[]{:S(2)}, u32[]{:S(2)}) collective-permute-start(bf16[2,2,128,128]{3,2,1,0:T(8,128)(2,1)S(1)} %get-tuple-element.29.own_ref.kv_ref), channel_id=1, source_target_pairs={{0,32},{32,0},{1,33},{33,1},{2,34},{34,2},{3,35},{35,3},{4,36},{36... | collective-permute-start | bytes 393224 | tf_op jit(solution)/shard_map/ppermute | solution.py:375
  22.4 5.9 %collective-permute-start.6 = (bf16[4,16,1024]{2,1,0:T(8,128)(2,1)S(1)}, bf16[4,16,1024]{2,1,0:T(8,128)(2,1)S(1)}, u32[]{:S(2)}, u32[]{:S(2)}) collective-permute-start(bf16[4,16,1024]{2,1,0:T(8,128)(2,1)S(1)} %pad_maximum_fusion), channel_id=1, source_target_pairs={{0,1},{1,0},{2,3},{3,2},{4,5},{5,4},{6,7},{7,6},{8,9},{9,8},{10,11... | collective-permute-start | bytes 393224 | tf_op jit(solution)/shard_map/ppermute | solution.py:354
  28.3 13.4 %copy-start = (bf16[128,1024]{1,0:T(8,128)(2,1)S(1)}, bf16[128,1024]{1,0:T(8,128)(2,1)}, u32[]{:S(2)}) copy-start(bf16[128,1024]{1,0:T(8,128)(2,1)} %weight_ref.3) | copy-start | bytes 786436
  28.3 25.8 %all-to-all-start.1 = ((bf16[16,256,128]{2,1,0:T(8,128)(2,1)}), bf16[16,256,128]{2,1,0:T(8,128)(2,1)S(1)}, u32[]{:S(2)}, u32[]{:S(2)}) async-start(bf16[16,256,128]{2,1,0:T(8,128)(2,1)} %get-tuple-element.34), calls=%async_computation.1 | async-start | bytes 2097152 | tf_op jit(solution)/shard_map/all_to_all | solution.py:372
  35.7 18.4 %collective-permute-start.1 = (bf16[2,2,128,128]{3,2,1,0:T(8,128)(2,1)S(1)}, bf16[2,2,128,128]{3,2,1,0:T(8,128)(2,1)S(1)}, u32[]{:S(2)}, u32[]{:S(2)}) collective-permute-start(bf16[2,2,128,128]{3,2,1,0:T(8,128)(2,1)S(1)} %get-tuple-element.30), channel_id=1, source_target_pairs={{0,8},{8,16},{16,24},{24,64},{32,40},{40,48},{48,56},{56,32},{64,7... | collective-permute-start | bytes 393224 | tf_op jit(solution)/shard_map/ppermute | solution.py:425
  39.1 15.0 %copy-start.2 = (bf16[2,128,128]{2,1,0:T(8,128)(2,1)S(1)}, bf16[2,128,128]{2,1,0:T(8,128)(2,1)}, u32[]{:S(2)}) copy-start(bf16[2,128,128]{2,1,0:T(8,128)(2,1)} %q_ref.1) | copy-start | bytes 196612
  39.1 15.0 %collective-permute-start.2 = (bf16[2,2,128,128]{3,2,1,0:T(8,128)(2,1)S(1)}, bf16[2,2,128,128]{3,2,1,0:T(8,128)(2,1)S(1)}, u32[]{:S(2)}, u32[]{:S(2)}) collective-permute-start(bf16[2,2,128,128]{3,2,1,0:T(8,128)(2,1)S(1)} %get-tuple-element.31), channel_id=1, source_target_pairs={{0,24},{8,0},{16,8},{24,16},{40,32},{48,40},{56,48},{64,88},{72,64... | collective-permute-start | bytes 393224 | tf_op jit(solution)/shard_map/ppermute | solution.py:426
  41.9 12.1 %collective-permute-start.7 = (bf16[128,128]{1,0:T(8,128)(2,1)S(1)}, bf16[128,128]{1,0:T(8,128)(2,1)S(1)}, u32[]{:S(2)}, u32[]{:S(2)}) collective-permute-start(bf16[128,128]{1,0:T(8,128)(2,1)S(1)} %context_grad.1.grad_ref), channel_id=1, source_target_pairs={{0,248},{8,240},{16,232},{24,224},{32,216},{40,208},{48,200},{56,1... | collective-permute-start | bytes 98312 | tf_op jit(solution)/shard_map/ppermute | solution.py:438
  62.0 21.5 %all-to-all-start.2 = ((bf16[16,256,128]{2,1,0:T(8,128)(2,1)}), bf16[16,256,128]{2,1,0:T(8,128)(2,1)S(1)}, u32[]{:S(2)}, u32[]{:S(2)}) async-start(bf16[16,256,128]{2,1,0:T(8,128)(2,1)} %get-tuple-element.37), calls=%async_computation.2 | async-start | bytes 2097152 | tf_op jit(solution)/shard_map/all_to_all | solution.py:372
  68.7 14.6 %collective-permute-start.8 = (bf16[128,128]{1,0:T(8,128)(2,1)S(1)}, bf16[128,128]{1,0:T(8,128)(2,1)S(1)}, u32[]{:S(2)}, u32[]{:S(2)}) collective-permute-start(bf16[128,128]{1,0:T(8,128)(2,1)S(1)} %get-tuple-element.39), channel_id=1, source_target_pairs={{0,248},{8,240},{16,232},{24,224},{32,216},{40,208},{48,200},{56,1... | collective-permute-start | bytes 98312 | tf_op jit(solution)/shard_map/ppermute | solution.py:456
  76.7 13.0 %collective-permute-start.9 = (bf16[2,2,128,128]{3,2,1,0:T(8,128)(2,1)S(1)}, bf16[2,2,128,128]{3,2,1,0:T(8,128)(2,1)S(1)}, u32[]{:S(2)}, u32[]{:S(2)}) collective-permute-start(bf16[2,2,128,128]{3,2,1,0:T(8,128)(2,1)S(1)} %get-tuple-element.43), channel_id=1, source_target_pairs={{24,0},{0,8},{8,16},{16,24},{32,40},{40,48},{48,56},{88,64},{64,72... | collective-permute-start | bytes 393224 | tf_op jit(solution)/shard_map/ppermute | solution.py:459
  81.3 11.4 %collective-permute-start.10 = (bf16[2,2,128,128]{3,2,1,0:T(8,128)(2,1)S(1)}, bf16[2,2,128,128]{3,2,1,0:T(8,128)(2,1)S(1)}, u32[]{:S(2)}, u32[]{:S(2)}) collective-permute-start(bf16[2,2,128,128]{3,2,1,0:T(8,128)(2,1)S(1)} %get-tuple-element.44), channel_id=1, source_target_pairs={{8,0},{16,8},{24,16},{64,24},{40,32},{48,40},{56,48},{32,56},{72,6... | collective-permute-start | bytes 393224 | tf_op jit(solution)/shard_map/ppermute | solution.py:460
  83.5 26.0 %all-to-all-start.3 = ((bf16[16,256,128]{2,1,0:T(8,128)(2,1)}), bf16[16,256,128]{2,1,0:T(8,128)(2,1)S(1)}, u32[]{:S(2)}, u32[]{:S(2)}) async-start(bf16[16,256,128]{2,1,0:T(8,128)(2,1)} %get-tuple-element.51), calls=%async_computation.3 | async-start | bytes 2097152 | tf_op jit(solution)/shard_map/all_to_all | solution.py:372
  93.3 1.6 %collective-permute-start.11 = (bf16[4,16,1024]{2,1,0:T(8,128)(2,1)S(1)}, bf16[4,16,1024]{2,1,0:T(8,128)(2,1)S(1)}, u32[]{:S(2)}, u32[]{:S(2)}) collective-permute-start(bf16[4,16,1024]{2,1,0:T(8,128)(2,1)S(1)} %get-tuple-element.47), channel_id=1, source_target_pairs={{0,1},{1,0},{2,3},{3,2},{4,5},{5,4},{6,7},{7,6},{8,9},{9,8},{10,11... | collective-permute-start | bytes 393224 | tf_op jit(solution)/shard_map/ppermute | solution.py:354
  94.9 9.8 %copy-start.3 = (bf16[16,1024]{1,0:T(8,128)(2,1)S(1)}, bf16[16,1024]{1,0:T(8,128)(2,1)}, u32[]{:S(2)}) copy-start(bf16[16,1024]{1,0:T(8,128)(2,1)} %param.9) | copy-start | bytes 98308
  95.0 4.7 %collective-permute-start.12 = (bf16[16,1024]{1,0:T(8,128)(2,1)S(1)}, bf16[16,1024]{1,0:T(8,128)(2,1)S(1)}, u32[]{:S(2)}, u32[]{:S(2)}) collective-permute-start(bf16[16,1024]{1,0:T(8,128)(2,1)S(1)} %get-tuple-element.56), channel_id=1, source_target_pairs={{0,2},{1,3},{2,0},{3,1},{4,6},{5,7},{6,4},{7,5},{8,10},{9,11},{10,... | collective-permute-start | bytes 98312 | tf_op jit(solution)/shard_map/ppermute | solution.py:354
  95.1 6.1 %collective-permute-start.14 = (bf16[16,1024]{1,0:T(8,128)(2,1)S(1)}, bf16[16,1024]{1,0:T(8,128)(2,1)S(1)}, u32[]{:S(2)}, u32[]{:S(2)}) collective-permute-start(bf16[16,1024]{1,0:T(8,128)(2,1)S(1)} %get-tuple-element.57), channel_id=1, source_target_pairs={{0,6},{1,7},{2,4},{3,5},{4,2},{5,3},{6,0},{7,1},{8,14},{9,15},{10,... | collective-permute-start | bytes 98312 | tf_op jit(solution)/shard_map/ppermute | solution.py:354
  96.4 8.3 %collective-permute-start.13 = (bf16[16,1024]{1,0:T(8,128)(2,1)S(1)}, bf16[16,1024]{1,0:T(8,128)(2,1)S(1)}, u32[]{:S(2)}, u32[]{:S(2)}) collective-permute-start(bf16[16,1024]{1,0:T(8,128)(2,1)S(1)} %get-tuple-element.58), channel_id=1, source_target_pairs={{0,4},{1,5},{2,6},{3,7},{4,0},{5,1},{6,2},{7,3},{8,12},{9,13},{10,... | collective-permute-start | bytes 98312 | tf_op jit(solution)/shard_map/ppermute | solution.py:354
  98.6 11.0 %collective-permute-start.15 = (bf16[2,2,128,128]{3,2,1,0:T(8,128)(2,1)S(1)}, bf16[2,2,128,128]{3,2,1,0:T(8,128)(2,1)S(1)}, u32[]{:S(2)}, u32[]{:S(2)}) collective-permute-start(bf16[2,2,128,128]{3,2,1,0:T(8,128)(2,1)S(1)} %combine_partner.1), channel_id=1, source_target_pairs={{0,32},{32,0},{1,33},{33,1},{2,34},{34,2},{3,35},{35,3},{4,36},{36... | collective-permute-start | bytes 393224 | tf_op jit(solution)/shard_map/ppermute | solution.py:375

commit v10 on v9

--- a/solution.py
+++ b/solution.py
@@ -487,7 +487,9 @@
     other = z_swap(other)
 
     held = even + swap(odd, 1).astype(f32)
-    parts = [swap(held[k].astype(bf16), 2 * k) for k in range(1, tp_count // 2)]
+    pieces_out = [held[k].astype(bf16) for k in range(1, tp_count // 2)]
+    pieces_out[0], other = lax.optimization_barrier((pieces_out[0], other))
+    parts = [swap(here, 2 * k + 2) for k, here in enumerate(pieces_out)]
     total = residual.astype(f32) + held[0]
     for part_here in parts:
         total = total + part_here.astype(f32)

time: 111 us -> 112 us (level); the launches traced: 111 us -> 110 us
    ppermute x2, waiting for transfers between devices: 8.8 us -> 12.9 us  [z_swap(): return lax.ppermute(x, 'zh', [(i, nz - 1 - i) for i in range(nz)])]
    ppermute x8, waiting for transfers between devices: 6.44 us -> 2.44 us  [swap(): return lax.ppermute(x, 'tp', [(i, i ^ bit) for i in range(count)])]
  transfers between devices with their start and end apart: 20 -> 20, of which waited for: 8 -> 7; matrix products, arithmetic and copies ran while one was open for 1% -> 1% of each run, Pallas kernels for 2% -> 2%
where the time goes in v10:
time: 112 us; the launch traced here: 110 us
  starting transfers between devices  73.6 us (66%)
  waiting for transfers between devices  21.2 us (19%)
  Pallas kernels  13.2 us (12%)
    all_to_all x4, starting transfers between devices, plane_a2a(): lax.all_to_all(x, ('x', 'y'), split_axis=0, concat_axis=0, tiled=True)  27.5 us
    ppermute x2, waiting for transfers between devices, z_swap(): return lax.ppermute(x, 'zh', [(i, nz - 1 - i) for i in range(nz)])  12.9 us
    ppermute x1, starting transfers between devices, per_device(): mirrored = lax.ppermute(grad_context, SEQ, mirror)  9.33 us
    ppermute x8, starting transfers between devices, swap(): return lax.ppermute(x, 'tp', [(i, i ^ bit) for i in range(count)])  8.67 us
    ppermute x1, starting transfers between devices, per_device(): context_back = lax.ppermute(context_rev, SEQ, mirror)  8.08 us
    pallas_call x1, Pallas kernels, per_device(): pl.pallas_call(attend_kernel, out_shape=(square, square, shape((2, tok_ro...  7.91 us
    ppermute x2, starting transfers between devices, z_swap(): return lax.ppermute(x, 'zh', [(i, nz - 1 - i) for i in range(nz)])  7.62 us
    ppermute x1, starting transfers between devices, per_device(): from_prev_grad = lax.ppermute(after, SEQ, [(b, a) for a, b in down])  4.57 us
  transfers between devices with their start and end apart: 20, of which 7 were waited for; matrix products, arithmetic and copies ran while one was open for 1% of the time, Pallas kernels for 2%

profile of v10, /device:TPU:24, one launch (start us, length us, event | category | flops | bytes accessed | tf_op | source)
XLA Modules:
  0.0 110.4 jit_solution(17964263802913639313)
XLA Ops:
  0.6 0.8 copy.14.fb_ref
  1.4 2.0 %pack_own.1 = (bf16[16,256,128]{2,1,0:T(8,128)(2,1)}, bf16[2,2,128,128]{3,2,1,0:T(8,128)(2,1)S(1)}) custom-call(s32[32,24]{1,0:T(8,128)S(1)} %copy.14.fb_ref, bf16[2,128,128]{2,1,0:T(8,128)(2,1)} %key_ref.1, bf16[2,128,128]{2,1,0:T(8,128)(2,1)} %value_ref.1), custom_call_target="tpu_custom_call" | custom-call | flops 500000 | bytes 1500000 | tf_op jit(solution)/shard_map/pack_own/pallas_call | solution.py:379
  3.4 7.2 %all-to-all-start = ((bf16[16,256,128]{2,1,0:T(8,128)(2,1)}), bf16[16,256,128]{2,1,0:T(8,128)(2,1)S(1)}, u32[]{:S(2)}, u32[]{:S(2)}) async-start(bf16[16,256,128]{2,1,0:T(8,128)(2,1)} %get-tuple-element.34), calls=%async_computation | async-start | bytes 2097152 | tf_op jit(solution)/shard_map/all_to_all | solution.py:372
  10.6 3.4 %collective-permute-start.4 = (bf16[16,1024]{1,0:T(8,128)(2,1)S(1)}, bf16[16,1024]{1,0:T(8,128)(2,1)S(1)}, u32[]{:S(2)}, u32[]{:S(2)}) collective-permute-start(bf16[16,1024]{1,0:T(8,128)(2,1)S(1)} %copy-done.1), channel_id=1, source_target_pairs={{0,4},{1,5},{2,6},{3,7},{4,0},{5,1},{6,2},{7,3},{8,12},{9,13},{10,... | collective-permute-start | bytes 98312 | tf_op jit(solution)/shard_map/ppermute | solution.py:354
  14.0 1.9 %collective-permute-start.3 = (bf16[16,1024]{1,0:T(8,128)(2,1)S(1)}, bf16[16,1024]{1,0:T(8,128)(2,1)S(1)}, u32[]{:S(2)}, u32[]{:S(2)}) collective-permute-start(bf16[16,1024]{1,0:T(8,128)(2,1)S(1)} %copy-done.1), channel_id=1, source_target_pairs={{0,2},{1,3},{2,0},{3,1},{4,6},{5,7},{6,4},{7,5},{8,10},{9,11},{10,... | collective-permute-start | bytes 98312 | tf_op jit(solution)/shard_map/ppermute | solution.py:354
  15.9 6.4 %collective-permute-start = (bf16[2,2,128,128]{3,2,1,0:T(8,128)(2,1)S(1)}, bf16[2,2,128,128]{3,2,1,0:T(8,128)(2,1)S(1)}, u32[]{:S(2)}, u32[]{:S(2)}) collective-permute-start(bf16[2,2,128,128]{3,2,1,0:T(8,128)(2,1)S(1)} %get-tuple-element.31.own_ref.kv_ref), channel_id=1, source_target_pairs={{0,32},{32,0},{1,33},{33,1},{2,34},{34,2},{3,35},{35,3},{4,36},{36... | collective-permute-start | bytes 393224 | tf_op jit(solution)/shard_map/ppermute | solution.py:375
  22.5 4.6 %collective-permute-done.partner_ref = bf16[2,2,128,128]{3,2,1,0:T(8,128)(2,1)S(1)} collective-permute-done((bf16[2,2,128,128]{3,2,1,0:T(8,128)(2,1)S(1)}, bf16[2,2,128,128]{3,2,1,0:T(8,128)(2,1)S(1)}, u32[]{:S(2)}, u32[]{:S(2)}) %collective-permute-start) | collective-permute-done | bytes 131104 | tf_op jit(solution)/shard_map/ppermute | solution.py:375
  27.1 1.1 %pack_partner.1 = (bf16[16,256,128]{2,1,0:T(8,128)(2,1)}, bf16[2,2,128,128]{3,2,1,0:T(8,128)(2,1)S(1)}, bf16[2,2,128,128]{3,2,1,0:T(8,128)(2,1)S(1)}) custom-call(s32[32,24]{1,0:T(8,128)S(1)} %copy.14.fb_ref, bf16[2,2,128,128]{3,2,1,0:T(8,128)(2,1)S(1)} %get-tuple-element.31.own_ref.kv_ref, bf16[2,2,128,128]{3,2,1,0:T(8,128)(2,1)S(1)} %collective-permute-done.partner_ref), custom_call_target="tpu_custom_call" | custom-call | flops 500000 | bytes 1500000 | tf_op jit(solution)/shard_map/pack_partner/pallas_call | solution.py:391
  28.3 7.4 %all-to-all-start.1 = ((bf16[16,256,128]{2,1,0:T(8,128)(2,1)}), bf16[16,256,128]{2,1,0:T(8,128)(2,1)S(1)}, u32[]{:S(2)}, u32[]{:S(2)}) async-start(bf16[16,256,128]{2,1,0:T(8,128)(2,1)} %get-tuple-element.36), calls=%async_computation.1 | async-start | bytes 2097152 | tf_op jit(solution)/shard_map/all_to_all | solution.py:372
  35.7 3.4 %collective-permute-start.1 = (bf16[2,2,128,128]{3,2,1,0:T(8,128)(2,1)S(1)}, bf16[2,2,128,128]{3,2,1,0:T(8,128)(2,1)S(1)}, u32[]{:S(2)}, u32[]{:S(2)}) collective-permute-start(bf16[2,2,128,128]{3,2,1,0:T(8,128)(2,1)S(1)} %get-tuple-element.32), channel_id=1, source_target_pairs={{0,8},{8,16},{16,24},{24,64},{32,40},{40,48},{48,56},{56,32},{64,7... | collective-permute-start | bytes 393224 | tf_op jit(solution)/shard_map/ppermute | solution.py:425
  39.1 2.6 %collective-permute-start.2 = (bf16[2,2,128,128]{3,2,1,0:T(8,128)(2,1)S(1)}, bf16[2,2,128,128]{3,2,1,0:T(8,128)(2,1)S(1)}, u32[]{:S(2)}, u32[]{:S(2)}) collective-permute-start(bf16[2,2,128,128]{3,2,1,0:T(8,128)(2,1)S(1)} %get-tuple-element.33), channel_id=1, source_target_pairs={{0,24},{8,0},{16,8},{24,16},{40,32},{48,40},{56,48},{64,88},{72,64... | collective-permute-start | bytes 393224 | tf_op jit(solution)/shard_map/ppermute | solution.py:426
  41.7 0.2 context_grad.1.grad_ref
  41.9 9.3 %collective-permute-start.7 = (bf16[128,128]{1,0:T(8,128)(2,1)S(1)}, bf16[128,128]{1,0:T(8,128)(2,1)S(1)}, u32[]{:S(2)}, u32[]{:S(2)}) collective-permute-start(bf16[128,128]{1,0:T(8,128)(2,1)S(1)} %context_grad.1.grad_ref), channel_id=1, source_target_pairs={{0,248},{8,240},{16,232},{24,224},{32,216},{40,208},{48,200},{56,1... | collective-permute-start | bytes 98312 | tf_op jit(solution)/shard_map/ppermute | solution.py:438
  51.3 2.8 %collective-permute-done.7.mirrored_ref = bf16[128,128]{1,0:T(8,128)(2,1)S(1)} collective-permute-done((bf16[128,128]{1,0:T(8,128)(2,1)S(1)}, bf16[128,128]{1,0:T(8,128)(2,1)S(1)}, u32[]{:S(2)}, u32[]{:S(2)}) %collective-permute-start.7) | collective-permute-done | bytes 32800 | tf_op jit(solution)/shard_map/ppermute | solution.py:438
  54.1 7.9 %attend.1 = (bf16[128,128]{1,0:T(8,128)(2,1)S(1)}, bf16[128,128]{1,0:T(8,128)(2,1)S(1)}, bf16[2,128,128]{2,1,0:T(8,128)(2,1)}, f32[2,2,128,128]{3,2,1,0:T(8,128)...) custom-call(s32[32,24]{1,0:T(8,128)S(1)} %copy.14.fb_ref, ...), custom_call_target="tpu_custom_call" | custom-call | flops 4000000000 | bytes 8000000 | tf_op jit(solution)/shard_map/attend/pallas_call | solution.py:442
  62.0 6.6 %all-to-all-start.2 = ((bf16[16,256,128]{2,1,0:T(8,128)(2,1)}), bf16[16,256,128]{2,1,0:T(8,128)(2,1)S(1)}, u32[]{:S(2)}, u32[]{:S(2)}) async-start(bf16[16,256,128]{2,1,0:T(8,128)(2,1)} %get-tuple-element.39), calls=%async_computation.2 | async-start | bytes 2097152 | tf_op jit(solution)/shard_map/all_to_all | solution.py:372
  68.7 8.1 %collective-permute-start.8 = (bf16[128,128]{1,0:T(8,128)(2,1)S(1)}, bf16[128,128]{1,0:T(8,128)(2,1)S(1)}, u32[]{:S(2)}, u32[]{:S(2)}) collective-permute-start(bf16[128,128]{1,0:T(8,128)(2,1)S(1)} %get-tuple-element.41), channel_id=1, source_target_pairs={{0,248},{8,240},{16,232},{24,224},{32,216},{40,208},{48,200},{56,1... | collective-permute-start | bytes 98312 | tf_op jit(solution)/shard_map/ppermute | solution.py:456
  76.7 4.6 %collective-permute-start.9 = (bf16[2,2,128,128]{3,2,1,0:T(8,128)(2,1)S(1)}, bf16[2,2,128,128]{3,2,1,0:T(8,128)(2,1)S(1)}, u32[]{:S(2)}, u32[]{:S(2)}) collective-permute-start(bf16[2,2,128,128]{3,2,1,0:T(8,128)(2,1)S(1)} %get-tuple-element.45), channel_id=1, source_target_pairs={{24,0},{0,8},{8,16},{16,24},{32,40},{40,48},{48,56},{88,64},{64,72... | collective-permute-start | bytes 393224 | tf_op jit(solution)/shard_map/ppermute | solution.py:459
  81.3 1.9 %collective-permute-start.10 = (bf16[2,2,128,128]{3,2,1,0:T(8,128)(2,1)S(1)}, bf16[2,2,128,128]{3,2,1,0:T(8,128)(2,1)S(1)}, u32[]{:S(2)}, u32[]{:S(2)}) collective-permute-start(bf16[2,2,128,128]{3,2,1,0:T(8,128)(2,1)S(1)} %get-tuple-element.46), channel_id=1, source_target_pairs={{8,0},{16,8},{24,16},{64,24},{40,32},{48,40},{56,48},{32,56},{72,6... | collective-permute-start | bytes 393224 | tf_op jit(solution)/shard_map/ppermute | solution.py:460
  83.3 0.2 project.1
  83.5 6.3 %all-to-all-start.3 = ((bf16[16,256,128]{2,1,0:T(8,128)(2,1)}), bf16[16,256,128]{2,1,0:T(8,128)(2,1)S(1)}, u32[]{:S(2)}, u32[]{:S(2)}) async-start(bf16[16,256,128]{2,1,0:T(8,128)(2,1)} %get-tuple-element.55), calls=%async_computation.3 | async-start | bytes 2097152 | tf_op jit(solution)/shard_map/all_to_all | solution.py:372
  89.8 3.0 %collective-permute-done.10.next_ref = bf16[2,2,128,128]{3,2,1,0:T(8,128)(2,1)S(1)} collective-permute-done((bf16[2,2,128,128]{3,2,1,0:T(8,128)(2,1)S(1)}, bf16[2,2,128,128]{3,2,1,0:T(8,128)(2,1)S(1)}, u32[]{:S(2)}, u32[]{:S(2)}) %collective-permute-start.10) | collective-permute-done | bytes 131104 | tf_op jit(solution)/shard_map/ppermute | solution.py:460
  92.8 0.5 combine_partner.1
  93.3 0.3 collective-permute-start.11
  93.6 1.2 %collective-permute-start.12 = (bf16[2,2,128,128]{3,2,1,0:T(8,128)(2,1)S(1)}, bf16[2,2,128,128]{3,2,1,0:T(8,128)(2,1)S(1)}, u32[]{:S(2)}, u32[]{:S(2)}) collective-permute-start(bf16[2,2,128,128]{3,2,1,0:T(8,128)(2,1)S(1)} %combine_partner.1), channel_id=1, source_target_pairs={{0,32},{32,0},{1,33},{33,1},{2,34},{34,2},{3,35},{35,3},{4,36},{36... | collective-permute-start | bytes 393224 | tf_op jit(solution)/shard_map/ppermute | solution.py:375
  95.0 0.6 collective-permute-start.15
  95.6 0.8 collective-permute-start.14
  96.3 8.3 %collective-permute-done.12.other_ref = bf16[2,2,128,128]{3,2,1,0:T(8,128)(2,1)S(1)} collective-permute-done((bf16[2,2,128,128]{3,2,1,0:T(8,128)(2,1)S(1)}, bf16[2,2,128,128]{3,2,1,0:T(8,128)(2,1)S(1)}, u32[]{:S(2)}, u32[]{:S(2)}) %collective-permute-start.12) | collective-permute-done | bytes 131104 | tf_op jit(solution)/shard_map/ppermute | solution.py:375
  104.6 1.7 %collective-permute-start.13 = (bf16[16,1024]{1,0:T(8,128)(2,1)S(1)}, bf16[16,1024]{1,0:T(8,128)(2,1)S(1)}, u32[]{:S(2)}, u32[]{:S(2)}) collective-permute-start(bf16[16,1024]{1,0:T(8,128)(2,1)S(1)} %get-tuple-element.51), channel_id=1, source_target_pairs={{0,2},{1,3},{2,0},{3,1},{4,6},{5,7},{6,4},{7,5},{8,10},{9,11},{10,... | collective-permute-start | bytes 98312 | tf_op jit(solution)/shard_map/ppermute | solution.py:354
  106.3 2.2 %collective-permute-done.13 = bf16[16,1024]{1,0:T(8,128)(2,1)S(1)} collective-permute-done((bf16[16,1024]{1,0:T(8,128)(2,1)S(1)}, bf16[16,1024]{1,0:T(8,128)(2,1)S(1)}, u32[]{:S(2)}, u32[]{:S(2)}) %collective-permute-start.13) | collective-permute-done | bytes 32800 | tf_op jit(solution)/shard_map/ppermute | solution.py:354
  108.5 0.6 fusion.4
  109.2 1.2 %combine_own.1 = (bf16[2,128,128]{2,1,0:T(8,128)(2,1)}, bf16[2,128,128]{2,1,0:T(8,128)(2,1)}) custom-call(s32[32,24]{1,0:T(8,128)S(1)} %copy.14.fb_ref, f32[2,2,128,128]{3,2,1,0:T(8,128)S(1)} %get-tuple-element.53.own_ref, bf16[2,2,128,128]{3,2,1,0:T(8,128)(2,1)S(1)} %collective-permute-done.9.prev_ref, ...), custom_call_target="tpu_custom_call" | custom-call | flops 2000000 | bytes 1500000 | tf_op jit(solution)/shard_map/combine_own/pallas_call | solution.py:498
  (28 shorter events, 0.4 us)
Async XLA Ops:
  3.4 7.2 %copy-start.1 = (bf16[16,1024]{1,0:T(8,128)(2,1)S(1)}, bf16[16,1024]{1,0:T(8,128)(2,1)}, u32[]{:S(2)}) copy-start(bf16[16,1024]{1,0:T(8,128)(2,1)} %ref0.1) | copy-start | bytes 98308
  3.4 24.9 %all-to-all-start = ((bf16[16,256,128]{2,1,0:T(8,128)(2,1)}), bf16[16,256,128]{2,1,0:T(8,128)(2,1)S(1)}, u32[]{:S(2)}, u32[]{:S(2)}) async-start(bf16[16,256,128]{2,1,0:T(8,128)(2,1)} %get-tuple-element.34), calls=%async_computation | async-start | bytes 2097152 | tf_op jit(solution)/shard_map/all_to_all | solution.py:372
  10.6 11.7 %collective-permute-start.4 = (bf16[16,1024]{1,0:T(8,128)(2,1)S(1)}, bf16[16,1024]{1,0:T(8,128)(2,1)S(1)}, u32[]{:S(2)}, u32[]{:S(2)}) collective-permute-start(bf16[16,1024]{1,0:T(8,128)(2,1)S(1)} %copy-done.1), channel_id=1, source_target_pairs={{0,4},{1,5},{2,6},{3,7},{4,0},{5,1},{6,2},{7,3},{8,12},{9,13},{10,... | collective-permute-start | bytes 98312 | tf_op jit(solution)/shard_map/ppermute | solution.py:354
  14.0 8.3 %collective-permute-start.3 = (bf16[16,1024]{1,0:T(8,128)(2,1)S(1)}, bf16[16,1024]{1,0:T(8,128)(2,1)S(1)}, u32[]{:S(2)}, u32[]{:S(2)}) collective-permute-start(bf16[16,1024]{1,0:T(8,128)(2,1)S(1)} %copy-done.1), channel_id=1, source_target_pairs={{0,2},{1,3},{2,0},{3,1},{4,6},{5,7},{6,4},{7,5},{8,10},{9,11},{10,... | collective-permute-start | bytes 98312 | tf_op jit(solution)/shard_map/ppermute | solution.py:354
  15.9 6.5 %collective-permute-start.5 = (bf16[16,1024]{1,0:T(8,128)(2,1)S(1)}, bf16[16,1024]{1,0:T(8,128)(2,1)S(1)}, u32[]{:S(2)}, u32[]{:S(2)}) collective-permute-start(bf16[16,1024]{1,0:T(8,128)(2,1)S(1)} %copy-done.1), channel_id=1, source_target_pairs={{0,6},{1,7},{2,4},{3,5},{4,2},{5,3},{6,0},{7,1},{8,14},{9,15},{10,... | collective-permute-start | bytes 98312 | tf_op jit(solution)/shard_map/ppermute | solution.py:354
  15.9 11.2 %collective-permute-start = (bf16[2,2,128,128]{3,2,1,0:T(8,128)(2,1)S(1)}, bf16[2,2,128,128]{3,2,1,0:T(8,128)(2,1)S(1)}, u32[]{:S(2)}, u32[]{:S(2)}) collective-permute-start(bf16[2,2,128,128]{3,2,1,0:T(8,128)(2,1)S(1)} %get-tuple-element.31.own_ref.kv_ref), channel_id=1, source_target_pairs={{0,32},{32,0},{1,33},{33,1},{2,34},{34,2},{3,35},{35,3},{4,36},{36... | collective-permute-start | bytes 393224 | tf_op jit(solution)/shard_map/ppermute | solution.py:375
  22.4 5.9 %collective-permute-start.6 = (bf16[4,16,1024]{2,1,0:T(8,128)(2,1)S(1)}, bf16[4,16,1024]{2,1,0:T(8,128)(2,1)S(1)}, u32[]{:S(2)}, u32[]{:S(2)}) collective-permute-start(bf16[4,16,1024]{2,1,0:T(8,128)(2,1)S(1)} %pad_maximum_fusion), channel_id=1, source_target_pairs={{0,1},{1,0},{2,3},{3,2},{4,5},{5,4},{6,7},{7,6},{8,9},{9,8},{10,11... | collective-permute-start | bytes 393224 | tf_op jit(solution)/shard_map/ppermute | solution.py:354
  28.3 13.4 %copy-start = (bf16[128,1024]{1,0:T(8,128)(2,1)S(1)}, bf16[128,1024]{1,0:T(8,128)(2,1)}, u32[]{:S(2)}) copy-start(bf16[128,1024]{1,0:T(8,128)(2,1)} %weight_ref.3) | copy-start | bytes 786436
  28.3 25.8 %all-to-all-start.1 = ((bf16[16,256,128]{2,1,0:T(8,128)(2,1)}), bf16[16,256,128]{2,1,0:T(8,128)(2,1)S(1)}, u32[]{:S(2)}, u32[]{:S(2)}) async-start(bf16[16,256,128]{2,1,0:T(8,128)(2,1)} %get-tuple-element.36), calls=%async_computation.1 | async-start | bytes 2097152 | tf_op jit(solution)/shard_map/all_to_all | solution.py:372
  35.7 18.4 %collective-permute-start.1 = (bf16[2,2,128,128]{3,2,1,0:T(8,128)(2,1)S(1)}, bf16[2,2,128,128]{3,2,1,0:T(8,128)(2,1)S(1)}, u32[]{:S(2)}, u32[]{:S(2)}) collective-permute-start(bf16[2,2,128,128]{3,2,1,0:T(8,128)(2,1)S(1)} %get-tuple-element.32), channel_id=1, source_target_pairs={{0,8},{8,16},{16,24},{24,64},{32,40},{40,48},{48,56},{56,32},{64,7... | collective-permute-start | bytes 393224 | tf_op jit(solution)/shard_map/ppermute | solution.py:425
  39.1 15.0 %copy-start.2 = (bf16[2,128,128]{2,1,0:T(8,128)(2,1)S(1)}, bf16[2,128,128]{2,1,0:T(8,128)(2,1)}, u32[]{:S(2)}) copy-start(bf16[2,128,128]{2,1,0:T(8,128)(2,1)} %q_ref.1) | copy-start | bytes 196612
  39.1 15.0 %collective-permute-start.2 = (bf16[2,2,128,128]{3,2,1,0:T(8,128)(2,1)S(1)}, bf16[2,2,128,128]{3,2,1,0:T(8,128)(2,1)S(1)}, u32[]{:S(2)}, u32[]{:S(2)}) collective-permute-start(bf16[2,2,128,128]{3,2,1,0:T(8,128)(2,1)S(1)} %get-tuple-element.33), channel_id=1, source_target_pairs={{0,24},{8,0},{16,8},{24,16},{40,32},{48,40},{56,48},{64,88},{72,64... | collective-permute-start | bytes 393224 | tf_op jit(solution)/shard_map/ppermute | solution.py:426
  41.9 12.1 %collective-permute-start.7 = (bf16[128,128]{1,0:T(8,128)(2,1)S(1)}, bf16[128,128]{1,0:T(8,128)(2,1)S(1)}, u32[]{:S(2)}, u32[]{:S(2)}) collective-permute-start(bf16[128,128]{1,0:T(8,128)(2,1)S(1)} %context_grad.1.grad_ref), channel_id=1, source_target_pairs={{0,248},{8,240},{16,232},{24,224},{32,216},{40,208},{48,200},{56,1... | collective-permute-start | bytes 98312 | tf_op jit(solution)/shard_map/ppermute | solution.py:438
  62.0 21.5 %all-to-all-start.2 = ((bf16[16,256,128]{2,1,0:T(8,128)(2,1)}), bf16[16,256,128]{2,1,0:T(8,128)(2,1)S(1)}, u32[]{:S(2)}, u32[]{:S(2)}) async-start(bf16[16,256,128]{2,1,0:T(8,128)(2,1)} %get-tuple-element.39), calls=%async_computation.2 | async-start | bytes 2097152 | tf_op jit(solution)/shard_map/all_to_all | solution.py:372
  68.7 14.6 %collective-permute-start.8 = (bf16[128,128]{1,0:T(8,128)(2,1)S(1)}, bf16[128,128]{1,0:T(8,128)(2,1)S(1)}, u32[]{:S(2)}, u32[]{:S(2)}) collective-permute-start(bf16[128,128]{1,0:T(8,128)(2,1)S(1)} %get-tuple-element.41), channel_id=1, source_target_pairs={{0,248},{8,240},{16,232},{24,224},{32,216},{40,208},{48,200},{56,1... | collective-permute-start | bytes 98312 | tf_op jit(solution)/shard_map/ppermute | solution.py:456
  76.7 13.0 %collective-permute-start.9 = (bf16[2,2,128,128]{3,2,1,0:T(8,128)(2,1)S(1)}, bf16[2,2,128,128]{3,2,1,0:T(8,128)(2,1)S(1)}, u32[]{:S(2)}, u32[]{:S(2)}) collective-permute-start(bf16[2,2,128,128]{3,2,1,0:T(8,128)(2,1)S(1)} %get-tuple-element.45), channel_id=1, source_target_pairs={{24,0},{0,8},{8,16},{16,24},{32,40},{40,48},{48,56},{88,64},{64,72... | collective-permute-start | bytes 393224 | tf_op jit(solution)/shard_map/ppermute | solution.py:459
  81.3 11.4 %collective-permute-start.10 = (bf16[2,2,128,128]{3,2,1,0:T(8,128)(2,1)S(1)}, bf16[2,2,128,128]{3,2,1,0:T(8,128)(2,1)S(1)}, u32[]{:S(2)}, u32[]{:S(2)}) collective-permute-start(bf16[2,2,128,128]{3,2,1,0:T(8,128)(2,1)S(1)} %get-tuple-element.46), channel_id=1, source_target_pairs={{8,0},{16,8},{24,16},{64,24},{40,32},{48,40},{56,48},{32,56},{72,6... | collective-permute-start | bytes 393224 | tf_op jit(solution)/shard_map/ppermute | solution.py:460
  83.5 25.7 %all-to-all-start.3 = ((bf16[16,256,128]{2,1,0:T(8,128)(2,1)}), bf16[16,256,128]{2,1,0:T(8,128)(2,1)S(1)}, u32[]{:S(2)}, u32[]{:S(2)}) async-start(bf16[16,256,128]{2,1,0:T(8,128)(2,1)} %get-tuple-element.55), calls=%async_computation.3 | async-start | bytes 2097152 | tf_op jit(solution)/shard_map/all_to_all | solution.py:372
  93.3 1.6 %collective-permute-start.11 = (bf16[4,16,1024]{2,1,0:T(8,128)(2,1)S(1)}, bf16[4,16,1024]{2,1,0:T(8,128)(2,1)S(1)}, u32[]{:S(2)}, u32[]{:S(2)}) collective-permute-start(bf16[4,16,1024]{2,1,0:T(8,128)(2,1)S(1)} %get-tuple-element.49), channel_id=1, source_target_pairs={{0,1},{1,0},{2,3},{3,2},{4,5},{5,4},{6,7},{7,6},{8,9},{9,8},{10,11... | collective-permute-start | bytes 393224 | tf_op jit(solution)/shard_map/ppermute | solution.py:354
  93.6 11.0 %collective-permute-start.12 = (bf16[2,2,128,128]{3,2,1,0:T(8,128)(2,1)S(1)}, bf16[2,2,128,128]{3,2,1,0:T(8,128)(2,1)S(1)}, u32[]{:S(2)}, u32[]{:S(2)}) collective-permute-start(bf16[2,2,128,128]{3,2,1,0:T(8,128)(2,1)S(1)} %combine_partner.1), channel_id=1, source_target_pairs={{0,32},{32,0},{1,33},{33,1},{2,34},{34,2},{3,35},{35,3},{4,36},{36... | collective-permute-start | bytes 393224 | tf_op jit(solution)/shard_map/ppermute | solution.py:375
  95.0 13.6 %copy-start.3 = (bf16[16,1024]{1,0:T(8,128)(2,1)S(1)}, bf16[16,1024]{1,0:T(8,128)(2,1)}, u32[]{:S(2)}) copy-start(bf16[16,1024]{1,0:T(8,128)(2,1)} %param.9) | copy-start | bytes 98308
  95.0 11.3 %collective-permute-start.15 = (bf16[16,1024]{1,0:T(8,128)(2,1)S(1)}, bf16[16,1024]{1,0:T(8,128)(2,1)S(1)}, u32[]{:S(2)}, u32[]{:S(2)}) collective-permute-start(bf16[16,1024]{1,0:T(8,128)(2,1)S(1)} %get-tuple-element.61), channel_id=1, source_target_pairs={{0,6},{1,7},{2,4},{3,5},{4,2},{5,3},{6,0},{7,1},{8,14},{9,15},{10,... | collective-permute-start | bytes 98312 | tf_op jit(solution)/shard_map/ppermute | solution.py:354
  95.6 10.7 %collective-permute-start.14 = (bf16[16,1024]{1,0:T(8,128)(2,1)S(1)}, bf16[16,1024]{1,0:T(8,128)(2,1)S(1)}, u32[]{:S(2)}, u32[]{:S(2)}) collective-permute-start(bf16[16,1024]{1,0:T(8,128)(2,1)S(1)} %get-tuple-element.62), channel_id=1, source_target_pairs={{0,4},{1,5},{2,6},{3,7},{4,0},{5,1},{6,2},{7,3},{8,12},{9,13},{10,... | collective-permute-start | bytes 98312 | tf_op jit(solution)/shard_map/ppermute | solution.py:354
  104.6 3.9 %collective-permute-start.13 = (bf16[16,1024]{1,0:T(8,128)(2,1)S(1)}, bf16[16,1024]{1,0:T(8,128)(2,1)S(1)}, u32[]{:S(2)}, u32[]{:S(2)}) collective-permute-start(bf16[16,1024]{1,0:T(8,128)(2,1)S(1)} %get-tuple-element.51), channel_id=1, source_target_pairs={{0,2},{1,3},{2,0},{3,1},{4,6},{5,7},{6,4},{7,5},{8,10},{9,11},{10,... | collective-permute-start | bytes 98312 | tf_op jit(solution)/shard_map/ppermute | solution.py:354

commit v11 on v8

--- a/solution.py
+++ b/solution.py
@@ -74,7 +74,7 @@
 
 
 def listed(fb_ref, t, shard, shards, zh, f):
-    entry = fb_ref[shard if t == 0 else shards - 1 - shard, f]
+    entry = fb_ref[f, shard if t == 0 else shards - 1 - shard]
     owner = lax.shift_right_arithmetic(entry, 1)
     owner = owner if t == 0 else shards - 1 - owner
     return entry >= 0, jnp.where(entry >= 0, slot_of(owner, zh), 0)
@@ -84,8 +84,8 @@
     mine = shard if t == 0 else shards - 1 - shard
     inner = fb & 1
     inner = inner + 1 if t == 0 else 2 - inner
-    hit = jnp.where(lax.shift_right_arithmetic(fb, 1) == mine, inner, 0)
-    return jnp.sum(hit, axis=1, keepdims=True)
+    hit = jnp.where(lax.shift_right_arithmetic(fb, 1) == mine, inner, 0).astype(f32)
+    return dot(hit, jnp.ones((fb.shape[0], 2 * HD), f32), TN).astype(jnp.int32)
 
 
 def asked_rows(fb_ref, asked_buf, rel):
@@ -93,7 +93,7 @@
     target = shard + rel * (1 - 2 * zh) * lax.axis_size("y")
     fb = fb_ref[...]
     for t in range(2):
-        asked_buf[t] = jnp.broadcast_to(asked_of(fb, t, target, shards), asked_buf.shape[1:])
+        asked_buf[t] = asked_of(fb, t, target, shards)
 
 
 def asked_by(asked_buf, t, reader, rows):
@@ -117,8 +117,9 @@
     return copies
 
 
-def pack_own_kernel(fb_ref, key_ref, value_ref, out_ref, kv_ref, asked_buf, out_buf, sems, in_sems):
-    loads = [
+def pack_own_kernel(fb_ref, key_ref, value_ref, out_ref, kv_ref, fb_buf, asked_buf, out_buf, sems, in_sems, fb_sem):
+    loads = [pltpu.make_async_copy(fb_ref, fb_buf, fb_sem)]
+    loads += [
         pltpu.make_async_copy(ref.at[t], kv_ref.at[t, which], in_sems.at[t, which])
         for t in range(2)
         for which, ref in ((0, key_ref), (1, value_ref))
@@ -127,7 +128,7 @@
         copy.start()
     for copy in loads:
         copy.wait()
-    for copy in pack(fb_ref, kv_ref, out_ref, asked_buf, out_buf, sems, 0):
+    for copy in pack(fb_buf, kv_ref, out_ref, asked_buf, out_buf, sems, 0):
         copy.wait()
 
 
@@ -147,7 +148,7 @@
         buf[0:128] = prev_ref[t, which]
         buf[128:256] = kv_ref[t, which]
         buf[256:384] = next_ref[t, which]
-    for f in range(fb_ref.shape[1]):
+    for f in range(fb_ref.shape[0]):
         _, slot = listed(fb_ref, t, shard, shards, zh, f)
         rows = slice(STEP + f * BLK, STEP + (f + 1) * BLK)
         here = slot < plane
@@ -215,7 +216,7 @@
     for t in range(2):
         far_buf = (far_buf0, far_buf1)[t]
         spare = far_buf.shape[0] - 1
-        to = [listed(fb_ref, t, shard, shards, zh, f) for f in range(fb_ref.shape[1])]
+        to = [listed(fb_ref, t, shard, shards, zh, f) for f in range(fb_ref.shape[0])]
         to = [jnp.where(there, slot, spare) for there, slot in to]
         stage(fb_ref, t, kv_ref, prev_ref, next_ref, (far_own, far_partner), kbuf, vbuf)
         q2 = two_heads(q_ref[t] * HD ** (-0.5))
@@ -374,18 +375,20 @@
     def z_swap(x):
         return lax.ppermute(x, "zh", [(i, nz - 1 - i) for i in range(nz)])
 
+    lists = far_blocks.T
     asked = pltpu.VMEM((2, seq_count, 2 * HD), jnp.int32)
     packed = [asked, pltpu.VMEM(slots, bf16), pltpu.SemaphoreType.DMA((nx * ny // 4,))]
-    outgoing, key_value = pl.pallas_call(
+    outgoing, key_value, near_lists = pl.pallas_call(
         pack_own_kernel,
-        out_shape=(pltpu.HBM(slots, bf16), shape(both)),
-        in_specs=[vmem(), hbm(), hbm()],
-        out_specs=(hbm(), vmem()),
-        scratch_shapes=packed + [pltpu.SemaphoreType.DMA((2, 2))],
+        out_shape=(pltpu.HBM(slots, bf16), shape(both), shape(lists.shape, jnp.int32)),
+        in_specs=[hbm()] * 3,
+        out_specs=(hbm(), vmem(), vmem()),
+        scratch_shapes=packed
+        + [pltpu.SemaphoreType.DMA((2, 2)), pltpu.SemaphoreType.DMA(())],
         cost_estimate=cost(500_000, 1_500_000),
         compiler_params=pltpu.CompilerParams(vmem_limit_bytes=LIMIT),
         name="pack_own",
-    )(far_blocks, *(pltpu.with_memory_space_constraint(x, pltpu.HBM) for x in (keys, values)))
+    )(*(pltpu.with_memory_space_constraint(x, pltpu.HBM) for x in (lists, keys, values)))
     far_own = plane_a2a(outgoing)
     partner = z_swap(key_value)
     outgoing, to_up, to_down = pl.pallas_call(
@@ -397,7 +400,7 @@
         cost_estimate=cost(500_000, 1_500_000),
         compiler_params=pltpu.CompilerParams(vmem_limit_bytes=LIMIT),
         name="pack_partner",
-    )(far_blocks, key_value, partner)
+    )(near_lists, key_value, partner)
     same_core = [cotangent] + [swap(cotangent, bit) for bit in (2, 4, 6)]
     other_core = swap(jnp.stack(same_core), 1)
     outgoing, other_core = lax.optimization_barrier((outgoing, other_core))
@@ -452,7 +455,7 @@
         compiler_params=pltpu.CompilerParams(vmem_limit_bytes=LIMIT),
         name="attend",
     )(
-        far_blocks, pltpu.with_memory_space_constraint(slopes, pltpu.HBM), queries, key_value, from_prev, from_next, far_own, far_partner, grad_context, mirrored)
+        near_lists, pltpu.with_memory_space_constraint(slopes, pltpu.HBM), queries, key_value, from_prev, from_next, far_own, far_partner, grad_context, mirrored)
     context_back = lax.ppermute(context_rev, SEQ, mirror)
 
     returned_partner = plane_a2a(partner_grads)
@@ -471,7 +474,7 @@
         cost_estimate=cost(2_000_000, 1_500_000),
         compiler_params=pltpu.CompilerParams(vmem_limit_bytes=LIMIT),
         name="combine_partner",
-    )(far_blocks, from_prev_grad, from_next_grad, returned_partner)
+    )(near_lists, from_prev_grad, from_next_grad, returned_partner)
     other, context_back = lax.optimization_barrier((other, context_back))
     other = z_swap(other)
 
@@ -504,7 +507,7 @@
         cost_estimate=cost(2_000_000, 1_500_000),
         compiler_params=pltpu.CompilerParams(vmem_limit_bytes=LIMIT),
         name="combine_own",
-    )(far_blocks, own, from_prev_grad, from_next_grad, other, returned_own)
+    )(near_lists, own, from_prev_grad, from_next_grad, other, returned_own)
     return (mixed, grad_queries, grad_keys, grad_values)
 
 

time: 112 us -> 111 us (level)
  no operation moved by 1% of the time
where the time goes in v11:
time: 111 us; the launch traced here: 110 us
  starting transfers between devices  74.3 us (67%)
  waiting for transfers between devices  20.9 us (19%)
  Pallas kernels  13.8 us (12%)
    all_to_all x4, starting transfers between devices, plane_a2a(): lax.all_to_all(x, ('x', 'y'), split_axis=0, concat_axis=0, tiled=True)  27.5 us
    ppermute x1, starting transfers between devices, per_device(): mirrored = lax.ppermute(grad_context, SEQ, mirror)  9.33 us
    ppermute x8, starting transfers between devices, swap(): return lax.ppermute(x, 'tp', [(i, i ^ bit) for i in range(count)])  9.22 us
    ppermute x2, waiting for transfers between devices, z_swap(): return lax.ppermute(x, 'zh', [(i, nz - 1 - i) for i in range(nz)])  8.88 us
    ppermute x1, starting transfers between devices, per_device(): context_back = lax.ppermute(context_rev, SEQ, mirror)  8.09 us
    pallas_call x1, Pallas kernels, per_device(): pl.pallas_call(attend_kernel, out_shape=(square, square, shape((2, tok_ro...  7.96 us
    ppermute x2, starting transfers between devices, z_swap(): return lax.ppermute(x, 'zh', [(i, nz - 1 - i) for i in range(nz)])  7.7 us
    ppermute x8, waiting for transfers between devices, swap(): return lax.ppermute(x, 'tp', [(i, i ^ bit) for i in range(count)])  6.18 us
  transfers between devices with their start and end apart: 20, of which 8 were waited for; matrix products, arithmetic and copies ran while one was open for 1% of the time, Pallas kernels for 2%

profile of v11, /device:TPU:24, one launch (start us, length us, event | category | flops | bytes accessed | tf_op | source)
XLA Modules:
  0.0 110.5 jit_solution(16781662031169753640)
XLA Ops:
  0.6 2.2 %pack_own.1 = (bf16[16,256,128]{2,1,0:T(8,128)(2,1)}, bf16[2,2,128,128]{3,2,1,0:T(8,128)(2,1)S(1)}, s32[24,32]{1,0:T(8,128)S(1)}) custom-call(s32[24,32]{1,0:T(8,128)} %bitcast.27, bf16[2,128,128]{2,1,0:T(8,128)(2,1)} %key_ref.1, bf16[2,128,128]{2,1,0:T(8,128)(2,1)} %value_ref.1), custom_call_target="tpu_custom_call" | custom-call | flops 500000 | bytes 1500000 | tf_op jit(solution)/shard_map/pack_own/pallas_call | solution.py:381
  2.8 7.2 %all-to-all-start = ((bf16[16,256,128]{2,1,0:T(8,128)(2,1)}), bf16[16,256,128]{2,1,0:T(8,128)(2,1)S(1)}, u32[]{:S(2)}, u32[]{:S(2)}) async-start(bf16[16,256,128]{2,1,0:T(8,128)(2,1)} %get-tuple-element.33), calls=%async_computation | async-start | bytes 2097152 | tf_op jit(solution)/shard_map/all_to_all | solution.py:373
  10.0 3.4 %collective-permute-start.4 = (bf16[16,1024]{1,0:T(8,128)(2,1)S(1)}, bf16[16,1024]{1,0:T(8,128)(2,1)S(1)}, u32[]{:S(2)}, u32[]{:S(2)}) collective-permute-start(bf16[16,1024]{1,0:T(8,128)(2,1)S(1)} %copy-done.1), channel_id=1, source_target_pairs={{0,4},{1,5},{2,6},{3,7},{4,0},{5,1},{6,2},{7,3},{8,12},{9,13},{10,... | collective-permute-start | bytes 98312 | tf_op jit(solution)/shard_map/ppermute | solution.py:355
  13.4 1.9 %collective-permute-start.3 = (bf16[16,1024]{1,0:T(8,128)(2,1)S(1)}, bf16[16,1024]{1,0:T(8,128)(2,1)S(1)}, u32[]{:S(2)}, u32[]{:S(2)}) collective-permute-start(bf16[16,1024]{1,0:T(8,128)(2,1)S(1)} %copy-done.1), channel_id=1, source_target_pairs={{0,2},{1,3},{2,0},{3,1},{4,6},{5,7},{6,4},{7,5},{8,10},{9,11},{10,... | collective-permute-start | bytes 98312 | tf_op jit(solution)/shard_map/ppermute | solution.py:355
  15.3 6.4 %collective-permute-start = (bf16[2,2,128,128]{3,2,1,0:T(8,128)(2,1)S(1)}, bf16[2,2,128,128]{3,2,1,0:T(8,128)(2,1)S(1)}, u32[]{:S(2)}, u32[]{:S(2)}) collective-permute-start(bf16[2,2,128,128]{3,2,1,0:T(8,128)(2,1)S(1)} %get-tuple-element.30.own_ref.kv_ref), channel_id=1, source_target_pairs={{0,32},{32,0},{1,33},{33,1},{2,34},{34,2},{3,35},{35,3},{4,36},{36... | collective-permute-start | bytes 393224 | tf_op jit(solution)/shard_map/ppermute | solution.py:376
  21.9 4.6 %collective-permute-done.partner_ref = bf16[2,2,128,128]{3,2,1,0:T(8,128)(2,1)S(1)} collective-permute-done((bf16[2,2,128,128]{3,2,1,0:T(8,128)(2,1)S(1)}, bf16[2,2,128,128]{3,2,1,0:T(8,128)(2,1)S(1)}, u32[]{:S(2)}, u32[]{:S(2)}) %collective-permute-start) | collective-permute-done | bytes 131104 | tf_op jit(solution)/shard_map/ppermute | solution.py:376
  26.5 1.3 %pack_partner.1 = (bf16[16,256,128]{2,1,0:T(8,128)(2,1)}, bf16[2,2,128,128]{3,2,1,0:T(8,128)(2,1)S(1)}, bf16[2,2,128,128]{3,2,1,0:T(8,128)(2,1)S(1)}) custom-call(s32[24,32]{1,0:T(8,128)S(1)} %get-tuple-element.29.fb_ref, bf16[2,2,128,128]{3,2,1,0:T(8,128)(2,1)S(1)} %get-tuple-element.30.own_ref.kv_ref, ...), custom_call_target="tpu_custom_call" | custom-call | flops 500000 | bytes 1500000 | tf_op jit(solution)/shard_map/pack_partner/pallas_call | solution.py:394
  27.8 7.4 %all-to-all-start.1 = ((bf16[16,256,128]{2,1,0:T(8,128)(2,1)}), bf16[16,256,128]{2,1,0:T(8,128)(2,1)S(1)}, u32[]{:S(2)}, u32[]{:S(2)}) async-start(bf16[16,256,128]{2,1,0:T(8,128)(2,1)} %get-tuple-element.35), calls=%async_computation.1 | async-start | bytes 2097152 | tf_op jit(solution)/shard_map/all_to_all | solution.py:373
  35.2 3.4 %collective-permute-start.1 = (bf16[2,2,128,128]{3,2,1,0:T(8,128)(2,1)S(1)}, bf16[2,2,128,128]{3,2,1,0:T(8,128)(2,1)S(1)}, u32[]{:S(2)}, u32[]{:S(2)}) collective-permute-start(bf16[2,2,128,128]{3,2,1,0:T(8,128)(2,1)S(1)} %get-tuple-element.31), channel_id=1, source_target_pairs={{0,8},{8,16},{16,24},{24,64},{32,40},{40,48},{48,56},{56,32},{64,7... | collective-permute-start | bytes 393224 | tf_op jit(solution)/shard_map/ppermute | solution.py:428
  38.6 2.6 %collective-permute-start.2 = (bf16[2,2,128,128]{3,2,1,0:T(8,128)(2,1)S(1)}, bf16[2,2,128,128]{3,2,1,0:T(8,128)(2,1)S(1)}, u32[]{:S(2)}, u32[]{:S(2)}) collective-permute-start(bf16[2,2,128,128]{3,2,1,0:T(8,128)(2,1)S(1)} %get-tuple-element.32), channel_id=1, source_target_pairs={{0,24},{8,0},{16,8},{24,16},{40,32},{48,40},{56,48},{64,88},{72,64... | collective-permute-start | bytes 393224 | tf_op jit(solution)/shard_map/ppermute | solution.py:429
  41.2 0.2 context_grad.1.grad_ref
  41.4 9.3 %collective-permute-start.7 = (bf16[128,128]{1,0:T(8,128)(2,1)S(1)}, bf16[128,128]{1,0:T(8,128)(2,1)S(1)}, u32[]{:S(2)}, u32[]{:S(2)}) collective-permute-start(bf16[128,128]{1,0:T(8,128)(2,1)S(1)} %context_grad.1.grad_ref), channel_id=1, source_target_pairs={{0,248},{8,240},{16,232},{24,224},{32,216},{40,208},{48,200},{56,1... | collective-permute-start | bytes 98312 | tf_op jit(solution)/shard_map/ppermute | solution.py:441
  50.7 2.8 %collective-permute-done.7.mirrored_ref = bf16[128,128]{1,0:T(8,128)(2,1)S(1)} collective-permute-done((bf16[128,128]{1,0:T(8,128)(2,1)S(1)}, bf16[128,128]{1,0:T(8,128)(2,1)S(1)}, u32[]{:S(2)}, u32[]{:S(2)}) %collective-permute-start.7) | collective-permute-done | bytes 32800 | tf_op jit(solution)/shard_map/ppermute | solution.py:441
  53.6 8.0 %attend.1 = (bf16[128,128]{1,0:T(8,128)(2,1)S(1)}, bf16[128,128]{1,0:T(8,128)(2,1)}, bf16[2,128,128]{2,1,0:T(8,128)(2,1)}, f32[2,2,128,128]{3,2,1,0:T(8,128)S(1)...) custom-call(s32[24,32]{1,0:T(8,128)S(1)} %get-tuple-element.29.fb_re, ...), custom_call_target="tpu_custom_call" | custom-call | flops 4000000000 | bytes 8000000 | tf_op jit(solution)/shard_map/attend/pallas_call | solution.py:445
  61.6 6.6 %all-to-all-start.2 = ((bf16[16,256,128]{2,1,0:T(8,128)(2,1)}), bf16[16,256,128]{2,1,0:T(8,128)(2,1)S(1)}, u32[]{:S(2)}, u32[]{:S(2)}) async-start(bf16[16,256,128]{2,1,0:T(8,128)(2,1)} %get-tuple-element.41), calls=%async_computation.2 | async-start | bytes 2097152 | tf_op jit(solution)/shard_map/all_to_all | solution.py:373
  68.2 8.1 %collective-permute-start.10 = (bf16[128,128]{1,0:T(8,128)(2,1)}, bf16[128,128]{1,0:T(8,128)(2,1)S(1)}, u32[]{:S(2)}, u32[]{:S(2)}) collective-permute-start(bf16[128,128]{1,0:T(8,128)(2,1)} %get-tuple-element.42), channel_id=1, source_target_pairs={{0,248},{8,240},{16,232},{24,224},{32,216},{40,208},{48,200},{56,1... | collective-permute-start | bytes 98312 | tf_op jit(solution)/shard_map/ppermute | solution.py:459
  76.3 4.6 %collective-permute-start.8 = (bf16[2,2,128,128]{3,2,1,0:T(8,128)(2,1)S(1)}, bf16[2,2,128,128]{3,2,1,0:T(8,128)(2,1)S(1)}, u32[]{:S(2)}, u32[]{:S(2)}) collective-permute-start(bf16[2,2,128,128]{3,2,1,0:T(8,128)(2,1)S(1)} %get-tuple-element.38), channel_id=1, source_target_pairs={{24,0},{0,8},{8,16},{16,24},{32,40},{40,48},{48,56},{88,64},{64,72... | collective-permute-start | bytes 393224 | tf_op jit(solution)/shard_map/ppermute | solution.py:462
  80.9 1.9 %collective-permute-start.9 = (bf16[2,2,128,128]{3,2,1,0:T(8,128)(2,1)S(1)}, bf16[2,2,128,128]{3,2,1,0:T(8,128)(2,1)S(1)}, u32[]{:S(2)}, u32[]{:S(2)}) collective-permute-start(bf16[2,2,128,128]{3,2,1,0:T(8,128)(2,1)S(1)} %get-tuple-element.39), channel_id=1, source_target_pairs={{8,0},{16,8},{24,16},{64,24},{40,32},{48,40},{56,48},{32,56},{72,6... | collective-permute-start | bytes 393224 | tf_op jit(solution)/shard_map/ppermute | solution.py:463
  82.8 6.3 %all-to-all-start.3 = ((bf16[16,256,128]{2,1,0:T(8,128)(2,1)}), bf16[16,256,128]{2,1,0:T(8,128)(2,1)S(1)}, u32[]{:S(2)}, u32[]{:S(2)}) async-start(bf16[16,256,128]{2,1,0:T(8,128)(2,1)} %get-tuple-element.51), calls=%async_computation.3 | async-start | bytes 2097152 | tf_op jit(solution)/shard_map/all_to_all | solution.py:373
  89.1 3.0 %collective-permute-done.9.next_ref = bf16[2,2,128,128]{3,2,1,0:T(8,128)(2,1)S(1)} collective-permute-done((bf16[2,2,128,128]{3,2,1,0:T(8,128)(2,1)S(1)}, bf16[2,2,128,128]{3,2,1,0:T(8,128)(2,1)S(1)}, u32[]{:S(2)}, u32[]{:S(2)}) %collective-permute-start.9) | collective-permute-done | bytes 131104 | tf_op jit(solution)/shard_map/ppermute | solution.py:463
  92.1 0.7 combine_partner.1
  93.0 0.3 collective-permute-start.11
  93.2 1.3 %collective-permute-done.11 = bf16[4,16,1024]{2,1,0:T(8,128)(2,1)S(1)} collective-permute-done((bf16[4,16,1024]{2,1,0:T(8,128)(2,1)S(1)}, bf16[4,16,1024]{2,1,0:T(8,128)(2,1)S(1)}, u32[]{:S(2)}, u32[]{:S(2)}) %collective-permute-start.11) | collective-permute-done | bytes 131104 | tf_op jit(solution)/shard_map/ppermute | solution.py:355
  94.6 0.4 collective-permute-start.12
  95.0 0.8 collective-permute-start.14
  95.8 2.4 %collective-permute-start.13 = (bf16[16,1024]{1,0:T(8,128)(2,1)S(1)}, bf16[16,1024]{1,0:T(8,128)(2,1)S(1)}, u32[]{:S(2)}, u32[]{:S(2)}) collective-permute-start(bf16[16,1024]{1,0:T(8,128)(2,1)S(1)} %get-tuple-element.58), channel_id=1, source_target_pairs={{0,4},{1,5},{2,6},{3,7},{4,0},{5,1},{6,2},{7,3},{8,12},{9,13},{10,... | collective-permute-start | bytes 98312 | tf_op jit(solution)/shard_map/ppermute | solution.py:355
  98.2 1.3 %collective-permute-start.15 = (bf16[2,2,128,128]{3,2,1,0:T(8,128)(2,1)S(1)}, bf16[2,2,128,128]{3,2,1,0:T(8,128)(2,1)S(1)}, u32[]{:S(2)}, u32[]{:S(2)}) collective-permute-start(bf16[2,2,128,128]{3,2,1,0:T(8,128)(2,1)S(1)} %combine_partner.1), channel_id=1, source_target_pairs={{0,32},{32,0},{1,33},{33,1},{2,34},{34,2},{3,35},{35,3},{4,36},{36... | collective-permute-start | bytes 393224 | tf_op jit(solution)/shard_map/ppermute | solution.py:376
  99.5 1.4 %collective-permute-done.14 = bf16[16,1024]{1,0:T(8,128)(2,1)S(1)} collective-permute-done((bf16[16,1024]{1,0:T(8,128)(2,1)S(1)}, bf16[16,1024]{1,0:T(8,128)(2,1)S(1)}, u32[]{:S(2)}, u32[]{:S(2)}) %collective-permute-start.14) | collective-permute-done | bytes 32800 | tf_op jit(solution)/shard_map/ppermute | solution.py:355
  101.0 3.3 %collective-permute-done.13 = bf16[16,1024]{1,0:T(8,128)(2,1)S(1)} collective-permute-done((bf16[16,1024]{1,0:T(8,128)(2,1)S(1)}, bf16[16,1024]{1,0:T(8,128)(2,1)S(1)}, u32[]{:S(2)}, u32[]{:S(2)}) %collective-permute-start.13) | collective-permute-done | bytes 32800 | tf_op jit(solution)/shard_map/ppermute | solution.py:355
  104.3 0.6 fusion.4
  104.9 4.2 %collective-permute-done.15.other_ref = bf16[2,2,128,128]{3,2,1,0:T(8,128)(2,1)S(1)} collective-permute-done((bf16[2,2,128,128]{3,2,1,0:T(8,128)(2,1)S(1)}, bf16[2,2,128,128]{3,2,1,0:T(8,128)(2,1)S(1)}, u32[]{:S(2)}, u32[]{:S(2)}) %collective-permute-start.15) | collective-permute-done | bytes 131104 | tf_op jit(solution)/shard_map/ppermute | solution.py:376
  109.2 1.3 %combine_own.1 = (bf16[2,128,128]{2,1,0:T(8,128)(2,1)}, bf16[2,128,128]{2,1,0:T(8,128)(2,1)}) custom-call(s32[24,32]{1,0:T(8,128)S(1)} %get-tuple-element.29.fb_ref, f32[2,2,128,128]{3,2,1,0:T(8,128)S(1)} %get-tuple-element.49.own_ref, bf16[2,2,128,128]{3,2,1,0:T(8,128)(2,1)S(1)} %collective-permute-done.8.prev_ref, ...), custom_call_target="tpu_custom_call" | custom-call | flops 2000000 | bytes 1500000 | tf_op jit(solution)/shard_map/combine_own/pallas_call | solution.py:501
  (27 shorter events, 0.5 us)
Async XLA Ops:
  2.8 7.2 %copy-start.1 = (bf16[16,1024]{1,0:T(8,128)(2,1)S(1)}, bf16[16,1024]{1,0:T(8,128)(2,1)}, u32[]{:S(2)}) copy-start(bf16[16,1024]{1,0:T(8,128)(2,1)} %ref0.1) | copy-start | bytes 98308
  2.8 25.0 %all-to-all-start = ((bf16[16,256,128]{2,1,0:T(8,128)(2,1)}), bf16[16,256,128]{2,1,0:T(8,128)(2,1)S(1)}, u32[]{:S(2)}, u32[]{:S(2)}) async-start(bf16[16,256,128]{2,1,0:T(8,128)(2,1)} %get-tuple-element.33), calls=%async_computation | async-start | bytes 2097152 | tf_op jit(solution)/shard_map/all_to_all | solution.py:373
  10.0 11.7 %collective-permute-start.4 = (bf16[16,1024]{1,0:T(8,128)(2,1)S(1)}, bf16[16,1024]{1,0:T(8,128)(2,1)S(1)}, u32[]{:S(2)}, u32[]{:S(2)}) collective-permute-start(bf16[16,1024]{1,0:T(8,128)(2,1)S(1)} %copy-done.1), channel_id=1, source_target_pairs={{0,4},{1,5},{2,6},{3,7},{4,0},{5,1},{6,2},{7,3},{8,12},{9,13},{10,... | collective-permute-start | bytes 98312 | tf_op jit(solution)/shard_map/ppermute | solution.py:355
  13.4 8.3 %collective-permute-start.3 = (bf16[16,1024]{1,0:T(8,128)(2,1)S(1)}, bf16[16,1024]{1,0:T(8,128)(2,1)S(1)}, u32[]{:S(2)}, u32[]{:S(2)}) collective-permute-start(bf16[16,1024]{1,0:T(8,128)(2,1)S(1)} %copy-done.1), channel_id=1, source_target_pairs={{0,2},{1,3},{2,0},{3,1},{4,6},{5,7},{6,4},{7,5},{8,10},{9,11},{10,... | collective-permute-start | bytes 98312 | tf_op jit(solution)/shard_map/ppermute | solution.py:355
  15.3 6.5 %collective-permute-start.5 = (bf16[16,1024]{1,0:T(8,128)(2,1)S(1)}, bf16[16,1024]{1,0:T(8,128)(2,1)S(1)}, u32[]{:S(2)}, u32[]{:S(2)}) collective-permute-start(bf16[16,1024]{1,0:T(8,128)(2,1)S(1)} %copy-done.1), channel_id=1, source_target_pairs={{0,6},{1,7},{2,4},{3,5},{4,2},{5,3},{6,0},{7,1},{8,14},{9,15},{10,... | collective-permute-start | bytes 98312 | tf_op jit(solution)/shard_map/ppermute | solution.py:355
  15.3 11.2 %collective-permute-start = (bf16[2,2,128,128]{3,2,1,0:T(8,128)(2,1)S(1)}, bf16[2,2,128,128]{3,2,1,0:T(8,128)(2,1)S(1)}, u32[]{:S(2)}, u32[]{:S(2)}) collective-permute-start(bf16[2,2,128,128]{3,2,1,0:T(8,128)(2,1)S(1)} %get-tuple-element.30.own_ref.kv_ref), channel_id=1, source_target_pairs={{0,32},{32,0},{1,33},{33,1},{2,34},{34,2},{3,35},{35,3},{4,36},{36... | collective-permute-start | bytes 393224 | tf_op jit(solution)/shard_map/ppermute | solution.py:376
  21.8 6.0 %collective-permute-start.6 = (bf16[4,16,1024]{2,1,0:T(8,128)(2,1)S(1)}, bf16[4,16,1024]{2,1,0:T(8,128)(2,1)S(1)}, u32[]{:S(2)}, u32[]{:S(2)}) collective-permute-start(bf16[4,16,1024]{2,1,0:T(8,128)(2,1)S(1)} %pad_maximum_fusion), channel_id=1, source_target_pairs={{0,1},{1,0},{2,3},{3,2},{4,5},{5,4},{6,7},{7,6},{8,9},{9,8},{10,11... | collective-permute-start | bytes 393224 | tf_op jit(solution)/shard_map/ppermute | solution.py:355
  27.8 13.4 %copy-start = (bf16[128,1024]{1,0:T(8,128)(2,1)S(1)}, bf16[128,1024]{1,0:T(8,128)(2,1)}, u32[]{:S(2)}) copy-start(bf16[128,1024]{1,0:T(8,128)(2,1)} %weight_ref.3) | copy-start | bytes 786436
  27.8 25.8 %all-to-all-start.1 = ((bf16[16,256,128]{2,1,0:T(8,128)(2,1)}), bf16[16,256,128]{2,1,0:T(8,128)(2,1)S(1)}, u32[]{:S(2)}, u32[]{:S(2)}) async-start(bf16[16,256,128]{2,1,0:T(8,128)(2,1)} %get-tuple-element.35), calls=%async_computation.1 | async-start | bytes 2097152 | tf_op jit(solution)/shard_map/all_to_all | solution.py:373
  35.2 18.4 %collective-permute-start.1 = (bf16[2,2,128,128]{3,2,1,0:T(8,128)(2,1)S(1)}, bf16[2,2,128,128]{3,2,1,0:T(8,128)(2,1)S(1)}, u32[]{:S(2)}, u32[]{:S(2)}) collective-permute-start(bf16[2,2,128,128]{3,2,1,0:T(8,128)(2,1)S(1)} %get-tuple-element.31), channel_id=1, source_target_pairs={{0,8},{8,16},{16,24},{24,64},{32,40},{40,48},{48,56},{56,32},{64,7... | collective-permute-start | bytes 393224 | tf_op jit(solution)/shard_map/ppermute | solution.py:428
  38.5 15.0 %copy-start.2 = (bf16[2,128,128]{2,1,0:T(8,128)(2,1)S(1)}, bf16[2,128,128]{2,1,0:T(8,128)(2,1)}, u32[]{:S(2)}) copy-start(bf16[2,128,128]{2,1,0:T(8,128)(2,1)} %q_ref.1) | copy-start | bytes 196612
  38.6 15.0 %collective-permute-start.2 = (bf16[2,2,128,128]{3,2,1,0:T(8,128)(2,1)S(1)}, bf16[2,2,128,128]{3,2,1,0:T(8,128)(2,1)S(1)}, u32[]{:S(2)}, u32[]{:S(2)}) collective-permute-start(bf16[2,2,128,128]{3,2,1,0:T(8,128)(2,1)S(1)} %get-tuple-element.32), channel_id=1, source_target_pairs={{0,24},{8,0},{16,8},{24,16},{40,32},{48,40},{56,48},{64,88},{72,64... | collective-permute-start | bytes 393224 | tf_op jit(solution)/shard_map/ppermute | solution.py:429
  41.4 12.1 %collective-permute-start.7 = (bf16[128,128]{1,0:T(8,128)(2,1)S(1)}, bf16[128,128]{1,0:T(8,128)(2,1)S(1)}, u32[]{:S(2)}, u32[]{:S(2)}) collective-permute-start(bf16[128,128]{1,0:T(8,128)(2,1)S(1)} %context_grad.1.grad_ref), channel_id=1, source_target_pairs={{0,248},{8,240},{16,232},{24,224},{32,216},{40,208},{48,200},{56,1... | collective-permute-start | bytes 98312 | tf_op jit(solution)/shard_map/ppermute | solution.py:441
  61.6 21.2 %all-to-all-start.2 = ((bf16[16,256,128]{2,1,0:T(8,128)(2,1)}), bf16[16,256,128]{2,1,0:T(8,128)(2,1)S(1)}, u32[]{:S(2)}, u32[]{:S(2)}) async-start(bf16[16,256,128]{2,1,0:T(8,128)(2,1)} %get-tuple-element.41), calls=%async_computation.2 | async-start | bytes 2097152 | tf_op jit(solution)/shard_map/all_to_all | solution.py:373
  68.2 14.6 %collective-permute-start.10 = (bf16[128,128]{1,0:T(8,128)(2,1)}, bf16[128,128]{1,0:T(8,128)(2,1)S(1)}, u32[]{:S(2)}, u32[]{:S(2)}) collective-permute-start(bf16[128,128]{1,0:T(8,128)(2,1)} %get-tuple-element.42), channel_id=1, source_target_pairs={{0,248},{8,240},{16,232},{24,224},{32,216},{40,208},{48,200},{56,1... | collective-permute-start | bytes 98312 | tf_op jit(solution)/shard_map/ppermute | solution.py:459
  76.3 12.8 %collective-permute-start.8 = (bf16[2,2,128,128]{3,2,1,0:T(8,128)(2,1)S(1)}, bf16[2,2,128,128]{3,2,1,0:T(8,128)(2,1)S(1)}, u32[]{:S(2)}, u32[]{:S(2)}) collective-permute-start(bf16[2,2,128,128]{3,2,1,0:T(8,128)(2,1)S(1)} %get-tuple-element.38), channel_id=1, source_target_pairs={{24,0},{0,8},{8,16},{16,24},{32,40},{40,48},{48,56},{88,64},{64,72... | collective-permute-start | bytes 393224 | tf_op jit(solution)/shard_map/ppermute | solution.py:462
  80.9 11.2 %collective-permute-start.9 = (bf16[2,2,128,128]{3,2,1,0:T(8,128)(2,1)S(1)}, bf16[2,2,128,128]{3,2,1,0:T(8,128)(2,1)S(1)}, u32[]{:S(2)}, u32[]{:S(2)}) collective-permute-start(bf16[2,2,128,128]{3,2,1,0:T(8,128)(2,1)S(1)} %get-tuple-element.39), channel_id=1, source_target_pairs={{8,0},{16,8},{24,16},{64,24},{40,32},{48,40},{56,48},{32,56},{72,6... | collective-permute-start | bytes 393224 | tf_op jit(solution)/shard_map/ppermute | solution.py:463
  82.8 26.4 %all-to-all-start.3 = ((bf16[16,256,128]{2,1,0:T(8,128)(2,1)}), bf16[16,256,128]{2,1,0:T(8,128)(2,1)S(1)}, u32[]{:S(2)}, u32[]{:S(2)}) async-start(bf16[16,256,128]{2,1,0:T(8,128)(2,1)} %get-tuple-element.51), calls=%async_computation.3 | async-start | bytes 2097152 | tf_op jit(solution)/shard_map/all_to_all | solution.py:373
  93.0 1.6 %collective-permute-start.11 = (bf16[4,16,1024]{2,1,0:T(8,128)(2,1)S(1)}, bf16[4,16,1024]{2,1,0:T(8,128)(2,1)S(1)}, u32[]{:S(2)}, u32[]{:S(2)}) collective-permute-start(bf16[4,16,1024]{2,1,0:T(8,128)(2,1)S(1)} %get-tuple-element.47), channel_id=1, source_target_pairs={{0,1},{1,0},{2,3},{3,2},{4,5},{5,4},{6,7},{7,6},{8,9},{9,8},{10,11... | collective-permute-start | bytes 393224 | tf_op jit(solution)/shard_map/ppermute | solution.py:355
  94.6 9.7 %copy-start.3 = (bf16[16,1024]{1,0:T(8,128)(2,1)S(1)}, bf16[16,1024]{1,0:T(8,128)(2,1)}, u32[]{:S(2)}) copy-start(bf16[16,1024]{1,0:T(8,128)(2,1)} %param.9) | copy-start | bytes 98308
  94.6 4.9 %collective-permute-start.12 = (bf16[16,1024]{1,0:T(8,128)(2,1)S(1)}, bf16[16,1024]{1,0:T(8,128)(2,1)S(1)}, u32[]{:S(2)}, u32[]{:S(2)}) collective-permute-start(bf16[16,1024]{1,0:T(8,128)(2,1)S(1)} %get-tuple-element.56), channel_id=1, source_target_pairs={{0,2},{1,3},{2,0},{3,1},{4,6},{5,7},{6,4},{7,5},{8,10},{9,11},{10,... | collective-permute-start | bytes 98312 | tf_op jit(solution)/shard_map/ppermute | solution.py:355
  95.0 6.0 %collective-permute-start.14 = (bf16[16,1024]{1,0:T(8,128)(2,1)S(1)}, bf16[16,1024]{1,0:T(8,128)(2,1)S(1)}, u32[]{:S(2)}, u32[]{:S(2)}) collective-permute-start(bf16[16,1024]{1,0:T(8,128)(2,1)S(1)} %get-tuple-element.57), channel_id=1, source_target_pairs={{0,6},{1,7},{2,4},{3,5},{4,2},{5,3},{6,0},{7,1},{8,14},{9,15},{10,... | collective-permute-start | bytes 98312 | tf_op jit(solution)/shard_map/ppermute | solution.py:355
  95.8 8.5 %collective-permute-start.13 = (bf16[16,1024]{1,0:T(8,128)(2,1)S(1)}, bf16[16,1024]{1,0:T(8,128)(2,1)S(1)}, u32[]{:S(2)}, u32[]{:S(2)}) collective-permute-start(bf16[16,1024]{1,0:T(8,128)(2,1)S(1)} %get-tuple-element.58), channel_id=1, source_target_pairs={{0,4},{1,5},{2,6},{3,7},{4,0},{5,1},{6,2},{7,3},{8,12},{9,13},{10,... | collective-permute-start | bytes 98312 | tf_op jit(solution)/shard_map/ppermute | solution.py:355
  98.2 11.0 %collective-permute-start.15 = (bf16[2,2,128,128]{3,2,1,0:T(8,128)(2,1)S(1)}, bf16[2,2,128,128]{3,2,1,0:T(8,128)(2,1)S(1)}, u32[]{:S(2)}, u32[]{:S(2)}) collective-permute-start(bf16[2,2,128,128]{3,2,1,0:T(8,128)(2,1)S(1)} %combine_partner.1), channel_id=1, source_target_pairs={{0,32},{32,0},{1,33},{33,1},{2,34},{34,2},{3,35},{35,3},{4,36},{36... | collective-permute-start | bytes 393224 | tf_op jit(solution)/shard_map/ppermute | solution.py:376

commit v12 on v11

--- a/solution.py
+++ b/solution.py
@@ -403,8 +403,6 @@
     )(near_lists, key_value, partner)
     same_core = [cotangent] + [swap(cotangent, bit) for bit in (2, 4, 6)]
     other_core = swap(jnp.stack(same_core), 1)
-    outgoing, other_core = lax.optimization_barrier((outgoing, other_core))
-    far_partner = plane_a2a(outgoing)
 
     def flat(x, zh, y):
         return (x * nz + zh) * ny + y
@@ -438,6 +436,8 @@
         compiler_params=pltpu.CompilerParams(vmem_limit_bytes=LIMIT),
         name="context_grad",
     )(*same_core, other_core, out_weight)
+    outgoing, grad_context = lax.optimization_barrier((outgoing, grad_context))
+    far_partner = plane_a2a(outgoing)
     mirrored = lax.ppermute(grad_context, SEQ, mirror)
 
     square = shape((tok_rows, width))

time: 111 us -> 111 us (level); the launches traced: 110 us -> 109 us
  waiting for transfers between devices: 20.9 us -> 18.2 us
    ppermute x2, waiting for transfers between devices: 8.88 us -> 6.66 us  [z_swap(): return lax.ppermute(x, 'zh', [(i, nz - 1 - i) for i in range(nz)])]
  transfers between devices with their start and end apart: 20 -> 20, of which waited for: 8 -> 7; matrix products, arithmetic and copies ran while one was open for 1% -> 1% of each run, Pallas kernels for 2% -> 2%
where the time goes in v12:
time: 111 us; the launch traced here: 109 us
  starting transfers between devices  75.1 us (68%)
  waiting for transfers between devices  18.2 us (16%)
  Pallas kernels  13.8 us (12%)
    all_to_all x4, starting transfers between devices, plane_a2a(): lax.all_to_all(x, ('x', 'y'), split_axis=0, concat_axis=0, tiled=True)  27.4 us
    ppermute x1, starting transfers between devices, per_device(): mirrored = lax.ppermute(grad_context, SEQ, mirror)  9.82 us
    ppermute x8, starting transfers between devices, swap(): return lax.ppermute(x, 'tp', [(i, i ^ bit) for i in range(count)])  9.31 us
    ppermute x1, starting transfers between devices, per_device(): context_back = lax.ppermute(context_rev, SEQ, mirror)  8.53 us
    pallas_call x1, Pallas kernels, per_device(): pl.pallas_call(attend_kernel, out_shape=(square, square, shape((2, tok_ro...  7.96 us
    ppermute x2, starting transfers between devices, z_swap(): return lax.ppermute(x, 'zh', [(i, nz - 1 - i) for i in range(nz)])  7.74 us
    ppermute x2, waiting for transfers between devices, z_swap(): return lax.ppermute(x, 'zh', [(i, nz - 1 - i) for i in range(nz)])  6.66 us
    ppermute x8, waiting for transfers between devices, swap(): return lax.ppermute(x, 'tp', [(i, i ^ bit) for i in range(count)])  6.49 us
  transfers between devices with their start and end apart: 20, of which 7 were waited for; matrix products, arithmetic and copies ran while one was open for 1% of the time, Pallas kernels for 2%

profile of v12, /device:TPU:24, one launch (start us, length us, event | category | flops | bytes accessed | tf_op | source)
XLA Modules:
  0.0 108.6 jit_solution(3330946763237560041)
XLA Ops:
  0.6 2.2 %pack_own.1 = (bf16[16,256,128]{2,1,0:T(8,128)(2,1)}, bf16[2,2,128,128]{3,2,1,0:T(8,128)(2,1)S(1)}, s32[24,32]{1,0:T(8,128)S(1)}) custom-call(s32[24,32]{1,0:T(8,128)} %bitcast.27, bf16[2,128,128]{2,1,0:T(8,128)(2,1)} %key_ref.1, bf16[2,128,128]{2,1,0:T(8,128)(2,1)} %value_ref.1), custom_call_target="tpu_custom_call" | custom-call | flops 500000 | bytes 1500000 | tf_op jit(solution)/shard_map/pack_own/pallas_call | solution.py:381
  2.8 7.2 %all-to-all-start = ((bf16[16,256,128]{2,1,0:T(8,128)(2,1)}), bf16[16,256,128]{2,1,0:T(8,128)(2,1)S(1)}, u32[]{:S(2)}, u32[]{:S(2)}) async-start(bf16[16,256,128]{2,1,0:T(8,128)(2,1)} %get-tuple-element.33), calls=%async_computation | async-start | bytes 2097152 | tf_op jit(solution)/shard_map/all_to_all | solution.py:373
  10.0 4.7 %collective-permute-start.5 = (bf16[16,1024]{1,0:T(8,128)(2,1)S(1)}, bf16[16,1024]{1,0:T(8,128)(2,1)S(1)}, u32[]{:S(2)}, u32[]{:S(2)}) collective-permute-start(bf16[16,1024]{1,0:T(8,128)(2,1)S(1)} %copy-done.1), channel_id=1, source_target_pairs={{0,6},{1,7},{2,4},{3,5},{4,2},{5,3},{6,0},{7,1},{8,14},{9,15},{10,... | collective-permute-start | bytes 98312 | tf_op jit(solution)/shard_map/ppermute | solution.py:355
  14.7 0.7 collective-permute-start.3
  15.4 6.3 %collective-permute-start = (bf16[2,2,128,128]{3,2,1,0:T(8,128)(2,1)S(1)}, bf16[2,2,128,128]{3,2,1,0:T(8,128)(2,1)S(1)}, u32[]{:S(2)}, u32[]{:S(2)}) collective-permute-start(bf16[2,2,128,128]{3,2,1,0:T(8,128)(2,1)S(1)} %get-tuple-element.30.own_ref.kv_ref), channel_id=1, source_target_pairs={{0,32},{32,0},{1,33},{33,1},{2,34},{34,2},{3,35},{35,3},{4,36},{36... | collective-permute-start | bytes 393224 | tf_op jit(solution)/shard_map/ppermute | solution.py:376
  21.8 4.6 %collective-permute-done.partner_ref = bf16[2,2,128,128]{3,2,1,0:T(8,128)(2,1)S(1)} collective-permute-done((bf16[2,2,128,128]{3,2,1,0:T(8,128)(2,1)S(1)}, bf16[2,2,128,128]{3,2,1,0:T(8,128)(2,1)S(1)}, u32[]{:S(2)}, u32[]{:S(2)}) %collective-permute-start) | collective-permute-done | bytes 131104 | tf_op jit(solution)/shard_map/ppermute | solution.py:376
  26.5 1.3 %pack_partner.1 = (bf16[16,256,128]{2,1,0:T(8,128)(2,1)}, bf16[2,2,128,128]{3,2,1,0:T(8,128)(2,1)S(1)}, bf16[2,2,128,128]{3,2,1,0:T(8,128)(2,1)S(1)}) custom-call(s32[24,32]{1,0:T(8,128)S(1)} %get-tuple-element.29.fb_ref, bf16[2,2,128,128]{3,2,1,0:T(8,128)(2,1)S(1)} %get-tuple-element.30.own_ref.kv_ref, ...), custom_call_target="tpu_custom_call" | custom-call | flops 500000 | bytes 1500000 | tf_op jit(solution)/shard_map/pack_partner/pallas_call | solution.py:394
  27.7 0.2 context_grad.1.grad_ref
  28.0 7.2 %all-to-all-start.1 = ((bf16[16,256,128]{2,1,0:T(8,128)(2,1)}), bf16[16,256,128]{2,1,0:T(8,128)(2,1)S(1)}, u32[]{:S(2)}, u32[]{:S(2)}) async-start(bf16[16,256,128]{2,1,0:T(8,128)(2,1)} %get-tuple-element.35), calls=%async_computation.1 | async-start | bytes 2097152 | tf_op jit(solution)/shard_map/all_to_all | solution.py:373
  35.2 3.4 %collective-permute-start.1 = (bf16[2,2,128,128]{3,2,1,0:T(8,128)(2,1)S(1)}, bf16[2,2,128,128]{3,2,1,0:T(8,128)(2,1)S(1)}, u32[]{:S(2)}, u32[]{:S(2)}) collective-permute-start(bf16[2,2,128,128]{3,2,1,0:T(8,128)(2,1)S(1)} %get-tuple-element.31), channel_id=1, source_target_pairs={{0,8},{8,16},{16,24},{24,64},{32,40},{40,48},{48,56},{56,32},{64,7... | collective-permute-start | bytes 393224 | tf_op jit(solution)/shard_map/ppermute | solution.py:426
  38.6 2.5 %collective-permute-start.2 = (bf16[2,2,128,128]{3,2,1,0:T(8,128)(2,1)S(1)}, bf16[2,2,128,128]{3,2,1,0:T(8,128)(2,1)S(1)}, u32[]{:S(2)}, u32[]{:S(2)}) collective-permute-start(bf16[2,2,128,128]{3,2,1,0:T(8,128)(2,1)S(1)} %get-tuple-element.32), channel_id=1, source_target_pairs={{0,24},{8,0},{16,8},{24,16},{40,32},{48,40},{56,48},{64,88},{72,64... | collective-permute-start | bytes 393224 | tf_op jit(solution)/shard_map/ppermute | solution.py:427
  41.1 9.8 %collective-permute-start.7 = (bf16[128,128]{1,0:T(8,128)(2,1)S(1)}, bf16[128,128]{1,0:T(8,128)(2,1)S(1)}, u32[]{:S(2)}, u32[]{:S(2)}) collective-permute-start(bf16[128,128]{1,0:T(8,128)(2,1)S(1)} %context_grad.1.grad_ref), channel_id=1, source_target_pairs={{0,248},{8,240},{16,232},{24,224},{32,216},{40,208},{48,200},{56,1... | collective-permute-start | bytes 98312 | tf_op jit(solution)/shard_map/ppermute | solution.py:441
  50.9 2.3 %collective-permute-done.7.mirrored_ref = bf16[128,128]{1,0:T(8,128)(2,1)S(1)} collective-permute-done((bf16[128,128]{1,0:T(8,128)(2,1)S(1)}, bf16[128,128]{1,0:T(8,128)(2,1)S(1)}, u32[]{:S(2)}, u32[]{:S(2)}) %collective-permute-start.7) | collective-permute-done | bytes 32800 | tf_op jit(solution)/shard_map/ppermute | solution.py:441
  53.2 8.0 %attend.1 = (bf16[128,128]{1,0:T(8,128)(2,1)S(1)}, bf16[128,128]{1,0:T(8,128)(2,1)}, bf16[2,128,128]{2,1,0:T(8,128)(2,1)}, f32[2,2,128,128]{3,2,1,0:T(8,128)S(1)...) custom-call(s32[24,32]{1,0:T(8,128)S(1)} %get-tuple-element.29.fb_re, ...), custom_call_target="tpu_custom_call" | custom-call | flops 4000000000 | bytes 8000000 | tf_op jit(solution)/shard_map/attend/pallas_call | solution.py:445
  61.2 6.7 %all-to-all-start.2 = ((bf16[16,256,128]{2,1,0:T(8,128)(2,1)}), bf16[16,256,128]{2,1,0:T(8,128)(2,1)S(1)}, u32[]{:S(2)}, u32[]{:S(2)}) async-start(bf16[16,256,128]{2,1,0:T(8,128)(2,1)} %get-tuple-element.41), calls=%async_computation.2 | async-start | bytes 2097152 | tf_op jit(solution)/shard_map/all_to_all | solution.py:373
  67.9 8.5 %collective-permute-start.10 = (bf16[128,128]{1,0:T(8,128)(2,1)}, bf16[128,128]{1,0:T(8,128)(2,1)S(1)}, u32[]{:S(2)}, u32[]{:S(2)}) collective-permute-start(bf16[128,128]{1,0:T(8,128)(2,1)} %get-tuple-element.42), channel_id=1, source_target_pairs={{0,248},{8,240},{16,232},{24,224},{32,216},{40,208},{48,200},{56,1... | collective-permute-start | bytes 98312 | tf_op jit(solution)/shard_map/ppermute | solution.py:459
  76.4 4.6 %collective-permute-start.8 = (bf16[2,2,128,128]{3,2,1,0:T(8,128)(2,1)S(1)}, bf16[2,2,128,128]{3,2,1,0:T(8,128)(2,1)S(1)}, u32[]{:S(2)}, u32[]{:S(2)}) collective-permute-start(bf16[2,2,128,128]{3,2,1,0:T(8,128)(2,1)S(1)} %get-tuple-element.38), channel_id=1, source_target_pairs={{24,0},{0,8},{8,16},{16,24},{32,40},{40,48},{48,56},{88,64},{64,72... | collective-permute-start | bytes 393224 | tf_op jit(solution)/shard_map/ppermute | solution.py:462
  81.0 1.9 %collective-permute-start.9 = (bf16[2,2,128,128]{3,2,1,0:T(8,128)(2,1)S(1)}, bf16[2,2,128,128]{3,2,1,0:T(8,128)(2,1)S(1)}, u32[]{:S(2)}, u32[]{:S(2)}) collective-permute-start(bf16[2,2,128,128]{3,2,1,0:T(8,128)(2,1)S(1)} %get-tuple-element.39), channel_id=1, source_target_pairs={{8,0},{16,8},{24,16},{64,24},{40,32},{48,40},{56,48},{32,56},{72,6... | collective-permute-start | bytes 393224 | tf_op jit(solution)/shard_map/ppermute | solution.py:463
  82.9 6.3 %all-to-all-start.3 = ((bf16[16,256,128]{2,1,0:T(8,128)(2,1)}), bf16[16,256,128]{2,1,0:T(8,128)(2,1)S(1)}, u32[]{:S(2)}, u32[]{:S(2)}) async-start(bf16[16,256,128]{2,1,0:T(8,128)(2,1)} %get-tuple-element.51), calls=%async_computation.3 | async-start | bytes 2097152 | tf_op jit(solution)/shard_map/all_to_all | solution.py:373
  89.2 2.7 %collective-permute-done.9.next_ref = bf16[2,2,128,128]{3,2,1,0:T(8,128)(2,1)S(1)} collective-permute-done((bf16[2,2,128,128]{3,2,1,0:T(8,128)(2,1)S(1)}, bf16[2,2,128,128]{3,2,1,0:T(8,128)(2,1)S(1)}, u32[]{:S(2)}, u32[]{:S(2)}) %collective-permute-start.9) | collective-permute-done | bytes 131104 | tf_op jit(solution)/shard_map/ppermute | solution.py:463
  91.9 0.7 combine_partner.1
  92.6 0.2 project.1
  92.8 0.3 collective-permute-start.11
  93.1 1.3 %collective-permute-done.11 = bf16[4,16,1024]{2,1,0:T(8,128)(2,1)S(1)} collective-permute-done((bf16[4,16,1024]{2,1,0:T(8,128)(2,1)S(1)}, bf16[4,16,1024]{2,1,0:T(8,128)(2,1)S(1)}, u32[]{:S(2)}, u32[]{:S(2)}) %collective-permute-start.11) | collective-permute-done | bytes 131104 | tf_op jit(solution)/shard_map/ppermute | solution.py:355
  94.6 2.2 %collective-permute-start.14 = (bf16[16,1024]{1,0:T(8,128)(2,1)S(1)}, bf16[16,1024]{1,0:T(8,128)(2,1)S(1)}, u32[]{:S(2)}, u32[]{:S(2)}) collective-permute-start(bf16[16,1024]{1,0:T(8,128)(2,1)S(1)} %get-tuple-element.57), channel_id=1, source_target_pairs={{0,6},{1,7},{2,4},{3,5},{4,2},{5,3},{6,0},{7,1},{8,14},{9,15},{10,... | collective-permute-start | bytes 98312 | tf_op jit(solution)/shard_map/ppermute | solution.py:355
  96.8 1.3 %collective-permute-start.13 = (bf16[16,1024]{1,0:T(8,128)(2,1)S(1)}, bf16[16,1024]{1,0:T(8,128)(2,1)S(1)}, u32[]{:S(2)}, u32[]{:S(2)}) collective-permute-start(bf16[16,1024]{1,0:T(8,128)(2,1)S(1)} %get-tuple-element.58), channel_id=1, source_target_pairs={{0,4},{1,5},{2,6},{3,7},{4,0},{5,1},{6,2},{7,3},{8,12},{9,13},{10,... | collective-permute-start | bytes 98312 | tf_op jit(solution)/shard_map/ppermute | solution.py:355
  98.0 1.5 %collective-permute-start.15 = (bf16[2,2,128,128]{3,2,1,0:T(8,128)(2,1)S(1)}, bf16[2,2,128,128]{3,2,1,0:T(8,128)(2,1)S(1)}, u32[]{:S(2)}, u32[]{:S(2)}) collective-permute-start(bf16[2,2,128,128]{3,2,1,0:T(8,128)(2,1)S(1)} %combine_partner.1), channel_id=1, source_target_pairs={{0,32},{32,0},{1,33},{33,1},{2,34},{34,2},{3,35},{35,3},{4,36},{36... | collective-permute-start | bytes 393224 | tf_op jit(solution)/shard_map/ppermute | solution.py:376
  99.5 0.9 collective-permute-done.14
  100.4 4.2 %collective-permute-done.13 = bf16[16,1024]{1,0:T(8,128)(2,1)S(1)} collective-permute-done((bf16[16,1024]{1,0:T(8,128)(2,1)S(1)}, bf16[16,1024]{1,0:T(8,128)(2,1)S(1)}, u32[]{:S(2)}, u32[]{:S(2)}) %collective-permute-start.13) | collective-permute-done | bytes 32800 | tf_op jit(solution)/shard_map/ppermute | solution.py:355
  104.6 0.6 fusion.4
  105.3 2.0 %collective-permute-done.15.other_ref = bf16[2,2,128,128]{3,2,1,0:T(8,128)(2,1)S(1)} collective-permute-done((bf16[2,2,128,128]{3,2,1,0:T(8,128)(2,1)S(1)}, bf16[2,2,128,128]{3,2,1,0:T(8,128)(2,1)S(1)}, u32[]{:S(2)}, u32[]{:S(2)}) %collective-permute-start.15) | collective-permute-done | bytes 131104 | tf_op jit(solution)/shard_map/ppermute | solution.py:376
  107.3 1.3 %combine_own.1 = (bf16[2,128,128]{2,1,0:T(8,128)(2,1)}, bf16[2,128,128]{2,1,0:T(8,128)(2,1)}) custom-call(s32[24,32]{1,0:T(8,128)S(1)} %get-tuple-element.29.fb_ref, f32[2,2,128,128]{3,2,1,0:T(8,128)S(1)} %get-tuple-element.49.own_ref, bf16[2,2,128,128]{3,2,1,0:T(8,128)(2,1)S(1)} %collective-permute-done.8.prev_ref, ...), custom_call_target="tpu_custom_call" | custom-call | flops 2000000 | bytes 1500000 | tf_op jit(solution)/shard_map/combine_own/pallas_call | solution.py:501
  (27 shorter events, 0.3 us)
Async XLA Ops:
  2.8 7.2 %copy-start.1 = (bf16[16,1024]{1,0:T(8,128)(2,1)S(1)}, bf16[16,1024]{1,0:T(8,128)(2,1)}, u32[]{:S(2)}) copy-start(bf16[16,1024]{1,0:T(8,128)(2,1)} %ref0.1) | copy-start | bytes 98308
  2.8 25.2 %all-to-all-start = ((bf16[16,256,128]{2,1,0:T(8,128)(2,1)}), bf16[16,256,128]{2,1,0:T(8,128)(2,1)S(1)}, u32[]{:S(2)}, u32[]{:S(2)}) async-start(bf16[16,256,128]{2,1,0:T(8,128)(2,1)} %get-tuple-element.33), calls=%async_computation | async-start | bytes 2097152 | tf_op jit(solution)/shard_map/all_to_all | solution.py:373
  10.0 11.7 %collective-permute-start.5 = (bf16[16,1024]{1,0:T(8,128)(2,1)S(1)}, bf16[16,1024]{1,0:T(8,128)(2,1)S(1)}, u32[]{:S(2)}, u32[]{:S(2)}) collective-permute-start(bf16[16,1024]{1,0:T(8,128)(2,1)S(1)} %copy-done.1), channel_id=1, source_target_pairs={{0,6},{1,7},{2,4},{3,5},{4,2},{5,3},{6,0},{7,1},{8,14},{9,15},{10,... | collective-permute-start | bytes 98312 | tf_op jit(solution)/shard_map/ppermute | solution.py:355
  14.7 7.0 %collective-permute-start.4 = (bf16[16,1024]{1,0:T(8,128)(2,1)S(1)}, bf16[16,1024]{1,0:T(8,128)(2,1)S(1)}, u32[]{:S(2)}, u32[]{:S(2)}) collective-permute-start(bf16[16,1024]{1,0:T(8,128)(2,1)S(1)} %copy-done.1), channel_id=1, source_target_pairs={{0,4},{1,5},{2,6},{3,7},{4,0},{5,1},{6,2},{7,3},{8,12},{9,13},{10,... | collective-permute-start | bytes 98312 | tf_op jit(solution)/shard_map/ppermute | solution.py:355
  14.7 7.0 %collective-permute-start.3 = (bf16[16,1024]{1,0:T(8,128)(2,1)S(1)}, bf16[16,1024]{1,0:T(8,128)(2,1)S(1)}, u32[]{:S(2)}, u32[]{:S(2)}) collective-permute-start(bf16[16,1024]{1,0:T(8,128)(2,1)S(1)} %copy-done.1), channel_id=1, source_target_pairs={{0,2},{1,3},{2,0},{3,1},{4,6},{5,7},{6,4},{7,5},{8,10},{9,11},{10,... | collective-permute-start | bytes 98312 | tf_op jit(solution)/shard_map/ppermute | solution.py:355
  15.4 11.1 %collective-permute-start = (bf16[2,2,128,128]{3,2,1,0:T(8,128)(2,1)S(1)}, bf16[2,2,128,128]{3,2,1,0:T(8,128)(2,1)S(1)}, u32[]{:S(2)}, u32[]{:S(2)}) collective-permute-start(bf16[2,2,128,128]{3,2,1,0:T(8,128)(2,1)S(1)} %get-tuple-element.30.own_ref.kv_ref), channel_id=1, source_target_pairs={{0,32},{32,0},{1,33},{33,1},{2,34},{34,2},{3,35},{35,3},{4,36},{36... | collective-permute-start | bytes 393224 | tf_op jit(solution)/shard_map/ppermute | solution.py:376
  21.7 6.1 %copy-start = (bf16[128,1024]{1,0:T(8,128)(2,1)S(1)}, bf16[128,1024]{1,0:T(8,128)(2,1)}, u32[]{:S(2)}) copy-start(bf16[128,1024]{1,0:T(8,128)(2,1)} %weight_ref.3) | copy-start | bytes 786436
  21.7 6.0 %collective-permute-start.6 = (bf16[4,16,1024]{2,1,0:T(8,128)(2,1)S(1)}, bf16[4,16,1024]{2,1,0:T(8,128)(2,1)S(1)}, u32[]{:S(2)}, u32[]{:S(2)}) collective-permute-start(bf16[4,16,1024]{2,1,0:T(8,128)(2,1)S(1)} %pad_maximum_fusion), channel_id=1, source_target_pairs={{0,1},{1,0},{2,3},{3,2},{4,5},{5,4},{6,7},{7,6},{8,9},{9,8},{10,11... | collective-permute-start | bytes 393224 | tf_op jit(solution)/shard_map/ppermute | solution.py:355
  28.0 25.3 %copy-start.2 = (bf16[2,128,128]{2,1,0:T(8,128)(2,1)S(1)}, bf16[2,128,128]{2,1,0:T(8,128)(2,1)}, u32[]{:S(2)}) copy-start(bf16[2,128,128]{2,1,0:T(8,128)(2,1)} %q_ref.1) | copy-start | bytes 196612
  28.0 25.2 %all-to-all-start.1 = ((bf16[16,256,128]{2,1,0:T(8,128)(2,1)}), bf16[16,256,128]{2,1,0:T(8,128)(2,1)S(1)}, u32[]{:S(2)}, u32[]{:S(2)}) async-start(bf16[16,256,128]{2,1,0:T(8,128)(2,1)} %get-tuple-element.35), calls=%async_computation.1 | async-start | bytes 2097152 | tf_op jit(solution)/shard_map/all_to_all | solution.py:373
  35.2 18.0 %collective-permute-start.1 = (bf16[2,2,128,128]{3,2,1,0:T(8,128)(2,1)S(1)}, bf16[2,2,128,128]{3,2,1,0:T(8,128)(2,1)S(1)}, u32[]{:S(2)}, u32[]{:S(2)}) collective-permute-start(bf16[2,2,128,128]{3,2,1,0:T(8,128)(2,1)S(1)} %get-tuple-element.31), channel_id=1, source_target_pairs={{0,8},{8,16},{16,24},{24,64},{32,40},{40,48},{48,56},{56,32},{64,7... | collective-permute-start | bytes 393224 | tf_op jit(solution)/shard_map/ppermute | solution.py:426
  38.6 14.6 %collective-permute-start.2 = (bf16[2,2,128,128]{3,2,1,0:T(8,128)(2,1)S(1)}, bf16[2,2,128,128]{3,2,1,0:T(8,128)(2,1)S(1)}, u32[]{:S(2)}, u32[]{:S(2)}) collective-permute-start(bf16[2,2,128,128]{3,2,1,0:T(8,128)(2,1)S(1)} %get-tuple-element.32), channel_id=1, source_target_pairs={{0,24},{8,0},{16,8},{24,16},{40,32},{48,40},{56,48},{64,88},{72,64... | collective-permute-start | bytes 393224 | tf_op jit(solution)/shard_map/ppermute | solution.py:427
  41.1 12.1 %collective-permute-start.7 = (bf16[128,128]{1,0:T(8,128)(2,1)S(1)}, bf16[128,128]{1,0:T(8,128)(2,1)S(1)}, u32[]{:S(2)}, u32[]{:S(2)}) collective-permute-start(bf16[128,128]{1,0:T(8,128)(2,1)S(1)} %context_grad.1.grad_ref), channel_id=1, source_target_pairs={{0,248},{8,240},{16,232},{24,224},{32,216},{40,208},{48,200},{56,1... | collective-permute-start | bytes 98312 | tf_op jit(solution)/shard_map/ppermute | solution.py:441
  61.2 21.7 %all-to-all-start.2 = ((bf16[16,256,128]{2,1,0:T(8,128)(2,1)}), bf16[16,256,128]{2,1,0:T(8,128)(2,1)S(1)}, u32[]{:S(2)}, u32[]{:S(2)}) async-start(bf16[16,256,128]{2,1,0:T(8,128)(2,1)} %get-tuple-element.41), calls=%async_computation.2 | async-start | bytes 2097152 | tf_op jit(solution)/shard_map/all_to_all | solution.py:373
  67.9 15.0 %collective-permute-start.10 = (bf16[128,128]{1,0:T(8,128)(2,1)}, bf16[128,128]{1,0:T(8,128)(2,1)S(1)}, u32[]{:S(2)}, u32[]{:S(2)}) collective-permute-start(bf16[128,128]{1,0:T(8,128)(2,1)} %get-tuple-element.42), channel_id=1, source_target_pairs={{0,248},{8,240},{16,232},{24,224},{32,216},{40,208},{48,200},{56,1... | collective-permute-start | bytes 98312 | tf_op jit(solution)/shard_map/ppermute | solution.py:459
  76.4 12.8 %collective-permute-start.8 = (bf16[2,2,128,128]{3,2,1,0:T(8,128)(2,1)S(1)}, bf16[2,2,128,128]{3,2,1,0:T(8,128)(2,1)S(1)}, u32[]{:S(2)}, u32[]{:S(2)}) collective-permute-start(bf16[2,2,128,128]{3,2,1,0:T(8,128)(2,1)S(1)} %get-tuple-element.38), channel_id=1, source_target_pairs={{24,0},{0,8},{8,16},{16,24},{32,40},{40,48},{48,56},{88,64},{64,72... | collective-permute-start | bytes 393224 | tf_op jit(solution)/shard_map/ppermute | solution.py:462
  81.0 10.9 %collective-permute-start.9 = (bf16[2,2,128,128]{3,2,1,0:T(8,128)(2,1)S(1)}, bf16[2,2,128,128]{3,2,1,0:T(8,128)(2,1)S(1)}, u32[]{:S(2)}, u32[]{:S(2)}) collective-permute-start(bf16[2,2,128,128]{3,2,1,0:T(8,128)(2,1)S(1)} %get-tuple-element.39), channel_id=1, source_target_pairs={{8,0},{16,8},{24,16},{64,24},{40,32},{48,40},{56,48},{32,56},{72,6... | collective-permute-start | bytes 393224 | tf_op jit(solution)/shard_map/ppermute | solution.py:463
  82.9 24.4 %all-to-all-start.3 = ((bf16[16,256,128]{2,1,0:T(8,128)(2,1)}), bf16[16,256,128]{2,1,0:T(8,128)(2,1)S(1)}, u32[]{:S(2)}, u32[]{:S(2)}) async-start(bf16[16,256,128]{2,1,0:T(8,128)(2,1)} %get-tuple-element.51), calls=%async_computation.3 | async-start | bytes 2097152 | tf_op jit(solution)/shard_map/all_to_all | solution.py:373
  92.8 1.6 %collective-permute-start.11 = (bf16[4,16,1024]{2,1,0:T(8,128)(2,1)S(1)}, bf16[4,16,1024]{2,1,0:T(8,128)(2,1)S(1)}, u32[]{:S(2)}, u32[]{:S(2)}) collective-permute-start(bf16[4,16,1024]{2,1,0:T(8,128)(2,1)S(1)} %get-tuple-element.47), channel_id=1, source_target_pairs={{0,1},{1,0},{2,3},{3,2},{4,5},{5,4},{6,7},{7,6},{8,9},{9,8},{10,11... | collective-permute-start | bytes 393224 | tf_op jit(solution)/shard_map/ppermute | solution.py:355
  94.4 10.2 %copy-start.3 = (bf16[16,1024]{1,0:T(8,128)(2,1)S(1)}, bf16[16,1024]{1,0:T(8,128)(2,1)}, u32[]{:S(2)}) copy-start(bf16[16,1024]{1,0:T(8,128)(2,1)} %param.9) | copy-start | bytes 98308
  94.5 5.0 %collective-permute-start.12 = (bf16[16,1024]{1,0:T(8,128)(2,1)S(1)}, bf16[16,1024]{1,0:T(8,128)(2,1)S(1)}, u32[]{:S(2)}, u32[]{:S(2)}) collective-permute-start(bf16[16,1024]{1,0:T(8,128)(2,1)S(1)} %get-tuple-element.56), channel_id=1, source_target_pairs={{0,2},{1,3},{2,0},{3,1},{4,6},{5,7},{6,4},{7,5},{8,10},{9,11},{10,... | collective-permute-start | bytes 98312 | tf_op jit(solution)/shard_map/ppermute | solution.py:355
  94.6 5.9 %collective-permute-start.14 = (bf16[16,1024]{1,0:T(8,128)(2,1)S(1)}, bf16[16,1024]{1,0:T(8,128)(2,1)S(1)}, u32[]{:S(2)}, u32[]{:S(2)}) collective-permute-start(bf16[16,1024]{1,0:T(8,128)(2,1)S(1)} %get-tuple-element.57), channel_id=1, source_target_pairs={{0,6},{1,7},{2,4},{3,5},{4,2},{5,3},{6,0},{7,1},{8,14},{9,15},{10,... | collective-permute-start | bytes 98312 | tf_op jit(solution)/shard_map/ppermute | solution.py:355
  96.8 7.9 %collective-permute-start.13 = (bf16[16,1024]{1,0:T(8,128)(2,1)S(1)}, bf16[16,1024]{1,0:T(8,128)(2,1)S(1)}, u32[]{:S(2)}, u32[]{:S(2)}) collective-permute-start(bf16[16,1024]{1,0:T(8,128)(2,1)S(1)} %get-tuple-element.58), channel_id=1, source_target_pairs={{0,4},{1,5},{2,6},{3,7},{4,0},{5,1},{6,2},{7,3},{8,12},{9,13},{10,... | collective-permute-start | bytes 98312 | tf_op jit(solution)/shard_map/ppermute | solution.py:355
  98.0 9.3 %collective-permute-start.15 = (bf16[2,2,128,128]{3,2,1,0:T(8,128)(2,1)S(1)}, bf16[2,2,128,128]{3,2,1,0:T(8,128)(2,1)S(1)}, u32[]{:S(2)}, u32[]{:S(2)}) collective-permute-start(bf16[2,2,128,128]{3,2,1,0:T(8,128)(2,1)S(1)} %combine_partner.1), channel_id=1, source_target_pairs={{0,32},{32,0},{1,33},{33,1},{2,34},{34,2},{3,35},{35,3},{4,36},{36... | collective-permute-start | bytes 393224 | tf_op jit(solution)/shard_map/ppermute | solution.py:376
